TPU v7x, 32 devices: a whole 2x2x4 slice. The times are simulated.
32 devices in a mesh: pack: 2 (over core), seq: 16 (over z, y, x).
Axes of the slice: x: 2, y: 2, z: 4, core: 2. Of those that a mesh axis runs over, the one named last changes fastest.
Arguments:
- hidden: bfloat16 [2, 8192, 1024], P('pack', 'seq'), may hold values from -6 to 6
- cotangent: bfloat16 [2, 8192, 1024], P('pack', 'seq'), may hold values from -6 to 6
- levels: int32 [2, 32], P('pack', 'seq'), may hold values from 0 to 999
- segments: int32 [2, 32], P('pack'), may hold values from 0 to 3, never falling along the last dimension, each value on 1 to 16 neighbouring positions
- live_frames: int32 [2, 32], P('pack'), may hold values 0 or 1
- noise_table: float32 [1000, 1024], replicated, may hold values from -6 to 6
- mod_weight: bfloat16 [1024, 6144], replicated, may hold values from -0.1875 to 0.1875
- mod_bias: float32 [6144], replicated, may hold values from -3 to 3
- qkv_weight: bfloat16 [1024, 3072], replicated, may hold values from -0.1875 to 0.1875
- qkv_bias: float32 [3072], replicated, may hold values from -3 to 3
- out_weight: bfloat16 [1024, 1024], replicated, may hold values from -3 to 3
- out_bias: float32 [1024], replicated, may hold values from -3 to 3
- up_weight: bfloat16 [1024, 4096], replicated, may hold values from -0.1875 to 0.1875
- up_bias: float32 [4096], replicated, may hold values from -3 to 3
- down_weight: bfloat16 [4096, 1024], replicated, may hold values from -0.09375 to 0.09375
- down_bias: float32 [1024], replicated, may hold values from -3 to 3
Outputs:
- layer_out: bfloat16 [2, 8192, 1024], P('pack', 'seq')
- hidden_grad: bfloat16 [2, 8192, 1024], P('pack', 'seq')
- table_grad: float32 [1000, 1024], P(None, 'seq')
- mod_weight_grad: float32 [1024, 6144], P('seq')
- mod_bias_grad: float32 [6144], P('seq')
- qkv_weight_grad: float32 [1024, 3072], P('seq')
- qkv_bias_grad: float32 [3072], P('seq')
- out_weight_grad: float32 [1024, 1024], P('seq')
- out_bias_grad: float32 [1024], P('seq')
- up_weight_grad: float32 [1024, 4096], P('seq')
- up_bias_grad: float32 [4096], P('seq')
- down_weight_grad: float32 [4096, 1024], P('seq')
- down_bias_grad: float32 [1024], P('seq')
Inputs may be any that keep to these rules, and one draw needn't show every extreme that they name: `segments`: in each pack, clip numbers never fall along the frames; each clip has at most 16 frames and one has exactly 16.
All inputs are finite; a program needn't handle non-finite values. No bound on the sum of `live_frames` on one device may be relied on, other than what follows from the above.
Results may differ from a plain program's by a relative error of at most 0.02.
Values may be sent and summed in bfloat16 or wider, within the bound.
No kernel may reach another device: no remote copies, remote signals or barrier semaphores. Data moves between devices by JAX's collectives and lax.ppermute only.
A program may use at most 320 MiB of HBM per device.

v0:
```python
import functools

import jax
import jax.numpy as jnp
from jax import lax
from jax.experimental import pallas as pl
from jax.experimental.pallas import tpu as pltpu
from jax.sharding import PartitionSpec as P

HEAD = 64
PATCHES = 256
SIDE = 16
EPSILON = 1e-06
PRECISE = lax.Precision.HIGHEST
HALF = HEAD // 2
F32 = jnp.float32
BF16 = jnp.bfloat16


def modulate_norm(rows, shift, scale):
    center = jnp.mean(rows, axis=-1, keepdims=True)
    centered = rows - center
    spread = jnp.mean(centered * centered, axis=-1, keepdims=True)
    normed = centered * lax.rsqrt(spread + EPSILON)
    return normed * (1.0 + scale[:, None, :]) + shift[:, None, :]


def gelu_tanh(values):
    return jax.nn.gelu(values, approximate=True)


def dot_over(first, second, first_dim, second_dim):
    return lax.dot_general(
        first, second, (((first_dim,), (second_dim,)), ((), ())), preferred_element_type=F32
    )


def spatial_angles():
    time_pairs = HALF // 4
    space_pairs = (HALF - time_pairs) // 2
    patch = jnp.arange(PATCHES, dtype=jnp.int32)
    row_pos = (patch // SIDE).astype(F32)
    col_pos = (patch % SIDE).astype(F32)
    time_freq = 10000.0 ** (-jnp.arange(time_pairs, dtype=F32) / time_pairs)
    space_freq = 10000.0 ** (-jnp.arange(space_pairs, dtype=F32) / space_pairs)
    space = jnp.concatenate(
        [space_freq[:, None] * row_pos[None, :], space_freq[:, None] * col_pos[None, :]], axis=0
    )
    return time_freq, space


def rotary_tables(time_frames):
    time_freq, space = spatial_angles()
    count = time_frames.shape[0]
    time_angle = time_frames[:, None] * time_freq[None, :]

    def whole(function):
        return jnp.concatenate(
            [
                jnp.broadcast_to(
                    function(time_angle)[:, :, None], (count, time_freq.shape[0], PATCHES)
                ),
                jnp.broadcast_to(function(space)[None], (count,) + space.shape),
            ],
            axis=1,
        )

    return whole(jnp.cos), whole(jnp.sin)


def walk_frames(frames, per_device, part, segments_ref, live_ref, list_ref, visit):
    def step(source, held):
        for place in range(per_device):
            frame = source * per_device + place
            before = jnp.maximum(frame - 1, 0)
            fresh = (frame == 0) | (segments_ref[frame] != segments_ref[before])
            held = jnp.where(fresh, 0, held)
            list_ref[held] = frame
            if place == part:
                visit(source, frame, held + 1)
            held = held + jnp.where(live_ref[frame] == 1, 1, 0)
        return held

    lax.fori_loop(0, frames // per_device, step, jnp.int32(0))


def attend_kernel(per_device, part, slot, segments_ref, live_ref, x_ref, q_ref, *refs):
    if part == 0:
        mix_ref, wide_ref, lse_ref, kv_ref, list_ref = refs
    else:
        kv_ref, mix_ref, wide_ref, lse_ref, list_ref = refs
    frames = kv_ref.shape[0]

    def turn(source, carry):
        for place in range(per_device):
            both = jnp.concatenate(
                [x_ref[source, place], x_ref[source, per_device + place]], axis=0
            )
            kv_ref[source * per_device + place] = both.astype(F32).T.astype(BF16)
        return carry

    if part == 0:
        lax.fori_loop(0, frames // per_device, turn, 0)

    def visit(source, frame, count):
        query = q_ref[source, slot]
        query_side = jnp.concatenate([query, jnp.zeros_like(query)], axis=0)

        def scores_of(other):
            return jnp.dot(kv_ref[other], query_side, preferred_element_type=F32)

        def mixed(other, weights):
            value = x_ref[lax.div(other, per_device), per_device + lax.rem(other, per_device)]
            return jnp.dot(value, weights.astype(BF16), preferred_element_type=F32)

        def join(others, carry):
            scores = [scores_of(other) for other in others]
            tops = [jnp.max(score, axis=0, keepdims=True) for score in scores]
            new_top = functools.reduce(jnp.maximum, tops)
            if carry is not None:
                top, total, accum = carry
                new_top = jnp.maximum(top, new_top)
                shrink = jnp.exp(top - new_top)
                total = total * shrink
                accum = accum * shrink
            for index, score in enumerate(scores):
                weights = jnp.exp(score - new_top)
                added = jnp.sum(weights, axis=0, keepdims=True)
                product = mixed(others[index], weights)
                if carry is None and index == 0:
                    total, accum = added, product
                else:
                    total, accum = total + added, accum + product
            return new_top, total, accum

        others = count - 1
        carry = join([frame], None)
        carry = lax.fori_loop(
            0,
            lax.div(others, 2),
            lambda index, state: join([list_ref[2 * index], list_ref[2 * index + 1]], state),
            carry,
        )
        top, total, accum = lax.fori_loop(
            0,
            lax.rem(others, 2),
            lambda unused, state: join([list_ref[others - 1]], state),
            carry,
        )
        result = accum * (1.0 / total)
        wide_ref[source] = result
        mix_ref[source] = result.astype(BF16)
        lse_ref[pl.ds(source, 1), :] = top + jnp.log(total)

    walk_frames(frames, per_device, part, segments_ref, live_ref, list_ref, visit)


def whole_spec():
    return pl.BlockSpec(memory_space=pltpu.VMEM)


def scalar_spec():
    return pl.BlockSpec(memory_space=pltpu.SMEM)


def attend(part, per_device, slot, segments, live, x, query, kv):
    sources = x.shape[0]
    frames = sources * per_device
    pairs = sources * 6
    outs = [
        jax.ShapeDtypeStruct((sources, HEAD, PATCHES), BF16),
        jax.ShapeDtypeStruct((sources, HEAD, PATCHES), F32),
        jax.ShapeDtypeStruct((sources, PATCHES), F32),
    ]
    args = [segments, live, x, query]
    if part == 0:
        outs.append(jax.ShapeDtypeStruct((frames, PATCHES, 2 * HEAD), BF16))
    else:
        args.append(kv)
    result = pl.pallas_call(
        functools.partial(attend_kernel, per_device, part, slot),
        out_shape=tuple(outs),
        in_specs=[scalar_spec(), scalar_spec()] + [whole_spec()] * (len(args) - 2),
        out_specs=(whole_spec(),) * len(outs),
        scratch_shapes=[pltpu.SMEM((frames,), jnp.int32)],
        cost_estimate=pl.CostEstimate(
            flops=pairs * 4 * PATCHES * PATCHES * 256,
            bytes_accessed=x.size * 2 * 3,
            transcendentals=pairs * PATCHES * PATCHES,
        ),
        compiler_params=pltpu.CompilerParams(vmem_limit_bytes=40 << 20),
        name="attend%d" % part,
    )(*args)
    return result if part == 0 else tuple(result) + (kv,)


def attend_back_kernel(
    per_device,
    part,
    slot,
    last,
    segments_ref,
    live_ref,
    x_ref,
    q_ref,
    kv_ref,
    wide_ref,
    lse_ref,
    d_mix_ref,
    cos_ref,
    sin_ref,
    *refs
):
    if last:
        before_ref, out_ref, dkv_ref, list_ref = refs
    else:
        out_ref, dkv_ref, list_ref = refs
    frames = kv_ref.shape[0]

    def clear(frame, carry):
        dkv_ref[frame] = jnp.zeros((PATCHES, 2 * HEAD), F32)
        return carry

    lax.fori_loop(0, frames, clear, 0)

    def unturn(frame, values):
        lower = values[:HALF]
        upper = values[HALF:]
        cosine = cos_ref[frame]
        sine = sin_ref[frame]
        return jnp.concatenate([lower * cosine + upper * sine, upper * cosine - lower * sine], axis=0)

    def visit(source, frame, count):
        query = q_ref[source, slot]
        d_mix = d_mix_ref[source]
        blank = jnp.zeros_like(query)
        query_side = jnp.concatenate([query, blank], axis=0)
        d_mix_side = jnp.concatenate([blank, d_mix], axis=0)
        both = jnp.concatenate(
            [query_side.astype(F32).T.astype(BF16), d_mix_side.astype(F32).T.astype(BF16)], axis=0
        )
        lse = lse_ref[pl.ds(source, 1), :]
        delta = jnp.sum(d_mix.astype(F32) * wide_ref[source], axis=0, keepdims=True)

        def block(other):
            key_value = kv_ref[other]
            scores = jnp.dot(key_value, query_side, preferred_element_type=F32)
            d_weights = jnp.dot(key_value, d_mix_side, preferred_element_type=F32)
            weights = jnp.exp(scores - lse)
            d_scores = (weights * (d_weights - delta)).astype(BF16)
            sides = jnp.concatenate([d_scores, weights.astype(BF16)], axis=1)
            dkv_ref[other] += jnp.dot(sides, both, preferred_element_type=F32)
            key = x_ref[lax.div(other, per_device), lax.rem(other, per_device)]
            return jnp.dot(key, d_scores, preferred_element_type=F32)

        d_query = lax.fori_loop(
            0,
            lax.div(count, 2),
            lambda index, state: state
            + block(list_ref[2 * index])
            + block(list_ref[2 * index + 1]),
            jnp.zeros((HEAD, PATCHES), F32),
        )
        d_query = lax.fori_loop(
            0,
            lax.rem(count, 2),
            lambda unused, state: state + block(list_ref[count - 1]),
            d_query,
        )
        d_query = unturn(frame, d_query * (HEAD**-0.5)).astype(BF16)
        if last:
            out_ref[source, 2 * per_device] = d_query
        else:
            out_ref[source] = d_query

    walk_frames(frames, per_device, part, segments_ref, live_ref, list_ref, visit)

    def finish(source, carry):
        for place in range(per_device):
            frame = source * per_device + place
            both = (dkv_ref[frame] + before_ref[frame]).T
            out_ref[source, place] = unturn(frame, both[:HEAD]).astype(BF16)
            out_ref[source, per_device + place] = both[HEAD:].astype(BF16)
        return carry

    if last:
        lax.fori_loop(0, frames // per_device, finish, 0)


def attend_back(
    part, per_device, slot, segments, live, x, query, kv, wide, lse, d_mix, cosine, sine, before
):
    sources = x.shape[0]
    frames = sources * per_device
    pairs = sources * 6
    last = part == per_device - 1
    args = [segments, live, x, query, kv, wide, lse, d_mix, cosine, sine]
    dkv = (frames, PATCHES, 2 * HEAD)
    lists = pltpu.SMEM((frames,), jnp.int32)
    if last:
        args.append(before)
        outs = jax.ShapeDtypeStruct((sources, 2 * per_device + 1, HEAD, PATCHES), BF16)
        out_specs = whole_spec()
        scratch = [pltpu.VMEM(dkv, F32), lists]
    else:
        outs = (
            jax.ShapeDtypeStruct((sources, HEAD, PATCHES), BF16),
            jax.ShapeDtypeStruct(dkv, F32),
        )
        out_specs = (whole_spec(), whole_spec())
        scratch = [lists]
    return pl.pallas_call(
        functools.partial(attend_back_kernel, per_device, part, slot, last),
        out_shape=outs,
        in_specs=[scalar_spec(), scalar_spec()] + [whole_spec()] * (len(args) - 2),
        out_specs=out_specs,
        scratch_shapes=scratch,
        cost_estimate=pl.CostEstimate(
            flops=pairs * 10 * PATCHES * PATCHES * 256,
            bytes_accessed=x.size * 2 * 5,
            transcendentals=pairs * PATCHES * PATCHES,
        ),
        compiler_params=pltpu.CompilerParams(vmem_limit_bytes=60 << 20),
        name="attend_back%d" % part,
    )(*args)


def exchange(value, axis, bit):
    count = lax.axis_size(axis)
    return lax.ppermute(value, axis, [(source, source ^ bit) for source in range(count)])


def after(value, *earlier):
    return lax.optimization_barrier((value,) + earlier)[0]


def gather_all(value):
    bit = lax.axis_size("seq") // 2
    while bit:
        value = jnp.concatenate([value, exchange(value, "seq", bit)], axis=0)
        bit //= 2
    bit = lax.axis_size("pack") // 2
    while bit:
        value = jnp.concatenate([value, exchange(value, "pack", bit)], axis=0)
        bit //= 2
    return value


def halving_fits():
    return lax.axis_size("pack") == 2 and lax.axis_size("seq") == 16


class RowSum:
    def __init__(self, term_of, rows, columns, order):
        self.direct = not halving_fits()
        self.rows, self.columns, self.order = rows, columns, list(order)
        if self.direct:
            part = lax.psum_scatter(
                term_of(0, columns).astype(BF16), "seq", scatter_dimension=0, tiled=True
            )
            self.value = lax.psum(part, "pack").astype(F32)
            return
        self.pack = lax.axis_index("pack")
        self.index = lax.axis_index("seq")
        self.width = columns // 2
        theirs = term_of((1 - self.pack) * self.width, self.width).astype(BF16)
        came = exchange(theirs, "pack", 1)
        mine = term_of(self.pack * self.width, self.width).astype(BF16)
        shape = [2, 2, 2, 2, rows // 16, self.width]
        self.parts = [mine.reshape(shape), came.reshape(shape)]

    def pick(self, bit, which):
        axis = {8: 0, 4: 1, 2: 2, 1: 3}[bit]
        pieces = [lax.dynamic_slice_in_dim(part, which, 1, axis) for part in self.parts]
        return (pieces[0].astype(F32) + pieces[1].astype(F32)).astype(BF16)

    def stage(self):
        if self.direct:
            return ()
        bit = self.order.pop(0)
        own_bit = lax.rem(lax.div(self.index, bit), 2)
        send = self.pick(bit, 1 - own_bit)
        came = exchange(send, "seq", bit)
        self.parts = [self.pick(bit, own_bit), came]
        return (send,)

    def finish(self):
        if self.direct:
            return self.value
        while self.order:
            self.stage()
        own = (self.parts[0].astype(F32) + self.parts[1].astype(F32)).astype(BF16)
        own = own.reshape(self.rows // 16, self.width)
        other = exchange(own, "pack", 1)
        left = jnp.where(self.pack == 0, own, other)
        right = jnp.where(self.pack == 0, other, own)
        return jnp.concatenate([left, right], axis=1).astype(F32)


def columns_of(matrix, start, width, axis=1):
    if isinstance(start, int) and start == 0 and width == matrix.shape[axis]:
        return matrix
    return lax.dynamic_slice_in_dim(matrix, start, width, axis)


def local(
    hidden,
    cotangent,
    levels,
    segments,
    live_frames,
    noise_table,
    mod_weight,
    mod_bias,
    qkv_weight,
    qkv_bias,
    out_weight,
    out_bias,
    up_weight,
    up_bias,
    down_weight,
    down_bias,
):
    seq_index = lax.axis_index("seq")
    seq_count = lax.axis_size("seq")
    tokens = hidden.shape[1]
    width = hidden.shape[2]
    per_device = tokens // PATCHES
    frames = segments.shape[1]
    heads = width // HEAD
    copies = seq_count // heads
    hidden_units = up_weight.shape[1]
    level_count = noise_table.shape[0]
    share = width // seq_count
    clip_ids = segments[0]
    live = live_frames[0]

    frame_ids = jnp.arange(frames, dtype=jnp.int32)
    same_clip = clip_ids[:, None] == clip_ids[None, :]
    clip_starts = jnp.min(jnp.where(same_clip, frame_ids[None, :], frames), axis=1)
    cos_all, sin_all = rotary_tables((frame_ids - clip_starts).astype(F32))
    first_frame = seq_index * per_device
    own_cos = lax.dynamic_slice_in_dim(cos_all, first_frame, per_device)
    own_sin = lax.dynamic_slice_in_dim(sin_all, first_frame, per_device)
    own_cos = own_cos.transpose(1, 0, 2).reshape(HALF, tokens)
    own_sin = own_sin.transpose(1, 0, 2).reshape(HALF, tokens)

    embed = jnp.concatenate(
        [
            lax.dynamic_slice_in_dim(noise_table, levels[0, frame], 1, 0)
            for frame in range(per_device)
        ],
        axis=0,
    )
    cond = jax.nn.silu(embed).astype(BF16)
    modulation = jnp.dot(cond, mod_weight, preferred_element_type=F32) + mod_bias
    attn_shift, attn_scale, attn_gate, feed_shift, feed_scale, feed_gate = jnp.split(
        modulation, 6, axis=1
    )
    frame_rows = hidden[0].astype(F32).reshape(per_device, PATCHES, width)
    attn_value, attn_norm_back = jax.vjp(modulate_norm, frame_rows, attn_shift, attn_scale)
    attn_in = attn_value.reshape(tokens, width).astype(BF16)

    qkv = dot_over(qkv_weight, attn_in, 0, 1) + qkv_bias[:, None]
    qkv = qkv.reshape(3, heads, 2, HALF, tokens)
    turned = qkv[:2]
    lower = turned[:, :, 0] * own_cos - turned[:, :, 1] * own_sin
    upper = turned[:, :, 1] * own_cos + turned[:, :, 0] * own_sin
    turned = jnp.stack([lower, upper], axis=2)

    def by_frame(array):
        split = array.astype(BF16).reshape(heads, HEAD, per_device, PATCHES)
        return [split[:, :, place] for place in range(per_device)]

    queries = by_frame(turned[0] * (HEAD**-0.5))
    keys = by_frame(turned[1])
    values = by_frame(qkv[2])
    sent = jnp.stack(keys + values + queries[:1], axis=1)

    def to_heads(array):
        if copies > 1:
            array = jnp.concatenate([array] * copies, axis=0)
        return lax.all_to_all(array, "seq", 0, 0, tiled=True)

    def to_tokens(array):
        return lax.all_to_all(array, "seq", 0, 0, tiled=True)[:heads]

    x = to_heads(sent)
    head_queries = [x] + [
        to_heads(after(query, x[0, 0, :8]).reshape(heads, 1, HEAD, PATCHES)) for query in queries[1:]
    ]
    slots = [2 * per_device] + [0] * (per_device - 1)
    kv = None
    attended = []
    mixes = []
    for part in range(per_device):
        mix, wide, lse, kv = attend(
            part, per_device, slots[part], clip_ids, live, x, head_queries[part], kv
        )
        attended.append((wide, lse))
        mixes.append(to_tokens(mix).reshape(width, PATCHES))
    attn_rows = jnp.stack([dot_over(mix, out_weight, 0, 0) for mix in mixes]) + out_bias
    attn_mix = jnp.concatenate(mixes, axis=1)

    middle = frame_rows + attn_gate[:, None, :] * attn_rows
    feed_value, feed_norm_back = jax.vjp(modulate_norm, middle, feed_shift, feed_scale)
    feed_in = feed_value.reshape(tokens, width).astype(BF16)
    pre = jnp.dot(feed_in, up_weight, preferred_element_type=F32) + up_bias
    act_value, act_back = jax.vjp(gelu_tanh, pre)
    act = act_value.astype(BF16)
    grad_rows = cotangent[0].astype(F32).reshape(per_device, PATCHES, width)
    d_feed_out = (feed_gate[:, None, :] * grad_rows).reshape(tokens, width).astype(BF16)
    d_pre = act_back(dot_over(d_feed_out, down_weight, 1, 1))[0].astype(BF16)
    down_sum = RowSum(
        lambda start, size: dot_over(act, columns_of(d_feed_out, start, size), 0, 0),
        hidden_units,
        width,
        (1, 2, 8, 4),
    )
    down_bias_term = jnp.sum(d_feed_out.astype(F32), axis=0)
    d_feed_in = dot_over(d_pre, up_weight, 1, 1).reshape(per_device, PATCHES, width)
    up_sum = RowSum(
        lambda start, size: dot_over(feed_in, columns_of(d_pre, start, size), 0, 0),
        width,
        hidden_units,
        (2, 1, 8, 4),
    )
    up_bias_term = jnp.sum(d_pre.astype(F32), axis=0)
    d_middle_norm, d_feed_shift, d_feed_scale = feed_norm_back(d_feed_in)
    d_middle = grad_rows + d_middle_norm
    d_attn_gate = jnp.sum(d_middle * attn_rows, axis=1)
    d_attn_rows = (attn_gate[:, None, :] * d_middle).astype(BF16)
    d_attn_out = d_attn_rows.reshape(tokens, width)
    d_mixes = []
    for part in range(per_device):
        d_mix = dot_over(out_weight, d_attn_rows[part], 1, 1).astype(BF16)
        d_mixes.append(to_heads(d_mix.reshape(heads, HEAD, PATCHES)))
    out_sum = RowSum(
        lambda start, size: dot_over(attn_mix, columns_of(d_attn_out, start, size), 1, 0),
        width,
        width,
        (1, 2, 8, 4),
    )
    out_bias_term = jnp.sum(d_attn_out.astype(F32), axis=0)

    feed_out = jnp.dot(act, down_weight, preferred_element_type=F32) + down_bias
    feed_rows = feed_out.reshape(per_device, PATCHES, width)
    layer_out = (middle + feed_gate[:, None, :] * feed_rows).reshape(1, tokens, width).astype(BF16)
    d_feed_gate = jnp.sum(grad_rows * feed_rows, axis=1)

    early_mod = jnp.concatenate([d_attn_gate, d_feed_shift, d_feed_scale, d_feed_gate], axis=1)
    own_levels = levels[0]
    early_bias = jnp.concatenate([out_bias_term, up_bias_term, down_bias_term])
    bias_rows = early_bias.reshape(per_device, early_bias.shape[0] // per_device)
    early = jnp.concatenate(
        [
            early_mod.astype(BF16),
            bias_rows.astype(BF16),
            jnp.broadcast_to(lax.div(own_levels, 32)[:, None], (per_device, 128)).astype(BF16),
            jnp.broadcast_to(lax.rem(own_levels, 32)[:, None], (per_device, 128)).astype(BF16),
        ],
        axis=1,
    )
    early_all = gather_all(early)

    before = None
    d_queries = []
    sums = (down_sum, up_sum, out_sum)
    for part in range(per_device):
        d_mix = after(d_mixes[part], *[send for each in sums for send in each.stage()])
        result = attend_back(
            part,
            per_device,
            slots[part],
            clip_ids,
            live,
            x,
            head_queries[part],
            kv,
            attended[part][0],
            attended[part][1],
            d_mix,
            cos_all,
            sin_all,
            before,
        )
        if part < per_device - 1:
            d_query, before = result
            d_queries.append(to_tokens(d_query))
    result = after(result, *[send for each in sums for send in each.stage()])
    back = to_tokens(result)
    d_queries.append(back[:, 2 * per_device])

    def joined(blocks):
        return jnp.stack(blocks, axis=2).reshape(width, tokens)

    d_qkv = jnp.concatenate(
        [
            joined(d_queries),
            joined([back[:, place] for place in range(per_device)]),
            joined([back[:, per_device + place] for place in range(per_device)]),
        ],
        axis=0,
    )
    d_attn_in = dot_over(d_qkv, qkv_weight, 0, 1).reshape(per_device, PATCHES, width)
    qkv_sum = RowSum(
        lambda start, size: dot_over(attn_in, columns_of(d_qkv, start, size, 0), 0, 1),
        width,
        3 * width,
        (1, 2, 8, 4),
    )
    d_hidden_norm, d_attn_shift, d_attn_scale = attn_norm_back(d_attn_in)
    hidden_grad = (d_middle + d_hidden_norm).reshape(1, tokens, width).astype(BF16)
    qkv_bias_term = jnp.sum(d_qkv.astype(F32), axis=1)
    late = jnp.concatenate(
        [
            d_attn_shift.astype(BF16),
            d_attn_scale.astype(BF16),
            qkv_bias_term.reshape(per_device, 3 * width // per_device).astype(BF16),
        ],
        axis=1,
    )
    late_all = gather_all(late)
    down_weight_grad = down_sum.finish()
    up_weight_grad = up_sum.finish()
    out_weight_grad = out_sum.finish()
    qkv_weight_grad = qkv_sum.finish()

    devices = late_all.shape[0] // per_device

    def bias_share(rows, sizes):
        flat = rows.reshape(devices, sum(sizes))
        shares = []
        at = 0
        for size in sizes:
            piece = size // seq_count
            own = lax.dynamic_slice_in_dim(flat, at + seq_index * piece, piece, 1)
            shares.append(jnp.sum(own.astype(F32), axis=0))
            at += size
        return shares

    early_width = 4 * width
    bias_width = early_bias.shape[0] // per_device
    out_bias_grad, up_bias_grad, down_bias_grad = bias_share(
        early_all[:, early_width : early_width + bias_width], (width, hidden_units, width)
    )
    (qkv_bias_grad,) = bias_share(late_all[:, 2 * width :], (3 * width,))
    coarse = early_all[:, early_width + bias_width].astype(jnp.int32)
    fine = early_all[:, early_width + bias_width + 128].astype(jnp.int32)
    all_levels = coarse * 32 + fine
    picks = (all_levels[:, None] == jnp.arange(level_count, dtype=jnp.int32)[None, :]).astype(F32)
    own_table = lax.dynamic_slice_in_dim(noise_table, seq_index * share, share, 1)
    all_embed = jnp.dot(picks, own_table, precision=PRECISE, preferred_element_type=F32)
    silu_value, silu_back = jax.vjp(jax.nn.silu, all_embed)
    all_cond = silu_value.astype(BF16)
    d_mod_early = early_all[:, :early_width]
    d_mod_late = late_all[:, : 2 * width]
    own_mod = lax.dynamic_slice_in_dim(mod_weight, seq_index * share, share, 0)
    d_cond_early = dot_over(d_mod_early, own_mod[:, 2 * width :], 1, 1)
    d_cond = d_cond_early + dot_over(d_mod_late, own_mod[:, : 2 * width], 1, 1)
    d_embed = silu_back(d_cond)[0]
    table_grad = lax.dot_general(
        picks, d_embed, (((0,), (0,)), ((), ())), precision=PRECISE, preferred_element_type=F32
    )
    mod_weight_grad = jnp.concatenate(
        [dot_over(all_cond, d_mod_late, 0, 0), dot_over(all_cond, d_mod_early, 0, 0)], axis=1
    )
    bias_piece = mod_bias.shape[0] // seq_count
    d_mod_sum = jnp.concatenate(
        [jnp.sum(d_mod_late.astype(F32), axis=0), jnp.sum(d_mod_early.astype(F32), axis=0)]
    )
    mod_bias_grad = lax.dynamic_slice_in_dim(d_mod_sum, seq_index * bias_piece, bias_piece)
    return (
        layer_out,
        hidden_grad,
        table_grad,
        mod_weight_grad,
        mod_bias_grad,
        qkv_weight_grad,
        qkv_bias_grad,
        out_weight_grad,
        out_bias_grad,
        up_weight_grad,
        up_bias_grad,
        down_weight_grad,
        down_bias_grad,
    )


def solution(mesh):
    in_specs = (
        P("pack", "seq", None),
        P("pack", "seq", None),
        P("pack", "seq"),
        P("pack", None),
        P("pack", None),
    ) + (P(),) * 11
    out_specs = (
        P("pack", "seq", None),
        P("pack", "seq", None),
        P(None, "seq"),
        P("seq", None),
        P("seq"),
        P("seq", None),
        P("seq"),
        P("seq", None),
        P("seq"),
        P("seq", None),
        P("seq"),
        P("seq", None),
        P("seq"),
    )
    return jax.shard_map(local, mesh=mesh, in_specs=in_specs, out_specs=out_specs, check_vma=False)
```

profile of v0, /device:TPU:0, one launch (start us, length us, event | category | flops | bytes accessed | tf_op | source)
XLA Modules:
  0.0 769.2 jit_solution(697618293220548098)
XLA Ops:
  10.0 6.5 convolution_add_fusion
  18.9 5.9 add_bitcast_fusion
  30.9 5.3 copy.73
  36.3 2.9 multiply_add_fusion
  45.0 4.0 reshape.636
  49.1 3.2 fusion.113
  52.3 2.8 copy.95
  55.1 2.8 copy.94
  57.8 4.2 fusion.114
  68.5 8.5 %all-to-all-start = ((bf16[16,5,64,256]{3,2,1,0:T(8,128)(2,1)}), bf16[16,5,64,256]{3,2,1,0:T(8,128)(2,1)}, u32[]{:S(2)}, u32[]{:S(2)}) async-start(bf16[16,5,64,256]{3,2,1,0:T(8,128)(2,1)} %fusion.42), calls=%async_computation | async-start | bytes 5242880 | tf_op jit(solution)/shard_map/all_to_all | solution.py:483
  78.0 51.0 %all-to-all-done.x_ref.q_ref = bf16[16,5,64,256]{3,2,1,0:T(8,128)(2,1)} async-done(((bf16[16,5,64,256]{3,2,1,0:T(8,128)(2,1)}), bf16[16,5,64,256]{3,2,1,0:T(8,128)(2,1)}, u32[]{:S(2)}, u32[]{:S(2)}) %all-to-all-start) | async-done | bytes 2621472 | tf_op jit(solution)/shard_map/all_to_all | solution.py:483
  129.0 12.5 %all-to-all-start.2 = ((bf16[16,1,64,256]{3,2,1,0:T(8,128)(2,1)}), bf16[16,1,64,256]{3,2,1,0:T(8,128)(2,1)S(1)}, u32[]{:S(2)}, u32[]{:S(2)}) async-start(bf16[16,1,64,256]{3,2,1,0:T(8,128)(2,1)} %bitcast.320), calls=%async_computation.2 | async-start | bytes 1048576 | tf_op jit(solution)/shard_map/all_to_all | solution.py:483
  141.5 24.4 %attend0.1 = (bf16[16,64,256]{2,1,0:T(8,128)(2,1)}, f32[16,64,256]{2,1,0:T(8,128)S(1)}, f32[16,256]{1,0:T(8,128)S(1)}, bf16[32,256,128]{2,1,0:T(8,128)(2,1)S(1)}) custom-call(s32[32]{0:T(128)S(1)} %bitcast.284, s32[32]{0:T(128)S(1)} %bitcast.288, bf16[16,5,64,256]{3,2,1,0:T(8,128)(2,1)} %all-to-all-done.x_ref.q_ref, ...), custom_call_target="tpu_custom_call" | custom-call | flops 6442450944 | bytes 7864320 | tf_op jit(solution)/shard_map/attend0/pallas_call | solution.py:180
  168.9 6.9 all-to-all-start.1
  177.4 26.4 %attend1.1 = (bf16[16,64,256]{2,1,0:T(8,128)(2,1)}, f32[16,64,256]{2,1,0:T(8,128)S(1)}, f32[16,256]{1,0:T(8,128)S(1)}) custom-call(s32[32]{0:T(128)S(1)} %bitcast.285, s32[32]{0:T(128)S(1)} %bitcast.289, bf16[16,5,64,256]{3,2,1,0:T(8,128)(2,1)} %all-to-all-done.x_ref.q_ref, bf16[16,1,64,256]{3,2,1,0:T(8,128)(2,1)S(1)} %all-to-all-done.2.q_ref, ...), custom_call_target="tpu_custom_call" | custom-call | flops 6442450944 | bytes 7864320 | tf_op jit(solution)/shard_map/attend1/pallas_call | solution.py:180
  205.3 7.5 all-to-all-start.3
  214.7 12.8 %all-to-all-done.3 = bf16[16,64,256]{2,1,0:T(8,128)(2,1)} async-done(((bf16[16,64,256]{2,1,0:T(8,128)(2,1)}), bf16[16,64,256]{2,1,0:T(8,128)(2,1)}, u32[]{:S(2)}, u32[]{:S(2)}) %all-to-all-start.3) | async-done | bytes 524320 | tf_op jit(solution)/shard_map/all_to_all | solution.py:486
  235.7 8.5 %multiply_convert_fusion = (bf16[512,4096]{1,0:T(8,128)(2,1)S(1)}, f32[512,4096]{1,0:T(8,128)}) fusion(f32[4096]{0:T(1024)S(1)} %copy-done.101, bf16[512,1024]{1,0:T(8,128)(2,1)S(1)} %fusion.17, bf16[1024,4096]{1,0:T(8,128)(2,1)S(1)} %bitcast.304), kind=kOutput, calls=%fused_computation.9 | convolution fusion | flops 4315938816 | bytes 22036480 | tf_op jit(solution)/shard_map/dot_general | solution.py:508
  244.2 4.4 convolution_convert_fusion
  248.7 13.2 %fusion.109 = (bf16[4096]{0:T(1024)(128)(2,1)}, bf16[512,4096]{1,0:T(8,128)(2,1)S(1)}) fusion(f32[512,4096]{1,0:T(8,128)} %get-tuple-element.128, f32[4096]{0:T(1024)S(1)} %copy-done.101, bf16[512,1024]{1,0:T(8,128)(2,1)S(1)} %copy-done.58, bf16[4096,1024]{1,0:T(8,128)(2,1)S(1)} %bitcast.301), kind=kOutput, calls=%fused_computation.301 | convolution fusion | flops 4341100544 | bytes 22044672 | tf_op jit(solution)/shard_map/dot_general | solution.py:33
  261.9 4.4 convolution_convert_fusion.4
  269.1 11.2 %bitcast_multiply_fusion = (f32[512,1024]{1,0:T(8,128)}, f32[512,1024]{1,0:T(8,128)}) fusion(f32[2,1024]{1,0:T(2,128)S(1)} %get-tuple-element.107, bf16[512,4096]{1,0:T(8,128)(2,1)} %copy-done.42, bf16[1024,4096]{1,0:T(8,128)(2,1)} %param.28), kind=kOutput, calls=%fused_computation.24 | convolution fusion | flops 4295491584 | bytes 16785408 | tf_op jit(solution)/shard_map/dot_general | solution.py:33
  280.3 3.5 fusion.25
  283.8 13.0 %fusion.112 = (f32[512]{0:T(512)S(1)}, f32[512,1024]{1,0:T(8,128)}, bf16[512,1024]{1,0:T(8,128)(2,1)}, f32[512,1024]{1,0:T(8,128)}) fusion(f32[512]{0:T(512)S(1)} %multiply_multiply_fusion.4, f32[512]{0:T(512)S(1)} %broadcast_multiply_fusion.2, f32[1024]{0:T(1024)S(1)} %copy-done.71, f32[2,256,1024]{2,1,0:T(8,128)} %copy-done.12, ...), kind=kOutput, calls=%fused_computation.302 | convolution fusion | flops 4302306816 | bytes 23101440 | tf_op jit(solution)/shard_map/dot_general | solution.py:546
  296.8 2.9 fusion.107
  299.8 3.2 convolution_convert_fusion.6
  305.5 2.7 multiply_convert_fusion.1
  312.8 4.2 all-to-all-start.4
  319.2 4.1 convolution_convert_fusion.5
  326.8 2.4 convolution_convert_fusion.1
  329.2 11.7 %collective-permute-done.5 = bf16[2,2,2,1,64,512]{5,4,3,2,1,0:T(8,128)(2,1)S(1)} collective-permute-done((bf16[2,2,2,1,64,512]{5,4,3,2,1,0:T(8,128)(2,1)S(1)}, bf16[2,2,2,1,64,512]{5,4,3,2,1,0:T(8,128)(2,1)S(1)}, u32[]{:S(2)}, u32[]{:S(2)}) %collective-permute-start.5) | collective-permute-done | bytes 524320 | tf_op jit(solution)/shard_map/ppermute | solution.py:330
  342.9 5.6 add_convert_fusion.1
  349.5 6.6 add_convert_fusion
  362.3 5.9 all-to-all-start.6
  368.2 30.7 %attend_back0.1 = (bf16[16,64,256]{2,1,0:T(8,128)(2,1)}, f32[32,256,128]{2,1,0:T(8,128)}) custom-call(s32[32]{0:T(128)} %bitcast.281, s32[32]{0:T(128)} %bitcast.286, bf16[16,5,64,256]{3,2,1,0:T(8,128)(2,1)} %all-to-all-done.x_ref.q_ref, bf16[16,5,64,256]{3,2,1,0:T(8,128)(2,1)} %all-to-all-done.x_ref.q_ref, bf16[32,256,128]{2,1,0:T(8,128)(2,1)} %copy-done.4, ...), custom_call_target="tpu_custom_call" | custom-call | flops 16106127360 | bytes 13107200 | tf_op jit(solution)/shard_map/attend_back0/pallas_call | solution.py:312
  400.4 4.3 add_convert_fusion.8
  405.9 3.3 collective-permute-done.4
  409.2 3.7 add_convert_fusion.7
  413.4 36.5 %attend_back1.1 = bf16[16,5,64,256]{3,2,1,0:T(8,128)(2,1)} custom-call(s32[32]{0:T(128)} %bitcast.282, s32[32]{0:T(128)} %bitcast.287, bf16[16,5,64,256]{3,2,1,0:T(8,128)(2,1)} %all-to-all-done.x_ref.q_ref, bf16[16,1,64,256]{3,2,1,0:T(8,128)(2,1)} %copy-done.1, bf16[32,256,128]{2,1,0:T(8,128)(2,1)} %copy-done.4, f32[16,64,256]{2,1,0:T(8,128)} %copy-done.6, ...), custom_call_target="tpu_custom_call" | custom-call | flops 16106127360 | bytes 13107200 | tf_op jit(solution)/shard_map/attend_back1/pallas_call | solution.py:312
  449.9 2.9 add_convert_fusion.13
  452.8 2.6 add_convert_fusion.14
  455.4 6.7 all-to-all-start.7
  464.3 2.8 collective-permute-start.25
  469.6 2.8 collective-permute-start.28
  472.4 74.8 %collective-permute-done.25 = bf16[1,2,1,1,64,512]{5,4,3,2,1,0:T(8,128)(2,1)S(1)} collective-permute-done((bf16[1,2,1,1,64,512]{5,4,3,2,1,0:T(8,128)(2,1)S(1)}, bf16[1,2,1,1,64,512]{5,4,3,2,1,0:T(8,128)(2,1)S(1)}, u32[]{:S(2)}, u32[]{:S(2)}) %collective-permute-start.25) | collective-permute-done | bytes 131104 | tf_op jit(solution)/shard_map/ppermute | solution.py:330
  551.8 18.2 %collective-permute-done.26 = bf16[1,1,1,1,64,512]{5,4,3,2,1,0:T(8,128)(2,1)S(1)} collective-permute-done((bf16[1,1,1,1,64,512]{5,4,3,2,1,0:T(8,128)(2,1)S(1)}, bf16[1,1,1,1,64,512]{5,4,3,2,1,0:T(8,128)(2,1)S(1)}, u32[]{:S(2)}, u32[]{:S(2)}) %collective-permute-start.26) | collective-permute-done | bytes 65568 | tf_op jit(solution)/shard_map/ppermute | solution.py:330
  574.6 6.0 collective-permute-done.32
  581.7 4.0 collective-permute-done.29
  589.2 4.6 all-to-all-start.5
  597.9 2.9 slice_bitcast_fusion.1
  603.2 6.1 all-to-all-done.5
  616.6 5.3 bitcast_multiply_fusion.4
  621.8 2.4 reduce_sum.271
  624.3 3.7 convolution_convert_fusion.2
  646.6 2.7 add_convert_fusion.5
  654.3 37.6 %collective-permute-done.17 = bf16[16,3584]{1,0:T(8,128)(2,1)} collective-permute-done((bf16[16,3584]{1,0:T(8,128)(2,1)S(1)}, bf16[16,3584]{1,0:T(8,128)(2,1)}, u32[]{:S(2)}, u32[]{:S(2)}) %collective-permute-start.17) | collective-permute-done | bytes 114720 | tf_op jit(solution)/shard_map/ppermute | solution.py:330
  691.9 4.5 concatenate.112
  696.4 3.1 concatenate.106
  700.0 4.4 fusion.39
  704.4 3.5 concatenate.113
  710.5 5.0 concatenate.107
  720.9 16.4 %collective-permute-done.21 = bf16[2,2,1,1,64,1536]{5,4,3,2,1,0:T(8,128)(2,1)S(1)} collective-permute-done((bf16[2,2,1,1,64,1536]{5,4,3,2,1,0:T(8,128)(2,1)S(1)}, bf16[2,2,1,1,64,1536]{5,4,3,2,1,0:T(8,128)(2,1)S(1)}, u32[]{:S(2)}, u32[]{:S(2)}) %collective-permute-start.21) | collective-permute-done | bytes 786464 | tf_op jit(solution)/shard_map/ppermute | solution.py:330
  745.7 12.5 %collective-permute-done.22 = bf16[1,2,1,1,64,1536]{5,4,3,2,1,0:T(8,128)(2,1)} collective-permute-done((bf16[1,2,1,1,64,1536]{5,4,3,2,1,0:T(8,128)(2,1)}, bf16[1,2,1,1,64,1536]{5,4,3,2,1,0:T(8,128)(2,1)}, u32[]{:S(2)}, u32[]{:S(2)}) %collective-permute-start.22) | collective-permute-done | bytes 393248 | tf_op jit(solution)/shard_map/ppermute | solution.py:330
  760.7 4.7 collective-permute-done.23
  (426 shorter events, 149.0 us)
Async XLA Ops:
  0.6 212.2 %copy-start = (bf16[1024,1024]{1,0:T(8,128)(2,1)S(1)}, bf16[1024,1024]{1,0:T(8,128)(2,1)}, u32[]{:S(2)}) copy-start(bf16[1024,1024]{1,0:T(8,128)(2,1)} %param.26) | copy-start | bytes 6291460
  0.7 9.3 %copy-start.88 = (f32[6144]{0:T(1024)S(1)}, f32[6144]{0:T(1024)}, u32[]{:S(2)}) copy-start(f32[6144]{0:T(1024)} %param.23) | copy-start | bytes 73732
  6.1 10.9 %copy-start.78 = (f32[512]{0:T(512)}, f32[512]{0:T(512)S(1)}, u32[]{:S(2)}) copy-start(f32[512]{0:T(512)S(1)} %broadcast_multiply_fusion.3) | copy-start | bytes 6148
  7.8 9.2 %copy-start.82 = (f32[512]{0:T(512)}, f32[512]{0:T(512)S(1)}, u32[]{:S(2)}) copy-start(f32[512]{0:T(512)S(1)} %fusion.93) | copy-start | bytes 6148
  17.0 266.8 %copy-start.74 = (f32[2,1024]{1,0:T(2,128)}, f32[2,1024]{1,0:T(2,128)S(1)}, u32[]{:S(2)}) copy-start(f32[2,1024]{1,0:T(2,128)S(1)} %get-tuple-element.105) | copy-start | bytes 24580
  68.5 60.5 %all-to-all-start = ((bf16[16,5,64,256]{3,2,1,0:T(8,128)(2,1)}), bf16[16,5,64,256]{3,2,1,0:T(8,128)(2,1)}, u32[]{:S(2)}, u32[]{:S(2)}) async-start(bf16[16,5,64,256]{3,2,1,0:T(8,128)(2,1)} %fusion.42), calls=%async_computation | async-start | bytes 5242880 | tf_op jit(solution)/shard_map/all_to_all | solution.py:483
  77.0 64.5 %copy-start.3 = (s32[1,32]{1,0:T(1,128)S(1)}, s32[1,32]{1,0:T(1,128)}, u32[]{:S(2)}) copy-start(s32[1,32]{1,0:T(1,128)} %param.20) | copy-start | bytes 388
  129.0 39.8 %all-to-all-start.2 = ((bf16[16,1,64,256]{3,2,1,0:T(8,128)(2,1)}), bf16[16,1,64,256]{3,2,1,0:T(8,128)(2,1)S(1)}, u32[]{:S(2)}, u32[]{:S(2)}) async-start(bf16[16,1,64,256]{3,2,1,0:T(8,128)(2,1)} %bitcast.320), calls=%async_computation.2 | async-start | bytes 1048576 | tf_op jit(solution)/shard_map/all_to_all | solution.py:483
  168.9 34.9 %copy-start.1 = (bf16[16,1,64,256]{3,2,1,0:T(8,128)(2,1)}, bf16[16,1,64,256]{3,2,1,0:T(8,128)(2,1)S(1)}, u32[]{:S(2)}) copy-start(bf16[16,1,64,256]{3,2,1,0:T(8,128)(2,1)S(1)} %all-to-all-done.2.q_ref) | copy-start | bytes 1572868
  168.9 36.5 %all-to-all-start.1 = ((bf16[16,64,256]{2,1,0:T(8,128)(2,1)}), bf16[16,64,256]{2,1,0:T(8,128)(2,1)S(1)}, u32[]{:S(2)}, u32[]{:S(2)}) async-start(bf16[16,64,256]{2,1,0:T(8,128)(2,1)} %get-tuple-element.25), calls=%async_computation.1 | async-start | bytes 1048576 | tf_op jit(solution)/shard_map/all_to_all | solution.py:486
  205.3 22.2 %all-to-all-start.3 = ((bf16[16,64,256]{2,1,0:T(8,128)(2,1)}), bf16[16,64,256]{2,1,0:T(8,128)(2,1)}, u32[]{:S(2)}, u32[]{:S(2)}) async-start(bf16[16,64,256]{2,1,0:T(8,128)(2,1)} %get-tuple-element.27), calls=%async_computation.3 | async-start | bytes 1048576 | tf_op jit(solution)/shard_map/all_to_all | solution.py:486
  214.7 14.6 %copy-start.22 = (f32[1,256,1024]{2,1,0:T(8,128)}, f32[1,256,1024]{2,1,0:T(8,128)S(1)}, u32[]{:S(2)}) copy-start(f32[1,256,1024]{2,1,0:T(8,128)S(1)} %convolution_bitcast_fusion.1) | copy-start | bytes 3145732
  234.0 14.7 %slice-start = ((s8[8388608]{0:T(1024)(128)(4,1)}), s8[4194304]{0:T(1024)(128)(4,1)S(1)}, s32[]{:S(2)}) async-start(s8[8388608]{0:T(1024)(128)(4,1)} %bitcast.300), calls=%async_computation.8 | async-start | bytes 8388608
  235.7 13.0 %slice-start.1 = ((s8[8388608]{0:T(1024)(128)(4,1)}), s8[4194304]{0:T(1024)(128)(4,1)S(1)}, s32[]{:S(2)}) async-start(s8[8388608]{0:T(1024)(128)(4,1)} %bitcast.300), calls=%async_computation.9 | async-start | bytes 8388608
  248.7 94.2 %collective-permute-start = (bf16[4096,512]{1,0:T(8,128)(2,1)}, bf16[4096,512]{1,0:T(8,128)(2,1)}, u32[]{:S(2)}, u32[]{:S(2)}) collective-permute-start(bf16[4096,512]{1,0:T(8,128)(2,1)} %convolution_convert_fusion), channel_id=1, source_target_pairs={{0,16},{16,0},{1,17},{17,1},{2,18},{18,2},{3,19},{19,3},{4,20},{20... | collective-permute-start | bytes 12582920 | tf_op jit(solution)/shard_map/ppermute | solution.py:330
  248.7 13.2 %copy-start.64 = (bf16[512,1024]{1,0:T(8,128)(2,1)S(1)}, bf16[512,1024]{1,0:T(8,128)(2,1)}, u32[]{:S(2)}) copy-start(bf16[512,1024]{1,0:T(8,128)(2,1)} %copy-done.63) | copy-start | bytes 3145732
  266.4 83.2 %collective-permute-start.1 = (bf16[1024,2048]{1,0:T(8,128)(2,1)}, bf16[1024,2048]{1,0:T(8,128)(2,1)}, u32[]{:S(2)}, u32[]{:S(2)}) collective-permute-start(bf16[1024,2048]{1,0:T(8,128)(2,1)} %convolution_convert_fusion.4), channel_id=1, source_target_pairs={{0,16},{16,0},{1,17},{17,1},{2,18},{18,2},{3,19},{19,3},{4,20},{20... | collective-permute-start | bytes 12582920 | tf_op jit(solution)/shard_map/ppermute | solution.py:330
  269.1 35.6 %copy-start.90 = (f32[2,256]{1,0:T(2,128)}, f32[2,256]{1,0:T(2,128)S(1)}, u32[]{:S(2)}) copy-start(f32[2,256]{1,0:T(2,128)S(1)} %div.133) | copy-start | bytes 6148
  303.0 20.4 %collective-permute-start.2 = (bf16[1024,512]{1,0:T(8,128)(2,1)}, bf16[1024,512]{1,0:T(8,128)(2,1)}, u32[]{:S(2)}, u32[]{:S(2)}) collective-permute-start(bf16[1024,512]{1,0:T(8,128)(2,1)} %convolution_convert_fusion.6), channel_id=1, source_target_pairs={{0,16},{16,0},{1,17},{17,1},{2,18},{18,2},{3,19},{19,3},{4,20},{20... | collective-permute-start | bytes 3145736 | tf_op jit(solution)/shard_map/ppermute | solution.py:330
  312.8 49.5 %all-to-all-start.4 = ((bf16[16,64,256]{2,1,0:T(8,128)(2,1)}), bf16[16,64,256]{2,1,0:T(8,128)(2,1)}, u32[]{:S(2)}, u32[]{:S(2)}) async-start(bf16[16,64,256]{2,1,0:T(8,128)(2,1)} %bitcast.321), calls=%async_computation.4 | async-start | bytes 1048576 | tf_op jit(solution)/shard_map/all_to_all | solution.py:483
  325.0 15.9 %collective-permute-start.5 = (bf16[2,2,2,1,64,512]{5,4,3,2,1,0:T(8,128)(2,1)S(1)}, bf16[2,2,2,1,64,512]{5,4,3,2,1,0:T(8,128)(2,1)S(1)}, u32[]{:S(2)}, u32[]{:S(2)}) collective-permute-start(bf16[2,2,2,1,64,512]{5,4,3,2,1,0:T(8,128)(2,1)S(1)} %get-tuple-element.84), channel_id=1, source_target_pairs={{0,1},{1,0},{2,3},{3,2},{4,5},{5,4},{6,7},{7,6},{8,9},{9,8},{10,11... | collective-permute-start | bytes 1572872 | tf_op jit(solution)/shard_map/ppermute | solution.py:330
  341.7 18.9 %collective-permute-start.8 = (bf16[2,2,1,1,64,512]{5,4,3,2,1,0:T(8,128)(2,1)}, bf16[2,2,1,1,64,512]{5,4,3,2,1,0:T(8,128)(2,1)}, u32[]{:S(2)}, u32[]{:S(2)}) collective-permute-start(bf16[2,2,1,1,64,512]{5,4,3,2,1,0:T(8,128)(2,1)} %get-tuple-element.90), channel_id=1, source_target_pairs={{0,2},{1,3},{2,0},{3,1},{4,6},{5,7},{6,4},{7,5},{8,10},{9,11},{10,... | collective-permute-start | bytes 786440 | tf_op jit(solution)/shard_map/ppermute | solution.py:330
  348.4 51.9 %collective-permute-start.3 = (bf16[2,2,2,1,256,512]{5,4,3,2,1,0:T(8,128)(2,1)}, bf16[2,2,2,1,256,512]{5,4,3,2,1,0:T(8,128)(2,1)}, u32[]{:S(2)}, u32[]{:S(2)}) collective-permute-start(bf16[2,2,2,1,256,512]{5,4,3,2,1,0:T(8,128)(2,1)} %get-tuple-element.60), channel_id=1, source_target_pairs={{0,1},{1,0},{2,3},{3,2},{4,5},{5,4},{6,7},{7,6},{8,9},{9,8},{10,11... | collective-permute-start | bytes 6291464 | tf_op jit(solution)/shard_map/ppermute | solution.py:330
  356.2 53.1 %collective-permute-start.4 = (bf16[2,2,1,2,64,2048]{5,4,3,2,1,0:T(8,128)(2,1)}, bf16[2,2,1,2,64,2048]{5,4,3,2,1,0:T(8,128)(2,1)}, u32[]{:S(2)}, u32[]{:S(2)}) collective-permute-start(bf16[2,2,1,2,64,2048]{5,4,3,2,1,0:T(8,128)(2,1)} %get-tuple-element.58), channel_id=1, source_target_pairs={{0,2},{1,3},{2,0},{3,1},{4,6},{5,7},{6,4},{7,5},{8,10},{9,11},{10,... | collective-permute-start | bytes 6291464 | tf_op jit(solution)/shard_map/ppermute | solution.py:330
  362.3 51.1 %all-to-all-start.6 = ((bf16[16,64,256]{2,1,0:T(8,128)(2,1)}), bf16[16,64,256]{2,1,0:T(8,128)(2,1)}, u32[]{:S(2)}, u32[]{:S(2)}) async-start(bf16[16,64,256]{2,1,0:T(8,128)(2,1)} %bitcast.322), calls=%async_computation.6 | async-start | bytes 1048576 | tf_op jit(solution)/shard_map/all_to_all | solution.py:483
  400.4 8.8 %copy-start.28 = (bf16[2,2,1,2,64,2048]{5,4,3,2,1,0:T(8,128)(2,1)S(1)}, bf16[2,2,1,2,64,2048]{5,4,3,2,1,0:T(8,128)(2,1)}, u32[]{:S(2)}) copy-start(bf16[2,2,1,2,64,2048]{5,4,3,2,1,0:T(8,128)(2,1)} %get-tuple-element.57) | copy-start | bytes 6291460
  404.7 45.1 %collective-permute-start.6 = (bf16[2,2,1,1,256,512]{5,4,3,2,1,0:T(8,128)(2,1)}, bf16[2,2,1,1,256,512]{5,4,3,2,1,0:T(8,128)(2,1)}, u32[]{:S(2)}, u32[]{:S(2)}) collective-permute-start(bf16[2,2,1,1,256,512]{5,4,3,2,1,0:T(8,128)(2,1)} %get-tuple-element.68), channel_id=1, source_target_pairs={{0,2},{1,3},{2,0},{3,1},{4,6},{5,7},{6,4},{7,5},{8,10},{9,11},{10,... | collective-permute-start | bytes 3145736 | tf_op jit(solution)/shard_map/ppermute | solution.py:330
  412.9 39.9 %collective-permute-start.7 = (bf16[2,2,1,1,64,2048]{5,4,3,2,1,0:T(8,128)(2,1)}, bf16[2,2,1,1,64,2048]{5,4,3,2,1,0:T(8,128)(2,1)}, u32[]{:S(2)}, u32[]{:S(2)}) collective-permute-start(bf16[2,2,1,1,64,2048]{5,4,3,2,1,0:T(8,128)(2,1)} %get-tuple-element.66), channel_id=1, source_target_pairs={{0,1},{1,0},{2,3},{3,2},{4,5},{5,4},{6,7},{7,6},{8,9},{9,8},{10,11... | collective-permute-start | bytes 3145736 | tf_op jit(solution)/shard_map/ppermute | solution.py:330
  455.4 133.8 %all-to-all-start.7 = ((bf16[16,5,64,256]{3,2,1,0:T(8,128)(2,1)}), bf16[16,5,64,256]{3,2,1,0:T(8,128)(2,1)}, u32[]{:S(2)}, u32[]{:S(2)}) async-start(bf16[16,5,64,256]{3,2,1,0:T(8,128)(2,1)} %attend_back1.1), calls=%async_computation.7 | async-start | bytes 5242880 | tf_op jit(solution)/shard_map/all_to_all | solution.py:486
  464.3 82.9 %collective-permute-start.25 = (bf16[1,2,1,1,64,512]{5,4,3,2,1,0:T(8,128)(2,1)S(1)}, bf16[1,2,1,1,64,512]{5,4,3,2,1,0:T(8,128)(2,1)S(1)}, u32[]{:S(2)}, u32[]{:S(2)}) collective-permute-start(bf16[1,2,1,1,64,512]{5,4,3,2,1,0:T(8,128)(2,1)S(1)} %copy-done.76), channel_id=1, source_target_pairs={{0,8},{1,9},{2,10},{3,11},{4,12},{5,13},{6,14},{7,15},{8,0},{9,1},... | collective-permute-start | bytes 393224 | tf_op jit(solution)/shard_map/ppermute | solution.py:330
  467.1 103.1 %collective-permute-start.31 = (bf16[1,2,1,1,256,512]{5,4,3,2,1,0:T(8,128)(2,1)}, bf16[1,2,1,1,256,512]{5,4,3,2,1,0:T(8,128)(2,1)}, u32[]{:S(2)}, u32[]{:S(2)}) collective-permute-start(bf16[1,2,1,1,256,512]{5,4,3,2,1,0:T(8,128)(2,1)} %get-tuple-element.80), channel_id=1, source_target_pairs={{0,8},{1,9},{2,10},{3,11},{4,12},{5,13},{6,14},{7,15},{8,0},{9,1},... | collective-permute-start | bytes 1572872 | tf_op jit(solution)/shard_map/ppermute | solution.py:330
  469.6 101.7 %collective-permute-start.28 = (bf16[1,2,1,1,64,2048]{5,4,3,2,1,0:T(8,128)(2,1)}, bf16[1,2,1,1,64,2048]{5,4,3,2,1,0:T(8,128)(2,1)}, u32[]{:S(2)}, u32[]{:S(2)}) collective-permute-start(bf16[1,2,1,1,64,2048]{5,4,3,2,1,0:T(8,128)(2,1)} %get-tuple-element.82), channel_id=1, source_target_pairs={{0,8},{1,9},{2,10},{3,11},{4,12},{5,13},{6,14},{7,15},{8,0},{9,1},... | collective-permute-start | bytes 1572872 | tf_op jit(solution)/shard_map/ppermute | solution.py:330
  547.2 22.9 %collective-permute-start.26 = (bf16[1,1,1,1,64,512]{5,4,3,2,1,0:T(8,128)(2,1)S(1)}, bf16[1,1,1,1,64,512]{5,4,3,2,1,0:T(8,128)(2,1)S(1)}, u32[]{:S(2)}, u32[]{:S(2)}) collective-permute-start(bf16[1,1,1,1,64,512]{5,4,3,2,1,0:T(8,128)(2,1)S(1)} %add_convert_fusion.35), channel_id=1, source_target_pairs={{0,4},{1,5},{2,6},{3,7},{4,0},{5,1},{6,2},{7,3},{8,12},{9,13},{10,... | collective-permute-start | bytes 196616 | tf_op jit(solution)/shard_map/ppermute | solution.py:330
  551.8 28.7 %copy-start.52 = (bf16[1,2,1,1,256,512]{5,4,3,2,1,0:T(8,128)(2,1)S(1)}, bf16[1,2,1,1,256,512]{5,4,3,2,1,0:T(8,128)(2,1)}, u32[]{:S(2)}) copy-start(bf16[1,2,1,1,256,512]{5,4,3,2,1,0:T(8,128)(2,1)} %get-tuple-element.79) | copy-start | bytes 1572868
  551.8 33.9 %copy-start.51 = (bf16[1,2,1,1,64,2048]{5,4,3,2,1,0:T(8,128)(2,1)S(1)}, bf16[1,2,1,1,64,2048]{5,4,3,2,1,0:T(8,128)(2,1)}, u32[]{:S(2)}) copy-start(bf16[1,2,1,1,64,2048]{5,4,3,2,1,0:T(8,128)(2,1)} %get-tuple-element.81) | copy-start | bytes 1572868
  570.1 4.5 collective-permute-start.27
  571.3 9.2 %collective-permute-start.32 = (bf16[1,1,1,1,256,512]{5,4,3,2,1,0:T(8,128)(2,1)S(1)}, bf16[1,1,1,1,256,512]{5,4,3,2,1,0:T(8,128)(2,1)S(1)}, u32[]{:S(2)}, u32[]{:S(2)}) collective-permute-start(bf16[1,1,1,1,256,512]{5,4,3,2,1,0:T(8,128)(2,1)S(1)} %add_convert_fusion.22), channel_id=1, source_target_pairs={{0,4},{1,5},{2,6},{3,7},{4,0},{5,1},{6,2},{7,3},{8,12},{9,13},{10,... | collective-permute-start | bytes 786440 | tf_op jit(solution)/shard_map/ppermute | solution.py:330
  572.5 13.2 %collective-permute-start.29 = (bf16[1,1,1,1,64,2048]{5,4,3,2,1,0:T(8,128)(2,1)S(1)}, bf16[1,1,1,1,64,2048]{5,4,3,2,1,0:T(8,128)(2,1)S(1)}, u32[]{:S(2)}, u32[]{:S(2)}) collective-permute-start(bf16[1,1,1,1,64,2048]{5,4,3,2,1,0:T(8,128)(2,1)S(1)} %add_convert_fusion.25), channel_id=1, source_target_pairs={{0,4},{1,5},{2,6},{3,7},{4,0},{5,1},{6,2},{7,3},{8,12},{9,13},{10,... | collective-permute-start | bytes 786440 | tf_op jit(solution)/shard_map/ppermute | solution.py:330
  581.6 5.9 collective-permute-start.33
  586.7 1.6 collective-permute-start.30
  589.2 20.2 %all-to-all-start.5 = ((bf16[16,64,256]{2,1,0:T(8,128)(2,1)}), bf16[16,64,256]{2,1,0:T(8,128)(2,1)}, u32[]{:S(2)}, u32[]{:S(2)}) async-start(bf16[16,64,256]{2,1,0:T(8,128)(2,1)} %get-tuple-element.31), calls=%async_computation.5 | async-start | bytes 1048576 | tf_op jit(solution)/shard_map/all_to_all | solution.py:486
  624.2 19.6 %copy-start.72 = (bf16[2,1536]{1,0:T(2,128)(2,1)}, bf16[2,1536]{1,0:T(2,128)(2,1)S(1)}, u32[]{:S(2)}) copy-start(bf16[2,1536]{1,0:T(2,128)(2,1)S(1)} %convert_element_type.664) | copy-start | bytes 18436
  634.9 10.8 %copy-start.77 = (bf16[2,3584]{1,0:T(2,128)(2,1)}, bf16[2,3584]{1,0:T(2,128)(2,1)S(1)}, u32[]{:S(2)}) copy-start(bf16[2,3584]{1,0:T(2,128)(2,1)S(1)} %pad_maximum_fusion.18) | copy-start | bytes 43012
  634.9 4.7 collective-permute-start.14
  635.9 10.7 %collective-permute-start.19 = (bf16[1024,1536]{1,0:T(8,128)(2,1)S(1)}, bf16[1024,1536]{1,0:T(8,128)(2,1)S(1)}, u32[]{:S(2)}, u32[]{:S(2)}) collective-permute-start(bf16[1024,1536]{1,0:T(8,128)(2,1)S(1)} %convolution_convert_fusion.2), channel_id=1, source_target_pairs={{0,16},{16,0},{1,17},{17,1},{2,18},{18,2},{3,19},{19,3},{4,20},{20... | collective-permute-start | bytes 9437192 | tf_op jit(solution)/shard_map/ppermute | solution.py:330
  636.2 5.1 collective-permute-start.9
  639.6 4.2 collective-permute-start.15
  641.3 9.4 %copy-start.68 = (bf16[2,7424]{1,0:T(2,128)(2,1)}, bf16[2,7424]{1,0:T(2,128)(2,1)S(1)}, u32[]{:S(2)}) copy-start(bf16[2,7424]{1,0:T(2,128)(2,1)S(1)} %collective-permute-done.9) | copy-start | bytes 89092
  641.4 4.3 collective-permute-start.10
  643.9 9.3 %copy-start.70 = (bf16[4,3584]{1,0:T(4,128)(2,1)}, bf16[4,3584]{1,0:T(4,128)(2,1)S(1)}, u32[]{:S(2)}) copy-start(bf16[4,3584]{1,0:T(4,128)(2,1)S(1)} %collective-permute-done.15) | copy-start | bytes 86020
  643.9 9.2 %collective-permute-start.16 = (bf16[8,3584]{1,0:T(8,128)(2,1)S(1)}, bf16[8,3584]{1,0:T(8,128)(2,1)S(1)}, u32[]{:S(2)}, u32[]{:S(2)}) collective-permute-start(bf16[8,3584]{1,0:T(8,128)(2,1)S(1)} %pad_maximum_fusion.15), channel_id=1, source_target_pairs={{0,2},{1,3},{2,0},{3,1},{4,6},{5,7},{6,4},{7,5},{8,10},{9,11},{10,... | collective-permute-start | bytes 172040 | tf_op jit(solution)/shard_map/ppermute | solution.py:330
  645.8 4.9 collective-permute-start.11
  649.4 66.1 %collective-permute-start.20 = (bf16[2,2,2,1,64,1536]{5,4,3,2,1,0:T(8,128)(2,1)}, bf16[2,2,2,1,64,1536]{5,4,3,2,1,0:T(8,128)(2,1)}, u32[]{:S(2)}, u32[]{:S(2)}) collective-permute-start(bf16[2,2,2,1,64,1536]{5,4,3,2,1,0:T(8,128)(2,1)} %get-tuple-element.62), channel_id=1, source_target_pairs={{0,1},{1,0},{2,3},{3,2},{4,5},{5,4},{6,7},{7,6},{8,9},{9,8},{10,11... | collective-permute-start | bytes 4718600 | tf_op jit(solution)/shard_map/ppermute | solution.py:330
  650.7 53.7 %copy-start.54 = (bf16[8,7424]{1,0:T(8,128)(2,1)}, bf16[8,7424]{1,0:T(8,128)(2,1)S(1)}, u32[]{:S(2)}) copy-start(bf16[8,7424]{1,0:T(8,128)(2,1)S(1)} %collective-permute-done.11) | copy-start | bytes 356356
  651.5 44.9 %collective-permute-start.12 = (bf16[16,7424]{1,0:T(8,128)(2,1)}, bf16[16,7424]{1,0:T(8,128)(2,1)S(1)}, u32[]{:S(2)}, u32[]{:S(2)}) collective-permute-start(bf16[16,7424]{1,0:T(8,128)(2,1)} %pad_maximum_fusion.11), channel_id=1, source_target_pairs={{0,1},{1,0},{2,3},{3,2},{4,5},{5,4},{6,7},{7,6},{8,9},{9,8},{10,11... | collective-permute-start | bytes 712712 | tf_op jit(solution)/shard_map/ppermute | solution.py:330
  653.8 38.1 %collective-permute-start.17 = (bf16[16,3584]{1,0:T(8,128)(2,1)S(1)}, bf16[16,3584]{1,0:T(8,128)(2,1)}, u32[]{:S(2)}, u32[]{:S(2)}) collective-permute-start(bf16[16,3584]{1,0:T(8,128)(2,1)S(1)} %pad_maximum_fusion.13), channel_id=1, source_target_pairs={{0,1},{1,0},{2,3},{3,2},{4,5},{5,4},{6,7},{7,6},{8,9},{9,8},{10,11... | collective-permute-start | bytes 344072 | tf_op jit(solution)/shard_map/ppermute | solution.py:330
  696.4 8.0 %collective-permute-start.18 = (bf16[32,3584]{1,0:T(8,128)(2,1)}, bf16[32,3584]{1,0:T(8,128)(2,1)}, u32[]{:S(2)}, u32[]{:S(2)}) collective-permute-start(bf16[32,3584]{1,0:T(8,128)(2,1)} %concatenate.112), channel_id=1, source_target_pairs={{0,16},{16,0},{1,17},{17,1},{2,18},{18,2},{3,19},{19,3},{4,20},{20... | collective-permute-start | bytes 688136 | tf_op jit(solution)/shard_map/ppermute | solution.py:330
  699.5 11.0 %collective-permute-start.13 = (bf16[32,7424]{1,0:T(8,128)(2,1)}, bf16[32,7424]{1,0:T(8,128)(2,1)}, u32[]{:S(2)}, u32[]{:S(2)}) collective-permute-start(bf16[32,7424]{1,0:T(8,128)(2,1)} %concatenate.106), channel_id=1, source_target_pairs={{0,16},{16,0},{1,17},{17,1},{2,18},{18,2},{3,19},{19,3},{4,20},{20... | collective-permute-start | bytes 1425416 | tf_op jit(solution)/shard_map/ppermute | solution.py:330
  717.8 19.5 %collective-permute-start.21 = (bf16[2,2,1,1,64,1536]{5,4,3,2,1,0:T(8,128)(2,1)S(1)}, bf16[2,2,1,1,64,1536]{5,4,3,2,1,0:T(8,128)(2,1)S(1)}, u32[]{:S(2)}, u32[]{:S(2)}) collective-permute-start(bf16[2,2,1,1,64,1536]{5,4,3,2,1,0:T(8,128)(2,1)S(1)} %get-tuple-element.73), channel_id=1, source_target_pairs={{0,2},{1,3},{2,0},{3,1},{4,6},{5,7},{6,4},{7,5},{8,10},{9,11},{10,... | collective-permute-start | bytes 2359304 | tf_op jit(solution)/shard_map/ppermute | solution.py:330
  738.4 19.8 %collective-permute-start.22 = (bf16[1,2,1,1,64,1536]{5,4,3,2,1,0:T(8,128)(2,1)}, bf16[1,2,1,1,64,1536]{5,4,3,2,1,0:T(8,128)(2,1)}, u32[]{:S(2)}, u32[]{:S(2)}) collective-permute-start(bf16[1,2,1,1,64,1536]{5,4,3,2,1,0:T(8,128)(2,1)} %get-tuple-element.88), channel_id=1, source_target_pairs={{0,8},{1,9},{2,10},{3,11},{4,12},{5,13},{6,14},{7,15},{8,0},{9,1},... | collective-permute-start | bytes 1179656 | tf_op jit(solution)/shard_map/ppermute | solution.py:330
  741.3 18.1 %copy-start.87 = (f32[64,64]{1,0:T(8,128)S(1)}, f32[64,64]{1,0:T(8,128)}, u32[]{:S(2)}) copy-start(f32[64,64]{1,0:T(8,128)} %fusion.57) | copy-start | bytes 49156
  742.3 23.2 %copy-start.53 = (bf16[1,2,1,1,64,1536]{5,4,3,2,1,0:T(8,128)(2,1)S(1)}, bf16[1,2,1,1,64,1536]{5,4,3,2,1,0:T(8,128)(2,1)}, u32[]{:S(2)}) copy-start(bf16[1,2,1,1,64,1536]{5,4,3,2,1,0:T(8,128)(2,1)} %get-tuple-element.87) | copy-start | bytes 1179652
  759.3 6.1 collective-permute-start.23
  766.5 1.5 collective-permute-start.24
  (89 other events, 287.6 us)
where the time goes:
time: 771 us; the launch traced here: 769 us
  waiting for transfers between devices  265 us (34%)
  Pallas kernels  118 us (15%)
  matrix products  103 us (13%)
  other arithmetic  96.9 us (13%)
  local copies, waits for them, and re-layouts  92.2 us (12%)
  starting transfers between devices  88.6 us (11%)
    ppermute x34, waiting for transfers between devices, exchange(): lax.ppermute(value, axis, [(source, source ^ bit) for source in range(cou...  195 us
    dot_general x20, matrix products, dot_over(): lax.dot_general(first, second, (((first_dim,), (second_dim,)), ((), ())),...  72.2 us
    pallas_call x2, Pallas kernels, attend_back(): pl.pallas_call(functools.partial(attend_back_kernel, per_device, part, sl...  67.2 us
    all_to_all x4, waiting for transfers between devices, to_heads(): return lax.all_to_all(array, 'seq', 0, 0, tiled=True)  51.1 us
    pallas_call x2, Pallas kernels, attend(): pl.pallas_call(functools.partial(attend_kernel, per_device, part, slot),...  50.8 us
    convert_element_type x16, other arithmetic, pick(): return (pieces[0].astype(F32) + pieces[1].astype(F32)).astype(BF16)  39.3 us
    unnamed x240, local copies, waits for them, and re-layouts  32 us
    ppermute x34, starting transfers between devices, exchange(): lax.ppermute(value, axis, [(source, source ^ bit) for source in range(cou...  31.7 us
  transfers between devices with their start and end apart: 42, of which 20 were waited for; matrix products, arithmetic and copies ran while one was open for 21% of the time, Pallas kernels for 15%

commit v1 on v0

--- a/solution.py
+++ b/solution.py
@@ -351,50 +351,357 @@
 
 
 class RowSum:
-    def __init__(self, term_of, rows, columns, order):
-        self.direct = not halving_fits()
-        self.rows, self.columns, self.order = rows, columns, list(order)
-        if self.direct:
-            part = lax.psum_scatter(
-                term_of(0, columns).astype(BF16), "seq", scatter_dimension=0, tiled=True
-            )
-            self.value = lax.psum(part, "pack").astype(F32)
-            return
-        self.pack = lax.axis_index("pack")
+    def __init__(self, mine, came, order):
+        self.order = list(order)
         self.index = lax.axis_index("seq")
-        self.width = columns // 2
-        theirs = term_of((1 - self.pack) * self.width, self.width).astype(BF16)
-        came = exchange(theirs, "pack", 1)
-        mine = term_of(self.pack * self.width, self.width).astype(BF16)
-        shape = [2, 2, 2, 2, rows // 16, self.width]
+        rows = mine.shape[-2]
+        self.tail = (rows // 16, mine.shape[-1])
+        self.lead = mine.shape[:-2]
+        shape = self.lead + (2, 2, 2, 2) + self.tail
         self.parts = [mine.reshape(shape), came.reshape(shape)]
 
     def pick(self, bit, which):
-        axis = {8: 0, 4: 1, 2: 2, 1: 3}[bit]
+        axis = len(self.lead) + {8: 0, 4: 1, 2: 2, 1: 3}[bit]
         pieces = [lax.dynamic_slice_in_dim(part, which, 1, axis) for part in self.parts]
         return (pieces[0].astype(F32) + pieces[1].astype(F32)).astype(BF16)
 
     def stage(self):
-        if self.direct:
-            return ()
         bit = self.order.pop(0)
         own_bit = lax.rem(lax.div(self.index, bit), 2)
         send = self.pick(bit, 1 - own_bit)
         came = exchange(send, "seq", bit)
         self.parts = [self.pick(bit, own_bit), came]
-        return (send,)
+        return send
 
     def finish(self):
-        if self.direct:
-            return self.value
         while self.order:
             self.stage()
         own = (self.parts[0].astype(F32) + self.parts[1].astype(F32)).astype(BF16)
-        own = own.reshape(self.rows // 16, self.width)
+        own = own.reshape(self.lead + self.tail)
         other = exchange(own, "pack", 1)
-        left = jnp.where(self.pack == 0, own, other)
-        right = jnp.where(self.pack == 0, other, own)
-        return jnp.concatenate([left, right], axis=1).astype(F32)
+        first = lax.axis_index("pack") == 0
+        return jnp.where(first, own, other), jnp.where(first, other, own)
+
+
+def row_sum_direct(term):
+    part = lax.psum_scatter(term.astype(BF16), "seq", scatter_dimension=0, tiled=True)
+    return lax.psum(part, "pack").astype(F32)
+
+
+def project_kernel(
+    per_device,
+    hidden_ref,
+    shift_ref,
+    scale_ref,
+    wq_ref,
+    wk_ref,
+    wv_ref,
+    bq_ref,
+    bk_ref,
+    bv_ref,
+    cos_ref,
+    sin_ref,
+    in_ref,
+    first_ref,
+    rest_ref,
+):
+    @pl.when(pl.program_id(0) == 0)
+    def _():
+        for place in range(per_device):
+            rows = pl.ds(place * PATCHES, PATCHES)
+            values = hidden_ref[rows, :].astype(F32)
+            centered = values - jnp.mean(values, axis=-1, keepdims=True)
+            spread = jnp.mean(centered * centered, axis=-1, keepdims=True)
+            normed = centered * lax.rsqrt(spread + EPSILON)
+            scale = scale_ref[pl.ds(place, 1), :]
+            in_ref[rows, :] = (normed * (1.0 + scale) + shift_ref[pl.ds(place, 1), :]).astype(BF16)
+
+    rows = in_ref[...]
+    group = wq_ref.shape[1] // HEAD
+
+    def turned(values, place):
+        lower = values[:HALF]
+        upper = values[HALF:]
+        cosine = cos_ref[place]
+        sine = sin_ref[place]
+        return jnp.concatenate([lower * cosine - upper * sine, upper * cosine + lower * sine], axis=0)
+
+    for kind, (weight_ref, bias_ref) in enumerate(
+        ((wq_ref, bq_ref), (wk_ref, bk_ref), (wv_ref, bv_ref))
+    ):
+        flat = jnp.dot(rows, weight_ref[...], preferred_element_type=F32) + bias_ref[...]
+        for place in range(per_device):
+            block = flat[place * PATCHES : (place + 1) * PATCHES].T
+            for head in range(group):
+                values = block[head * HEAD : (head + 1) * HEAD]
+                if kind == 0:
+                    values = (turned(values, place) * (HEAD**-0.5)).astype(BF16)
+                    if place == 0:
+                        first_ref[head, 2 * per_device] = values
+                    else:
+                        rest_ref[head, place - 1] = values
+                elif kind == 1:
+                    first_ref[head, place] = turned(values, place).astype(BF16)
+                else:
+                    first_ref[head, per_device + place] = values.astype(BF16)
+
+
+def project(per_device, hidden, shift, scale, weight, bias, cosine, sine):
+    tokens, width = hidden.shape
+    heads = width // HEAD
+    group = 2
+    lanes = group * HEAD
+    steps = heads // group
+    bias_row = bias[None, :]
+
+    def whole(shape):
+        return pl.BlockSpec(shape, lambda step: (0,) * len(shape))
+
+    def part(kind, rows):
+        return pl.BlockSpec((rows, lanes), lambda step: (0, kind * steps + step))
+
+    first = (heads, 2 * per_device + 1, HEAD, PATCHES)
+    rest = (heads, per_device - 1, HEAD, PATCHES)
+    return pl.pallas_call(
+        functools.partial(project_kernel, per_device),
+        grid=(steps,),
+        out_shape=(
+            jax.ShapeDtypeStruct((tokens, width), BF16),
+            jax.ShapeDtypeStruct(first, BF16),
+            jax.ShapeDtypeStruct(rest, BF16),
+        ),
+        in_specs=[whole((tokens, width)), whole(shift.shape), whole(scale.shape)]
+        + [part(kind, width) for kind in range(3)]
+        + [part(kind, 1) for kind in range(3)]
+        + [whole(cosine.shape), whole(sine.shape)],
+        out_specs=(
+            whole((tokens, width)),
+            pl.BlockSpec((group,) + first[1:], lambda step: (step, 0, 0, 0)),
+            pl.BlockSpec((group,) + rest[1:], lambda step: (step, 0, 0, 0)),
+        ),
+        cost_estimate=pl.CostEstimate(
+            flops=2 * tokens * width * 3 * width,
+            bytes_accessed=2 * (weight.size + 5 * tokens * width),
+            transcendentals=0,
+        ),
+        compiler_params=pltpu.CompilerParams(vmem_limit_bytes=40 << 20),
+        name="project",
+    )(hidden, shift, scale, weight, weight, weight, bias_row, bias_row, bias_row, cosine, sine)
+
+
+GELU_SLOPE = 0.7978845608028654
+GELU_CUBE = 0.044715
+
+
+def feed_kernel(
+    carried,
+    which_ref,
+    in_ref,
+    d_out_ref,
+    up_a_ref,
+    up_b_ref,
+    bias_a_ref,
+    bias_b_ref,
+    down_a_ref,
+    down_b_ref,
+    *refs
+):
+    if carried:
+        out_before_ref, d_in_before_ref = refs[:2]
+        refs = refs[2:]
+    out_ref, d_in_ref, d_up_ref, d_down_ref, d_bias_ref, turned_ref = refs
+
+    @pl.when(pl.program_id(0) == 0)
+    def _():
+        turned_ref[...] = in_ref[...].astype(F32).T.astype(BF16)
+        if carried:
+            out_ref[...] = out_before_ref[...]
+            d_in_ref[...] = d_in_before_ref[...]
+        else:
+            out_ref[...] = jnp.zeros_like(out_ref)
+            d_in_ref[...] = jnp.zeros_like(d_in_ref)
+
+    up = jnp.concatenate([up_a_ref[...], up_b_ref[...]], axis=1)
+    down = jnp.concatenate([down_a_ref[...], down_b_ref[...]], axis=0)
+    bias = jnp.concatenate([bias_a_ref[...], bias_b_ref[...]], axis=1)
+    d_out = d_out_ref[...]
+    pre = jnp.dot(in_ref[...], up, preferred_element_type=F32) + bias
+    d_act = dot_over(d_out, down, 1, 1)
+    square = pre * pre
+    bend = jnp.tanh(GELU_SLOPE * pre * (1.0 + GELU_CUBE * square))
+    half = 0.5 * (1.0 + bend)
+    act = (pre * half).astype(BF16)
+    slope = half + (0.5 * GELU_SLOPE) * pre * (1.0 - bend * bend) * (
+        1.0 + (3.0 * GELU_CUBE) * square
+    )
+    d_pre = (d_act * slope).astype(BF16)
+    out_ref[...] += jnp.dot(act, down, preferred_element_type=F32)
+    d_in_ref[...] += dot_over(d_pre, up, 1, 1)
+    d_up_ref[...] = jnp.dot(turned_ref[...], d_pre, preferred_element_type=F32).astype(BF16)
+    d_down_ref[...] = jnp.dot(
+        act.astype(F32).T.astype(BF16), d_out, preferred_element_type=F32
+    ).astype(BF16)
+    d_bias_ref[...] = jnp.sum(d_pre.astype(F32), axis=0, keepdims=True)
+
+
+def feed(which, feed_in, d_feed_out, up_weight, up_bias, down_weight, before):
+    tokens, width = feed_in.shape
+    hidden_units = up_weight.shape[1]
+    small = 128
+    steps = hidden_units // (4 * small)
+    own = hidden_units // 2
+
+    def whole(shape):
+        return pl.BlockSpec(shape, lambda step, which: (0,) * len(shape))
+
+    def group(nth):
+        return lambda step, which: 2 * (2 * step + nth) + which[0]
+
+    def columns(nth, rows):
+        return pl.BlockSpec((rows, small), lambda step, which: (0, group(nth)(step, which)))
+
+    def rows_of(nth):
+        return pl.BlockSpec((small, width), lambda step, which: (group(nth)(step, which), 0))
+
+    args = [feed_in, d_feed_out, up_weight, up_weight, up_bias[None], up_bias[None]]
+    args += [down_weight, down_weight]
+    specs = [whole((tokens, width)), whole((tokens, width)), columns(0, width), columns(1, width)]
+    specs += [columns(0, 1), columns(1, 1), rows_of(0), rows_of(1)]
+    if before is not None:
+        args += list(before)
+        specs += [whole((tokens, width)), whole((tokens, width))]
+    return pl.pallas_call(
+        functools.partial(feed_kernel, before is not None),
+        grid_spec=pltpu.PrefetchScalarGridSpec(
+            num_scalar_prefetch=1,
+            grid=(steps,),
+            in_specs=specs,
+            out_specs=(
+                whole((tokens, width)),
+                whole((tokens, width)),
+                pl.BlockSpec((width, 2 * small), lambda step, which: (0, step)),
+                pl.BlockSpec((2 * small, width), lambda step, which: (step, 0)),
+                pl.BlockSpec((1, 2 * small), lambda step, which: (0, step)),
+            ),
+            scratch_shapes=[pltpu.VMEM((width, tokens), BF16)],
+        ),
+        out_shape=(
+            jax.ShapeDtypeStruct((tokens, width), F32),
+            jax.ShapeDtypeStruct((tokens, width), F32),
+            jax.ShapeDtypeStruct((width, own), BF16),
+            jax.ShapeDtypeStruct((own, width), BF16),
+            jax.ShapeDtypeStruct((1, own), F32),
+        ),
+        cost_estimate=pl.CostEstimate(
+            flops=12 * tokens * width * own,
+            bytes_accessed=2 * (4 * own * width + 8 * tokens * width),
+            transcendentals=tokens * own,
+        ),
+        compiler_params=pltpu.CompilerParams(vmem_limit_bytes=56 << 20),
+        name="feed%d" % (before is not None),
+    )(which.reshape(1), *args)
+
+
+def unproject_kernel(
+    per_device, carried, which_ref, in_ref, first_ref, back_ref, wq_ref, wk_ref, wv_ref, *refs
+):
+    if carried:
+        before_ref = refs[0]
+        refs = refs[1:]
+    d_in_ref, d_weight_ref, d_bias_ref, turned_ref = refs
+
+    @pl.when(pl.program_id(0) == 0)
+    def _():
+        turned_ref[...] = in_ref[...].astype(F32).T.astype(BF16)
+        if carried:
+            d_in_ref[...] = before_ref[...]
+        else:
+            d_in_ref[...] = jnp.zeros_like(d_in_ref)
+
+    group = wq_ref.shape[1] // HEAD
+
+    def token_major(block_of):
+        rows = []
+        for place in range(per_device):
+            block = jnp.concatenate([block_of(head, place) for head in range(group)], axis=0)
+            rows.append(block.astype(F32).T.astype(BF16))
+        return jnp.concatenate(rows, axis=0)
+
+    def query_block(head, place):
+        if place == per_device - 1:
+            return back_ref[head, 2 * per_device]
+        return first_ref[head, place]
+
+    sides = jnp.concatenate(
+        [
+            token_major(query_block),
+            token_major(lambda head, place: back_ref[head, place]),
+            token_major(lambda head, place: back_ref[head, per_device + place]),
+        ],
+        axis=1,
+    )
+    weights = jnp.concatenate([wq_ref[...], wk_ref[...], wv_ref[...]], axis=1)
+    d_in_ref[...] += dot_over(sides, weights, 1, 1)
+    d_weight = jnp.dot(turned_ref[...], sides, preferred_element_type=F32).astype(BF16)
+    d_bias = jnp.sum(sides.astype(F32), axis=0, keepdims=True)
+    lanes = group * HEAD
+    for kind in range(3):
+        d_weight_ref[kind] = d_weight[:, kind * lanes : (kind + 1) * lanes]
+        d_bias_ref[kind] = d_bias[:, kind * lanes : (kind + 1) * lanes]
+
+
+def unproject(per_device, which, attn_in, first, back, weight, before):
+    tokens, width = attn_in.shape
+    heads = width // HEAD
+    group = 2
+    lanes = group * HEAD
+    groups = heads // group
+    steps = groups // 2
+
+    def whole(shape):
+        return pl.BlockSpec(shape, lambda step, which: (0,) * len(shape))
+
+    def blocks(array):
+        return pl.BlockSpec(
+            (group,) + array.shape[1:], lambda step, which: (which[0] * steps + step, 0, 0, 0)
+        )
+
+    def part(kind):
+        return pl.BlockSpec(
+            (width, lanes), lambda step, which: (0, kind * groups + which[0] * steps + step)
+        )
+
+    args = [attn_in, first, back, weight, weight, weight]
+    specs = [whole((tokens, width)), blocks(first), blocks(back), part(0), part(1), part(2)]
+    if before is not None:
+        args.append(before)
+        specs.append(whole((tokens, width)))
+    return pl.pallas_call(
+        functools.partial(unproject_kernel, per_device, before is not None),
+        grid_spec=pltpu.PrefetchScalarGridSpec(
+            num_scalar_prefetch=1,
+            grid=(steps,),
+            in_specs=specs,
+            out_specs=(
+                whole((tokens, width)),
+                pl.BlockSpec((3, width, lanes), lambda step, which: (0, 0, step)),
+                pl.BlockSpec((3, 1, lanes), lambda step, which: (0, 0, step)),
+            ),
+            scratch_shapes=[pltpu.VMEM((width, tokens), BF16)],
+        ),
+        out_shape=(
+            jax.ShapeDtypeStruct((tokens, width), F32),
+            jax.ShapeDtypeStruct((3, width, width // 2), BF16),
+            jax.ShapeDtypeStruct((3, 1, width // 2), F32),
+        ),
+        cost_estimate=pl.CostEstimate(
+            flops=6 * tokens * width * width,
+            bytes_accessed=2 * (3 * width * width + 6 * tokens * width),
+            transcendentals=0,
+        ),
+        compiler_params=pltpu.CompilerParams(vmem_limit_bytes=40 << 20),
+        name="unproject%d" % (before is not None),
+    )(which.reshape(1), *args)
 
 
 def columns_of(matrix, start, width, axis=1):
@@ -435,15 +742,15 @@
     clip_ids = segments[0]
     live = live_frames[0]
 
+    pack = lax.axis_index("pack")
+    halves = halving_fits()
     frame_ids = jnp.arange(frames, dtype=jnp.int32)
     same_clip = clip_ids[:, None] == clip_ids[None, :]
     clip_starts = jnp.min(jnp.where(same_clip, frame_ids[None, :], frames), axis=1)
-    cos_all, sin_all = rotary_tables((frame_ids - clip_starts).astype(F32))
-    first_frame = seq_index * per_device
-    own_cos = lax.dynamic_slice_in_dim(cos_all, first_frame, per_device)
-    own_sin = lax.dynamic_slice_in_dim(sin_all, first_frame, per_device)
-    own_cos = own_cos.transpose(1, 0, 2).reshape(HALF, tokens)
-    own_sin = own_sin.transpose(1, 0, 2).reshape(HALF, tokens)
+    frame_times = (frame_ids - clip_starts).astype(F32)
+    own_cos, own_sin = rotary_tables(
+        lax.dynamic_slice_in_dim(frame_times, seq_index * per_device, per_device)
+    )
 
     embed = jnp.concatenate(
         [
@@ -453,29 +760,11 @@
         axis=0,
     )
     cond = jax.nn.silu(embed).astype(BF16)
-    modulation = jnp.dot(cond, mod_weight, preferred_element_type=F32) + mod_bias
-    attn_shift, attn_scale, attn_gate, feed_shift, feed_scale, feed_gate = jnp.split(
-        modulation, 6, axis=1
-    )
-    frame_rows = hidden[0].astype(F32).reshape(per_device, PATCHES, width)
-    attn_value, attn_norm_back = jax.vjp(modulate_norm, frame_rows, attn_shift, attn_scale)
-    attn_in = attn_value.reshape(tokens, width).astype(BF16)
-
-    qkv = dot_over(qkv_weight, attn_in, 0, 1) + qkv_bias[:, None]
-    qkv = qkv.reshape(3, heads, 2, HALF, tokens)
-    turned = qkv[:2]
-    lower = turned[:, :, 0] * own_cos - turned[:, :, 1] * own_sin
-    upper = turned[:, :, 1] * own_cos + turned[:, :, 0] * own_sin
-    turned = jnp.stack([lower, upper], axis=2)
-
-    def by_frame(array):
-        split = array.astype(BF16).reshape(heads, HEAD, per_device, PATCHES)
-        return [split[:, :, place] for place in range(per_device)]
-
-    queries = by_frame(turned[0] * (HEAD**-0.5))
-    keys = by_frame(turned[1])
-    values = by_frame(qkv[2])
-    sent = jnp.stack(keys + values + queries[:1], axis=1)
+    modulation = jnp.dot(cond, mod_weight[:, : 2 * width], preferred_element_type=F32)
+    attn_shift, attn_scale = jnp.split(modulation + mod_bias[: 2 * width], 2, axis=1)
+    attn_in, sent, rest = project(
+        per_device, hidden[0], attn_shift, attn_scale, qkv_weight, qkv_bias, own_cos, own_sin
+    )
 
     def to_heads(array):
         if copies > 1:
@@ -486,8 +775,17 @@
         return lax.all_to_all(array, "seq", 0, 0, tiled=True)[:heads]
 
     x = to_heads(sent)
+    late_modulation = jnp.dot(
+        after(cond, attn_in), mod_weight[:, 2 * width :], preferred_element_type=F32
+    )
+    attn_gate, feed_shift, feed_scale, feed_gate = jnp.split(
+        late_modulation + mod_bias[2 * width :], 4, axis=1
+    )
+    cos_all, sin_all = rotary_tables(after(frame_times, attn_in))
+    grad_rows = cotangent[0].astype(F32).reshape(per_device, PATCHES, width)
+    d_feed_out = (feed_gate[:, None, :] * grad_rows).reshape(tokens, width).astype(BF16)
     head_queries = [x] + [
-        to_heads(after(query, x[0, 0, :8]).reshape(heads, 1, HEAD, PATCHES)) for query in queries[1:]
+        to_heads(after(rest[:, place : place + 1], x[0, 0, :8])) for place in range(per_device - 1)
     ]
     slots = [2 * per_device] + [0] * (per_device - 1)
     kv = None
@@ -502,30 +800,28 @@
     attn_rows = jnp.stack([dot_over(mix, out_weight, 0, 0) for mix in mixes]) + out_bias
     attn_mix = jnp.concatenate(mixes, axis=1)
 
+    frame_rows = hidden[0].astype(F32).reshape(per_device, PATCHES, width)
     middle = frame_rows + attn_gate[:, None, :] * attn_rows
     feed_value, feed_norm_back = jax.vjp(modulate_norm, middle, feed_shift, feed_scale)
     feed_in = feed_value.reshape(tokens, width).astype(BF16)
-    pre = jnp.dot(feed_in, up_weight, preferred_element_type=F32) + up_bias
-    act_value, act_back = jax.vjp(gelu_tanh, pre)
-    act = act_value.astype(BF16)
-    grad_rows = cotangent[0].astype(F32).reshape(per_device, PATCHES, width)
-    d_feed_out = (feed_gate[:, None, :] * grad_rows).reshape(tokens, width).astype(BF16)
-    d_pre = act_back(dot_over(d_feed_out, down_weight, 1, 1))[0].astype(BF16)
-    down_sum = RowSum(
-        lambda start, size: dot_over(act, columns_of(d_feed_out, start, size), 0, 0),
-        hidden_units,
-        width,
-        (1, 2, 8, 4),
-    )
+    feed_args = (feed_in, d_feed_out, up_weight, up_bias, down_weight)
+    theirs = feed(1 - pack if halves else pack * 0 + 1, *feed_args, None)
+    mine = feed(pack if halves else pack * 0, *feed_args, theirs[:2])
+    feed_rows, d_feed_in = [each.reshape(per_device, PATCHES, width) for each in mine[:2]]
+    small = 128
+
+    def in_order(own, other):
+        if halves:
+            even, odd = jnp.where(pack == 0, own, other), jnp.where(pack == 0, other, own)
+        else:
+            even, odd = own, other
+        rows = own.shape[0]
+        return jnp.stack(
+            [even.reshape(rows, -1, small), odd.reshape(rows, -1, small)], axis=2
+        ).reshape(rows, -1)
+
+    up_bias_term = in_order(mine[4], theirs[4])[0]
     down_bias_term = jnp.sum(d_feed_out.astype(F32), axis=0)
-    d_feed_in = dot_over(d_pre, up_weight, 1, 1).reshape(per_device, PATCHES, width)
-    up_sum = RowSum(
-        lambda start, size: dot_over(feed_in, columns_of(d_pre, start, size), 0, 0),
-        width,
-        hidden_units,
-        (2, 1, 8, 4),
-    )
-    up_bias_term = jnp.sum(d_pre.astype(F32), axis=0)
     d_middle_norm, d_feed_shift, d_feed_scale = feed_norm_back(d_feed_in)
     d_middle = grad_rows + d_middle_norm
     d_attn_gate = jnp.sum(d_middle * attn_rows, axis=1)
@@ -535,16 +831,20 @@
     for part in range(per_device):
         d_mix = dot_over(out_weight, d_attn_rows[part], 1, 1).astype(BF16)
         d_mixes.append(to_heads(d_mix.reshape(heads, HEAD, PATCHES)))
-    out_sum = RowSum(
-        lambda start, size: dot_over(attn_mix, columns_of(d_attn_out, start, size), 1, 0),
-        width,
-        width,
-        (1, 2, 8, 4),
-    )
+
+    def out_term(start, size):
+        return dot_over(attn_mix, columns_of(d_attn_out, start, size), 1, 0).astype(BF16)
+
+    sums = ()
+    if halves:
+        up_sum = RowSum(mine[2], exchange(theirs[2], "pack", 1), (2, 1, 4, 8))
+        down_sum = RowSum(mine[3], exchange(theirs[3], "pack", 1), (1, 2, 4, 8))
+        out_theirs = exchange(out_term((1 - pack) * (width // 2), width // 2), "pack", 1)
+        out_sum = RowSum(out_term(pack * (width // 2), width // 2), out_theirs, (1, 2, 4, 8))
+        sums = (down_sum, up_sum, out_sum)
     out_bias_term = jnp.sum(d_attn_out.astype(F32), axis=0)
 
-    feed_out = jnp.dot(act, down_weight, preferred_element_type=F32) + down_bias
-    feed_rows = feed_out.reshape(per_device, PATCHES, width)
+    feed_rows = feed_rows + down_bias
     layer_out = (middle + feed_gate[:, None, :] * feed_rows).reshape(1, tokens, width).astype(BF16)
     d_feed_gate = jnp.sum(grad_rows * feed_rows, axis=1)
 
@@ -565,9 +865,8 @@
 
     before = None
     d_queries = []
-    sums = (down_sum, up_sum, out_sum)
     for part in range(per_device):
-        d_mix = after(d_mixes[part], *[send for each in sums for send in each.stage()])
+        d_mix = after(d_mixes[part], *[each.stage() for each in sums])
         result = attend_back(
             part,
             per_device,
@@ -587,31 +886,25 @@
         if part < per_device - 1:
             d_query, before = result
             d_queries.append(to_tokens(d_query))
-    result = after(result, *[send for each in sums for send in each.stage()])
+    firsts = jnp.stack(d_queries, axis=1)
+    result = after(result, firsts[0, 0, :8], *[each.stage() for each in sums])
     back = to_tokens(result)
-    d_queries.append(back[:, 2 * per_device])
-
-    def joined(blocks):
-        return jnp.stack(blocks, axis=2).reshape(width, tokens)
-
-    d_qkv = jnp.concatenate(
-        [
-            joined(d_queries),
-            joined([back[:, place] for place in range(per_device)]),
-            joined([back[:, per_device + place] for place in range(per_device)]),
-        ],
-        axis=0,
-    )
-    d_attn_in = dot_over(d_qkv, qkv_weight, 0, 1).reshape(per_device, PATCHES, width)
-    qkv_sum = RowSum(
-        lambda start, size: dot_over(attn_in, columns_of(d_qkv, start, size, 0), 0, 1),
-        width,
-        3 * width,
-        (1, 2, 8, 4),
-    )
+    which = (1 - pack, pack) if halves else (pack * 0, pack * 0 + 1)
+    qkv_theirs = unproject(per_device, which[0], attn_in, firsts, back, qkv_weight, None)
+    qkv_mine = unproject(per_device, which[1], attn_in, firsts, back, qkv_weight, qkv_theirs[0])
+    d_attn_in = qkv_mine[0].reshape(per_device, PATCHES, width)
+    _, attn_norm_back = jax.vjp(modulate_norm, frame_rows, attn_shift, attn_scale)
     d_hidden_norm, d_attn_shift, d_attn_scale = attn_norm_back(d_attn_in)
     hidden_grad = (d_middle + d_hidden_norm).reshape(1, tokens, width).astype(BF16)
-    qkv_bias_term = jnp.sum(d_qkv.astype(F32), axis=1)
+
+    def halves_in_order(own, other):
+        if halves:
+            return jnp.where(pack == 0, own, other), jnp.where(pack == 0, other, own)
+        return other, own
+
+    qkv_bias_term = jnp.concatenate(
+        halves_in_order(qkv_mine[2][:, 0], qkv_theirs[2][:, 0]), axis=1
+    ).reshape(3 * width)
     late = jnp.concatenate(
         [
             d_attn_shift.astype(BF16),
@@ -621,10 +914,32 @@
         axis=1,
     )
     late_all = gather_all(late)
-    down_weight_grad = down_sum.finish()
-    up_weight_grad = up_sum.finish()
-    out_weight_grad = out_sum.finish()
-    qkv_weight_grad = qkv_sum.finish()
+    if halves:
+        came = exchange(qkv_theirs[1], "pack", 1)
+        split = width // 4
+        qkv_sums = [
+            RowSum(qkv_mine[1][..., :split], came[..., :split], (1, 2, 4, 8)),
+            RowSum(qkv_mine[1][..., split:], came[..., split:], (2, 1, 4, 8)),
+        ]
+        down_weight_grad = jnp.concatenate(down_sum.finish(), axis=0).astype(F32)
+        even, odd = up_sum.finish()
+        up_weight_grad = jnp.stack(
+            [even.reshape(share, -1, small), odd.reshape(share, -1, small)], axis=2
+        ).reshape(share, hidden_units)
+        up_weight_grad = up_weight_grad.astype(F32)
+        out_weight_grad = jnp.concatenate(out_sum.finish(), axis=1).astype(F32)
+        done = [each.finish() for each in qkv_sums]
+        qkv_weight_grad = jnp.concatenate(
+            [done[0][0], done[1][0], done[0][1], done[1][1]], axis=-1
+        )
+        qkv_weight_grad = qkv_weight_grad.transpose(1, 0, 2).reshape(share, 3 * width).astype(F32)
+    else:
+        up_weight_grad = row_sum_direct(in_order(mine[2], theirs[2]))
+        pairs = [each[3].reshape(-1, small, width) for each in (mine, theirs)]
+        down_weight_grad = row_sum_direct(jnp.stack(pairs, axis=1).reshape(hidden_units, width))
+        out_weight_grad = row_sum_direct(out_term(0, width))
+        qkv_term = jnp.concatenate(halves_in_order(qkv_mine[1], qkv_theirs[1]), axis=-1)
+        qkv_weight_grad = row_sum_direct(qkv_term.transpose(1, 0, 2).reshape(width, 3 * width))
 
     devices = late_all.shape[0] // per_device
 

time: 771 us -> 644 us (0.84); the launches traced: 769 us -> 634 us
  waiting for transfers between devices: 265 us -> 171 us
  matrix products: 103 us -> 26.3 us
  Pallas kernels: 118 us -> 185 us
  local copies, waits for them, and re-layouts: 92.2 us -> 57.8 us
  starting transfers between devices: 88.6 us -> 100 us
  other arithmetic: 96.9 us -> 87 us
    ppermute x34 -> x39, waiting for transfers between devices: 195 us -> 107 us  [exchange(): lax.ppermute(value, axis, [(source, source ^ bit) for source in range(cou...]
    pallas_call x0 -> x5, Pallas kernels: none -> 72.9 us  [the longest x2 45.6 us: feed(): pl.pallas_call(functools.partial(feed_kernel, before is not None), grid_s...]
    dot_general x20 -> x10, matrix products: 72.2 us -> 15.9 us  [dot_over(): lax.dot_general(first, second, (((first_dim,), (second_dim,)), ((), ())),...]
    dot_general x3 -> x2, matrix products: 27.9 us -> 7.59 us  [the longest x1 4.66 us: local(): jnp.dot(after(cond, attn_in), mod_weight[:, 2 * width:], preferred_elemen...]
    ppermute x34 -> x39, starting transfers between devices: 31.7 us -> 45.6 us  [exchange(): lax.ppermute(value, axis, [(source, source ^ bit) for source in range(cou...]
    slice x6 -> x5, local copies, waits for them, and re-layouts: 18.1 us -> 6.71 us  [the longest x1 3.81 us: local(): qkv_mine[1][..., :split]]
    unnamed x240 -> x168, local copies, waits for them, and re-layouts: 32 us -> 23.1 us
    convert_element_type x16 -> x21, other arithmetic: 39.3 us -> 41.4 us  [pick(): return (pieces[0].astype(F32) + pieces[1].astype(F32)).astype(BF16)]
  transfers between devices with their start and end apart: 42 -> 47, of which waited for: 20 -> 24; matrix products, arithmetic and copies ran while one was open for 21% -> 21% of each run, Pallas kernels for 15% -> 19%
where the time goes in v1:
time: 644 us; the launch traced here: 634 us
  Pallas kernels  185 us (29%)
  waiting for transfers between devices  171 us (27%)
  starting transfers between devices  100 us (16%)
  other arithmetic  87 us (14%)
  local copies, waits for them, and re-layouts  57.8 us (9%)
  matrix products  26.3 us (4%)
    ppermute x39, waiting for transfers between devices, exchange(): lax.ppermute(value, axis, [(source, source ^ bit) for source in range(cou...  107 us
    pallas_call x2, Pallas kernels, attend_back(): pl.pallas_call(functools.partial(attend_back_kernel, per_device, part, sl...  64.9 us
    all_to_all x4, waiting for transfers between devices, to_heads(): return lax.all_to_all(array, 'seq', 0, 0, tiled=True)  52 us
    pallas_call x2, Pallas kernels, attend(): pl.pallas_call(functools.partial(attend_kernel, per_device, part, slot),...  47.5 us
    ppermute x39, starting transfers between devices, exchange(): lax.ppermute(value, axis, [(source, source ^ bit) for source in range(cou...  45.6 us
    pallas_call x2, Pallas kernels, feed(): pl.pallas_call(functools.partial(feed_kernel, before is not None), grid_s...  45.6 us
    convert_element_type x21, other arithmetic, pick(): return (pieces[0].astype(F32) + pieces[1].astype(F32)).astype(BF16)  41.4 us
    all_to_all x4, starting transfers between devices, to_heads(): return lax.all_to_all(array, 'seq', 0, 0, tiled=True)  30.4 us
  transfers between devices with their start and end apart: 47, of which 24 were waited for; matrix products, arithmetic and copies ran while one was open for 21% of the time, Pallas kernels for 19%

profile of v1, /device:TPU:0, one launch (start us, length us, event | category | flops | bytes accessed | tf_op | source)
XLA Modules:
  0.0 633.8 jit_solution(7856428712567617080)
XLA Ops:
  8.5 2.9 fusion.7
  12.6 2.8 copy-done.2
  15.4 11.4 %project.1 = (bf16[512,1024]{1,0:T(8,128)(2,1)S(1)}, bf16[16,5,64,256]{3,2,1,0:T(8,128)(2,1)S(1)}, bf16[16,1,64,256]{3,2,1,0:T(8,128)(2,1)S(1)}) custom-call(bf16[512,1024]{1,0:T(8,128)(2,1)S(1)} %bitcast.210, f32[2,1024]{1,0:T(2,128)S(1)} %get-tuple-element.158.shift_ref, f32[2,1024]{1,0:T(2,128)S(1)} %get-tuple-element.157.scale_ref, ...), custom_call_target="tpu_custom_call" | custom-call | flops 3221225472 | bytes 11534336 | tf_op jit(solution)/shard_map/project/pallas_call | solution.py:465
  30.0 8.5 %all-to-all-start = ((bf16[16,5,64,256]{3,2,1,0:T(8,128)(2,1)}), bf16[16,5,64,256]{3,2,1,0:T(8,128)(2,1)}, u32[]{:S(2)}, u32[]{:S(2)}) async-start(bf16[16,5,64,256]{3,2,1,0:T(8,128)(2,1)} %copy-done.10), calls=%async_computation | async-start | bytes 5242880 | tf_op jit(solution)/shard_map/all_to_all | solution.py:772
  38.5 52.0 %all-to-all-done.x_ref.q_ref = bf16[16,5,64,256]{3,2,1,0:T(8,128)(2,1)} async-done(((bf16[16,5,64,256]{3,2,1,0:T(8,128)(2,1)}), bf16[16,5,64,256]{3,2,1,0:T(8,128)(2,1)}, u32[]{:S(2)}, u32[]{:S(2)}) %all-to-all-start) | async-done | bytes 2621472 | tf_op jit(solution)/shard_map/all_to_all | solution.py:772
  90.5 12.5 %all-to-all-start.2 = ((bf16[16,1,64,256]{3,2,1,0:T(8,128)(2,1)}), bf16[16,1,64,256]{3,2,1,0:T(8,128)(2,1)}, u32[]{:S(2)}, u32[]{:S(2)}) async-start(bf16[16,1,64,256]{3,2,1,0:T(8,128)(2,1)} %copy-done.12), calls=%async_computation.2 | async-start | bytes 1048576 | tf_op jit(solution)/shard_map/all_to_all | solution.py:772
  103.1 26.3 %attend0.1 = (bf16[16,64,256]{2,1,0:T(8,128)(2,1)S(1)}, f32[16,64,256]{2,1,0:T(8,128)S(1)}, f32[16,256]{1,0:T(8,128)S(1)}, bf16[32,256,128]{2,1,0:T(8,128)(2,1)S(1)}) custom-call(s32[32]{0:T(128)S(1)} %bitcast.220, s32[32]{0:T(128)S(1)} %bitcast.224, bf16[16,5,64,256]{3,2,1,0:T(8,128)(2,1)} %all-to-all-done.x_ref.q_ref, ...), custom_call_target="tpu_custom_call" | custom-call | flops 6442450944 | bytes 7864320 | tf_op jit(solution)/shard_map/attend0/pallas_call | solution.py:180
  134.7 21.2 %attend1.1 = (bf16[16,64,256]{2,1,0:T(8,128)(2,1)S(1)}, f32[16,64,256]{2,1,0:T(8,128)S(1)}, f32[16,256]{1,0:T(8,128)S(1)}) custom-call(s32[32]{0:T(128)S(1)} %bitcast.221, s32[32]{0:T(128)S(1)} %bitcast.225, bf16[16,5,64,256]{3,2,1,0:T(8,128)(2,1)} %all-to-all-done.x_ref.q_ref, bf16[16,1,64,256]{3,2,1,0:T(8,128)(2,1)} %all-to-all-done.2.q_ref, ...), custom_call_target="tpu_custom_call" | custom-call | flops 6442450944 | bytes 7864320 | tf_op jit(solution)/shard_map/attend1/pallas_call | solution.py:180
  158.3 7.0 %all-to-all-start.3 = ((bf16[16,64,256]{2,1,0:T(8,128)(2,1)}), bf16[16,64,256]{2,1,0:T(8,128)(2,1)}, u32[]{:S(2)}, u32[]{:S(2)}) async-start(bf16[16,64,256]{2,1,0:T(8,128)(2,1)} %copy-done.13), calls=%async_computation.3 | async-start | bytes 1048576 | tf_op jit(solution)/shard_map/all_to_all | solution.py:775
  165.4 10.8 %all-to-all-done.3 = bf16[16,64,256]{2,1,0:T(8,128)(2,1)} async-done(((bf16[16,64,256]{2,1,0:T(8,128)(2,1)}), bf16[16,64,256]{2,1,0:T(8,128)(2,1)}, u32[]{:S(2)}, u32[]{:S(2)}) %all-to-all-start.3) | async-done | bytes 524320 | tf_op jit(solution)/shard_map/all_to_all | solution.py:775
  176.2 4.5 all-to-all-start.1
  180.8 4.7 fusion.2
  186.7 2.7 convolution_bitcast_fusion
  189.5 2.1 all-to-all-done.1
  198.3 21.9 %feed0.1 = (f32[512,1024]{1,0:T(8,128)}, f32[512,1024]{1,0:T(8,128)}, bf16[1024,2048]{1,0:T(8,128)(2,1)}, bf16[2048,1024]{1,0:T(8,128)(2,1)}, f32[1,2048]{1,0:T(1,128)}) custom-call(s32[1]{0:T(128)} %bitcast.20.which_ref, bf16[512,1024]{1,0:T(8,128)(2,1)} %fusion.18.in_ref, bf16[512,1024]{1,0:T(8,128)(2,1)} %fusion.14.d_out_ref, ...), custom_call_target="tpu_custom_call" | custom-call | flops 12884901888 | bytes 25165824 | tf_op jit(solution)/shard_map/feed0/pallas_call | solution.py:573
  220.8 23.7 %feed1.1 = (f32[512,1024]{1,0:T(8,128)}, f32[512,1024]{1,0:T(8,128)}, bf16[1024,2048]{1,0:T(8,128)(2,1)}, bf16[2048,1024]{1,0:T(8,128)(2,1)}, f32[1,2048]{1,0:T(1,128)}) custom-call(s32[1]{0:T(128)} %bitcast.13.which_ref, bf16[512,1024]{1,0:T(8,128)(2,1)} %fusion.18.in_ref, bf16[512,1024]{1,0:T(8,128)(2,1)} %fusion.14.d_out_ref, ...), custom_call_target="tpu_custom_call" | custom-call | flops 12884901888 | bytes 25165824 | tf_op jit(solution)/shard_map/feed1/pallas_call | solution.py:573
  247.9 2.1 fusion.87
  252.3 2.9 convolution_convert_fusion
  258.1 2.2 convolution_convert_fusion.1
  261.4 2.7 add_convert_fusion.17
  265.6 2.7 multiply_convert_fusion
  271.0 2.1 copy.80
  273.0 4.4 all-to-all-start.4
  278.7 2.0 add_convert_fusion.29
  281.8 7.9 %add_convert_fusion.1 = (bf16[2,2,2,1,128,1024]{5,4,3,2,1,0:T(8,128)(2,1)}, bf16[2,2,2,1,128,1024]{5,4,3,2,1,0:T(8,128)(2,1)}) fusion(bf16[2,2,2,2,128,1024]{5,4,3,2,1,0:T(8,128)(2,1)} %bitcast.30, s32[]{:T(128)S(6)} %select_n.253, bf16[2,2,2,2,128,1024]{5,4,3,2,1,0:T(8,128)(2,1)} %bitcast.243, s32[]{:T(128)S(6)} %select_n.249), kind=kLoop, calls=%fused_computation.4 | loop fusion | flops 8388608 | bytes 12582920 | tf_op jit(solution)/shard_map/convert_element_type | solution.py:366
  290.8 6.7 %add_convert_fusion = (bf16[2,2,1,2,64,2048]{5,4,3,2,1,0:T(8,128)(2,1)}, bf16[2,2,1,2,64,2048]{5,4,3,2,1,0:T(8,128)(2,1)}) fusion(bf16[2,2,2,2,64,2048]{5,4,3,2,1,0:T(8,128)(2,1)} %bitcast.32, s32[]{:T(128)S(6)} %select_n.254, bf16[2,2,2,2,64,2048]{5,4,3,2,1,0:T(8,128)(2,1)S(1)} %bitcast.242, s32[]{:T(128)S(6)} %select_n.250), kind=kLoop, calls=%fused_computation.3 | loop fusion | flops 8388608 | bytes 12582920 | tf_op jit(solution)/shard_map/convert_element_type | solution.py:366
  300.3 2.0 copy.81
  304.1 4.9 all-to-all-start.6
  309.0 32.1 %attend_back0.1 = (bf16[16,64,256]{2,1,0:T(8,128)(2,1)}, f32[32,256,128]{2,1,0:T(8,128)}) custom-call(s32[32]{0:T(128)} %bitcast.218, s32[32]{0:T(128)} %bitcast.222, bf16[16,5,64,256]{3,2,1,0:T(8,128)(2,1)} %all-to-all-done.x_ref.q_ref, bf16[16,5,64,256]{3,2,1,0:T(8,128)(2,1)} %all-to-all-done.x_ref.q_ref, bf16[32,256,128]{2,1,0:T(8,128)(2,1)} %copy-done.17, ...), custom_call_target="tpu_custom_call" | custom-call | flops 16106127360 | bytes 13107200 | tf_op jit(solution)/shard_map/attend_back0/pallas_call | solution.py:312
  342.2 4.7 add_convert_fusion.6
  348.0 3.2 collective-permute-done.4
  351.2 3.8 add_convert_fusion.5
  355.9 5.3 all-to-all-start.5
  361.2 32.7 %attend_back1.1 = bf16[16,5,64,256]{3,2,1,0:T(8,128)(2,1)} custom-call(s32[32]{0:T(128)} %bitcast.219, s32[32]{0:T(128)} %bitcast.223, bf16[16,5,64,256]{3,2,1,0:T(8,128)(2,1)} %all-to-all-done.x_ref.q_ref, bf16[16,1,64,256]{3,2,1,0:T(8,128)(2,1)} %all-to-all-done.2.q_ref, bf16[32,256,128]{2,1,0:T(8,128)(2,1)} %copy-done.17, f32[16,64,256]{2,1,0:T(8,128)} %copy-done.19, ...), custom_call_target="tpu_custom_call" | custom-call | flops 16106127360 | bytes 13107200 | tf_op jit(solution)/shard_map/attend_back1/pallas_call | solution.py:312
  393.9 2.5 add_convert_fusion.13
  396.5 2.6 add_convert_fusion.14
  399.1 7.2 %all-to-all-start.7 = ((bf16[16,5,64,256]{3,2,1,0:T(8,128)(2,1)}), bf16[16,5,64,256]{3,2,1,0:T(8,128)(2,1)}, u32[]{:S(2)}, u32[]{:S(2)}) async-start(bf16[16,5,64,256]{3,2,1,0:T(8,128)(2,1)} %attend_back1.1), calls=%async_computation.7 | async-start | bytes 5242880 | tf_op jit(solution)/shard_map/all_to_all | solution.py:775
  409.1 2.0 collective-permute-start.30
  412.5 39.8 %collective-permute-done.30 = bf16[2,1,1,1,64,512]{5,4,3,2,1,0:T(8,128)(2,1)S(1)} collective-permute-done((bf16[2,1,1,1,64,512]{5,4,3,2,1,0:T(8,128)(2,1)S(1)}, bf16[2,1,1,1,64,512]{5,4,3,2,1,0:T(8,128)(2,1)S(1)}, u32[]{:S(2)}, u32[]{:S(2)}) %collective-permute-start.30) | collective-permute-done | bytes 131104 | tf_op jit(solution)/shard_map/ppermute | solution.py:330
  452.4 4.9 collective-permute-start.31
  459.9 5.1 collective-permute-done.31
  466.3 3.4 collective-permute-start.34
  469.8 7.4 %collective-permute-done.36 = bf16[2,1,1,1,128,1024]{5,4,3,2,1,0:T(8,128)(2,1)S(1)} collective-permute-done((bf16[2,1,1,1,128,1024]{5,4,3,2,1,0:T(8,128)(2,1)}, bf16[2,1,1,1,128,1024]{5,4,3,2,1,0:T(8,128)(2,1)S(1)}, u32[]{:S(2)}, u32[]{:S(2)}) %collective-permute-start.36) | collective-permute-done | bytes 524320 | tf_op jit(solution)/shard_map/ppermute | solution.py:330
  477.4 10.8 %collective-permute-done.34 = bf16[1,1,1,1,64,2048]{5,4,3,2,1,0:T(8,128)(2,1)S(1)} collective-permute-done((bf16[1,1,1,1,64,2048]{5,4,3,2,1,0:T(8,128)(2,1)S(1)}, bf16[1,1,1,1,64,2048]{5,4,3,2,1,0:T(8,128)(2,1)S(1)}, u32[]{:S(2)}, u32[]{:S(2)}) %collective-permute-start.34) | collective-permute-done | bytes 262176 | tf_op jit(solution)/shard_map/ppermute | solution.py:330
  490.1 3.5 collective-permute-done.37
  494.8 2.2 maximum_convert_fusion
  497.0 3.1 reshape.676
  502.2 8.3 %unproject0.1 = (f32[512,1024]{1,0:T(8,128)S(1)}, bf16[3,1024,512]{2,1,0:T(8,128)(2,1)}, f32[3,1,512]{2,1,0:T(1,128)S(1)}) custom-call(s32[1]{0:T(128)} %bitcast.20.which_ref, bf16[512,1024]{1,0:T(8,128)(2,1)S(1)} %copy-done.7, bf16[16,1,64,256]{3,2,1,0:T(8,128)(2,1)S(1)} %bitcast.212, bf16[16,5,64,256]{3,2,1,0:T(8,128)(2,1)} %all-to-all-done.7.back_ref, ...), custom_call_target="tpu_custom_call" | custom-call | flops 3221225472 | bytes 12582912 | tf_op jit(solution)/shard_map/unproject0/pallas_call | solution.py:679
  512.0 7.6 %unproject1.1 = (f32[512,1024]{1,0:T(8,128)S(1)}, bf16[3,1024,512]{2,1,0:T(8,128)(2,1)S(1)}, f32[3,1,512]{2,1,0:T(1,128)S(1)}) custom-call(s32[1]{0:T(128)} %bitcast.13.which_ref, bf16[512,1024]{1,0:T(8,128)(2,1)S(1)} %copy-done.8, bf16[16,1,64,256]{3,2,1,0:T(8,128)(2,1)S(1)} %bitcast.213, bf16[16,5,64,256]{3,2,1,0:T(8,128)(2,1)} %all-to-all-done.7.back_ref, ...), custom_call_target="tpu_custom_call" | custom-call | flops 3221225472 | bytes 12582912 | tf_op jit(solution)/shard_map/unproject1/pallas_call | solution.py:679
  523.8 4.6 bitcast_reduce_fusion
  528.8 2.9 collective-permute-start.9
  534.6 3.3 collective-permute-start.10
  548.8 4.4 concatenate.119
  553.2 3.8 fusion.88
  558.4 3.0 concatenate.112
  562.5 3.3 fusion.28
  565.8 3.5 concatenate.120
  571.4 2.1 concatenate.113
  577.3 2.2 fusion.89
  585.4 14.4 %collective-permute-done.20 = bf16[3,2,2,2,1,64,256]{6,5,4,3,2,1,0:T(8,128)(2,1)S(1)} collective-permute-done((bf16[3,2,2,2,1,64,256]{6,5,4,3,2,1,0:T(8,128)(2,1)S(1)}, bf16[3,2,2,2,1,64,256]{6,5,4,3,2,1,0:T(8,128)(2,1)S(1)}, u32[]{:S(2)}, u32[]{:S(2)}) %collective-permute-start.20) | collective-permute-done | bytes 786464 | tf_op jit(solution)/shard_map/ppermute | solution.py:330
  607.7 3.7 collective-permute-done.21
  617.2 3.9 collective-permute-done.22
  623.6 2.1 collective-permute-start.28
  625.7 4.3 collective-permute-done.23
  (361 shorter events, 116.0 us)
Async XLA Ops:
  0.6 186.1 %copy-start = (bf16[1024,1024]{1,0:T(8,128)(2,1)S(1)}, bf16[1024,1024]{1,0:T(8,128)(2,1)}, u32[]{:S(2)}) copy-start(bf16[1024,1024]{1,0:T(8,128)(2,1)} %param.26) | copy-start | bytes 6291460
  30.0 73.1 %copy-start.15 = (s32[1,32]{1,0:T(1,128)S(1)}, s32[1,32]{1,0:T(1,128)}, u32[]{:S(2)}) copy-start(s32[1,32]{1,0:T(1,128)} %param.19) | copy-start | bytes 388
  30.0 73.1 %copy-start.16 = (s32[1,32]{1,0:T(1,128)S(1)}, s32[1,32]{1,0:T(1,128)}, u32[]{:S(2)}) copy-start(s32[1,32]{1,0:T(1,128)} %param.20) | copy-start | bytes 388
  30.0 60.5 %all-to-all-start = ((bf16[16,5,64,256]{3,2,1,0:T(8,128)(2,1)}), bf16[16,5,64,256]{3,2,1,0:T(8,128)(2,1)}, u32[]{:S(2)}, u32[]{:S(2)}) async-start(bf16[16,5,64,256]{3,2,1,0:T(8,128)(2,1)} %copy-done.10), calls=%async_computation | async-start | bytes 5242880 | tf_op jit(solution)/shard_map/all_to_all | solution.py:772
  90.5 42.6 %all-to-all-start.2 = ((bf16[16,1,64,256]{3,2,1,0:T(8,128)(2,1)}), bf16[16,1,64,256]{3,2,1,0:T(8,128)(2,1)}, u32[]{:S(2)}, u32[]{:S(2)}) async-start(bf16[16,1,64,256]{3,2,1,0:T(8,128)(2,1)} %copy-done.12), calls=%async_computation.2 | async-start | bytes 1048576 | tf_op jit(solution)/shard_map/all_to_all | solution.py:772
  158.3 22.4 %slice-start.1 = ((f32[6144]{0:T(1024)}), f32[4096]{0:T(1024)S(1)}, s32[]{:S(2)}) async-start(f32[6144]{0:T(1024)} %param.23), calls=%async_computation.9 | async-start | bytes 32768 | tf_op jit(solution)/shard_map/slice | solution.py:782
  158.3 17.9 %all-to-all-start.3 = ((bf16[16,64,256]{2,1,0:T(8,128)(2,1)}), bf16[16,64,256]{2,1,0:T(8,128)(2,1)}, u32[]{:S(2)}, u32[]{:S(2)}) async-start(bf16[16,64,256]{2,1,0:T(8,128)(2,1)} %copy-done.13), calls=%async_computation.3 | async-start | bytes 1048576 | tf_op jit(solution)/shard_map/all_to_all | solution.py:775
  176.2 15.3 %all-to-all-start.1 = ((bf16[16,64,256]{2,1,0:T(8,128)(2,1)}), bf16[16,64,256]{2,1,0:T(8,128)(2,1)}, u32[]{:S(2)}, u32[]{:S(2)}) async-start(bf16[16,64,256]{2,1,0:T(8,128)(2,1)} %copy-done.11), calls=%async_computation.1 | async-start | bytes 1048576 | tf_op jit(solution)/shard_map/all_to_all | solution.py:775
  185.5 61.5 %copy-start.56 = (f32[2,1024]{1,0:T(2,128)}, f32[2,1024]{1,0:T(2,128)S(1)}, u32[]{:S(2)}) copy-start(f32[2,1024]{1,0:T(2,128)S(1)} %get-tuple-element.148) | copy-start | bytes 24580
  220.2 61.6 %collective-permute-start = (bf16[2048,1024]{1,0:T(8,128)(2,1)}, bf16[2048,1024]{1,0:T(8,128)(2,1)}, u32[]{:S(2)}, u32[]{:S(2)}) collective-permute-start(bf16[2048,1024]{1,0:T(8,128)(2,1)} %get-tuple-element.60), channel_id=1, source_target_pairs={{0,16},{16,0},{1,17},{17,1},{2,18},{18,2},{3,19},{19,3},{4,20},{20... | collective-permute-start | bytes 12582920 | tf_op jit(solution)/shard_map/ppermute | solution.py:330
  220.3 70.5 %collective-permute-start.1 = (bf16[1024,2048]{1,0:T(8,128)(2,1)}, bf16[1024,2048]{1,0:T(8,128)(2,1)}, u32[]{:S(2)}, u32[]{:S(2)}) collective-permute-start(bf16[1024,2048]{1,0:T(8,128)(2,1)} %get-tuple-element.62), channel_id=1, source_target_pairs={{0,16},{16,0},{1,17},{17,1},{2,18},{18,2},{3,19},{19,3},{4,20},{20... | collective-permute-start | bytes 12582920 | tf_op jit(solution)/shard_map/ppermute | solution.py:330
  250.0 8.0 %copy-start.63 = (f32[512]{0:T(512)}, f32[512]{0:T(512)S(1)}, u32[]{:S(2)}) copy-start(f32[512]{0:T(512)S(1)} %negate_multiply_fusion.1) | copy-start | bytes 6148
  255.2 6.2 collective-permute-start.2
  264.1 14.6 %collective-permute-start.5 = (bf16[2,2,2,1,64,512]{5,4,3,2,1,0:T(8,128)(2,1)}, bf16[2,2,2,1,64,512]{5,4,3,2,1,0:T(8,128)(2,1)}, u32[]{:S(2)}, u32[]{:S(2)}) collective-permute-start(bf16[2,2,2,1,64,512]{5,4,3,2,1,0:T(8,128)(2,1)} %get-tuple-element.123), channel_id=1, source_target_pairs={{0,1},{1,0},{2,3},{3,2},{4,5},{5,4},{6,7},{7,6},{8,9},{9,8},{10,11... | collective-permute-start | bytes 1572872 | tf_op jit(solution)/shard_map/ppermute | solution.py:330
  273.0 31.1 %all-to-all-start.4 = ((bf16[16,64,256]{2,1,0:T(8,128)(2,1)}), bf16[16,64,256]{2,1,0:T(8,128)(2,1)}, u32[]{:S(2)}, u32[]{:S(2)}) async-start(bf16[16,64,256]{2,1,0:T(8,128)(2,1)} %bitcast.244), calls=%async_computation.4 | async-start | bytes 1048576 | tf_op jit(solution)/shard_map/all_to_all | solution.py:772
  280.7 21.6 %collective-permute-start.8 = (bf16[2,2,1,1,64,512]{5,4,3,2,1,0:T(8,128)(2,1)}, bf16[2,2,1,1,64,512]{5,4,3,2,1,0:T(8,128)(2,1)}, u32[]{:S(2)}, u32[]{:S(2)}) collective-permute-start(bf16[2,2,1,1,64,512]{5,4,3,2,1,0:T(8,128)(2,1)} %get-tuple-element.127), channel_id=1, source_target_pairs={{0,2},{1,3},{2,0},{3,1},{4,6},{5,7},{6,4},{7,5},{8,10},{9,11},{10,... | collective-permute-start | bytes 786440 | tf_op jit(solution)/shard_map/ppermute | solution.py:330
  281.8 9.0 %copy-start.40 = (bf16[1024,2048]{1,0:T(8,128)(2,1)S(1)}, bf16[1024,2048]{1,0:T(8,128)(2,1)}, u32[]{:S(2)}) copy-start(bf16[1024,2048]{1,0:T(8,128)(2,1)} %get-tuple-element.61) | copy-start | bytes 12582916
  289.7 52.5 %collective-permute-start.3 = (bf16[2,2,2,1,128,1024]{5,4,3,2,1,0:T(8,128)(2,1)}, bf16[2,2,2,1,128,1024]{5,4,3,2,1,0:T(8,128)(2,1)}, u32[]{:S(2)}, u32[]{:S(2)}) collective-permute-start(bf16[2,2,2,1,128,1024]{5,4,3,2,1,0:T(8,128)(2,1)} %get-tuple-element.104), channel_id=1, source_target_pairs={{0,1},{1,0},{2,3},{3,2},{4,5},{5,4},{6,7},{7,6},{8,9},{9,8},{10,11... | collective-permute-start | bytes 6291464 | tf_op jit(solution)/shard_map/ppermute | solution.py:330
  297.5 53.7 %collective-permute-start.4 = (bf16[2,2,1,2,64,2048]{5,4,3,2,1,0:T(8,128)(2,1)}, bf16[2,2,1,2,64,2048]{5,4,3,2,1,0:T(8,128)(2,1)}, u32[]{:S(2)}, u32[]{:S(2)}) collective-permute-start(bf16[2,2,1,2,64,2048]{5,4,3,2,1,0:T(8,128)(2,1)} %get-tuple-element.102), channel_id=1, source_target_pairs={{0,2},{1,3},{2,0},{3,1},{4,6},{5,7},{6,4},{7,5},{8,10},{9,11},{10,... | collective-permute-start | bytes 6291464 | tf_op jit(solution)/shard_map/ppermute | solution.py:330
  304.1 51.9 %all-to-all-start.6 = ((bf16[16,64,256]{2,1,0:T(8,128)(2,1)}), bf16[16,64,256]{2,1,0:T(8,128)(2,1)}, u32[]{:S(2)}, u32[]{:S(2)}) async-start(bf16[16,64,256]{2,1,0:T(8,128)(2,1)} %bitcast.38), calls=%async_computation.6 | async-start | bytes 1048576 | tf_op jit(solution)/shard_map/all_to_all | solution.py:772
  342.2 9.0 %copy-start.35 = (bf16[2,2,1,2,64,2048]{5,4,3,2,1,0:T(8,128)(2,1)S(1)}, bf16[2,2,1,2,64,2048]{5,4,3,2,1,0:T(8,128)(2,1)}, u32[]{:S(2)}) copy-start(bf16[2,2,1,2,64,2048]{5,4,3,2,1,0:T(8,128)(2,1)} %get-tuple-element.101) | copy-start | bytes 6291460
  346.9 47.0 %collective-permute-start.6 = (bf16[2,2,1,1,128,1024]{5,4,3,2,1,0:T(8,128)(2,1)}, bf16[2,2,1,1,128,1024]{5,4,3,2,1,0:T(8,128)(2,1)}, u32[]{:S(2)}, u32[]{:S(2)}) collective-permute-start(bf16[2,2,1,1,128,1024]{5,4,3,2,1,0:T(8,128)(2,1)} %get-tuple-element.108), channel_id=1, source_target_pairs={{0,2},{1,3},{2,0},{3,1},{4,6},{5,7},{6,4},{7,5},{8,10},{9,11},{10,... | collective-permute-start | bytes 3145736 | tf_op jit(solution)/shard_map/ppermute | solution.py:330
  355.0 41.5 %collective-permute-start.7 = (bf16[2,2,1,1,64,2048]{5,4,3,2,1,0:T(8,128)(2,1)}, bf16[2,2,1,1,64,2048]{5,4,3,2,1,0:T(8,128)(2,1)}, u32[]{:S(2)}, u32[]{:S(2)}) collective-permute-start(bf16[2,2,1,1,64,2048]{5,4,3,2,1,0:T(8,128)(2,1)} %get-tuple-element.106), channel_id=1, source_target_pairs={{0,1},{1,0},{2,3},{3,2},{4,5},{5,4},{6,7},{7,6},{8,9},{9,8},{10,11... | collective-permute-start | bytes 3145736 | tf_op jit(solution)/shard_map/ppermute | solution.py:330
  355.9 43.1 %all-to-all-start.5 = ((bf16[16,64,256]{2,1,0:T(8,128)(2,1)}), bf16[16,64,256]{2,1,0:T(8,128)(2,1)S(1)}, u32[]{:S(2)}, u32[]{:S(2)}) async-start(bf16[16,64,256]{2,1,0:T(8,128)(2,1)} %get-tuple-element.65), calls=%async_computation.5 | async-start | bytes 1048576 | tf_op jit(solution)/shard_map/all_to_all | solution.py:775
  361.2 32.7 %copy-start.41 = (bf16[2,2,1,1,128,1024]{5,4,3,2,1,0:T(8,128)(2,1)S(1)}, bf16[2,2,1,1,128,1024]{5,4,3,2,1,0:T(8,128)(2,1)}, u32[]{:S(2)}) copy-start(bf16[2,2,1,1,128,1024]{5,4,3,2,1,0:T(8,128)(2,1)} %get-tuple-element.107) | copy-start | bytes 3145732
  399.1 103.1 %copy-start.4 = (bf16[16,64,256]{2,1,0:T(8,128)(2,1)}, bf16[16,64,256]{2,1,0:T(8,128)(2,1)S(1)}, u32[]{:S(2)}) copy-start(bf16[16,64,256]{2,1,0:T(8,128)(2,1)S(1)} %all-to-all-done.5) | copy-start | bytes 1572868
  399.1 103.1 %all-to-all-start.7 = ((bf16[16,5,64,256]{3,2,1,0:T(8,128)(2,1)}), bf16[16,5,64,256]{3,2,1,0:T(8,128)(2,1)}, u32[]{:S(2)}, u32[]{:S(2)}) async-start(bf16[16,5,64,256]{3,2,1,0:T(8,128)(2,1)} %attend_back1.1), calls=%async_computation.7 | async-start | bytes 5242880 | tf_op jit(solution)/shard_map/all_to_all | solution.py:775
  408.5 79.7 %copy-start.43 = (bf16[2,1,1,1,64,2048]{5,4,3,2,1,0:T(8,128)(2,1)S(1)}, bf16[2,1,1,1,64,2048]{5,4,3,2,1,0:T(8,128)(2,1)}, u32[]{:S(2)}) copy-start(bf16[2,1,1,1,64,2048]{5,4,3,2,1,0:T(8,128)(2,1)} %get-tuple-element.120) | copy-start | bytes 1572868
  409.1 43.2 %collective-permute-start.30 = (bf16[2,1,1,1,64,512]{5,4,3,2,1,0:T(8,128)(2,1)S(1)}, bf16[2,1,1,1,64,512]{5,4,3,2,1,0:T(8,128)(2,1)S(1)}, u32[]{:S(2)}, u32[]{:S(2)}) collective-permute-start(bf16[2,1,1,1,64,512]{5,4,3,2,1,0:T(8,128)(2,1)S(1)} %copy-done.58), channel_id=1, source_target_pairs={{0,4},{1,5},{2,6},{3,7},{4,0},{5,1},{6,2},{7,3},{8,12},{9,13},{10,... | collective-permute-start | bytes 393224 | tf_op jit(solution)/shard_map/ppermute | solution.py:330
  411.8 53.3 %collective-permute-start.33 = (bf16[2,1,1,1,64,2048]{5,4,3,2,1,0:T(8,128)(2,1)}, bf16[2,1,1,1,64,2048]{5,4,3,2,1,0:T(8,128)(2,1)S(1)}, u32[]{:S(2)}, u32[]{:S(2)}) collective-permute-start(bf16[2,1,1,1,64,2048]{5,4,3,2,1,0:T(8,128)(2,1)} %get-tuple-element.121), channel_id=1, source_target_pairs={{0,4},{1,5},{2,6},{3,7},{4,0},{5,1},{6,2},{7,3},{8,12},{9,13},{10,... | collective-permute-start | bytes 1572872 | tf_op jit(solution)/shard_map/ppermute | solution.py:330
  452.4 12.6 %collective-permute-start.31 = (bf16[1,1,1,1,64,512]{5,4,3,2,1,0:T(8,128)(2,1)S(1)}, bf16[1,1,1,1,64,512]{5,4,3,2,1,0:T(8,128)(2,1)S(1)}, u32[]{:S(2)}, u32[]{:S(2)}) collective-permute-start(bf16[1,1,1,1,64,512]{5,4,3,2,1,0:T(8,128)(2,1)S(1)} %add_convert_fusion.44), channel_id=1, source_target_pairs={{0,8},{1,9},{2,10},{3,11},{4,12},{5,13},{6,14},{7,15},{8,0},{9,1},... | collective-permute-start | bytes 196616 | tf_op jit(solution)/shard_map/ppermute | solution.py:330
  459.9 17.4 %collective-permute-start.36 = (bf16[2,1,1,1,128,1024]{5,4,3,2,1,0:T(8,128)(2,1)}, bf16[2,1,1,1,128,1024]{5,4,3,2,1,0:T(8,128)(2,1)S(1)}, u32[]{:S(2)}, u32[]{:S(2)}) collective-permute-start(bf16[2,1,1,1,128,1024]{5,4,3,2,1,0:T(8,128)(2,1)} %get-tuple-element.119), channel_id=1, source_target_pairs={{0,4},{1,5},{2,6},{3,7},{4,0},{5,1},{6,2},{7,3},{8,12},{9,13},{10,... | collective-permute-start | bytes 1572872 | tf_op jit(solution)/shard_map/ppermute | solution.py:330
  465.0 4.8 collective-permute-start.32
  465.1 12.3 %copy-start.51 = (bf16[2,1,1,1,64,2048]{5,4,3,2,1,0:T(8,128)(2,1)}, bf16[2,1,1,1,64,2048]{5,4,3,2,1,0:T(8,128)(2,1)S(1)}, u32[]{:S(2)}) copy-start(bf16[2,1,1,1,64,2048]{5,4,3,2,1,0:T(8,128)(2,1)S(1)} %collective-permute-done.33) | copy-start | bytes 1572868
  466.3 21.9 %collective-permute-start.34 = (bf16[1,1,1,1,64,2048]{5,4,3,2,1,0:T(8,128)(2,1)S(1)}, bf16[1,1,1,1,64,2048]{5,4,3,2,1,0:T(8,128)(2,1)S(1)}, u32[]{:S(2)}, u32[]{:S(2)}) collective-permute-start(bf16[1,1,1,1,64,2048]{5,4,3,2,1,0:T(8,128)(2,1)S(1)} %add_convert_fusion.27), channel_id=1, source_target_pairs={{0,8},{1,9},{2,10},{3,11},{4,12},{5,13},{6,14},{7,15},{8,0},{9,1},... | collective-permute-start | bytes 786440 | tf_op jit(solution)/shard_map/ppermute | solution.py:330
  477.3 16.3 %collective-permute-start.37 = (bf16[1,1,1,1,128,1024]{5,4,3,2,1,0:T(8,128)(2,1)S(1)}, bf16[1,1,1,1,128,1024]{5,4,3,2,1,0:T(8,128)(2,1)S(1)}, u32[]{:S(2)}, u32[]{:S(2)}) collective-permute-start(bf16[1,1,1,1,128,1024]{5,4,3,2,1,0:T(8,128)(2,1)S(1)} %add_convert_fusion.24), channel_id=1, source_target_pairs={{0,8},{1,9},{2,10},{3,11},{4,12},{5,13},{6,14},{7,15},{8,0},{9,1},... | collective-permute-start | bytes 786440 | tf_op jit(solution)/shard_map/ppermute | solution.py:330
  489.3 4.5 collective-permute-start.35
  493.7 6.4 %collective-permute-start.38 = (bf16[128,1024]{1,0:T(8,128)(2,1)S(1)}, bf16[128,1024]{1,0:T(8,128)(2,1)}, u32[]{:S(2)}, u32[]{:S(2)}) collective-permute-start(bf16[128,1024]{1,0:T(8,128)(2,1)S(1)} %fusion.40), channel_id=1, source_target_pairs={{0,16},{16,0},{1,17},{17,1},{2,18},{18,2},{3,19},{19,3},{4,20},{20... | collective-permute-start | bytes 786440 | tf_op jit(solution)/shard_map/ppermute | solution.py:330
  502.2 8.8 %copy-start.8 = (bf16[512,1024]{1,0:T(8,128)(2,1)S(1)}, bf16[512,1024]{1,0:T(8,128)(2,1)}, u32[]{:S(2)}) copy-start(bf16[512,1024]{1,0:T(8,128)(2,1)} %copy-done.6) | copy-start | bytes 3145732
  510.5 66.9 %collective-permute-start.19 = (bf16[3,1024,512]{2,1,0:T(8,128)(2,1)}, bf16[3,1024,512]{2,1,0:T(8,128)(2,1)}, u32[]{:S(2)}, u32[]{:S(2)}) collective-permute-start(bf16[3,1024,512]{2,1,0:T(8,128)(2,1)} %get-tuple-element.78), channel_id=1, source_target_pairs={{0,16},{16,0},{1,17},{17,1},{2,18},{18,2},{3,19},{19,3},{4,20},{20... | collective-permute-start | bytes 9437192 | tf_op jit(solution)/shard_map/ppermute | solution.py:330
  512.0 9.5 %copy-start.59 = (f32[2,1024]{1,0:T(2,128)S(1)}, f32[2,1024]{1,0:T(2,128)}, u32[]{:S(2)}) copy-start(f32[2,1024]{1,0:T(2,128)} %get-tuple-element.156) | copy-start | bytes 24580
  528.4 9.5 %copy-start.61 = (bf16[2,3584]{1,0:T(2,128)(2,1)}, bf16[2,3584]{1,0:T(2,128)(2,1)S(1)}, u32[]{:S(2)}) copy-start(bf16[2,3584]{1,0:T(2,128)(2,1)S(1)} %pad_maximum_fusion.16) | copy-start | bytes 43012
  528.5 4.7 collective-permute-start.14
  528.8 5.7 collective-permute-start.9
  533.2 4.7 collective-permute-start.15
  534.5 10.6 %copy-start.49 = (bf16[2,7424]{1,0:T(2,128)(2,1)}, bf16[2,7424]{1,0:T(2,128)(2,1)S(1)}, u32[]{:S(2)}) copy-start(bf16[2,7424]{1,0:T(2,128)(2,1)S(1)} %collective-permute-done.9) | copy-start | bytes 89092
  534.6 5.5 collective-permute-start.10
  538.0 4.5 collective-permute-start.16
  540.2 4.9 collective-permute-start.11
  542.6 6.2 collective-permute-start.17
  546.0 12.4 %collective-permute-start.12 = (bf16[16,7424]{1,0:T(8,128)(2,1)}, bf16[16,7424]{1,0:T(8,128)(2,1)S(1)}, u32[]{:S(2)}, u32[]{:S(2)}) collective-permute-start(bf16[16,7424]{1,0:T(8,128)(2,1)} %pad_maximum_fusion.7), channel_id=1, source_target_pairs={{0,1},{1,0},{2,3},{3,2},{4,5},{5,4},{6,7},{7,6},{8,9},{9,8},{10,11... | collective-permute-start | bytes 712712 | tf_op jit(solution)/shard_map/ppermute | solution.py:330
  553.2 12.6 %collective-permute-start.18 = (bf16[32,3584]{1,0:T(8,128)(2,1)}, bf16[32,3584]{1,0:T(8,128)(2,1)}, u32[]{:S(2)}, u32[]{:S(2)}) collective-permute-start(bf16[32,3584]{1,0:T(8,128)(2,1)} %concatenate.119), channel_id=1, source_target_pairs={{0,16},{16,0},{1,17},{17,1},{2,18},{18,2},{3,19},{19,3},{4,20},{20... | collective-permute-start | bytes 688136 | tf_op jit(solution)/shard_map/ppermute | solution.py:330
  561.3 10.0 %collective-permute-start.13 = (bf16[32,7424]{1,0:T(8,128)(2,1)}, bf16[32,7424]{1,0:T(8,128)(2,1)}, u32[]{:S(2)}, u32[]{:S(2)}) collective-permute-start(bf16[32,7424]{1,0:T(8,128)(2,1)} %concatenate.112), channel_id=1, source_target_pairs={{0,16},{16,0},{1,17},{17,1},{2,18},{18,2},{3,19},{19,3},{4,20},{20... | collective-permute-start | bytes 1425416 | tf_op jit(solution)/shard_map/ppermute | solution.py:330
  580.3 19.5 %collective-permute-start.20 = (bf16[3,2,2,2,1,64,256]{6,5,4,3,2,1,0:T(8,128)(2,1)S(1)}, bf16[3,2,2,2,1,64,256]{6,5,4,3,2,1,0:T(8,128)(2,1)S(1)}, u32[]{:S(2)}, u32[]{:S(2)}) collective-permute-start(bf16[3,2,2,2,1,64,256]{6,5,4,3,2,1,0:T(8,128)(2,1)S(1)} %get-tuple-element.113), channel_id=1, source_target_pairs={{0,1},{1,0},{2,3},{3,2},{4,5},{5,4},{6,7},{7,6},{8,9},{9,8},{10,11... | collective-permute-start | bytes 2359304 | tf_op jit(solution)/shard_map/ppermute | solution.py:330
  582.4 20.2 %collective-permute-start.25 = (bf16[3,2,2,1,2,64,256]{6,5,4,3,2,1,0:T(8,128)(2,1)S(1)}, bf16[3,2,2,1,2,64,256]{6,5,4,3,2,1,0:T(8,128)(2,1)S(1)}, u32[]{:S(2)}, u32[]{:S(2)}) collective-permute-start(bf16[3,2,2,1,2,64,256]{6,5,4,3,2,1,0:T(8,128)(2,1)S(1)} %add_convert_fusion.9), channel_id=1, source_target_pairs={{0,2},{1,3},{2,0},{3,1},{4,6},{5,7},{6,4},{7,5},{8,10},{9,11},{10,... | collective-permute-start | bytes 2359304 | tf_op jit(solution)/shard_map/ppermute | solution.py:330
  600.9 10.5 %collective-permute-start.21 = (bf16[3,2,2,1,1,64,256]{6,5,4,3,2,1,0:T(8,128)(2,1)}, bf16[3,2,2,1,1,64,256]{6,5,4,3,2,1,0:T(8,128)(2,1)}, u32[]{:S(2)}, u32[]{:S(2)}) collective-permute-start(bf16[3,2,2,1,1,64,256]{6,5,4,3,2,1,0:T(8,128)(2,1)} %get-tuple-element.125), channel_id=1, source_target_pairs={{0,2},{1,3},{2,0},{3,1},{4,6},{5,7},{6,4},{7,5},{8,10},{9,11},{10,... | collective-permute-start | bytes 1179656 | tf_op jit(solution)/shard_map/ppermute | solution.py:330
  603.7 10.3 %collective-permute-start.26 = (bf16[3,2,2,1,1,64,256]{6,5,0,4,3,2,1:T(8,128)(2,1)}, bf16[3,2,2,1,1,64,256]{6,5,0,4,3,2,1:T(8,128)(2,1)S(1)}, u32[]{:S(2)}, u32[]{:S(2)}) collective-permute-start(bf16[3,2,2,1,1,64,256]{6,5,0,4,3,2,1:T(8,128)(2,1)} %get-tuple-element.133), channel_id=1, source_target_pairs={{0,1},{1,0},{2,3},{3,2},{4,5},{5,4},{6,7},{7,6},{8,9},{9,8},{10,11... | collective-permute-start | bytes 1179656 | tf_op jit(solution)/shard_map/ppermute | solution.py:330
  612.5 8.5 %collective-permute-start.22 = (bf16[3,2,1,1,1,64,256]{6,5,4,3,2,1,0:T(8,128)(2,1)S(1)}, bf16[3,2,1,1,1,64,256]{6,5,4,3,2,1,0:T(8,128)(2,1)S(1)}, u32[]{:S(2)}, u32[]{:S(2)}) collective-permute-start(bf16[3,2,1,1,1,64,256]{6,5,4,3,2,1,0:T(8,128)(2,1)S(1)} %get-tuple-element.129), channel_id=1, source_target_pairs={{0,4},{1,5},{2,6},{3,7},{4,0},{5,1},{6,2},{7,3},{8,12},{9,13},{10,... | collective-permute-start | bytes 589832 | tf_op jit(solution)/shard_map/ppermute | solution.py:330
  615.8 7.7 %collective-permute-start.27 = (bf16[3,2,1,1,1,64,256]{6,5,0,4,3,2,1:T(8,128)(2,1)S(1)}, bf16[3,2,1,1,1,64,256]{6,5,0,4,3,2,1:T(8,128)(2,1)S(1)}, u32[]{:S(2)}, u32[]{:S(2)}) collective-permute-start(bf16[3,2,1,1,1,64,256]{6,5,0,4,3,2,1:T(8,128)(2,1)S(1)} %get-tuple-element.131), channel_id=1, source_target_pairs={{0,4},{1,5},{2,6},{3,7},{4,0},{5,1},{6,2},{7,3},{8,12},{9,13},{10,... | collective-permute-start | bytes 589832 | tf_op jit(solution)/shard_map/ppermute | solution.py:330
  621.1 8.9 %collective-permute-start.23 = (bf16[3,1,1,1,1,64,256]{6,5,4,3,2,1,0:T(8,128)(2,1)S(1)}, bf16[3,1,1,1,1,64,256]{6,5,4,3,2,1,0:T(8,128)(2,1)S(1)}, u32[]{:S(2)}, u32[]{:S(2)}) collective-permute-start(bf16[3,1,1,1,1,64,256]{6,5,4,3,2,1,0:T(8,128)(2,1)S(1)} %add_convert_fusion.41), channel_id=1, source_target_pairs={{0,8},{1,9},{2,10},{3,11},{4,12},{5,13},{6,14},{7,15},{8,0},{9,1},... | collective-permute-start | bytes 294920 | tf_op jit(solution)/shard_map/ppermute | solution.py:330
  623.5 10.0 %copy-start.1 = (bf16[1024,1024]{1,0:T(8,128)(2,1)S(1)}, bf16[1024,1024]{1,0:T(8,128)(2,1)}, u32[]{:S(2)}) copy-start(bf16[1024,1024]{1,0:T(8,128)(2,1)} %param.26) | copy-start | bytes 6291460
  623.6 7.5 %collective-permute-start.28 = (bf16[3,1,1,1,1,64,256]{6,5,0,4,3,2,1:T(8,128)(2,1)S(1)}, bf16[3,1,1,1,1,64,256]{6,5,0,4,3,2,1:T(8,128)(2,1)S(1)}, u32[]{:S(2)}, u32[]{:S(2)}) collective-permute-start(bf16[3,1,1,1,1,64,256]{6,5,0,4,3,2,1:T(8,128)(2,1)S(1)} %add_convert_fusion.38), channel_id=1, source_target_pairs={{0,8},{1,9},{2,10},{3,11},{4,12},{5,13},{6,14},{7,15},{8,0},{9,1},... | collective-permute-start | bytes 294920 | tf_op jit(solution)/shard_map/ppermute | solution.py:330
  630.1 1.4 collective-permute-start.24
  631.1 1.4 collective-permute-start.29
  (65 other events, 192.8 us)

commit v2 on v1

--- a/solution.py
+++ b/solution.py
@@ -68,7 +68,7 @@
     return whole(jnp.cos), whole(jnp.sin)
 
 
-def walk_frames(frames, per_device, part, segments_ref, live_ref, list_ref, visit):
+def walk_frames(frames, per_device, parts, segments_ref, live_ref, list_ref, visit):
     def step(source, held):
         for place in range(per_device):
             frame = source * per_device + place
@@ -76,19 +76,15 @@
             fresh = (frame == 0) | (segments_ref[frame] != segments_ref[before])
             held = jnp.where(fresh, 0, held)
             list_ref[held] = frame
-            if place == part:
-                visit(source, frame, held + 1)
+            if place in parts:
+                visit(source, place, frame, held + 1)
             held = held + jnp.where(live_ref[frame] == 1, 1, 0)
         return held
 
     lax.fori_loop(0, frames // per_device, step, jnp.int32(0))
 
 
-def attend_kernel(per_device, part, slot, segments_ref, live_ref, x_ref, q_ref, *refs):
-    if part == 0:
-        mix_ref, wide_ref, lse_ref, kv_ref, list_ref = refs
-    else:
-        kv_ref, mix_ref, wide_ref, lse_ref, list_ref = refs
+def attend_kernel(per_device, segments_ref, live_ref, x_ref, mix_ref, wide_ref, lse_ref, kv_ref, list_ref):
     frames = kv_ref.shape[0]
 
     def turn(source, carry):
@@ -99,11 +95,10 @@
             kv_ref[source * per_device + place] = both.astype(F32).T.astype(BF16)
         return carry
 
-    if part == 0:
-        lax.fori_loop(0, frames // per_device, turn, 0)
-
-    def visit(source, frame, count):
-        query = q_ref[source, slot]
+    lax.fori_loop(0, frames // per_device, turn, 0)
+
+    def visit(source, place, frame, count):
+        query = x_ref[source, 2 * per_device + place]
         query_side = jnp.concatenate([query, jnp.zeros_like(query)], axis=0)
 
         def scores_of(other):
@@ -148,11 +143,11 @@
             carry,
         )
         result = accum * (1.0 / total)
-        wide_ref[source] = result
-        mix_ref[source] = result.astype(BF16)
-        lse_ref[pl.ds(source, 1), :] = top + jnp.log(total)
-
-    walk_frames(frames, per_device, part, segments_ref, live_ref, list_ref, visit)
+        wide_ref[source, place] = result
+        mix_ref[source, place] = result.astype(BF16)
+        lse_ref[pl.ds(frame, 1), :] = top + jnp.log(total)
+
+    walk_frames(frames, per_device, range(per_device), segments_ref, live_ref, list_ref, visit)
 
 
 def whole_spec():
@@ -163,24 +158,20 @@
     return pl.BlockSpec(memory_space=pltpu.SMEM)
 
 
-def attend(part, per_device, slot, segments, live, x, query, kv):
+def attend(per_device, segments, live, x):
     sources = x.shape[0]
     frames = sources * per_device
-    pairs = sources * 6
-    outs = [
-        jax.ShapeDtypeStruct((sources, HEAD, PATCHES), BF16),
-        jax.ShapeDtypeStruct((sources, HEAD, PATCHES), F32),
-        jax.ShapeDtypeStruct((sources, PATCHES), F32),
-    ]
-    args = [segments, live, x, query]
-    if part == 0:
-        outs.append(jax.ShapeDtypeStruct((frames, PATCHES, 2 * HEAD), BF16))
-    else:
-        args.append(kv)
-    result = pl.pallas_call(
-        functools.partial(attend_kernel, per_device, part, slot),
-        out_shape=tuple(outs),
-        in_specs=[scalar_spec(), scalar_spec()] + [whole_spec()] * (len(args) - 2),
+    pairs = frames * 6
+    outs = (
+        jax.ShapeDtypeStruct((sources, per_device, HEAD, PATCHES), BF16),
+        jax.ShapeDtypeStruct((sources, per_device, HEAD, PATCHES), F32),
+        jax.ShapeDtypeStruct((frames, PATCHES), F32),
+        jax.ShapeDtypeStruct((frames, PATCHES, 2 * HEAD), BF16),
+    )
+    return pl.pallas_call(
+        functools.partial(attend_kernel, per_device),
+        out_shape=outs,
+        in_specs=[scalar_spec(), scalar_spec(), whole_spec()],
         out_specs=(whole_spec(),) * len(outs),
         scratch_shapes=[pltpu.SMEM((frames,), jnp.int32)],
         cost_estimate=pl.CostEstimate(
@@ -189,20 +180,17 @@
             transcendentals=pairs * PATCHES * PATCHES,
         ),
         compiler_params=pltpu.CompilerParams(vmem_limit_bytes=40 << 20),
-        name="attend%d" % part,
-    )(*args)
-    return result if part == 0 else tuple(result) + (kv,)
+        name="attend",
+    )(segments, live, x)
 
 
 def attend_back_kernel(
     per_device,
     part,
-    slot,
     last,
     segments_ref,
     live_ref,
     x_ref,
-    q_ref,
     kv_ref,
     wide_ref,
     lse_ref,
@@ -230,17 +218,17 @@
         sine = sin_ref[frame]
         return jnp.concatenate([lower * cosine + upper * sine, upper * cosine - lower * sine], axis=0)
 
-    def visit(source, frame, count):
-        query = q_ref[source, slot]
-        d_mix = d_mix_ref[source]
+    def visit(source, place, frame, count):
+        query = x_ref[source, 2 * per_device + place]
+        d_mix = d_mix_ref[source, place]
         blank = jnp.zeros_like(query)
         query_side = jnp.concatenate([query, blank], axis=0)
         d_mix_side = jnp.concatenate([blank, d_mix], axis=0)
         both = jnp.concatenate(
             [query_side.astype(F32).T.astype(BF16), d_mix_side.astype(F32).T.astype(BF16)], axis=0
         )
-        lse = lse_ref[pl.ds(source, 1), :]
-        delta = jnp.sum(d_mix.astype(F32) * wide_ref[source], axis=0, keepdims=True)
+        lse = lse_ref[pl.ds(frame, 1), :]
+        delta = jnp.sum(d_mix.astype(F32) * wide_ref[source, place], axis=0, keepdims=True)
 
         def block(other):
             key_value = kv_ref[other]
@@ -273,7 +261,7 @@
         else:
             out_ref[source] = d_query
 
-    walk_frames(frames, per_device, part, segments_ref, live_ref, list_ref, visit)
+    walk_frames(frames, per_device, (part,), segments_ref, live_ref, list_ref, visit)
 
     def finish(source, carry):
         for place in range(per_device):
@@ -288,13 +276,13 @@
 
 
 def attend_back(
-    part, per_device, slot, segments, live, x, query, kv, wide, lse, d_mix, cosine, sine, before
+    part, per_device, segments, live, x, kv, wide, lse, d_mix, cosine, sine, before
 ):
     sources = x.shape[0]
     frames = sources * per_device
     pairs = sources * 6
     last = part == per_device - 1
-    args = [segments, live, x, query, kv, wide, lse, d_mix, cosine, sine]
+    args = [segments, live, x, kv, wide, lse, d_mix, cosine, sine]
     dkv = (frames, PATCHES, 2 * HEAD)
     lists = pltpu.SMEM((frames,), jnp.int32)
     if last:
@@ -310,7 +298,7 @@
         out_specs = (whole_spec(), whole_spec())
         scratch = [lists]
     return pl.pallas_call(
-        functools.partial(attend_back_kernel, per_device, part, slot, last),
+        functools.partial(attend_back_kernel, per_device, part, last),
         out_shape=outs,
         in_specs=[scalar_spec(), scalar_spec()] + [whole_spec()] * (len(args) - 2),
         out_specs=out_specs,
@@ -335,14 +323,12 @@
 
 
 def gather_all(value):
-    bit = lax.axis_size("seq") // 2
-    while bit:
-        value = jnp.concatenate([value, exchange(value, "seq", bit)], axis=0)
-        bit //= 2
-    bit = lax.axis_size("pack") // 2
-    while bit:
-        value = jnp.concatenate([value, exchange(value, "pack", bit)], axis=0)
-        bit //= 2
+    value = value[None]
+    for axis in ("seq", "pack"):
+        bit = lax.axis_size(axis) // 2
+        while bit:
+            value = jnp.concatenate([value, exchange(value, axis, bit)], axis=0)
+            bit //= 2
     return value
 
 
@@ -364,6 +350,9 @@
         axis = len(self.lead) + {8: 0, 4: 1, 2: 2, 1: 3}[bit]
         pieces = [lax.dynamic_slice_in_dim(part, which, 1, axis) for part in self.parts]
         return (pieces[0].astype(F32) + pieces[1].astype(F32)).astype(BF16)
+
+    def hold(self, *earlier):
+        self.parts = [after(part, *earlier) for part in self.parts]
 
     def stage(self):
         bit = self.order.pop(0)
@@ -402,8 +391,7 @@
     cos_ref,
     sin_ref,
     in_ref,
-    first_ref,
-    rest_ref,
+    x_ref,
 ):
     @pl.when(pl.program_id(0) == 0)
     def _():
@@ -435,15 +423,12 @@
             for head in range(group):
                 values = block[head * HEAD : (head + 1) * HEAD]
                 if kind == 0:
-                    values = (turned(values, place) * (HEAD**-0.5)).astype(BF16)
-                    if place == 0:
-                        first_ref[head, 2 * per_device] = values
-                    else:
-                        rest_ref[head, place - 1] = values
+                    values = turned(values, place) * (HEAD**-0.5)
+                    x_ref[head, 2 * per_device + place] = values.astype(BF16)
                 elif kind == 1:
-                    first_ref[head, place] = turned(values, place).astype(BF16)
+                    x_ref[head, place] = turned(values, place).astype(BF16)
                 else:
-                    first_ref[head, per_device + place] = values.astype(BF16)
+                    x_ref[head, per_device + place] = values.astype(BF16)
 
 
 def project(per_device, hidden, shift, scale, weight, bias, cosine, sine):
@@ -460,15 +445,13 @@
     def part(kind, rows):
         return pl.BlockSpec((rows, lanes), lambda step: (0, kind * steps + step))
 
-    first = (heads, 2 * per_device + 1, HEAD, PATCHES)
-    rest = (heads, per_device - 1, HEAD, PATCHES)
+    blocks = (heads, 3 * per_device, HEAD, PATCHES)
     return pl.pallas_call(
         functools.partial(project_kernel, per_device),
         grid=(steps,),
         out_shape=(
             jax.ShapeDtypeStruct((tokens, width), BF16),
-            jax.ShapeDtypeStruct(first, BF16),
-            jax.ShapeDtypeStruct(rest, BF16),
+            jax.ShapeDtypeStruct(blocks, BF16),
         ),
         in_specs=[whole((tokens, width)), whole(shift.shape), whole(scale.shape)]
         + [part(kind, width) for kind in range(3)]
@@ -476,8 +459,7 @@
         + [whole(cosine.shape), whole(sine.shape)],
         out_specs=(
             whole((tokens, width)),
-            pl.BlockSpec((group,) + first[1:], lambda step: (step, 0, 0, 0)),
-            pl.BlockSpec((group,) + rest[1:], lambda step: (step, 0, 0, 0)),
+            pl.BlockSpec((group,) + blocks[1:], lambda step: (step, 0, 0, 0)),
         ),
         cost_estimate=pl.CostEstimate(
             flops=2 * tokens * width * 3 * width,
@@ -602,13 +584,94 @@
     )(which.reshape(1), *args)
 
 
+def norm_back(values, d_in, scale):
+    centered = values - jnp.mean(values, axis=-1, keepdims=True)
+    spread = jnp.mean(centered * centered, axis=-1, keepdims=True)
+    inverse = lax.rsqrt(spread + EPSILON)
+    normed = centered * inverse
+    product = d_in * normed
+    d_shift = jnp.sum(d_in, axis=0, keepdims=True)
+    d_scale = jnp.sum(product, axis=0, keepdims=True)
+    scaled = 1.0 + scale
+    mean_d = jnp.mean(d_in * scaled, axis=-1, keepdims=True)
+    mean_p = jnp.mean(product * scaled, axis=-1, keepdims=True)
+    return (d_in * scaled - mean_d - normed * mean_p) * inverse, d_shift, d_scale
+
+
+def middle_back_kernel(
+    d_in_ref,
+    middle_ref,
+    grad_ref,
+    attn_ref,
+    scale_ref,
+    gate_ref,
+    weight_ref,
+    d_middle_ref,
+    d_attn_ref,
+    d_mix_ref,
+    d_shift_ref,
+    d_scale_ref,
+    d_gate_ref,
+    d_bias_ref,
+):
+    frame = pl.program_id(0)
+    mine = pl.ds(frame, 1)
+    back, d_shift, d_scale = norm_back(middle_ref[...], d_in_ref[...], scale_ref[mine, :])
+    d_middle = grad_ref[...].astype(F32) + back
+    d_middle_ref[...] = d_middle
+    d_shift_ref[mine, :] = d_shift
+    d_scale_ref[mine, :] = d_scale
+    d_gate_ref[mine, :] = jnp.sum(d_middle * attn_ref[...], axis=0, keepdims=True)
+    d_attn = (d_middle * gate_ref[mine, :]).astype(BF16)
+    d_attn_ref[...] = d_attn
+    d_bias_ref[mine, :] = jnp.sum(d_attn.astype(F32), axis=0, keepdims=True)
+    d_mix = dot_over(weight_ref[...], d_attn, 1, 1).astype(BF16)
+    for head in range(d_mix_ref.shape[0]):
+        d_mix_ref[head, 0] = d_mix[head * HEAD : (head + 1) * HEAD]
+
+
+def middle_back(per_device, d_in, middle, grads, attn_rows, scale, gate, weight):
+    tokens, width = d_in.shape
+    heads = width // HEAD
+    rows = pl.BlockSpec((PATCHES, width), lambda frame: (frame, 0))
+
+    def whole(shape):
+        return pl.BlockSpec(shape, lambda frame: (0,) * len(shape))
+
+    small = whole((per_device, width))
+    small_shape = jax.ShapeDtypeStruct((per_device, width), F32)
+    return pl.pallas_call(
+        middle_back_kernel,
+        grid=(per_device,),
+        out_shape=(
+            jax.ShapeDtypeStruct((tokens, width), F32),
+            jax.ShapeDtypeStruct((tokens, width), BF16),
+            jax.ShapeDtypeStruct((heads, per_device, HEAD, PATCHES), BF16),
+        )
+        + (small_shape,) * 4,
+        in_specs=[rows] * 4 + [small, small, whole(weight.shape)],
+        out_specs=(
+            rows,
+            rows,
+            pl.BlockSpec((heads, 1, HEAD, PATCHES), lambda frame: (0, frame, 0, 0)),
+        )
+        + (small,) * 4,
+        cost_estimate=pl.CostEstimate(
+            flops=2 * tokens * width * width, bytes_accessed=24 * tokens * width, transcendentals=0
+        ),
+        compiler_params=pltpu.CompilerParams(vmem_limit_bytes=40 << 20),
+        name="middle_back",
+    )(d_in, middle, grads, attn_rows, scale, gate, weight)
+
+
 def unproject_kernel(
     per_device, carried, which_ref, in_ref, first_ref, back_ref, wq_ref, wk_ref, wv_ref, *refs
 ):
     if carried:
-        before_ref = refs[0]
-        refs = refs[1:]
-    d_in_ref, d_weight_ref, d_bias_ref, turned_ref = refs
+        before_ref, hidden_ref, d_middle_ref, scale_ref = refs[:4]
+        d_weight_ref, d_bias_ref, grad_ref, d_shift_ref, d_scale_ref, d_in_ref, turned_ref = refs[4:]
+    else:
+        d_in_ref, d_weight_ref, d_bias_ref, turned_ref = refs
 
     @pl.when(pl.program_id(0) == 0)
     def _():
@@ -649,8 +712,22 @@
         d_weight_ref[kind] = d_weight[:, kind * lanes : (kind + 1) * lanes]
         d_bias_ref[kind] = d_bias[:, kind * lanes : (kind + 1) * lanes]
 
-
-def unproject(per_device, which, attn_in, first, back, weight, before):
+    if carried:
+
+        @pl.when(pl.program_id(0) == pl.num_programs(0) - 1)
+        def _():
+            for place in range(per_device):
+                rows = pl.ds(place * PATCHES, PATCHES)
+                mine = pl.ds(place, 1)
+                back, d_shift, d_scale = norm_back(
+                    hidden_ref[rows, :].astype(F32), d_in_ref[rows, :], scale_ref[mine, :]
+                )
+                grad_ref[rows, :] = (d_middle_ref[rows, :] + back).astype(BF16)
+                d_shift_ref[mine, :] = d_shift
+                d_scale_ref[mine, :] = d_scale
+
+
+def unproject(per_device, which, attn_in, first, back, weight, before=None, norm_args=()):
     tokens, width = attn_in.shape
     heads = width // HEAD
     group = 2
@@ -673,33 +750,45 @@
 
     args = [attn_in, first, back, weight, weight, weight]
     specs = [whole((tokens, width)), blocks(first), blocks(back), part(0), part(1), part(2)]
+    weight_shape = (
+        jax.ShapeDtypeStruct((3, width, width // 2), BF16),
+        jax.ShapeDtypeStruct((3, 1, width // 2), F32),
+    )
+    weight_specs = (
+        pl.BlockSpec((3, width, lanes), lambda step, which: (0, 0, step)),
+        pl.BlockSpec((3, 1, lanes), lambda step, which: (0, 0, step)),
+    )
+    scratch = [pltpu.VMEM((width, tokens), BF16)]
+    small = (per_device, width)
     if before is not None:
-        args.append(before)
-        specs.append(whole((tokens, width)))
+        args += [before] + list(norm_args)
+        specs += [whole((tokens, width))] * 3 + [whole(small)]
+        outs = weight_shape + (
+            jax.ShapeDtypeStruct((tokens, width), BF16),
+            jax.ShapeDtypeStruct(small, F32),
+            jax.ShapeDtypeStruct(small, F32),
+        )
+        out_specs = weight_specs + (whole((tokens, width)), whole(small), whole(small))
+        scratch = [pltpu.VMEM((tokens, width), F32)] + scratch
+    else:
+        outs = (jax.ShapeDtypeStruct((tokens, width), F32),) + weight_shape
+        out_specs = (whole((tokens, width)),) + weight_specs
     return pl.pallas_call(
         functools.partial(unproject_kernel, per_device, before is not None),
         grid_spec=pltpu.PrefetchScalarGridSpec(
             num_scalar_prefetch=1,
             grid=(steps,),
             in_specs=specs,
-            out_specs=(
-                whole((tokens, width)),
-                pl.BlockSpec((3, width, lanes), lambda step, which: (0, 0, step)),
-                pl.BlockSpec((3, 1, lanes), lambda step, which: (0, 0, step)),
-            ),
-            scratch_shapes=[pltpu.VMEM((width, tokens), BF16)],
+            out_specs=out_specs,
+            scratch_shapes=scratch,
         ),
-        out_shape=(
-            jax.ShapeDtypeStruct((tokens, width), F32),
-            jax.ShapeDtypeStruct((3, width, width // 2), BF16),
-            jax.ShapeDtypeStruct((3, 1, width // 2), F32),
-        ),
+        out_shape=outs,
         cost_estimate=pl.CostEstimate(
             flops=6 * tokens * width * width,
             bytes_accessed=2 * (3 * width * width + 6 * tokens * width),
             transcendentals=0,
         ),
-        compiler_params=pltpu.CompilerParams(vmem_limit_bytes=40 << 20),
+        compiler_params=pltpu.CompilerParams(vmem_limit_bytes=48 << 20),
         name="unproject%d" % (before is not None),
     )(which.reshape(1), *args)
 
@@ -762,7 +851,7 @@
     cond = jax.nn.silu(embed).astype(BF16)
     modulation = jnp.dot(cond, mod_weight[:, : 2 * width], preferred_element_type=F32)
     attn_shift, attn_scale = jnp.split(modulation + mod_bias[: 2 * width], 2, axis=1)
-    attn_in, sent, rest = project(
+    attn_in, sent = project(
         per_device, hidden[0], attn_shift, attn_scale, qkv_weight, qkv_bias, own_cos, own_sin
     )
 
@@ -784,30 +873,23 @@
     cos_all, sin_all = rotary_tables(after(frame_times, attn_in))
     grad_rows = cotangent[0].astype(F32).reshape(per_device, PATCHES, width)
     d_feed_out = (feed_gate[:, None, :] * grad_rows).reshape(tokens, width).astype(BF16)
-    head_queries = [x] + [
-        to_heads(after(rest[:, place : place + 1], x[0, 0, :8])) for place in range(per_device - 1)
-    ]
-    slots = [2 * per_device] + [0] * (per_device - 1)
-    kv = None
-    attended = []
-    mixes = []
-    for part in range(per_device):
-        mix, wide, lse, kv = attend(
-            part, per_device, slots[part], clip_ids, live, x, head_queries[part], kv
-        )
-        attended.append((wide, lse))
-        mixes.append(to_tokens(mix).reshape(width, PATCHES))
-    attn_rows = jnp.stack([dot_over(mix, out_weight, 0, 0) for mix in mixes]) + out_bias
+    down_bias_term = jnp.sum(d_feed_out.astype(F32), axis=0)
+    x, d_feed_out, down_bias_term, cos_all, sin_all = lax.optimization_barrier(
+        (x, d_feed_out, down_bias_term, cos_all, sin_all)
+    )
+    mix, wide, lse, kv = attend(per_device, clip_ids, live, x)
+    mix = to_tokens(mix)
+    mixes = [mix[:, place].reshape(width, PATCHES) for place in range(per_device)]
+    attn_rows = jnp.stack([dot_over(each, out_weight, 0, 0) for each in mixes]) + out_bias
     attn_mix = jnp.concatenate(mixes, axis=1)
 
     frame_rows = hidden[0].astype(F32).reshape(per_device, PATCHES, width)
     middle = frame_rows + attn_gate[:, None, :] * attn_rows
-    feed_value, feed_norm_back = jax.vjp(modulate_norm, middle, feed_shift, feed_scale)
-    feed_in = feed_value.reshape(tokens, width).astype(BF16)
+    feed_in = modulate_norm(middle, feed_shift, feed_scale).reshape(tokens, width).astype(BF16)
     feed_args = (feed_in, d_feed_out, up_weight, up_bias, down_weight)
     theirs = feed(1 - pack if halves else pack * 0 + 1, *feed_args, None)
     mine = feed(pack if halves else pack * 0, *feed_args, theirs[:2])
-    feed_rows, d_feed_in = [each.reshape(per_device, PATCHES, width) for each in mine[:2]]
+    feed_rows = mine[0].reshape(per_device, PATCHES, width)
     small = 128
 
     def in_order(own, other):
@@ -821,16 +903,18 @@
         ).reshape(rows, -1)
 
     up_bias_term = in_order(mine[4], theirs[4])[0]
-    down_bias_term = jnp.sum(d_feed_out.astype(F32), axis=0)
-    d_middle_norm, d_feed_shift, d_feed_scale = feed_norm_back(d_feed_in)
-    d_middle = grad_rows + d_middle_norm
-    d_attn_gate = jnp.sum(d_middle * attn_rows, axis=1)
-    d_attn_rows = (attn_gate[:, None, :] * d_middle).astype(BF16)
-    d_attn_out = d_attn_rows.reshape(tokens, width)
-    d_mixes = []
-    for part in range(per_device):
-        d_mix = dot_over(out_weight, d_attn_rows[part], 1, 1).astype(BF16)
-        d_mixes.append(to_heads(d_mix.reshape(heads, HEAD, PATCHES)))
+    d_middle, d_attn_out, d_mix, d_feed_shift, d_feed_scale, d_attn_gate, out_bias_rows = middle_back(
+        per_device,
+        mine[1],
+        middle.reshape(tokens, width),
+        cotangent[0],
+        attn_rows.reshape(tokens, width),
+        feed_scale,
+        attn_gate,
+        out_weight,
+    )
+    d_mix = to_heads(d_mix)
+    out_bias_term = jnp.sum(out_bias_rows, axis=0)
 
     def out_term(start, size):
         return dot_over(attn_mix, columns_of(d_attn_out, start, size), 1, 0).astype(BF16)
@@ -842,43 +926,75 @@
         out_theirs = exchange(out_term((1 - pack) * (width // 2), width // 2), "pack", 1)
         out_sum = RowSum(out_term(pack * (width // 2), width // 2), out_theirs, (1, 2, 4, 8))
         sums = (down_sum, up_sum, out_sum)
-    out_bias_term = jnp.sum(d_attn_out.astype(F32), axis=0)
-
     feed_rows = feed_rows + down_bias
     layer_out = (middle + feed_gate[:, None, :] * feed_rows).reshape(1, tokens, width).astype(BF16)
     d_feed_gate = jnp.sum(grad_rows * feed_rows, axis=1)
 
-    early_mod = jnp.concatenate([d_attn_gate, d_feed_shift, d_feed_scale, d_feed_gate], axis=1)
     own_levels = levels[0]
-    early_bias = jnp.concatenate([out_bias_term, up_bias_term, down_bias_term])
-    bias_rows = early_bias.reshape(per_device, early_bias.shape[0] // per_device)
-    early = jnp.concatenate(
+    chunk = width
+    early_bias = [out_bias_term, up_bias_term, down_bias_term]
+    bias_sizes = [each.shape[0] for each in early_bias]
+    rows = [
+        each.astype(BF16) for each in (d_attn_gate, d_feed_shift, d_feed_scale, d_feed_gate)
+    ] + [each.astype(BF16).reshape(-1, chunk) for each in early_bias]
+    rows.append(
+        jnp.broadcast_to(
+            jnp.concatenate([lax.div(own_levels, 32), lax.rem(own_levels, 32)])[:, None],
+            (2 * per_device, chunk),
+        ).astype(BF16)
+    )
+    early = jnp.concatenate(rows, axis=0)
+    early_all = gather_all(early)
+
+    def bias_share(rows, size):
+        flat = jnp.sum(rows.astype(F32), axis=0).reshape(size)
+        piece = size // seq_count
+        return lax.dynamic_slice_in_dim(flat, seq_index * piece, piece)
+
+    def frames_of(rows):
+        return rows.reshape(-1, rows.shape[-1])
+
+    at = 4 * per_device
+    early_bias_grads = []
+    for size in bias_sizes:
+        early_bias_grads.append(bias_share(early_all[:, at : at + size // chunk], size))
+        at += size // chunk
+    coarse = early_all[:, at : at + per_device, 0].astype(jnp.int32)
+    fine = early_all[:, at + per_device : at + 2 * per_device, 0].astype(jnp.int32)
+    all_levels = (coarse * 32 + fine).reshape(-1)
+    picks = (all_levels[:, None] == jnp.arange(level_count, dtype=jnp.int32)[None, :]).astype(F32)
+    own_table = lax.dynamic_slice_in_dim(noise_table, seq_index * share, share, 1)
+    all_embed = jnp.dot(picks, own_table, precision=PRECISE, preferred_element_type=F32)
+    silu_value, silu_back = jax.vjp(jax.nn.silu, all_embed)
+    all_cond = silu_value.astype(BF16)
+    d_mod_early = jnp.concatenate(
         [
-            early_mod.astype(BF16),
-            bias_rows.astype(BF16),
-            jnp.broadcast_to(lax.div(own_levels, 32)[:, None], (per_device, 128)).astype(BF16),
-            jnp.broadcast_to(lax.rem(own_levels, 32)[:, None], (per_device, 128)).astype(BF16),
+            frames_of(early_all[:, kind * per_device : (kind + 1) * per_device])
+            for kind in range(4)
         ],
         axis=1,
     )
-    early_all = gather_all(early)
+    own_mod = lax.dynamic_slice_in_dim(mod_weight, seq_index * share, share, 0)
+    d_cond_early = dot_over(d_mod_early, own_mod[:, 2 * width :], 1, 1)
+    mod_grad_early = dot_over(all_cond, d_mod_early, 0, 0)
+    mod_sum_early = jnp.sum(d_mod_early.astype(F32), axis=0)
+    early_done = [d_cond_early, mod_grad_early, mod_sum_early, all_embed, layer_out]
+    early_done += early_bias_grads
 
     before = None
     d_queries = []
     for part in range(per_device):
-        d_mix = after(d_mixes[part], *[each.stage() for each in sums])
+        sends = [each.stage() for each in sums]
         result = attend_back(
             part,
             per_device,
-            slots[part],
             clip_ids,
             live,
             x,
-            head_queries[part],
             kv,
-            attended[part][0],
-            attended[part][1],
-            d_mix,
+            wide,
+            lse,
+            after(d_mix, *sends),
             cos_all,
             sin_all,
             before,
@@ -889,37 +1005,41 @@
     firsts = jnp.stack(d_queries, axis=1)
     result = after(result, firsts[0, 0, :8], *[each.stage() for each in sums])
     back = to_tokens(result)
+    for each in sums:
+        each.hold(back[0, 0, :8])
+    back = after(back, *early_done)
     which = (1 - pack, pack) if halves else (pack * 0, pack * 0 + 1)
-    qkv_theirs = unproject(per_device, which[0], attn_in, firsts, back, qkv_weight, None)
-    qkv_mine = unproject(per_device, which[1], attn_in, firsts, back, qkv_weight, qkv_theirs[0])
-    d_attn_in = qkv_mine[0].reshape(per_device, PATCHES, width)
-    _, attn_norm_back = jax.vjp(modulate_norm, frame_rows, attn_shift, attn_scale)
-    d_hidden_norm, d_attn_shift, d_attn_scale = attn_norm_back(d_attn_in)
-    hidden_grad = (d_middle + d_hidden_norm).reshape(1, tokens, width).astype(BF16)
+    d_in_theirs, qkv_theirs, bias_theirs = unproject(
+        per_device, which[0], attn_in, firsts, back, qkv_weight
+    )
+    qkv_mine, bias_mine, hidden_grad, d_attn_shift, d_attn_scale = unproject(
+        per_device,
+        which[1],
+        attn_in,
+        firsts,
+        back,
+        qkv_weight,
+        d_in_theirs,
+        (hidden[0], d_middle, attn_scale),
+    )
+    hidden_grad = hidden_grad.reshape(1, tokens, width)
 
     def halves_in_order(own, other):
         if halves:
             return jnp.where(pack == 0, own, other), jnp.where(pack == 0, other, own)
         return other, own
 
-    qkv_bias_term = jnp.concatenate(
-        halves_in_order(qkv_mine[2][:, 0], qkv_theirs[2][:, 0]), axis=1
-    ).reshape(3 * width)
+    qkv_bias_term = jnp.concatenate(halves_in_order(bias_mine[:, 0], bias_theirs[:, 0]), axis=1)
     late = jnp.concatenate(
-        [
-            d_attn_shift.astype(BF16),
-            d_attn_scale.astype(BF16),
-            qkv_bias_term.reshape(per_device, 3 * width // per_device).astype(BF16),
-        ],
-        axis=1,
+        [d_attn_shift.astype(BF16), d_attn_scale.astype(BF16), qkv_bias_term.astype(BF16)], axis=0
     )
     late_all = gather_all(late)
     if halves:
-        came = exchange(qkv_theirs[1], "pack", 1)
+        came = exchange(qkv_theirs, "pack", 1)
         split = width // 4
         qkv_sums = [
-            RowSum(qkv_mine[1][..., :split], came[..., :split], (1, 2, 4, 8)),
-            RowSum(qkv_mine[1][..., split:], came[..., split:], (2, 1, 4, 8)),
+            RowSum(qkv_mine[..., :split], came[..., :split], (1, 2, 4, 8)),
+            RowSum(qkv_mine[..., split:], came[..., split:], (2, 1, 4, 8)),
         ]
         down_weight_grad = jnp.concatenate(down_sum.finish(), axis=0).astype(F32)
         even, odd = up_sum.finish()
@@ -938,52 +1058,26 @@
         pairs = [each[3].reshape(-1, small, width) for each in (mine, theirs)]
         down_weight_grad = row_sum_direct(jnp.stack(pairs, axis=1).reshape(hidden_units, width))
         out_weight_grad = row_sum_direct(out_term(0, width))
-        qkv_term = jnp.concatenate(halves_in_order(qkv_mine[1], qkv_theirs[1]), axis=-1)
+        qkv_term = jnp.concatenate(halves_in_order(qkv_mine, qkv_theirs), axis=-1)
         qkv_weight_grad = row_sum_direct(qkv_term.transpose(1, 0, 2).reshape(width, 3 * width))
 
-    devices = late_all.shape[0] // per_device
-
-    def bias_share(rows, sizes):
-        flat = rows.reshape(devices, sum(sizes))
-        shares = []
-        at = 0
-        for size in sizes:
-            piece = size // seq_count
-            own = lax.dynamic_slice_in_dim(flat, at + seq_index * piece, piece, 1)
-            shares.append(jnp.sum(own.astype(F32), axis=0))
-            at += size
-        return shares
-
-    early_width = 4 * width
-    bias_width = early_bias.shape[0] // per_device
-    out_bias_grad, up_bias_grad, down_bias_grad = bias_share(
-        early_all[:, early_width : early_width + bias_width], (width, hidden_units, width)
-    )
-    (qkv_bias_grad,) = bias_share(late_all[:, 2 * width :], (3 * width,))
-    coarse = early_all[:, early_width + bias_width].astype(jnp.int32)
-    fine = early_all[:, early_width + bias_width + 128].astype(jnp.int32)
-    all_levels = coarse * 32 + fine
-    picks = (all_levels[:, None] == jnp.arange(level_count, dtype=jnp.int32)[None, :]).astype(F32)
-    own_table = lax.dynamic_slice_in_dim(noise_table, seq_index * share, share, 1)
-    all_embed = jnp.dot(picks, own_table, precision=PRECISE, preferred_element_type=F32)
-    silu_value, silu_back = jax.vjp(jax.nn.silu, all_embed)
-    all_cond = silu_value.astype(BF16)
-    d_mod_early = early_all[:, :early_width]
-    d_mod_late = late_all[:, : 2 * width]
-    own_mod = lax.dynamic_slice_in_dim(mod_weight, seq_index * share, share, 0)
-    d_cond_early = dot_over(d_mod_early, own_mod[:, 2 * width :], 1, 1)
+    out_bias_grad, up_bias_grad, down_bias_grad = early_bias_grads
+    qkv_bias_grad = bias_share(late_all[:, 2 * per_device :], 3 * width)
+    d_mod_late = jnp.concatenate(
+        [
+            frames_of(late_all[:, kind * per_device : (kind + 1) * per_device])
+            for kind in range(2)
+        ],
+        axis=1,
+    )
     d_cond = d_cond_early + dot_over(d_mod_late, own_mod[:, : 2 * width], 1, 1)
     d_embed = silu_back(d_cond)[0]
     table_grad = lax.dot_general(
         picks, d_embed, (((0,), (0,)), ((), ())), precision=PRECISE, preferred_element_type=F32
     )
-    mod_weight_grad = jnp.concatenate(
-        [dot_over(all_cond, d_mod_late, 0, 0), dot_over(all_cond, d_mod_early, 0, 0)], axis=1
-    )
+    mod_weight_grad = jnp.concatenate([dot_over(all_cond, d_mod_late, 0, 0), mod_grad_early], axis=1)
     bias_piece = mod_bias.shape[0] // seq_count
-    d_mod_sum = jnp.concatenate(
-        [jnp.sum(d_mod_late.astype(F32), axis=0), jnp.sum(d_mod_early.astype(F32), axis=0)]
-    )
+    d_mod_sum = jnp.concatenate([jnp.sum(d_mod_late.astype(F32), axis=0), mod_sum_early])
     mod_bias_grad = lax.dynamic_slice_in_dim(d_mod_sum, seq_index * bias_piece, bias_piece)
     return (
         layer_out,

time: 644 us -> 734 us (1.14)
  local copies, waits for them, and re-layouts: 57.8 us -> 126 us
  waiting for transfers between devices: 171 us -> 226 us
  starting transfers between devices: 100 us -> 78.9 us
  other arithmetic: 87 us -> 74.2 us
  Pallas kernels: 185 us -> 196 us
  matrix products: 26.3 us -> 18.1 us
    ppermute x39, waiting for transfers between devices: 107 us -> 151 us  [exchange(): lax.ppermute(value, axis, [(source, source ^ bit) for source in range(cou...]
    ppermute x0 -> x6, local copies, waits for them, and re-layouts: none -> 31.7 us  [exchange(): lax.ppermute(value, axis, [(source, source ^ bit) for source in range(cou...]
    concatenate x5 -> x7, local copies, waits for them, and re-layouts: 13.2 us -> 40.4 us  [the longest x4 39.3 us: gather_all(): value = jnp.concatenate([value, exchange(value, axis, bit)], axis=0)]
    all_to_all x4 -> x2, starting transfers between devices: 30.4 us -> 13.5 us  [to_heads(): return lax.all_to_all(array, 'seq', 0, 0, tiled=True)]
    all_to_all x4 -> x3, waiting for transfers between devices: 12.9 us -> 23.2 us  [to_tokens(): return lax.all_to_all(array, 'seq', 0, 0, tiled=True)[:heads]]
    slice x4 -> x8, local copies, waits for them, and re-layouts: 3.83 us -> 12.2 us  [the longest x5 6.78 us: local(): early_all[:, kind * per_device:(kind + 1) * per_device]]
    dot_general x10 -> x8, matrix products: 15.9 us -> 7.95 us  [dot_over(): lax.dot_general(first, second, (((first_dim,), (second_dim,)), ((), ())),...]
    pallas_call x4, Pallas kernels: 112 us -> 120 us  [the longest x2 68.9 us: attend_back(): pl.pallas_call(functools.partial(attend_back_kernel, per_device, part, la...]
  transfers between devices with their start and end apart: 47 -> 44, of which waited for: 24 -> 22; matrix products, arithmetic and copies ran while one was open for 21% -> 26% of each run, Pallas kernels for 19% -> 16%
where the time goes in v2:
time: 734 us; the launch traced here: 726 us
  waiting for transfers between devices  226 us (31%)
  Pallas kernels  196 us (27%)
  local copies, waits for them, and re-layouts  126 us (17%)
  starting transfers between devices  78.9 us (11%)
  other arithmetic  74.2 us (10%)
  matrix products  18.1 us (2%)
    ppermute x39, waiting for transfers between devices, exchange(): lax.ppermute(value, axis, [(source, source ^ bit) for source in range(cou...  151 us
    pallas_call x2, Pallas kernels, attend_back(): pl.pallas_call(functools.partial(attend_back_kernel, per_device, part, la...  68.9 us
    all_to_all x2, waiting for transfers between devices, to_heads(): return lax.all_to_all(array, 'seq', 0, 0, tiled=True)  51.7 us
    pallas_call x1, Pallas kernels, attend(): pl.pallas_call(functools.partial(attend_kernel, per_device), out_shape=ou...  47.8 us
    pallas_call x2, Pallas kernels, feed(): pl.pallas_call(functools.partial(feed_kernel, before is not None), grid_s...  45.3 us
    concatenate x4, local copies, waits for them, and re-layouts, gather_all(): value = jnp.concatenate([value, exchange(value, axis, bit)], axis=0)  39.3 us
    ppermute x39, starting transfers between devices, exchange(): lax.ppermute(value, axis, [(source, source ^ bit) for source in range(cou...  38.7 us
    convert_element_type x21, other arithmetic, pick(): return (pieces[0].astype(F32) + pieces[1].astype(F32)).astype(BF16)  38.4 us
  transfers between devices with their start and end apart: 44, of which 22 were waited for; matrix products, arithmetic and copies ran while one was open for 26% of the time, Pallas kernels for 16%

profile of v2, /device:TPU:0, one launch (start us, length us, event | category | flops | bytes accessed | tf_op | source)
XLA Modules:
  0.0 725.5 jit_solution(10556243456887221292)
XLA Ops:
  7.5 2.9 fusion.7
  11.2 2.8 copy-done
  14.0 11.4 %project.1 = (bf16[512,1024]{1,0:T(8,128)(2,1)S(1)}, bf16[16,6,64,256]{3,2,1,0:T(8,128)(2,1)S(1)}) custom-call(bf16[512,1024]{1,0:T(8,128)(2,1)S(1)} %bitcast.149, f32[2,1024]{1,0:T(2,128)S(1)} %get-tuple-element.192.shift_ref, f32[2,1024]{1,0:T(2,128)S(1)} %get-tuple-element.191.scale_ref.refs_3_, bf16[1024,3072]{1,0:T(8,128)(2,1)S(1)} %copy-done, ...), custom_call_target="tpu_custom_call" | custom-call | flops 3221225472 | bytes 11534336 | tf_op jit(solution)/shard_map/project/pallas_call | solution.py:449
  28.0 8.5 %all-to-all-start = ((bf16[16,6,64,256]{3,2,1,0:T(8,128)(2,1)}), bf16[16,6,64,256]{3,2,1,0:T(8,128)(2,1)}, u32[]{:S(2)}, u32[]{:S(2)}) async-start(bf16[16,6,64,256]{3,2,1,0:T(8,128)(2,1)} %copy-done.11), calls=%async_computation | async-start | bytes 6291456 | tf_op jit(solution)/shard_map/all_to_all | solution.py:861
  36.5 4.7 fusion.2
  45.8 51.6 %all-to-all-done.x_ref = bf16[16,6,64,256]{3,2,1,0:T(8,128)(2,1)} async-done(((bf16[16,6,64,256]{3,2,1,0:T(8,128)(2,1)}), bf16[16,6,64,256]{3,2,1,0:T(8,128)(2,1)}, u32[]{:S(2)}, u32[]{:S(2)}) %all-to-all-start) | async-done | bytes 3145760 | tf_op jit(solution)/shard_map/all_to_all | solution.py:861
  97.5 47.8 %attend.1 = (bf16[16,2,64,256]{3,2,1,0:T(8,128)(2,1)S(1)}, f32[16,2,64,256]{3,2,1,0:T(8,128)S(1)}, f32[32,256]{1,0:T(8,128)S(1)}, bf16[32,256,128]{2,1,0:T(8,128)(2,1)S(1)}) custom-call(s32[32]{0:T(128)S(1)} %bitcast.161, s32[32]{0:T(128)S(1)} %bitcast.164, bf16[16,6,64,256]{3,2,1,0:T(8,128)(2,1)} %all-to-all-done.x_ref), custom_call_target="tpu_custom_call" | custom-call | flops 12884901888 | bytes 9437184 | tf_op jit(solution)/shard_map/attend/pallas_call | solution.py:171
  148.9 15.9 %all-to-all-start.1 = ((bf16[16,2,64,256]{3,2,1,0:T(8,128)(2,1)}), bf16[16,2,64,256]{3,2,1,0:T(8,128)(2,1)}, u32[]{:S(2)}, u32[]{:S(2)}) async-start(bf16[16,2,64,256]{3,2,1,0:T(8,128)(2,1)} %copy-done.15), calls=%async_computation.1 | async-start | bytes 2097152 | tf_op jit(solution)/shard_map/all_to_all | solution.py:864
  164.8 18.9 %all-to-all-done.1 = bf16[16,2,64,256]{3,2,1,0:T(8,128)(2,1)} async-done(((bf16[16,2,64,256]{3,2,1,0:T(8,128)(2,1)}), bf16[16,2,64,256]{3,2,1,0:T(8,128)(2,1)}, u32[]{:S(2)}, u32[]{:S(2)}) %all-to-all-start.1) | async-done | bytes 1048608 | tf_op jit(solution)/shard_map/all_to_all | solution.py:864
  188.7 3.2 fusion.13
  191.9 21.9 %feed0.1 = (f32[512,1024]{1,0:T(8,128)}, f32[512,1024]{1,0:T(8,128)}, bf16[1024,2048]{1,0:T(8,128)(2,1)}, bf16[2048,1024]{1,0:T(8,128)(2,1)}, f32[1,2048]{1,0:T(1,128)}) custom-call(s32[1]{0:T(128)} %bitcast.21.which_ref, bf16[512,1024]{1,0:T(8,128)(2,1)} %get-tuple-element.115.in_ref, bf16[512,1024]{1,0:T(8,128)(2,1)} %fusion.10.d_out_ref, ...), custom_call_target="tpu_custom_call" | custom-call | flops 12884901888 | bytes 25165824 | tf_op jit(solution)/shard_map/feed0/pallas_call | solution.py:555
  214.4 23.4 %feed1.1 = (f32[512,1024]{1,0:T(8,128)}, f32[512,1024]{1,0:T(8,128)}, bf16[1024,2048]{1,0:T(8,128)(2,1)}, bf16[2048,1024]{1,0:T(8,128)(2,1)}, f32[1,2048]{1,0:T(1,128)}) custom-call(s32[1]{0:T(128)} %bitcast.15.which_ref, bf16[512,1024]{1,0:T(8,128)(2,1)} %get-tuple-element.115.in_ref, bf16[512,1024]{1,0:T(8,128)(2,1)} %fusion.10.d_out_ref, ...), custom_call_target="tpu_custom_call" | custom-call | flops 12884901888 | bytes 25165824 | tf_op jit(solution)/shard_map/feed1/pallas_call | solution.py:555
  241.0 3.4 middle_back.1
  248.4 5.0 all-to-all-start.2
  256.2 2.1 collective-permute-start.5
  258.3 6.5 add_convert_fusion.1
  264.9 5.6 add_convert_fusion
  272.5 7.0 collective-permute-done.5
  280.4 2.0 collective-permute-start.8
  282.4 43.9 %collective-permute-done.8 = bf16[2,2,1,1,64,512]{5,4,3,2,1,0:T(8,128)(2,1)} collective-permute-done((bf16[2,2,1,1,64,512]{5,4,3,2,1,0:T(8,128)(2,1)}, bf16[2,2,1,1,64,512]{5,4,3,2,1,0:T(8,128)(2,1)}, u32[]{:S(2)}, u32[]{:S(2)}) %collective-permute-start.8) | collective-permute-done | bytes 262176 | tf_op jit(solution)/shard_map/ppermute | solution.py:318
  328.0 32.4 %attend_back0.1 = (bf16[16,64,256]{2,1,0:T(8,128)(2,1)}, f32[32,256,128]{2,1,0:T(8,128)}) custom-call(s32[32]{0:T(128)} %bitcast.158, s32[32]{0:T(128)} %bitcast.162, bf16[16,6,64,256]{3,2,1,0:T(8,128)(2,1)} %all-to-all-done.x_ref, bf16[32,256,128]{2,1,0:T(8,128)(2,1)} %copy-done.22, f32[16,2,64,256]{3,2,1,0:T(8,128)} %copy-done.21, f32[32,256]{1,0:T(8,128)} %copy-done.23, ...), custom_call_target="tpu_custom_call" | custom-call | flops 16106127360 | bytes 15728640 | tf_op jit(solution)/shard_map/attend_back0/pallas_call | solution.py:300
  360.4 4.6 add_convert_fusion.5
  365.3 3.7 add_convert_fusion.4
  370.4 36.5 %attend_back1.1 = bf16[16,5,64,256]{3,2,1,0:T(8,128)(2,1)} custom-call(s32[32]{0:T(128)} %bitcast.159, s32[32]{0:T(128)} %bitcast.163, bf16[16,6,64,256]{3,2,1,0:T(8,128)(2,1)} %all-to-all-done.x_ref, bf16[32,256,128]{2,1,0:T(8,128)(2,1)} %copy-done.22, f32[16,2,64,256]{3,2,1,0:T(8,128)} %copy-done.21, f32[32,256]{1,0:T(8,128)} %copy-done.23, ...), custom_call_target="tpu_custom_call" | custom-call | flops 16106127360 | bytes 15728640 | tf_op jit(solution)/shard_map/attend_back1/pallas_call | solution.py:300
  406.9 2.7 add_convert_fusion.12
  411.0 5.5 all-to-all-start.4
  419.1 3.0 collective-permute-start.9
  422.2 46.3 %collective-permute-done.9 = bf16[1,18,1024]{2,1,0:T(8,128)(2,1)S(1)} collective-permute-done((bf16[1,18,1024]{2,1,0:T(8,128)(2,1)S(1)}, bf16[1,18,1024]{2,1,0:T(8,128)(2,1)S(1)}, u32[]{:S(2)}, u32[]{:S(2)}) %collective-permute-start.9) | collective-permute-done | bytes 36896 | tf_op jit(solution)/shard_map/ppermute | solution.py:318
  468.9 4.3 collective-permute-done.10
  473.5 2.4 collective-permute-start.11
  475.9 3.1 collective-permute-done.11
  480.5 5.7 collective-permute-done.12
  486.2 4.1 concatenate.115
  490.3 3.1 fusion.12
  493.4 5.8 copy.193
  499.3 6.0 copy.194
  505.3 5.8 copy.195
  511.1 5.9 copy.196
  517.0 6.8 copy.197
  523.8 7.1 copy.198
  530.9 35.2 %concatenate.116 = bf16[32,18,1024]{0,1,2:T(8,128)(2,1)} concatenate(bf16[1,18,1024]{0,1,2:T(8,128)(2,1)} %copy.193, bf16[1,18,1024]{0,1,2:T(8,128)(2,1)} %copy.194, bf16[2,18,1024]{0,1,2:T(8,128)(2,1)} %copy.195, bf16[4,18,1024]{0,1,2:T(8,128)(2,1)} %copy.196, bf16[8,18,1024]{0,1,2:T(8,128)(2,1)} %copy.197, bf16[16,18,1024]{0,1,2:T(8,128)(2,1)} %copy.198), dimensions={0} | concatenate | bytes 2359296 | tf_op jit(solution)/shard_map/concatenate | solution.py:330
  566.1 5.1 fusion.68
  573.4 2.8 convert_reduce_fusion
  576.2 7.5 %fusion.19 = (f32[1024]{0:T(1024)S(1)}, f32[1024]{0:T(1024)S(1)}) fusion(bf16[32,18,1024]{0,1,2:T(8,128)(2,1)} %concatenate.116), kind=kLoop, calls=%fused_computation.62 | loop fusion | flops 129024 | bytes 139264 | tf_op jit(solution)/shard_map/reduce_sum | solution.py:950
  583.8 5.2 all-to-all-start.3
  596.0 2.0 collective-permute-start.30
  598.0 2.0 collective-permute-start.36
  600.0 4.2 all-to-all-done.3
  604.2 8.2 %unproject0.1 = (f32[512,1024]{1,0:T(8,128)S(1)}, bf16[3,1024,512]{2,1,0:T(8,128)(2,1)}, f32[3,1,512]{2,1,0:T(1,128)S(1)}) custom-call(s32[1]{0:T(128)} %bitcast.21.which_ref, bf16[512,1024]{1,0:T(8,128)(2,1)S(1)} %copy-done.10, bf16[16,1,64,256]{3,2,1,0:T(8,128)(2,1)S(1)} %bitcast.153, bf16[16,5,64,256]{3,2,1,0:T(8,128)(2,1)} %all-to-all-done.4.back_ref, ...), custom_call_target="tpu_custom_call" | custom-call | flops 3221225472 | bytes 12582912 | tf_op jit(solution)/shard_map/unproject0/pallas_call | solution.py:776
  612.4 11.0 %unproject1.1 = (bf16[3,1024,512]{2,1,0:T(8,128)(2,1)}, f32[3,1,512]{2,1,0:T(1,128)S(1)}, bf16[512,1024]{1,0:T(8,128)(2,1)}, f32[2,1024]{1,0:T(2,128)S(1)}, f32[2,1024]{1,0:T(2,128)S(1)}) custom-call(s32[1]{0:T(128)} %bitcast.15.which_ref, bf16[512,1024]{1,0:T(8,128)(2,1)S(1)} %copy-done.10, bf16[16,1,64,256]{3,2,1,0:T(8,128)(2,1)S(1)} %bitcast.154, ...), custom_call_target="tpu_custom_call" | custom-call | flops 3221225472 | bytes 12582912 | tf_op jit(solution)/shard_map/unproject1/pallas_call | solution.py:776
  628.7 3.3 fusion.69
  636.8 4.5 collective-permute-done.15
  643.0 2.6 collective-permute-done.16
  647.7 3.0 collective-permute-done.17
  651.5 3.0 collective-permute-done.37
  666.2 3.4 fusion.70
  673.0 2.8 add_convert_fusion.11
  680.6 10.6 %collective-permute-done.25 = bf16[3,2,2,1,2,64,256]{6,5,4,3,2,1,0:T(8,128)(2,1)} collective-permute-done((bf16[3,2,2,1,2,64,256]{6,5,4,3,2,1,0:T(8,128)(2,1)}, bf16[3,2,2,1,2,64,256]{6,5,4,3,2,1,0:T(8,128)(2,1)}, u32[]{:S(2)}, u32[]{:S(2)}) %collective-permute-start.25) | collective-permute-done | bytes 786464 | tf_op jit(solution)/shard_map/ppermute | solution.py:318
  694.0 2.6 collective-permute-done.20
  696.6 2.1 add_convert_fusion.21
  704.6 3.9 collective-permute-done.21
  713.7 2.1 collective-permute-done.22
  717.6 2.6 collective-permute-done.28
  720.4 2.5 collective-permute-done.23
  (316 shorter events, 103.8 us)
Async XLA Ops:
  28.0 8.5 %slice-start = ((f32[6144]{0:T(1024)}), f32[4096]{0:T(1024)S(1)}, s32[]{:S(2)}) async-start(f32[6144]{0:T(1024)} %param.23), calls=%async_computation.5 | async-start | bytes 32768 | tf_op jit(solution)/shard_map/slice | solution.py:871
  28.0 69.5 %all-to-all-start = ((bf16[16,6,64,256]{3,2,1,0:T(8,128)(2,1)}), bf16[16,6,64,256]{3,2,1,0:T(8,128)(2,1)}, u32[]{:S(2)}, u32[]{:S(2)}) async-start(bf16[16,6,64,256]{3,2,1,0:T(8,128)(2,1)} %copy-done.11), calls=%async_computation | async-start | bytes 6291456 | tf_op jit(solution)/shard_map/all_to_all | solution.py:861
  45.4 52.1 %copy-start.20 = (s32[1,32]{1,0:T(1,128)S(1)}, s32[1,32]{1,0:T(1,128)}, u32[]{:S(2)}) copy-start(s32[1,32]{1,0:T(1,128)} %param.20) | copy-start | bytes 388
  148.9 36.1 %copy-start.23 = (f32[32,256]{1,0:T(8,128)}, f32[32,256]{1,0:T(8,128)S(1)}, u32[]{:S(2)}) copy-start(f32[32,256]{1,0:T(8,128)S(1)} %get-tuple-element.75.lse_ref) | copy-start | bytes 98308
  148.9 36.1 %copy-start.2 = (bf16[1024,1024]{1,0:T(8,128)(2,1)S(1)}, bf16[1024,1024]{1,0:T(8,128)(2,1)}, u32[]{:S(2)}) copy-start(bf16[1024,1024]{1,0:T(8,128)(2,1)} %weight_ref.1) | copy-start | bytes 6291460
  148.9 34.8 %all-to-all-start.1 = ((bf16[16,2,64,256]{3,2,1,0:T(8,128)(2,1)}), bf16[16,2,64,256]{3,2,1,0:T(8,128)(2,1)}, u32[]{:S(2)}, u32[]{:S(2)}) async-start(bf16[16,2,64,256]{3,2,1,0:T(8,128)(2,1)} %copy-done.15), calls=%async_computation.1 | async-start | bytes 2097152 | tf_op jit(solution)/shard_map/all_to_all | solution.py:864
  213.8 44.5 %collective-permute-start = (bf16[2048,1024]{1,0:T(8,128)(2,1)}, bf16[2048,1024]{1,0:T(8,128)(2,1)}, u32[]{:S(2)}, u32[]{:S(2)}) collective-permute-start(bf16[2048,1024]{1,0:T(8,128)(2,1)} %get-tuple-element.79), channel_id=1, source_target_pairs={{0,16},{16,0},{1,17},{17,1},{2,18},{18,2},{3,19},{19,3},{4,20},{20... | collective-permute-start | bytes 12582920 | tf_op jit(solution)/shard_map/ppermute | solution.py:318
  213.9 51.0 %collective-permute-start.1 = (bf16[1024,2048]{1,0:T(8,128)(2,1)}, bf16[1024,2048]{1,0:T(8,128)(2,1)}, u32[]{:S(2)}, u32[]{:S(2)}) collective-permute-start(bf16[1024,2048]{1,0:T(8,128)(2,1)} %get-tuple-element.81), channel_id=1, source_target_pairs={{0,16},{16,0},{1,17},{17,1},{2,18},{18,2},{3,19},{19,3},{4,20},{20... | collective-permute-start | bytes 12582920 | tf_op jit(solution)/shard_map/ppermute | solution.py:318
  214.4 23.4 %copy-start.3 = (f32[512,1024]{1,0:T(8,128)S(1)}, f32[512,1024]{1,0:T(8,128)}, u32[]{:S(2)}) copy-start(f32[512,1024]{1,0:T(8,128)} %get-tuple-element.116.middle_ref) | copy-start | bytes 6291460
  214.4 23.4 %copy-start.6 = (bf16[1,512,1024]{2,1,0:T(8,128)(2,1)S(1)}, bf16[1,512,1024]{2,1,0:T(8,128)(2,1)}, u32[]{:S(2)}) copy-start(bf16[1,512,1024]{2,1,0:T(8,128)(2,1)} %param.17) | copy-start | bytes 3145732
  246.7 6.9 copy-start.34
  246.7 6.9 copy-start.37
  248.4 5.9 collective-permute-start.2
  248.4 79.6 %all-to-all-start.2 = ((bf16[16,2,64,256]{3,2,1,0:T(8,128)(2,1)}), bf16[16,2,64,256]{3,2,1,0:T(8,128)(2,1)}, u32[]{:S(2)}, u32[]{:S(2)}) async-start(bf16[16,2,64,256]{3,2,1,0:T(8,128)(2,1)} %copy-done.14), calls=%async_computation.2 | async-start | bytes 2097152 | tf_op jit(solution)/shard_map/all_to_all | solution.py:861
  256.2 23.3 %collective-permute-start.5 = (bf16[2,2,2,1,64,512]{5,4,3,2,1,0:T(8,128)(2,1)S(1)}, bf16[2,2,2,1,64,512]{5,4,3,2,1,0:T(8,128)(2,1)S(1)}, u32[]{:S(2)}, u32[]{:S(2)}) collective-permute-start(bf16[2,2,2,1,64,512]{5,4,3,2,1,0:T(8,128)(2,1)S(1)} %get-tuple-element.143), channel_id=1, source_target_pairs={{0,1},{1,0},{2,3},{3,2},{4,5},{5,4},{6,7},{7,6},{8,9},{9,8},{10,11... | collective-permute-start | bytes 1572872 | tf_op jit(solution)/shard_map/ppermute | solution.py:318
  258.3 6.6 copy-start.27
  264.9 95.6 %collective-permute-start.3 = (bf16[2,2,2,1,128,1024]{5,4,3,2,1,0:T(8,128)(2,1)}, bf16[2,2,2,1,128,1024]{5,4,3,2,1,0:T(8,128)(2,1)}, u32[]{:S(2)}, u32[]{:S(2)}) collective-permute-start(bf16[2,2,2,1,128,1024]{5,4,3,2,1,0:T(8,128)(2,1)} %get-tuple-element.121), channel_id=1, source_target_pairs={{0,1},{1,0},{2,3},{3,2},{4,5},{5,4},{6,7},{7,6},{8,9},{9,8},{10,11... | collective-permute-start | bytes 6291464 | tf_op jit(solution)/shard_map/ppermute | solution.py:318
  270.5 94.8 %collective-permute-start.4 = (bf16[2,2,1,2,64,2048]{5,4,3,2,1,0:T(8,128)(2,1)}, bf16[2,2,1,2,64,2048]{5,4,3,2,1,0:T(8,128)(2,1)}, u32[]{:S(2)}, u32[]{:S(2)}) collective-permute-start(bf16[2,2,1,2,64,2048]{5,4,3,2,1,0:T(8,128)(2,1)} %get-tuple-element.119), channel_id=1, source_target_pairs={{0,2},{1,3},{2,0},{3,1},{4,6},{5,7},{6,4},{7,5},{8,10},{9,11},{10,... | collective-permute-start | bytes 6291464 | tf_op jit(solution)/shard_map/ppermute | solution.py:318
  280.4 45.9 %collective-permute-start.8 = (bf16[2,2,1,1,64,512]{5,4,3,2,1,0:T(8,128)(2,1)}, bf16[2,2,1,1,64,512]{5,4,3,2,1,0:T(8,128)(2,1)}, u32[]{:S(2)}, u32[]{:S(2)}) collective-permute-start(bf16[2,2,1,1,64,512]{5,4,3,2,1,0:T(8,128)(2,1)} %get-tuple-element.147), channel_id=1, source_target_pairs={{0,2},{1,3},{2,0},{3,1},{4,6},{5,7},{6,4},{7,5},{8,10},{9,11},{10,... | collective-permute-start | bytes 786440 | tf_op jit(solution)/shard_map/ppermute | solution.py:318
  365.0 41.9 %collective-permute-start.6 = (bf16[2,2,1,1,128,1024]{5,4,3,2,1,0:T(8,128)(2,1)}, bf16[2,2,1,1,128,1024]{5,4,3,2,1,0:T(8,128)(2,1)}, u32[]{:S(2)}, u32[]{:S(2)}) collective-permute-start(bf16[2,2,1,1,128,1024]{5,4,3,2,1,0:T(8,128)(2,1)} %get-tuple-element.129), channel_id=1, source_target_pairs={{0,2},{1,3},{2,0},{3,1},{4,6},{5,7},{6,4},{7,5},{8,10},{9,11},{10,... | collective-permute-start | bytes 3145736 | tf_op jit(solution)/shard_map/ppermute | solution.py:318
  368.9 40.7 %collective-permute-start.7 = (bf16[2,2,1,1,64,2048]{5,4,3,2,1,0:T(8,128)(2,1)}, bf16[2,2,1,1,64,2048]{5,4,3,2,1,0:T(8,128)(2,1)S(1)}, u32[]{:S(2)}, u32[]{:S(2)}) collective-permute-start(bf16[2,2,1,1,64,2048]{5,4,3,2,1,0:T(8,128)(2,1)} %get-tuple-element.127), channel_id=1, source_target_pairs={{0,1},{1,0},{2,3},{3,2},{4,5},{5,4},{6,7},{7,6},{8,9},{9,8},{10,11... | collective-permute-start | bytes 3145736 | tf_op jit(solution)/shard_map/ppermute | solution.py:318
  370.4 36.5 %copy-start.30 = (bf16[2,2,1,1,128,1024]{5,4,3,2,1,0:T(8,128)(2,1)S(1)}, bf16[2,2,1,1,128,1024]{5,4,3,2,1,0:T(8,128)(2,1)}, u32[]{:S(2)}) copy-start(bf16[2,2,1,1,128,1024]{5,4,3,2,1,0:T(8,128)(2,1)} %get-tuple-element.128) | copy-start | bytes 3145732
  411.0 172.7 %all-to-all-start.4 = ((bf16[16,5,64,256]{3,2,1,0:T(8,128)(2,1)}), bf16[16,5,64,256]{3,2,1,0:T(8,128)(2,1)}, u32[]{:S(2)}, u32[]{:S(2)}) async-start(bf16[16,5,64,256]{3,2,1,0:T(8,128)(2,1)} %attend_back1.1), calls=%async_computation.4 | async-start | bytes 5242880 | tf_op jit(solution)/shard_map/all_to_all | solution.py:864
  418.8 71.5 %copy-start.4 = (f32[512,1024]{1,0:T(8,128)S(1)}, f32[512,1024]{1,0:T(8,128)}, u32[]{:S(2)}) copy-start(f32[512,1024]{1,0:T(8,128)} %get-tuple-element.116.middle_ref) | copy-start | bytes 6291460
  419.1 49.4 %collective-permute-start.9 = (bf16[1,18,1024]{2,1,0:T(8,128)(2,1)S(1)}, bf16[1,18,1024]{2,1,0:T(8,128)(2,1)S(1)}, u32[]{:S(2)}, u32[]{:S(2)}) collective-permute-start(bf16[1,18,1024]{2,1,0:T(8,128)(2,1)S(1)} %bitcast.187), channel_id=1, source_target_pairs={{0,8},{1,9},{2,10},{3,11},{4,12},{5,13},{6,14},{7,15},{8,0},{9,1},... | collective-permute-start | bytes 110600 | tf_op jit(solution)/shard_map/ppermute | solution.py:318
  468.5 7.3 %copy-start.46 = (bf16[1,18,1024]{2,1,0:T(8,128)(2,1)}, bf16[1,18,1024]{2,1,0:T(8,128)(2,1)S(1)}, u32[]{:S(2)}) copy-start(bf16[1,18,1024]{2,1,0:T(8,128)(2,1)S(1)} %collective-permute-done.9) | copy-start | bytes 110596
  468.8 4.4 collective-permute-start.10
  473.5 5.5 collective-permute-start.11
  479.3 6.9 collective-permute-start.12
  490.3 33.5 %collective-permute-start.13 = (bf16[16,18,1024]{2,0,1:T(8,128)(2,1)}, bf16[16,18,1024]{2,0,1:T(8,128)(2,1)}, u32[]{:S(2)}, u32[]{:S(2)}) collective-permute-start(bf16[16,18,1024]{2,0,1:T(8,128)(2,1)} %concatenate.115), channel_id=1, source_target_pairs={{0,16},{16,0},{1,17},{17,1},{2,18},{18,2},{3,19},{19,3},{4,20},{20... | collective-permute-start | bytes 1769480 | tf_op jit(solution)/shard_map/ppermute | solution.py:318
  493.4 5.8 copy-start.47
  583.8 20.5 %all-to-all-start.3 = ((bf16[16,64,256]{2,1,0:T(8,128)(2,1)}), bf16[16,64,256]{2,1,0:T(8,128)(2,1)S(1)}, u32[]{:S(2)}, u32[]{:S(2)}) async-start(bf16[16,64,256]{2,1,0:T(8,128)(2,1)} %get-tuple-element.86), calls=%async_computation.3 | async-start | bytes 1048576 | tf_op jit(solution)/shard_map/all_to_all | solution.py:864
  589.9 14.4 %copy-start.10 = (bf16[512,1024]{1,0:T(8,128)(2,1)S(1)}, bf16[512,1024]{1,0:T(8,128)(2,1)}, u32[]{:S(2)}) copy-start(bf16[512,1024]{1,0:T(8,128)(2,1)} %copy-done.9) | copy-start | bytes 3145732
  596.0 28.9 %collective-permute-start.30 = (bf16[2,1,1,1,64,512]{5,4,3,2,1,0:T(8,128)(2,1)}, bf16[2,1,1,1,64,512]{5,4,3,2,1,0:T(8,128)(2,1)S(1)}, u32[]{:S(2)}, u32[]{:S(2)}) collective-permute-start(bf16[2,1,1,1,64,512]{5,4,3,2,1,0:T(8,128)(2,1)} %get-tuple-element.163), channel_id=1, source_target_pairs={{0,4},{1,5},{2,6},{3,7},{4,0},{5,1},{6,2},{7,3},{8,12},{9,13},{10,... | collective-permute-start | bytes 393224 | tf_op jit(solution)/shard_map/ppermute | solution.py:318
  598.0 28.7 %collective-permute-start.33 = (bf16[2,1,1,1,64,2048]{5,4,3,2,1,0:T(8,128)(2,1)}, bf16[2,1,1,1,64,2048]{5,4,3,2,1,0:T(8,128)(2,1)S(1)}, u32[]{:S(2)}, u32[]{:S(2)}) collective-permute-start(bf16[2,1,1,1,64,2048]{5,4,3,2,1,0:T(8,128)(2,1)} %get-tuple-element.141), channel_id=1, source_target_pairs={{0,4},{1,5},{2,6},{3,7},{4,0},{5,1},{6,2},{7,3},{8,12},{9,13},{10,... | collective-permute-start | bytes 1572872 | tf_op jit(solution)/shard_map/ppermute | solution.py:318
  598.0 34.1 %collective-permute-start.36 = (bf16[2,1,1,1,128,1024]{5,4,3,2,1,0:T(8,128)(2,1)}, bf16[2,1,1,1,128,1024]{5,4,3,2,1,0:T(8,128)(2,1)}, u32[]{:S(2)}, u32[]{:S(2)}) collective-permute-start(bf16[2,1,1,1,128,1024]{5,4,3,2,1,0:T(8,128)(2,1)} %get-tuple-element.139), channel_id=1, source_target_pairs={{0,4},{1,5},{2,6},{3,7},{4,0},{5,1},{6,2},{7,3},{8,12},{9,13},{10,... | collective-permute-start | bytes 1572872 | tf_op jit(solution)/shard_map/ppermute | solution.py:318
  612.4 12.4 %copy-start.41 = (bf16[2,1,1,1,64,512]{5,4,3,2,1,0:T(8,128)(2,1)S(1)}, bf16[2,1,1,1,64,512]{5,4,3,2,1,0:T(8,128)(2,1)}, u32[]{:S(2)}) copy-start(bf16[2,1,1,1,64,512]{5,4,3,2,1,0:T(8,128)(2,1)} %get-tuple-element.107) | copy-start | bytes 393220
  612.4 14.2 %copy-start.40 = (bf16[2,1,1,1,64,2048]{5,4,3,2,1,0:T(8,128)(2,1)S(1)}, bf16[2,1,1,1,64,2048]{5,4,3,2,1,0:T(8,128)(2,1)}, u32[]{:S(2)}) copy-start(bf16[2,1,1,1,64,2048]{5,4,3,2,1,0:T(8,128)(2,1)} %get-tuple-element.109) | copy-start | bytes 1572868
  623.5 11.4 %collective-permute-start.14 = (bf16[1,7,1024]{2,1,0:T(8,128)(2,1)S(1)}, bf16[1,7,1024]{2,1,0:T(8,128)(2,1)S(1)}, u32[]{:S(2)}, u32[]{:S(2)}) collective-permute-start(bf16[1,7,1024]{2,1,0:T(8,128)(2,1)S(1)} %maximum_bitcast_fusion), channel_id=1, source_target_pairs={{0,8},{1,9},{2,10},{3,11},{4,12},{5,13},{6,14},{7,15},{8,0},{9,1},... | collective-permute-start | bytes 43016 | tf_op jit(solution)/shard_map/ppermute | solution.py:318
  624.8 41.3 %collective-permute-start.19 = (bf16[3,1024,512]{2,1,0:T(8,128)(2,1)}, bf16[3,1024,512]{2,1,0:T(8,128)(2,1)}, u32[]{:S(2)}, u32[]{:S(2)}) collective-permute-start(bf16[3,1024,512]{2,1,0:T(8,128)(2,1)} %get-tuple-element.106), channel_id=1, source_target_pairs={{0,16},{16,0},{1,17},{17,1},{2,18},{18,2},{3,19},{19,3},{4,20},{20... | collective-permute-start | bytes 9437192 | tf_op jit(solution)/shard_map/ppermute | solution.py:318
  624.9 17.9 %collective-permute-start.31 = (bf16[1,1,1,1,64,512]{5,4,3,2,1,0:T(8,128)(2,1)S(1)}, bf16[1,1,1,1,64,512]{5,4,3,2,1,0:T(8,128)(2,1)S(1)}, u32[]{:S(2)}, u32[]{:S(2)}) collective-permute-start(bf16[1,1,1,1,64,512]{5,4,3,2,1,0:T(8,128)(2,1)S(1)} %add_convert_fusion.43), channel_id=1, source_target_pairs={{0,8},{1,9},{2,10},{3,11},{4,12},{5,13},{6,14},{7,15},{8,0},{9,1},... | collective-permute-start | bytes 196616 | tf_op jit(solution)/shard_map/ppermute | solution.py:318
  627.4 23.3 %collective-permute-start.34 = (bf16[1,1,1,1,64,2048]{5,4,3,2,1,0:T(8,128)(2,1)S(1)}, bf16[1,1,1,1,64,2048]{5,4,3,2,1,0:T(8,128)(2,1)S(1)}, u32[]{:S(2)}, u32[]{:S(2)}) collective-permute-start(bf16[1,1,1,1,64,2048]{5,4,3,2,1,0:T(8,128)(2,1)S(1)} %add_convert_fusion.26), channel_id=1, source_target_pairs={{0,8},{1,9},{2,10},{3,11},{4,12},{5,13},{6,14},{7,15},{8,0},{9,1},... | collective-permute-start | bytes 786440 | tf_op jit(solution)/shard_map/ppermute | solution.py:318
  628.7 14.1 %copy-start.49 = (bf16[2,1,1,1,64,512]{5,4,3,2,1,0:T(8,128)(2,1)S(1)}, bf16[2,1,1,1,64,512]{5,4,3,2,1,0:T(8,128)(2,1)}, u32[]{:S(2)}) copy-start(bf16[2,1,1,1,64,512]{5,4,3,2,1,0:T(8,128)(2,1)} %copy-done.48) | copy-start | bytes 393220
  632.1 18.7 %copy-start.43 = (bf16[2,1,1,1,64,2048]{5,4,3,2,1,0:T(8,128)(2,1)S(1)}, bf16[2,1,1,1,64,2048]{5,4,3,2,1,0:T(8,128)(2,1)}, u32[]{:S(2)}) copy-start(bf16[2,1,1,1,64,2048]{5,4,3,2,1,0:T(8,128)(2,1)} %copy-done.42) | copy-start | bytes 1572868
  633.1 21.3 %collective-permute-start.37 = (bf16[1,1,1,1,128,1024]{5,4,3,2,1,0:T(8,128)(2,1)S(1)}, bf16[1,1,1,1,128,1024]{5,4,3,2,1,0:T(8,128)(2,1)S(1)}, u32[]{:S(2)}, u32[]{:S(2)}) collective-permute-start(bf16[1,1,1,1,128,1024]{5,4,3,2,1,0:T(8,128)(2,1)S(1)} %add_convert_fusion.23), channel_id=1, source_target_pairs={{0,8},{1,9},{2,10},{3,11},{4,12},{5,13},{6,14},{7,15},{8,0},{9,1},... | collective-permute-start | bytes 786440 | tf_op jit(solution)/shard_map/ppermute | solution.py:318
  634.9 6.3 collective-permute-start.15
  641.3 4.3 collective-permute-start.16
  642.9 4.0 collective-permute-start.32
  645.6 5.0 collective-permute-start.17
  650.7 5.5 collective-permute-start.18
  650.9 25.5 %collective-permute-start.35 = (bf16[64,2048]{1,0:T(8,128)(2,1)S(1)}, bf16[64,2048]{1,0:T(8,128)(2,1)}, u32[]{:S(2)}, u32[]{:S(2)}) collective-permute-start(bf16[64,2048]{1,0:T(8,128)(2,1)S(1)} %fusion.27), channel_id=1, source_target_pairs={{0,16},{16,0},{1,17},{17,1},{2,18},{18,2},{3,19},{19,3},{4,20},{20... | collective-permute-start | bytes 786440 | tf_op jit(solution)/shard_map/ppermute | solution.py:318
  656.2 46.8 %collective-permute-start.38 = (bf16[128,1024]{1,0:T(8,128)(2,1)}, bf16[128,1024]{1,0:T(8,128)(2,1)}, u32[]{:S(2)}, u32[]{:S(2)}) collective-permute-start(bf16[128,1024]{1,0:T(8,128)(2,1)} %fusion.28), channel_id=1, source_target_pairs={{0,16},{16,0},{1,17},{17,1},{2,18},{18,2},{3,19},{19,3},{4,20},{20... | collective-permute-start | bytes 786440 | tf_op jit(solution)/shard_map/ppermute | solution.py:318
  656.2 8.7 %copy-start.29 = (f32[64,4096]{1,0:T(8,128)S(1)}, f32[64,4096]{1,0:T(8,128)}, u32[]{:S(2)}) copy-start(f32[64,4096]{1,0:T(8,128)} %fusion.66) | copy-start | bytes 3145732
  670.9 20.3 %collective-permute-start.25 = (bf16[3,2,2,1,2,64,256]{6,5,4,3,2,1,0:T(8,128)(2,1)}, bf16[3,2,2,1,2,64,256]{6,5,4,3,2,1,0:T(8,128)(2,1)}, u32[]{:S(2)}, u32[]{:S(2)}) collective-permute-start(bf16[3,2,2,1,2,64,256]{6,5,4,3,2,1,0:T(8,128)(2,1)} %add_convert_fusion.8), channel_id=1, source_target_pairs={{0,2},{1,3},{2,0},{3,1},{4,6},{5,7},{6,4},{7,5},{8,10},{9,11},{10,... | collective-permute-start | bytes 2359304 | tf_op jit(solution)/shard_map/ppermute | solution.py:318
  675.9 20.7 %collective-permute-start.20 = (bf16[3,2,2,2,1,64,256]{6,5,4,3,2,1,0:T(8,128)(2,1)}, bf16[3,2,2,2,1,64,256]{6,5,4,3,2,1,0:T(8,128)(2,1)}, u32[]{:S(2)}, u32[]{:S(2)}) collective-permute-start(bf16[3,2,2,2,1,64,256]{6,5,4,3,2,1,0:T(8,128)(2,1)} %get-tuple-element.133), channel_id=1, source_target_pairs={{0,1},{1,0},{2,3},{3,2},{4,5},{5,4},{6,7},{7,6},{8,9},{9,8},{10,11... | collective-permute-start | bytes 2359304 | tf_op jit(solution)/shard_map/ppermute | solution.py:318
  692.4 7.6 %copy-start.38 = (bf16[64,16,1,128]{3,2,1,0:T(2,128)(2,1)S(1)}, bf16[64,16,1,128]{3,2,1,0:T(2,128)(2,1)}, u32[]{:S(2)}) copy-start(bf16[64,16,1,128]{3,2,1,0:T(2,128)(2,1)} %stack_reshape.18) | copy-start | bytes 786436
  692.7 11.5 %collective-permute-start.26 = (bf16[3,2,2,1,1,64,256]{6,5,0,4,3,2,1:T(8,128)(2,1)S(1)}, bf16[3,2,2,1,1,64,256]{6,5,0,4,3,2,1:T(8,128)(2,1)S(1)}, u32[]{:S(2)}, u32[]{:S(2)}) collective-permute-start(bf16[3,2,2,1,1,64,256]{6,5,0,4,3,2,1:T(8,128)(2,1)S(1)} %get-tuple-element.155), channel_id=1, source_target_pairs={{0,1},{1,0},{2,3},{3,2},{4,5},{5,4},{6,7},{7,6},{8,9},{9,8},{10,11... | collective-permute-start | bytes 1179656 | tf_op jit(solution)/shard_map/ppermute | solution.py:318
  698.7 9.8 %collective-permute-start.21 = (bf16[3,2,2,1,1,64,256]{6,5,4,3,2,1,0:T(8,128)(2,1)}, bf16[3,2,2,1,1,64,256]{6,5,4,3,2,1,0:T(8,128)(2,1)S(1)}, u32[]{:S(2)}, u32[]{:S(2)}) collective-permute-start(bf16[3,2,2,1,1,64,256]{6,5,4,3,2,1,0:T(8,128)(2,1)} %get-tuple-element.145), channel_id=1, source_target_pairs={{0,2},{1,3},{2,0},{3,1},{4,6},{5,7},{6,4},{7,5},{8,10},{9,11},{10,... | collective-permute-start | bytes 1179656 | tf_op jit(solution)/shard_map/ppermute | solution.py:318
  704.3 7.7 %collective-permute-start.27 = (bf16[3,2,1,1,1,64,256]{6,5,0,4,3,2,1:T(8,128)(2,1)S(1)}, bf16[3,2,1,1,1,64,256]{6,5,0,4,3,2,1:T(8,128)(2,1)S(1)}, u32[]{:S(2)}, u32[]{:S(2)}) collective-permute-start(bf16[3,2,1,1,1,64,256]{6,5,0,4,3,2,1:T(8,128)(2,1)S(1)} %get-tuple-element.153), channel_id=1, source_target_pairs={{0,4},{1,5},{2,6},{3,7},{4,0},{5,1},{6,2},{7,3},{8,12},{9,13},{10,... | collective-permute-start | bytes 589832 | tf_op jit(solution)/shard_map/ppermute | solution.py:318
  708.7 7.2 collective-permute-start.22
  712.0 8.2 %collective-permute-start.28 = (bf16[3,1,1,1,1,64,256]{6,5,0,4,3,2,1:T(8,128)(2,1)S(1)}, bf16[3,1,1,1,1,64,256]{6,5,0,4,3,2,1:T(8,128)(2,1)S(1)}, u32[]{:S(2)}, u32[]{:S(2)}) collective-permute-start(bf16[3,1,1,1,1,64,256]{6,5,0,4,3,2,1:T(8,128)(2,1)S(1)} %add_convert_fusion.37), channel_id=1, source_target_pairs={{0,8},{1,9},{2,10},{3,11},{4,12},{5,13},{6,14},{7,15},{8,0},{9,1},... | collective-permute-start | bytes 294920 | tf_op jit(solution)/shard_map/ppermute | solution.py:318
  715.8 7.0 collective-permute-start.23
  720.3 2.7 collective-permute-start.29
  722.9 1.4 collective-permute-start.24
  (36 other events, 107.9 us)

commit v3 on v2

--- a/solution.py
+++ b/solution.py
@@ -200,7 +200,7 @@
     *refs
 ):
     if last:
-        before_ref, out_ref, dkv_ref, list_ref = refs
+        before_ref, d_query_ref, out_ref, dkv_ref, list_ref = refs
     else:
         out_ref, dkv_ref, list_ref = refs
     frames = kv_ref.shape[0]
@@ -257,7 +257,7 @@
         )
         d_query = unturn(frame, d_query * (HEAD**-0.5)).astype(BF16)
         if last:
-            out_ref[source, 2 * per_device] = d_query
+            out_ref[source, 2 * per_device + part] = d_query
         else:
             out_ref[source] = d_query
 
@@ -269,6 +269,8 @@
             both = (dkv_ref[frame] + before_ref[frame]).T
             out_ref[source, place] = unturn(frame, both[:HEAD]).astype(BF16)
             out_ref[source, per_device + place] = both[HEAD:].astype(BF16)
+        for place in range(part):
+            out_ref[source, 2 * per_device + place] = d_query_ref[source]
         return carry
 
     if last:
@@ -286,8 +288,8 @@
     dkv = (frames, PATCHES, 2 * HEAD)
     lists = pltpu.SMEM((frames,), jnp.int32)
     if last:
-        args.append(before)
-        outs = jax.ShapeDtypeStruct((sources, 2 * per_device + 1, HEAD, PATCHES), BF16)
+        args += [before[1], before[0]]
+        outs = jax.ShapeDtypeStruct(x.shape, BF16)
         out_specs = whole_spec()
         scratch = [pltpu.VMEM(dkv, F32), lists]
     else:
@@ -322,14 +324,13 @@
     return lax.optimization_barrier((value,) + earlier)[0]
 
 
-def gather_all(value):
-    value = value[None]
-    for axis in ("seq", "pack"):
-        bit = lax.axis_size(axis) // 2
-        while bit:
-            value = jnp.concatenate([value, exchange(value, axis, bit)], axis=0)
-            bit //= 2
-    return value
+def of_packs(value):
+    values = [value]
+    bit = lax.axis_size("pack") // 2
+    while bit:
+        values = values + [exchange(each, "pack", bit) for each in values]
+        bit //= 2
+    return values
 
 
 def halving_fits():
@@ -603,73 +604,124 @@
     middle_ref,
     grad_ref,
     attn_ref,
+    feed_ref,
     scale_ref,
     gate_ref,
+    feed_gate_ref,
+    down_bias_ref,
+    rows_ref,
     weight_ref,
     d_middle_ref,
     d_attn_ref,
-    d_mix_ref,
-    d_shift_ref,
-    d_scale_ref,
-    d_gate_ref,
-    d_bias_ref,
+    layer_ref,
+    blocks_ref,
+    sums_ref,
 ):
     frame = pl.program_id(0)
-    mine = pl.ds(frame, 1)
-    back, d_shift, d_scale = norm_back(middle_ref[...], d_in_ref[...], scale_ref[mine, :])
-    d_middle = grad_ref[...].astype(F32) + back
-    d_middle_ref[...] = d_middle
-    d_shift_ref[mine, :] = d_shift
-    d_scale_ref[mine, :] = d_scale
-    d_gate_ref[mine, :] = jnp.sum(d_middle * attn_ref[...], axis=0, keepdims=True)
-    d_attn = (d_middle * gate_ref[mine, :]).astype(BF16)
-    d_attn_ref[...] = d_attn
-    d_bias_ref[mine, :] = jnp.sum(d_attn.astype(F32), axis=0, keepdims=True)
-    d_mix = dot_over(weight_ref[...], d_attn, 1, 1).astype(BF16)
-    for head in range(d_mix_ref.shape[0]):
-        d_mix_ref[head, 0] = d_mix[head * HEAD : (head + 1) * HEAD]
-
-
-def middle_back(per_device, d_in, middle, grads, attn_rows, scale, gate, weight):
+    per_device = pl.num_programs(0) - 1
+
+    @pl.when(frame < per_device)
+    def _():
+        mine = pl.ds(frame, 1)
+        middle = middle_ref[...]
+        grads = grad_ref[...].astype(F32)
+        back, d_shift, d_scale = norm_back(middle, d_in_ref[...], scale_ref[mine, :])
+        d_middle = grads + back
+        d_middle_ref[...] = d_middle
+        d_attn = (d_middle * gate_ref[mine, :]).astype(BF16)
+        d_attn_ref[...] = d_attn
+        feed_rows = feed_ref[...] + down_bias_ref[...]
+        feed_gate = feed_gate_ref[mine, :]
+        layer_ref[...] = (middle + feed_gate * feed_rows).astype(BF16)
+        d_feed_out = (feed_gate * grads).astype(BF16).astype(F32)
+        sums_ref[frame] = jnp.concatenate(
+            [
+                jnp.sum(d_middle * attn_ref[...], axis=0, keepdims=True),
+                d_shift,
+                d_scale,
+                jnp.sum(grads * feed_rows, axis=0, keepdims=True),
+                jnp.sum(d_attn.astype(F32), axis=0, keepdims=True),
+                jnp.sum(d_feed_out, axis=0, keepdims=True),
+                jnp.zeros((2, d_shift.shape[1]), F32),
+            ],
+            axis=0,
+        )
+        d_mix = dot_over(weight_ref[...], d_attn, 1, 1).astype(BF16)
+        for head in range(blocks_ref.shape[0]):
+            blocks_ref[head, 0] = d_mix[head * HEAD : (head + 1) * HEAD]
+
+    @pl.when(frame == per_device)
+    def _():
+        first = sums_ref[0]
+        second = sums_ref[1]
+        rows = jnp.concatenate(
+            [first[:4], second[:4], first[4:6] + second[4:6], rows_ref[...]], axis=0
+        ).astype(BF16)
+        count = rows.shape[1] // PATCHES
+        block = jnp.concatenate(
+            [rows[:, nth * PATCHES : (nth + 1) * PATCHES] for nth in range(count)], axis=0
+        )
+        for head in range(blocks_ref.shape[0]):
+            blocks_ref[head, 0] = block
+
+
+def middle_back(
+    per_device, d_in, middle, grads, attn_rows, feed_rows, scale, gate, feed_gate, down_bias, rows, weight
+):
     tokens, width = d_in.shape
     heads = width // HEAD
-    rows = pl.BlockSpec((PATCHES, width), lambda frame: (frame, 0))
+    last = per_device - 1
+    per_frame = pl.BlockSpec((PATCHES, width), lambda frame: (jnp.minimum(frame, last), 0))
 
     def whole(shape):
         return pl.BlockSpec(shape, lambda frame: (0,) * len(shape))
 
     small = whole((per_device, width))
-    small_shape = jax.ShapeDtypeStruct((per_device, width), F32)
     return pl.pallas_call(
         middle_back_kernel,
-        grid=(per_device,),
+        grid=(per_device + 1,),
         out_shape=(
             jax.ShapeDtypeStruct((tokens, width), F32),
             jax.ShapeDtypeStruct((tokens, width), BF16),
-            jax.ShapeDtypeStruct((heads, per_device, HEAD, PATCHES), BF16),
-        )
-        + (small_shape,) * 4,
-        in_specs=[rows] * 4 + [small, small, whole(weight.shape)],
+            jax.ShapeDtypeStruct((tokens, width), BF16),
+            jax.ShapeDtypeStruct((heads, per_device + 1, HEAD, PATCHES), BF16),
+        ),
+        in_specs=[per_frame] * 5
+        + [small] * 3
+        + [whole((1, width)), whole(rows.shape), whole(weight.shape)],
         out_specs=(
-            rows,
-            rows,
+            per_frame,
+            per_frame,
+            per_frame,
             pl.BlockSpec((heads, 1, HEAD, PATCHES), lambda frame: (0, frame, 0, 0)),
-        )
-        + (small,) * 4,
+        ),
+        scratch_shapes=[pltpu.VMEM((per_device, 8, width), F32)],
         cost_estimate=pl.CostEstimate(
             flops=2 * tokens * width * width, bytes_accessed=24 * tokens * width, transcendentals=0
         ),
-        compiler_params=pltpu.CompilerParams(vmem_limit_bytes=40 << 20),
+        compiler_params=pltpu.CompilerParams(vmem_limit_bytes=48 << 20),
         name="middle_back",
-    )(d_in, middle, grads, attn_rows, scale, gate, weight)
+    )(
+        d_in,
+        middle,
+        grads,
+        attn_rows,
+        feed_rows,
+        scale,
+        gate,
+        feed_gate,
+        down_bias[None],
+        rows,
+        weight,
+    )
 
 
 def unproject_kernel(
-    per_device, carried, which_ref, in_ref, first_ref, back_ref, wq_ref, wk_ref, wv_ref, *refs
+    per_device, carried, which_ref, in_ref, back_ref, wq_ref, wk_ref, wv_ref, *refs
 ):
     if carried:
-        before_ref, hidden_ref, d_middle_ref, scale_ref = refs[:4]
-        d_weight_ref, d_bias_ref, grad_ref, d_shift_ref, d_scale_ref, d_in_ref, turned_ref = refs[4:]
+        before_ref, hidden_ref, d_middle_ref, scale_ref, bias_theirs_ref = refs[:5]
+        d_weight_ref, grad_ref, rows_ref, d_in_ref, d_bias_ref, turned_ref = refs[5:]
     else:
         d_in_ref, d_weight_ref, d_bias_ref, turned_ref = refs
 
@@ -690,14 +742,9 @@
             rows.append(block.astype(F32).T.astype(BF16))
         return jnp.concatenate(rows, axis=0)
 
-    def query_block(head, place):
-        if place == per_device - 1:
-            return back_ref[head, 2 * per_device]
-        return first_ref[head, place]
-
     sides = jnp.concatenate(
         [
-            token_major(query_block),
+            token_major(lambda head, place: back_ref[head, 2 * per_device + place]),
             token_major(lambda head, place: back_ref[head, place]),
             token_major(lambda head, place: back_ref[head, per_device + place]),
         ],
@@ -710,12 +757,18 @@
     lanes = group * HEAD
     for kind in range(3):
         d_weight_ref[kind] = d_weight[:, kind * lanes : (kind + 1) * lanes]
-        d_bias_ref[kind] = d_bias[:, kind * lanes : (kind + 1) * lanes]
+        part = d_bias[:, kind * lanes : (kind + 1) * lanes]
+        if carried:
+            start = pl.multiple_of(pl.program_id(0) * lanes, lanes)
+            d_bias_ref[pl.ds(kind, 1), pl.ds(start, lanes)] = part
+        else:
+            d_bias_ref[kind] = part
 
     if carried:
 
         @pl.when(pl.program_id(0) == pl.num_programs(0) - 1)
         def _():
+            sums = []
             for place in range(per_device):
                 rows = pl.ds(place * PATCHES, PATCHES)
                 mine = pl.ds(place, 1)
@@ -723,11 +776,20 @@
                     hidden_ref[rows, :].astype(F32), d_in_ref[rows, :], scale_ref[mine, :]
                 )
                 grad_ref[rows, :] = (d_middle_ref[rows, :] + back).astype(BF16)
-                d_shift_ref[mine, :] = d_shift
-                d_scale_ref[mine, :] = d_scale
-
-
-def unproject(per_device, which, attn_in, first, back, weight, before=None, norm_args=()):
+                sums += [d_shift, d_scale]
+            for kind in range(3):
+                sums.append(
+                    jnp.concatenate([d_bias_ref[pl.ds(kind, 1), :], bias_theirs_ref[kind]], axis=1)
+                )
+            count = 16 - len(sums)
+            late = jnp.concatenate(
+                sums + [jnp.zeros((count, d_in_ref.shape[1]), F32)], axis=0
+            ).astype(BF16)
+            for target in range(rows_ref.shape[0]):
+                rows_ref[target] = late
+
+
+def unproject(per_device, targets, which, attn_in, back, weight, before=None, norm_args=()):
     tokens, width = attn_in.shape
     heads = width // HEAD
     group = 2
@@ -748,8 +810,8 @@
             (width, lanes), lambda step, which: (0, kind * groups + which[0] * steps + step)
         )
 
-    args = [attn_in, first, back, weight, weight, weight]
-    specs = [whole((tokens, width)), blocks(first), blocks(back), part(0), part(1), part(2)]
+    args = [attn_in, back, weight, weight, weight]
+    specs = [whole((tokens, width)), blocks(back), part(0), part(1), part(2)]
     weight_shape = (
         jax.ShapeDtypeStruct((3, width, width // 2), BF16),
         jax.ShapeDtypeStruct((3, 1, width // 2), F32),
@@ -762,14 +824,14 @@
     small = (per_device, width)
     if before is not None:
         args += [before] + list(norm_args)
-        specs += [whole((tokens, width))] * 3 + [whole(small)]
-        outs = weight_shape + (
+        specs += [whole((tokens, width))] * 3 + [whole(small), whole((3, 1, width // 2))]
+        late = (targets, 16, width)
+        outs = weight_shape[:1] + (
             jax.ShapeDtypeStruct((tokens, width), BF16),
-            jax.ShapeDtypeStruct(small, F32),
-            jax.ShapeDtypeStruct(small, F32),
-        )
-        out_specs = weight_specs + (whole((tokens, width)), whole(small), whole(small))
-        scratch = [pltpu.VMEM((tokens, width), F32)] + scratch
+            jax.ShapeDtypeStruct(late, BF16),
+        )
+        out_specs = weight_specs[:1] + (whole((tokens, width)), whole(late))
+        scratch = [pltpu.VMEM((tokens, width), F32), pltpu.VMEM((3, width // 2), F32)] + scratch
     else:
         outs = (jax.ShapeDtypeStruct((tokens, width), F32),) + weight_shape
         out_specs = (whole((tokens, width)),) + weight_specs
@@ -873,10 +935,7 @@
     cos_all, sin_all = rotary_tables(after(frame_times, attn_in))
     grad_rows = cotangent[0].astype(F32).reshape(per_device, PATCHES, width)
     d_feed_out = (feed_gate[:, None, :] * grad_rows).reshape(tokens, width).astype(BF16)
-    down_bias_term = jnp.sum(d_feed_out.astype(F32), axis=0)
-    x, d_feed_out, down_bias_term, cos_all, sin_all = lax.optimization_barrier(
-        (x, d_feed_out, down_bias_term, cos_all, sin_all)
-    )
+    x, d_feed_out, cos_all, sin_all = lax.optimization_barrier((x, d_feed_out, cos_all, sin_all))
     mix, wide, lse, kv = attend(per_device, clip_ids, live, x)
     mix = to_tokens(mix)
     mixes = [mix[:, place].reshape(width, PATCHES) for place in range(per_device)]
@@ -889,7 +948,6 @@
     feed_args = (feed_in, d_feed_out, up_weight, up_bias, down_weight)
     theirs = feed(1 - pack if halves else pack * 0 + 1, *feed_args, None)
     mine = feed(pack if halves else pack * 0, *feed_args, theirs[:2])
-    feed_rows = mine[0].reshape(per_device, PATCHES, width)
     small = 128
 
     def in_order(own, other):
@@ -902,19 +960,38 @@
             [even.reshape(rows, -1, small), odd.reshape(rows, -1, small)], axis=2
         ).reshape(rows, -1)
 
-    up_bias_term = in_order(mine[4], theirs[4])[0]
-    d_middle, d_attn_out, d_mix, d_feed_shift, d_feed_scale, d_attn_gate, out_bias_rows = middle_back(
+    own_levels = levels[0]
+    level_row = jnp.concatenate(
+        [
+            jnp.broadcast_to(part[frame], (width // (2 * per_device),))
+            for frame in range(per_device)
+            for part in (lax.div(own_levels, 32), lax.rem(own_levels, 32))
+        ]
+    ).astype(F32)[None]
+    extra_rows = jnp.concatenate(
+        [
+            in_order(mine[4], theirs[4]).reshape(-1, width),
+            level_row,
+            jnp.zeros((1, width), F32),
+        ],
+        axis=0,
+    )
+    d_middle, d_attn_out, layer_out, blocks = middle_back(
         per_device,
         mine[1],
         middle.reshape(tokens, width),
         cotangent[0],
         attn_rows.reshape(tokens, width),
+        mine[0],
         feed_scale,
         attn_gate,
+        feed_gate,
+        down_bias,
+        extra_rows,
         out_weight,
     )
-    d_mix = to_heads(d_mix)
-    out_bias_term = jnp.sum(out_bias_rows, axis=0)
+    layer_out = layer_out.reshape(1, tokens, width)
+    d_mix = to_heads(blocks)
 
     def out_term(start, size):
         return dot_over(attn_mix, columns_of(d_attn_out, start, size), 1, 0).astype(BF16)
@@ -925,66 +1002,64 @@
         down_sum = RowSum(mine[3], exchange(theirs[3], "pack", 1), (1, 2, 4, 8))
         out_theirs = exchange(out_term((1 - pack) * (width // 2), width // 2), "pack", 1)
         out_sum = RowSum(out_term(pack * (width // 2), width // 2), out_theirs, (1, 2, 4, 8))
-        sums = (down_sum, up_sum, out_sum)
-    feed_rows = feed_rows + down_bias
-    layer_out = (middle + feed_gate[:, None, :] * feed_rows).reshape(1, tokens, width).astype(BF16)
-    d_feed_gate = jnp.sum(grad_rows * feed_rows, axis=1)
-
-    own_levels = levels[0]
-    chunk = width
-    early_bias = [out_bias_term, up_bias_term, down_bias_term]
-    bias_sizes = [each.shape[0] for each in early_bias]
-    rows = [
-        each.astype(BF16) for each in (d_attn_gate, d_feed_shift, d_feed_scale, d_feed_gate)
-    ] + [each.astype(BF16).reshape(-1, chunk) for each in early_bias]
-    rows.append(
-        jnp.broadcast_to(
-            jnp.concatenate([lax.div(own_levels, 32), lax.rem(own_levels, 32)])[:, None],
-            (2 * per_device, chunk),
-        ).astype(BF16)
-    )
-    early = jnp.concatenate(rows, axis=0)
-    early_all = gather_all(early)
-
-    def bias_share(rows, size):
-        flat = jnp.sum(rows.astype(F32), axis=0).reshape(size)
-        piece = size // seq_count
-        return lax.dynamic_slice_in_dim(flat, seq_index * piece, piece)
-
-    def frames_of(rows):
-        return rows.reshape(-1, rows.shape[-1])
-
-    at = 4 * per_device
-    early_bias_grads = []
-    for size in bias_sizes:
-        early_bias_grads.append(bias_share(early_all[:, at : at + size // chunk], size))
-        at += size // chunk
-    coarse = early_all[:, at : at + per_device, 0].astype(jnp.int32)
-    fine = early_all[:, at + per_device : at + 2 * per_device, 0].astype(jnp.int32)
-    all_levels = (coarse * 32 + fine).reshape(-1)
-    picks = (all_levels[:, None] == jnp.arange(level_count, dtype=jnp.int32)[None, :]).astype(F32)
+        sums = (down_sum, up_sum)
+    def own_share(row):
+        piece = row.shape[0] // seq_count
+        return lax.dynamic_slice_in_dim(row, seq_index * piece, piece)
+
+    chunks = width // PATCHES
+    early_rows = d_mix[:, per_device].reshape(seq_count, chunks, 16, PATCHES)
+    early_rows = early_rows.transpose(0, 2, 1, 3).reshape(seq_count, 16, width)
+    early_sets = of_packs(early_rows)
+    early_sum = functools.reduce(
+        jnp.add, [jnp.sum(each.astype(F32), axis=0) for each in early_sets]
+    )
+    out_bias_grad = own_share(early_sum[8])
+    down_bias_grad = own_share(early_sum[9])
+    up_bias_grad = own_share(early_sum[10:14].reshape(hidden_units))
+
+    def frames_of(rows, per_frame, kinds):
+        return jnp.concatenate(
+            [
+                jnp.stack(
+                    [rows[:, frame * per_frame + kind] for frame in range(per_device)], axis=1
+                ).reshape(-1, width)
+                for kind in range(kinds)
+            ],
+            axis=1,
+        )
+
     own_table = lax.dynamic_slice_in_dim(noise_table, seq_index * share, share, 1)
-    all_embed = jnp.dot(picks, own_table, precision=PRECISE, preferred_element_type=F32)
-    silu_value, silu_back = jax.vjp(jax.nn.silu, all_embed)
-    all_cond = silu_value.astype(BF16)
-    d_mod_early = jnp.concatenate(
-        [
-            frames_of(early_all[:, kind * per_device : (kind + 1) * per_device])
-            for kind in range(4)
-        ],
-        axis=1,
-    )
     own_mod = lax.dynamic_slice_in_dim(mod_weight, seq_index * share, share, 0)
-    d_cond_early = dot_over(d_mod_early, own_mod[:, 2 * width :], 1, 1)
-    mod_grad_early = dot_over(all_cond, d_mod_early, 0, 0)
-    mod_sum_early = jnp.sum(d_mod_early.astype(F32), axis=0)
-    early_done = [d_cond_early, mod_grad_early, mod_sum_early, all_embed, layer_out]
-    early_done += early_bias_grads
+    stride = width // (2 * per_device)
+    parts = []
+    for rows in early_sets:
+        coded = rows[:, 14, ::stride].astype(jnp.int32).reshape(-1, 2)
+        set_levels = coded[:, 0] * 32 + coded[:, 1]
+        picks = (set_levels[:, None] == jnp.arange(level_count, dtype=jnp.int32)[None, :]).astype(F32)
+        embeds = jnp.dot(picks, own_table, precision=PRECISE, preferred_element_type=F32)
+        set_cond = jax.nn.silu(embeds).astype(BF16)
+        d_mod = frames_of(rows, 4, 4)
+        parts.append(
+            (
+                picks,
+                embeds,
+                set_cond,
+                dot_over(d_mod, own_mod[:, 2 * width :], 1, 1),
+                dot_over(set_cond, d_mod, 0, 0),
+            )
+        )
+    mod_grad_early = functools.reduce(jnp.add, [each[4] for each in parts])
+    mod_sum_early = (early_sum[:4] + early_sum[4:8]).reshape(4 * width)
+    early_done = [mod_grad_early, mod_sum_early, out_bias_grad, down_bias_grad, up_bias_grad]
+    for part in parts:
+        early_done += [part[1], part[3]]
 
     before = None
-    d_queries = []
     for part in range(per_device):
         sends = [each.stage() for each in sums]
+        if halves and part:
+            sends.append(out_sum.stage())
         result = attend_back(
             part,
             per_device,
@@ -999,41 +1074,36 @@
             sin_all,
             before,
         )
-        if part < per_device - 1:
-            d_query, before = result
-            d_queries.append(to_tokens(d_query))
-    firsts = jnp.stack(d_queries, axis=1)
-    result = after(result, firsts[0, 0, :8], *[each.stage() for each in sums])
-    back = to_tokens(result)
+        before = result
+    sends = [each.stage() for each in sums]
+    if halves:
+        sends.append(out_sum.stage())
+    back = to_tokens(after(result, *sends))
     for each in sums:
         each.hold(back[0, 0, :8])
     back = after(back, *early_done)
     which = (1 - pack, pack) if halves else (pack * 0, pack * 0 + 1)
     d_in_theirs, qkv_theirs, bias_theirs = unproject(
-        per_device, which[0], attn_in, firsts, back, qkv_weight
-    )
-    qkv_mine, bias_mine, hidden_grad, d_attn_shift, d_attn_scale = unproject(
+        per_device, seq_count, which[0], attn_in, back, qkv_weight
+    )
+    qkv_mine, hidden_grad, late = unproject(
         per_device,
+        seq_count,
         which[1],
         attn_in,
-        firsts,
         back,
         qkv_weight,
         d_in_theirs,
-        (hidden[0], d_middle, attn_scale),
+        (hidden[0], d_middle, attn_scale, bias_theirs),
     )
     hidden_grad = hidden_grad.reshape(1, tokens, width)
+    late_rows = lax.all_to_all(late, "seq", 0, 0, tiled=True)
 
     def halves_in_order(own, other):
         if halves:
             return jnp.where(pack == 0, own, other), jnp.where(pack == 0, other, own)
         return other, own
 
-    qkv_bias_term = jnp.concatenate(halves_in_order(bias_mine[:, 0], bias_theirs[:, 0]), axis=1)
-    late = jnp.concatenate(
-        [d_attn_shift.astype(BF16), d_attn_scale.astype(BF16), qkv_bias_term.astype(BF16)], axis=0
-    )
-    late_all = gather_all(late)
     if halves:
         came = exchange(qkv_theirs, "pack", 1)
         split = width // 4
@@ -1061,24 +1131,41 @@
         qkv_term = jnp.concatenate(halves_in_order(qkv_mine, qkv_theirs), axis=-1)
         qkv_weight_grad = row_sum_direct(qkv_term.transpose(1, 0, 2).reshape(width, 3 * width))
 
-    out_bias_grad, up_bias_grad, down_bias_grad = early_bias_grads
-    qkv_bias_grad = bias_share(late_all[:, 2 * per_device :], 3 * width)
-    d_mod_late = jnp.concatenate(
-        [
-            frames_of(late_all[:, kind * per_device : (kind + 1) * per_device])
-            for kind in range(2)
-        ],
-        axis=1,
-    )
-    d_cond = d_cond_early + dot_over(d_mod_late, own_mod[:, : 2 * width], 1, 1)
-    d_embed = silu_back(d_cond)[0]
+    late_sets = of_packs(late_rows[:, :8])
+    bias_at = 2 * per_device
+    bias_sums = [
+        jnp.sum(rows[:, bias_at : bias_at + 3].astype(F32), axis=0) for rows in late_sets
+    ]
+    if halves:
+        ones, twos = bias_sums
+        half = width // 2
+        own_half = ones[:, :half] + twos[:, half:]
+        other_half = ones[:, half:] + twos[:, :half]
+    else:
+        total = functools.reduce(jnp.add, bias_sums)
+        own_half, other_half = total[:, : width // 2], total[:, width // 2 :]
+    bias_total = jnp.concatenate(halves_in_order(own_half, other_half), axis=1)
+    qkv_bias_grad = own_share(bias_total.reshape(3 * width))
+    late_mods = [frames_of(rows, 2, 2) for rows in late_sets]
+    mod_sum_late = functools.reduce(
+        jnp.add, [jnp.sum(each.astype(F32), axis=0) for each in late_mods]
+    )
+    d_embeds = []
+    for part, d_mod in zip(parts, late_mods):
+        d_cond = part[3] + dot_over(d_mod, own_mod[:, : 2 * width], 1, 1)
+        d_embeds.append(jax.vjp(jax.nn.silu, part[1])[1](d_cond)[0])
     table_grad = lax.dot_general(
-        picks, d_embed, (((0,), (0,)), ((), ())), precision=PRECISE, preferred_element_type=F32
-    )
-    mod_weight_grad = jnp.concatenate([dot_over(all_cond, d_mod_late, 0, 0), mod_grad_early], axis=1)
-    bias_piece = mod_bias.shape[0] // seq_count
-    d_mod_sum = jnp.concatenate([jnp.sum(d_mod_late.astype(F32), axis=0), mod_sum_early])
-    mod_bias_grad = lax.dynamic_slice_in_dim(d_mod_sum, seq_index * bias_piece, bias_piece)
+        jnp.concatenate([part[0] for part in parts], axis=0),
+        jnp.concatenate(d_embeds, axis=0),
+        (((0,), (0,)), ((), ())),
+        precision=PRECISE,
+        preferred_element_type=F32,
+    )
+    mod_grad_late = functools.reduce(
+        jnp.add, [dot_over(part[2], d_mod, 0, 0) for part, d_mod in zip(parts, late_mods)]
+    )
+    mod_weight_grad = jnp.concatenate([mod_grad_late, mod_grad_early], axis=1)
+    mod_bias_grad = own_share(jnp.concatenate([mod_sum_late, mod_sum_early]))
     return (
         layer_out,
         hidden_grad,

time: 734 us -> 681 us (0.928)
  local copies, waits for them, and re-layouts: 126 us -> 49 us
  waiting for transfers between devices: 226 us -> 253 us
  other arithmetic: 74.2 us -> 64.2 us
  matrix products: 18.1 us -> 25.7 us
    concatenate x7 -> x9, local copies, waits for them, and re-layouts: 40.4 us -> 0.96 us  [the longest x4 0.86 us: frames_of(): jnp.concatenate([jnp.stack([rows[:, frame * per_frame + kind] for frame i...]
    ppermute x6 -> x0, local copies, waits for them, and re-layouts: 31.7 us -> none  [exchange(): lax.ppermute(value, axis, [(source, source ^ bit) for source in range(cou...]
    ppermute x39 -> x31, waiting for transfers between devices: 151 us -> 177 us  [exchange(): lax.ppermute(value, axis, [(source, source ^ bit) for source in range(cou...]
    reduce_sum x8 -> x6, other arithmetic: 13.1 us -> 0.43 us  [the longest x4 0.23 us: local(): jnp.sum(each.astype(F32), axis=0)]
    all_to_all x3 -> x2, starting transfers between devices: 26.6 us -> 20.7 us  [to_tokens(): return lax.all_to_all(array, 'seq', 0, 0, tiled=True)[:heads]]
    ppermute x39 -> x31, starting transfers between devices: 38.7 us -> 34.9 us  [exchange(): lax.ppermute(value, axis, [(source, source ^ bit) for source in range(cou...]
    unnamed x120 -> x70, local copies, waits for them, and re-layouts: 17 us -> 13.9 us
    all_to_all x3 -> x2, waiting for transfers between devices: 23.2 us -> 23.4 us  [to_tokens(): return lax.all_to_all(array, 'seq', 0, 0, tiled=True)[:heads]]
  transfers between devices with their start and end apart: 44 -> 36, of which waited for: 22 -> 17; matrix products, arithmetic and copies ran while one was open for 26% -> 16% of each run, Pallas kernels for 16% -> 17%
where the time goes in v3:
time: 681 us; the launch traced here: 671 us
  waiting for transfers between devices  253 us (37%)
  Pallas kernels  196 us (29%)
  starting transfers between devices  77.2 us (11%)
  other arithmetic  64.2 us (9%)
  local copies, waits for them, and re-layouts  49 us (7%)
  matrix products  25.7 us (4%)
    ppermute x31, waiting for transfers between devices, exchange(): lax.ppermute(value, axis, [(source, source ^ bit) for source in range(cou...  177 us
    pallas_call x2, Pallas kernels, attend_back(): pl.pallas_call(functools.partial(attend_back_kernel, per_device, part, la...  66.4 us
    all_to_all x2, waiting for transfers between devices, to_heads(): return lax.all_to_all(array, 'seq', 0, 0, tiled=True)  52.3 us
    pallas_call x1, Pallas kernels, attend(): pl.pallas_call(functools.partial(attend_kernel, per_device), out_shape=ou...  45.3 us
    pallas_call x2, Pallas kernels, feed(): pl.pallas_call(functools.partial(feed_kernel, before is not None), grid_s...  45.2 us
    convert_element_type x21, other arithmetic, pick(): return (pieces[0].astype(F32) + pieces[1].astype(F32)).astype(BF16)  35.9 us
    ppermute x31, starting transfers between devices, exchange(): lax.ppermute(value, axis, [(source, source ^ bit) for source in range(cou...  34.9 us
    all_to_all x2, waiting for transfers between devices, to_tokens(): return lax.all_to_all(array, 'seq', 0, 0, tiled=True)[:heads]  23.4 us
  transfers between devices with their start and end apart: 36, of which 17 were waited for; matrix products, arithmetic and copies ran while one was open for 16% of the time, Pallas kernels for 17%

profile of v3, /device:TPU:0, one launch (start us, length us, event | category | flops | bytes accessed | tf_op | source)
XLA Modules:
  0.0 670.6 jit_solution(13100186812377176955)
XLA Ops:
  7.5 2.9 fusion.7
  11.2 2.8 copy-done
  14.0 11.4 %project.1 = (bf16[512,1024]{1,0:T(8,128)(2,1)S(1)}, bf16[16,6,64,256]{3,2,1,0:T(8,128)(2,1)S(1)}) custom-call(bf16[512,1024]{1,0:T(8,128)(2,1)S(1)} %bitcast.146, f32[2,1024]{1,0:T(2,128)S(1)} %get-tuple-element.188.shift_ref, f32[2,1024]{1,0:T(2,128)S(1)} %get-tuple-element.187.scale_ref.refs_3_, bf16[1024,3072]{1,0:T(8,128)(2,1)S(1)} %copy-done, ...), custom_call_target="tpu_custom_call" | custom-call | flops 3221225472 | bytes 11534336 | tf_op jit(solution)/shard_map/project/pallas_call | solution.py:450
  25.4 1.6 copy-done.3
  27.0 8.5 %all-to-all-start = ((bf16[16,6,64,256]{3,2,1,0:T(8,128)(2,1)}), bf16[16,6,64,256]{3,2,1,0:T(8,128)(2,1)}, u32[]{:S(2)}, u32[]{:S(2)}) async-start(bf16[16,6,64,256]{3,2,1,0:T(8,128)(2,1)} %copy-done.3), calls=%async_computation | async-start | bytes 6291456 | tf_op jit(solution)/shard_map/all_to_all | solution.py:923
  35.5 4.7 fusion.2
  44.2 52.3 %all-to-all-done.x_ref = bf16[16,6,64,256]{3,2,1,0:T(8,128)(2,1)} async-done(((bf16[16,6,64,256]{3,2,1,0:T(8,128)(2,1)}), bf16[16,6,64,256]{3,2,1,0:T(8,128)(2,1)}, u32[]{:S(2)}, u32[]{:S(2)}) %all-to-all-start) | async-done | bytes 3145760 | tf_op jit(solution)/shard_map/all_to_all | solution.py:923
  96.5 45.3 %attend.1 = (bf16[16,2,64,256]{3,2,1,0:T(8,128)(2,1)S(1)}, f32[16,2,64,256]{3,2,1,0:T(8,128)S(1)}, f32[32,256]{1,0:T(8,128)S(1)}, bf16[32,256,128]{2,1,0:T(8,128)(2,1)S(1)}) custom-call(s32[32]{0:T(128)S(1)} %bitcast.156, s32[32]{0:T(128)S(1)} %bitcast.159, bf16[16,6,64,256]{3,2,1,0:T(8,128)(2,1)} %all-to-all-done.x_ref), custom_call_target="tpu_custom_call" | custom-call | flops 12884901888 | bytes 9437184 | tf_op jit(solution)/shard_map/attend/pallas_call | solution.py:171
  145.9 15.8 %all-to-all-start.1 = ((bf16[16,2,64,256]{3,2,1,0:T(8,128)(2,1)}), bf16[16,2,64,256]{3,2,1,0:T(8,128)(2,1)}, u32[]{:S(2)}, u32[]{:S(2)}) async-start(bf16[16,2,64,256]{3,2,1,0:T(8,128)(2,1)} %copy-done.6), calls=%async_computation.1 | async-start | bytes 2097152 | tf_op jit(solution)/shard_map/all_to_all | solution.py:926
  161.7 23.4 %all-to-all-done.1 = bf16[16,2,64,256]{3,2,1,0:T(8,128)(2,1)} async-done(((bf16[16,2,64,256]{3,2,1,0:T(8,128)(2,1)}), bf16[16,2,64,256]{3,2,1,0:T(8,128)(2,1)}, u32[]{:S(2)}, u32[]{:S(2)}) %all-to-all-start.1) | async-done | bytes 1048608 | tf_op jit(solution)/shard_map/all_to_all | solution.py:926
  190.6 3.2 fusion.10
  193.7 21.9 %feed0.1 = (f32[512,1024]{1,0:T(8,128)}, f32[512,1024]{1,0:T(8,128)}, bf16[1024,2048]{1,0:T(8,128)(2,1)}, bf16[2048,1024]{1,0:T(8,128)(2,1)}, f32[1,2048]{1,0:T(1,128)}) custom-call(s32[1]{0:T(128)} %bitcast.20.which_ref, bf16[512,1024]{1,0:T(8,128)(2,1)} %get-tuple-element.97.in_ref, bf16[512,1024]{1,0:T(8,128)(2,1)} %fusion.13.d_out_ref, ...), custom_call_target="tpu_custom_call" | custom-call | flops 12884901888 | bytes 25165824 | tf_op jit(solution)/shard_map/feed0/pallas_call | solution.py:556
  215.6 2.3 collective-permute-start.2
  222.0 23.3 %feed1.1 = (f32[512,1024]{1,0:T(8,128)}, f32[512,1024]{1,0:T(8,128)}, bf16[1024,2048]{1,0:T(8,128)(2,1)}, bf16[2048,1024]{1,0:T(8,128)(2,1)}, f32[1,2048]{1,0:T(1,128)}) custom-call(s32[1]{0:T(128)} %bitcast.which_ref, bf16[512,1024]{1,0:T(8,128)(2,1)} %get-tuple-element.97.in_ref, bf16[512,1024]{1,0:T(8,128)(2,1)} %fusion.13.d_out_ref, ...), custom_call_target="tpu_custom_call" | custom-call | flops 12884901888 | bytes 25165824 | tf_op jit(solution)/shard_map/feed1/pallas_call | solution.py:556
  246.1 8.1 %middle_back.1 = (f32[512,1024]{1,0:T(8,128)S(1)}, bf16[512,1024]{1,0:T(8,128)(2,1)S(1)}, bf16[512,1024]{1,0:T(8,128)(2,1)}, bf16[16,3,64,256]{3,2,1,0:T(8,128)(2,1)S(1)}) custom-call(f32[512,1024]{1,0:T(8,128)} %get-tuple-element.64.d_in_ref, f32[512,1024]{1,0:T(8,128)} %get-tuple-element.98.middle_ref, bf16[512,1024]{1,0:T(8,128)(2,1)S(1)} %bitcast.148, ...), custom_call_target="tpu_custom_call" | custom-call | flops 1073741824 | bytes 12582912 | tf_op jit(solution)/shard_map/middle_back/pallas_call | solution.py:680
  257.7 6.7 %all-to-all-start.2 = ((bf16[16,3,64,256]{3,2,1,0:T(8,128)(2,1)}), bf16[16,3,64,256]{3,2,1,0:T(8,128)(2,1)}, u32[]{:S(2)}, u32[]{:S(2)}) async-start(bf16[16,3,64,256]{3,2,1,0:T(8,128)(2,1)} %copy-done.5), calls=%async_computation.2 | async-start | bytes 3145728 | tf_op jit(solution)/shard_map/all_to_all | solution.py:923
  264.4 2.9 convolution_convert_fusion
  267.5 1.9 convolution_convert_fusion.1
  270.3 2.3 add_convert_fusion.14
  272.6 2.0 collective-permute-start.7
  274.7 7.9 %add_convert_fusion.1 = (bf16[2,2,1,2,64,2048]{5,4,3,2,1,0:T(8,128)(2,1)}, bf16[2,2,1,2,64,2048]{5,4,3,2,1,0:T(8,128)(2,1)}) fusion(bf16[2,2,2,2,64,2048]{5,4,3,2,1,0:T(8,128)(2,1)} %bitcast.35, s32[]{:T(128)S(6)} %select_n.245, bf16[2,2,2,2,64,2048]{5,4,3,2,1,0:T(8,128)(2,1)} %bitcast.173, s32[]{:T(128)S(6)} %select_n.243), kind=kLoop, calls=%fused_computation.5 | loop fusion | flops 8388608 | bytes 12582920 | tf_op jit(solution)/shard_map/convert_element_type | solution.py:353
  284.0 15.7 %collective-permute-done.7 = bf16[2,2,2,1,64,512]{5,4,3,2,1,0:T(8,128)(2,1)S(1)} collective-permute-done((bf16[2,2,2,1,64,512]{5,4,3,2,1,0:T(8,128)(2,1)}, bf16[2,2,2,1,64,512]{5,4,3,2,1,0:T(8,128)(2,1)S(1)}, u32[]{:S(2)}, u32[]{:S(2)}) %collective-permute-start.7) | collective-permute-done | bytes 524320 | tf_op jit(solution)/shard_map/ppermute | solution.py:320
  301.4 6.4 add_convert_fusion.3
  307.9 1.6 collective-permute-start.1
  309.5 30.9 %collective-permute-done.21 = bf16[2,2,1,1,64,512]{5,4,3,2,1,0:T(8,128)(2,1)S(1)} collective-permute-done((bf16[2,2,1,1,64,512]{5,4,3,2,1,0:T(8,128)(2,1)}, bf16[2,2,1,1,64,512]{5,4,3,2,1,0:T(8,128)(2,1)S(1)}, u32[]{:S(2)}, u32[]{:S(2)}) %collective-permute-start.21) | collective-permute-done | bytes 262176 | tf_op jit(solution)/shard_map/ppermute | solution.py:320
  340.5 3.9 collective-permute-start.22
  344.4 30.0 %attend_back0.1 = (bf16[16,64,256]{2,1,0:T(8,128)(2,1)}, f32[32,256,128]{2,1,0:T(8,128)}) custom-call(s32[32]{0:T(128)} %bitcast.153, s32[32]{0:T(128)} %bitcast.157, bf16[16,6,64,256]{3,2,1,0:T(8,128)(2,1)} %all-to-all-done.x_ref, bf16[32,256,128]{2,1,0:T(8,128)(2,1)} %copy-done.14, f32[16,2,64,256]{3,2,1,0:T(8,128)} %copy-done.13, f32[32,256]{1,0:T(8,128)} %copy-done.15, ...), custom_call_target="tpu_custom_call" | custom-call | flops 16106127360 | bytes 15728640 | tf_op jit(solution)/shard_map/attend_back0/pallas_call | solution.py:302
  374.4 4.2 add_convert_fusion.4
  379.5 3.6 add_convert_fusion.5
  383.5 36.4 %attend_back1.1 = bf16[16,6,64,256]{3,2,1,0:T(8,128)(2,1)} custom-call(s32[32]{0:T(128)} %bitcast.154, s32[32]{0:T(128)} %bitcast.158, bf16[16,6,64,256]{3,2,1,0:T(8,128)(2,1)} %all-to-all-done.x_ref, bf16[32,256,128]{2,1,0:T(8,128)(2,1)} %copy-done.14, f32[16,2,64,256]{3,2,1,0:T(8,128)} %copy-done.13, f32[32,256]{1,0:T(8,128)} %copy-done.15, ...), custom_call_target="tpu_custom_call" | custom-call | flops 16106127360 | bytes 15728640 | tf_op jit(solution)/shard_map/attend_back1/pallas_call | solution.py:302
  419.9 2.7 add_convert_fusion.13
  422.6 2.5 add_convert_fusion.12
  425.0 4.9 all-to-all-start.3
  430.0 3.0 collective-permute-start.23
  433.0 70.8 %collective-permute-done.23 = bf16[1,1,1,1,64,512]{5,4,3,2,1,0:T(8,128)(2,1)S(1)} collective-permute-done((bf16[1,1,1,1,64,512]{5,4,3,2,1,0:T(8,128)(2,1)S(1)}, bf16[1,1,1,1,64,512]{5,4,3,2,1,0:T(8,128)(2,1)S(1)}, u32[]{:S(2)}, u32[]{:S(2)}) %collective-permute-start.23) | collective-permute-done | bytes 65568 | tf_op jit(solution)/shard_map/ppermute | solution.py:320
  509.9 2.6 fusion.81
  513.3 1.9 fusion.24
  521.3 1.9 fusion.22
  524.5 2.0 collective-permute-start.25
  527.2 11.8 %collective-permute-done.28 = bf16[2,1,1,1,128,1024]{5,4,3,2,1,0:T(8,128)(2,1)} collective-permute-done((bf16[2,1,1,1,128,1024]{5,4,3,2,1,0:T(8,128)(2,1)}, bf16[2,1,1,1,128,1024]{5,4,3,2,1,0:T(8,128)(2,1)}, u32[]{:S(2)}, u32[]{:S(2)}) %collective-permute-start.28) | collective-permute-done | bytes 524320 | tf_op jit(solution)/shard_map/ppermute | solution.py:320
  539.0 1.8 add_convert_fusion.23
  540.8 14.3 %collective-permute-done.25 = bf16[2,1,1,1,64,2048]{5,4,3,2,1,0:T(8,128)(2,1)} collective-permute-done((bf16[2,1,1,1,64,2048]{5,4,3,2,1,0:T(8,128)(2,1)}, bf16[2,1,1,1,64,2048]{5,4,3,2,1,0:T(8,128)(2,1)}, u32[]{:S(2)}, u32[]{:S(2)}) %collective-permute-start.25) | collective-permute-done | bytes 524320 | tf_op jit(solution)/shard_map/ppermute | solution.py:320
  555.1 1.8 add_convert_fusion.26
  556.9 8.3 %unproject0.1 = (f32[512,1024]{1,0:T(8,128)S(1)}, bf16[3,1024,512]{2,1,0:T(8,128)(2,1)}, f32[3,1,512]{2,1,0:T(1,128)S(1)}) custom-call(s32[1]{0:T(128)} %bitcast.20.which_ref, bf16[512,1024]{1,0:T(8,128)(2,1)S(1)} %get-tuple-element.55.in_ref, bf16[16,6,64,256]{3,2,1,0:T(8,128)(2,1)} %all-to-all-done.3.back_ref, bf16[1024,3072]{1,0:T(8,128)(2,1)} %wv_ref.5, ...), custom_call_target="tpu_custom_call" | custom-call | flops 3221225472 | bytes 12582912 | tf_op jit(solution)/shard_map/unproject0/pallas_call | solution.py:838
  565.2 11.1 %unproject1.1 = (bf16[3,1024,512]{2,1,0:T(8,128)(2,1)}, bf16[512,1024]{1,0:T(8,128)(2,1)}, bf16[16,16,1024]{2,1,0:T(8,128)(2,1)}) custom-call(s32[1]{0:T(128)} %bitcast.which_ref, bf16[512,1024]{1,0:T(8,128)(2,1)S(1)} %get-tuple-element.55.in_ref, bf16[16,6,64,256]{3,2,1,0:T(8,128)(2,1)} %all-to-all-done.3.back_ref, bf16[1024,3072]{1,0:T(8,128)(2,1)} %wv_ref.5, ...), custom_call_target="tpu_custom_call" | custom-call | flops 3221225472 | bytes 12582912 | tf_op jit(solution)/shard_map/unproject1/pallas_call | solution.py:838
  576.3 6.4 all-to-all-start.4
  584.0 3.3 fusion.76
  587.8 1.8 fusion.27
  590.3 2.0 stack_reshape.16
  593.8 1.8 broadcast_select_fusion.1
  595.6 3.4 maximum_convert_fusion
  599.0 3.0 reshape.518
  602.0 2.1 maximum_convert_fusion.1
  610.3 1.8 fusion.47
  615.5 2.1 fusion.77
  618.2 2.1 collective-permute-start.11
  620.6 1.5 collective-permute-start.16
  623.6 14.5 %collective-permute-done.11 = bf16[3,2,2,2,1,64,256]{6,5,4,3,2,1,0:T(8,128)(2,1)S(1)} collective-permute-done((bf16[3,2,2,2,1,64,256]{6,5,4,3,2,1,0:T(8,128)(2,1)S(1)}, bf16[3,2,2,2,1,64,256]{6,5,4,3,2,1,0:T(8,128)(2,1)S(1)}, u32[]{:S(2)}, u32[]{:S(2)}) %collective-permute-start.11) | collective-permute-done | bytes 786464 | tf_op jit(solution)/shard_map/ppermute | solution.py:320
  638.5 1.8 collective-permute-start.12
  644.3 4.8 collective-permute-done.12
  653.0 5.0 collective-permute-done.13
  660.1 2.4 collective-permute-start.19
  662.5 3.1 collective-permute-done.14
  665.7 2.0 collective-permute-done.19
  (263 shorter events, 74.4 us)
Async XLA Ops:
  7.4 3.0 copy-start.11
  7.4 3.7 copy-start.1
  7.5 3.7 copy-start.7
  11.2 2.8 copy-start
  25.4 1.6 copy-start.3
  27.0 8.5 %slice-start = ((f32[6144]{0:T(1024)}), f32[4096]{0:T(1024)S(1)}, s32[]{:S(2)}) async-start(f32[6144]{0:T(1024)} %param.23), calls=%async_computation.5 | async-start | bytes 32768 | tf_op jit(solution)/shard_map/slice | solution.py:933
  27.0 69.4 %all-to-all-start = ((bf16[16,6,64,256]{3,2,1,0:T(8,128)(2,1)}), bf16[16,6,64,256]{3,2,1,0:T(8,128)(2,1)}, u32[]{:S(2)}, u32[]{:S(2)}) async-start(bf16[16,6,64,256]{3,2,1,0:T(8,128)(2,1)} %copy-done.3), calls=%async_computation | async-start | bytes 6291456 | tf_op jit(solution)/shard_map/all_to_all | solution.py:923
  35.5 4.7 copy-start.2
  42.9 53.6 %copy-start.12 = (s32[1,32]{1,0:T(1,128)S(1)}, s32[1,32]{1,0:T(1,128)}, u32[]{:S(2)}) copy-start(s32[1,32]{1,0:T(1,128)} %param.20) | copy-start | bytes 388
  142.7 1.3 copy-start.13
  144.0 1.3 copy-start.14
  145.9 15.8 %copy-start.30 = (s32[1,2]{1,0:T(1,128)S(1)}, s32[1,2]{1,0:T(1,128)}, u32[]{:S(2)}) copy-start(s32[1,2]{1,0:T(1,128)} %param.18) | copy-start | bytes 28
  145.9 39.2 %all-to-all-start.1 = ((bf16[16,2,64,256]{3,2,1,0:T(8,128)(2,1)}), bf16[16,2,64,256]{3,2,1,0:T(8,128)(2,1)}, u32[]{:S(2)}, u32[]{:S(2)}) async-start(bf16[16,2,64,256]{3,2,1,0:T(8,128)(2,1)} %copy-done.6), calls=%async_computation.1 | async-start | bytes 2097152 | tf_op jit(solution)/shard_map/all_to_all | solution.py:926
  185.2 1.9 copy-start.16
  186.6 1.2 copy-start.21
  186.6 1.2 copy-start.22
  215.6 59.0 %collective-permute-start.2 = (bf16[1024,2048]{1,0:T(8,128)(2,1)}, bf16[1024,2048]{1,0:T(8,128)(2,1)}, u32[]{:S(2)}, u32[]{:S(2)}) collective-permute-start(bf16[1024,2048]{1,0:T(8,128)(2,1)} %get-tuple-element.76), channel_id=1, source_target_pairs={{0,16},{16,0},{1,17},{17,1},{2,18},{18,2},{3,19},{19,3},{4,20},{20... | collective-permute-start | bytes 12582920 | tf_op jit(solution)/shard_map/ppermute | solution.py:320
  221.9 79.6 %collective-permute-start = (bf16[2048,1024]{1,0:T(8,128)(2,1)}, bf16[2048,1024]{1,0:T(8,128)(2,1)}, u32[]{:S(2)}, u32[]{:S(2)}) collective-permute-start(bf16[2048,1024]{1,0:T(8,128)(2,1)} %get-tuple-element.74), channel_id=1, source_target_pairs={{0,16},{16,0},{1,17},{17,1},{2,18},{18,2},{3,19},{19,3},{4,20},{20... | collective-permute-start | bytes 12582920 | tf_op jit(solution)/shard_map/ppermute | solution.py:320
  222.0 23.3 %copy-start.29 = (f32[1,2048]{1,0:T(1,128)S(1)}, f32[1,2048]{1,0:T(1,128)}, u32[]{:S(2)}) copy-start(f32[1,2048]{1,0:T(1,128)} %get-tuple-element.67) | copy-start | bytes 24580
  222.0 24.2 %copy-start.8 = (f32[1024]{0:T(1024)S(1)}, f32[1024]{0:T(1024)}, u32[]{:S(2)}) copy-start(f32[1024]{0:T(1024)} %param.31) | copy-start | bytes 12292
  254.3 1.3 copy-start.4
  255.6 1.1 copy-start.5
  257.7 6.7 %copy-start.10 = (bf16[512,1024]{1,0:T(8,128)(2,1)S(1)}, bf16[512,1024]{1,0:T(8,128)(2,1)}, u32[]{:S(2)}) copy-start(bf16[512,1024]{1,0:T(8,128)(2,1)} %copy-done.9) | copy-start | bytes 3145732
  257.7 86.7 %all-to-all-start.2 = ((bf16[16,3,64,256]{3,2,1,0:T(8,128)(2,1)}), bf16[16,3,64,256]{3,2,1,0:T(8,128)(2,1)}, u32[]{:S(2)}, u32[]{:S(2)}) async-start(bf16[16,3,64,256]{3,2,1,0:T(8,128)(2,1)} %copy-done.5), calls=%async_computation.2 | async-start | bytes 3145728 | tf_op jit(solution)/shard_map/all_to_all | solution.py:923
  267.3 3.0 collective-permute-start.4
  272.6 27.1 %collective-permute-start.7 = (bf16[2,2,2,1,64,512]{5,4,3,2,1,0:T(8,128)(2,1)}, bf16[2,2,2,1,64,512]{5,4,3,2,1,0:T(8,128)(2,1)S(1)}, u32[]{:S(2)}, u32[]{:S(2)}) collective-permute-start(bf16[2,2,2,1,64,512]{5,4,3,2,1,0:T(8,128)(2,1)} %get-tuple-element.121), channel_id=1, source_target_pairs={{0,1},{1,0},{2,3},{3,2},{4,5},{5,4},{6,7},{7,6},{8,9},{9,8},{10,11... | collective-permute-start | bytes 1572872 | tf_op jit(solution)/shard_map/ppermute | solution.py:320
  274.7 26.8 %copy-start.19 = (bf16[2048,1024]{1,0:T(8,128)(2,1)S(1)}, bf16[2048,1024]{1,0:T(8,128)(2,1)}, u32[]{:S(2)}) copy-start(bf16[2048,1024]{1,0:T(8,128)(2,1)} %get-tuple-element.73) | copy-start | bytes 12582916
  282.5 91.8 %collective-permute-start.3 = (bf16[2,2,1,2,64,2048]{5,4,3,2,1,0:T(8,128)(2,1)}, bf16[2,2,1,2,64,2048]{5,4,3,2,1,0:T(8,128)(2,1)}, u32[]{:S(2)}, u32[]{:S(2)}) collective-permute-start(bf16[2,2,1,2,64,2048]{5,4,3,2,1,0:T(8,128)(2,1)} %get-tuple-element.101), channel_id=1, source_target_pairs={{0,2},{1,3},{2,0},{3,1},{4,6},{5,7},{6,4},{7,5},{8,10},{9,11},{10,... | collective-permute-start | bytes 6291464 | tf_op jit(solution)/shard_map/ppermute | solution.py:320
  300.6 39.9 %collective-permute-start.21 = (bf16[2,2,1,1,64,512]{5,4,3,2,1,0:T(8,128)(2,1)}, bf16[2,2,1,1,64,512]{5,4,3,2,1,0:T(8,128)(2,1)S(1)}, u32[]{:S(2)}, u32[]{:S(2)}) collective-permute-start(bf16[2,2,1,1,64,512]{5,4,3,2,1,0:T(8,128)(2,1)} %get-tuple-element.125), channel_id=1, source_target_pairs={{0,2},{1,3},{2,0},{3,1},{4,6},{5,7},{6,4},{7,5},{8,10},{9,11},{10,... | collective-permute-start | bytes 786440 | tf_op jit(solution)/shard_map/ppermute | solution.py:320
  307.9 71.6 %collective-permute-start.1 = (bf16[2,2,2,1,128,1024]{5,4,3,2,1,0:T(8,128)(2,1)}, bf16[2,2,2,1,128,1024]{5,4,3,2,1,0:T(8,128)(2,1)}, u32[]{:S(2)}, u32[]{:S(2)}) collective-permute-start(bf16[2,2,2,1,128,1024]{5,4,3,2,1,0:T(8,128)(2,1)} %get-tuple-element.103), channel_id=1, source_target_pairs={{0,1},{1,0},{2,3},{3,2},{4,5},{5,4},{6,7},{7,6},{8,9},{9,8},{10,11... | collective-permute-start | bytes 6291464 | tf_op jit(solution)/shard_map/ppermute | solution.py:320
  340.5 89.5 %collective-permute-start.22 = (bf16[2,1,1,1,64,512]{5,4,3,2,1,0:T(8,128)(2,1)S(1)}, bf16[2,1,1,1,64,512]{5,4,3,2,1,0:T(8,128)(2,1)S(1)}, u32[]{:S(2)}, u32[]{:S(2)}) collective-permute-start(bf16[2,1,1,1,64,512]{5,4,3,2,1,0:T(8,128)(2,1)S(1)} %get-tuple-element.141), channel_id=1, source_target_pairs={{0,4},{1,5},{2,6},{3,7},{4,0},{5,1},{6,2},{7,3},{8,12},{9,13},{10,... | collective-permute-start | bytes 393224 | tf_op jit(solution)/shard_map/ppermute | solution.py:320
  374.4 5.1 copy-start.17
  378.6 41.3 %collective-permute-start.6 = (bf16[2,2,1,1,64,2048]{5,4,3,2,1,0:T(8,128)(2,1)}, bf16[2,2,1,1,64,2048]{5,4,3,2,1,0:T(8,128)(2,1)}, u32[]{:S(2)}, u32[]{:S(2)}) collective-permute-start(bf16[2,2,1,1,64,2048]{5,4,3,2,1,0:T(8,128)(2,1)} %get-tuple-element.105), channel_id=1, source_target_pairs={{0,1},{1,0},{2,3},{3,2},{4,5},{5,4},{6,7},{7,6},{8,9},{9,8},{10,11... | collective-permute-start | bytes 3145736 | tf_op jit(solution)/shard_map/ppermute | solution.py:320
  383.1 39.5 %collective-permute-start.5 = (bf16[2,2,1,1,128,1024]{5,4,3,2,1,0:T(8,128)(2,1)}, bf16[2,2,1,1,128,1024]{5,4,3,2,1,0:T(8,128)(2,1)}, u32[]{:S(2)}, u32[]{:S(2)}) collective-permute-start(bf16[2,2,1,1,128,1024]{5,4,3,2,1,0:T(8,128)(2,1)} %get-tuple-element.107), channel_id=1, source_target_pairs={{0,2},{1,3},{2,0},{3,1},{4,6},{5,7},{6,4},{7,5},{8,10},{9,11},{10,... | collective-permute-start | bytes 3145736 | tf_op jit(solution)/shard_map/ppermute | solution.py:320
  419.9 2.7 copy-start.20
  425.0 102.2 %all-to-all-start.3 = ((bf16[16,6,64,256]{3,2,1,0:T(8,128)(2,1)}), bf16[16,6,64,256]{3,2,1,0:T(8,128)(2,1)}, u32[]{:S(2)}, u32[]{:S(2)}) async-start(bf16[16,6,64,256]{3,2,1,0:T(8,128)(2,1)} %attend_back1.1), calls=%async_computation.3 | async-start | bytes 6291456 | tf_op jit(solution)/shard_map/all_to_all | solution.py:926
  430.0 73.8 %collective-permute-start.23 = (bf16[1,1,1,1,64,512]{5,4,3,2,1,0:T(8,128)(2,1)S(1)}, bf16[1,1,1,1,64,512]{5,4,3,2,1,0:T(8,128)(2,1)S(1)}, u32[]{:S(2)}, u32[]{:S(2)}) collective-permute-start(bf16[1,1,1,1,64,512]{5,4,3,2,1,0:T(8,128)(2,1)S(1)} %add_convert_fusion.43), channel_id=1, source_target_pairs={{0,8},{1,9},{2,10},{3,11},{4,12},{5,13},{6,14},{7,15},{8,0},{9,1},... | collective-permute-start | bytes 196616 | tf_op jit(solution)/shard_map/ppermute | solution.py:320
  503.8 1.8 collective-permute-start.24
  508.3 6.9 %collective-permute-start.8 = (bf16[16,16,1024]{2,1,0:T(8,128)(2,1)}, bf16[16,16,1024]{2,1,0:T(8,128)(2,1)S(1)}, u32[]{:S(2)}, u32[]{:S(2)}) collective-permute-start(bf16[16,16,1024]{2,1,0:T(8,128)(2,1)} %bitcast.63), channel_id=1, source_target_pairs={{0,16},{16,0},{1,17},{17,1},{2,18},{18,2},{3,19},{19,3},{4,20},{20... | collective-permute-start | bytes 1572872 | tf_op jit(solution)/shard_map/ppermute | solution.py:320
  523.9 15.2 %collective-permute-start.28 = (bf16[2,1,1,1,128,1024]{5,4,3,2,1,0:T(8,128)(2,1)}, bf16[2,1,1,1,128,1024]{5,4,3,2,1,0:T(8,128)(2,1)}, u32[]{:S(2)}, u32[]{:S(2)}) collective-permute-start(bf16[2,1,1,1,128,1024]{5,4,3,2,1,0:T(8,128)(2,1)} %get-tuple-element.117), channel_id=1, source_target_pairs={{0,4},{1,5},{2,6},{3,7},{4,0},{5,1},{6,2},{7,3},{8,12},{9,13},{10,... | collective-permute-start | bytes 1572872 | tf_op jit(solution)/shard_map/ppermute | solution.py:320
  524.5 30.5 %collective-permute-start.25 = (bf16[2,1,1,1,64,2048]{5,4,3,2,1,0:T(8,128)(2,1)}, bf16[2,1,1,1,64,2048]{5,4,3,2,1,0:T(8,128)(2,1)}, u32[]{:S(2)}, u32[]{:S(2)}) collective-permute-start(bf16[2,1,1,1,64,2048]{5,4,3,2,1,0:T(8,128)(2,1)} %get-tuple-element.119), channel_id=1, source_target_pairs={{0,4},{1,5},{2,6},{3,7},{4,0},{5,1},{6,2},{7,3},{8,12},{9,13},{10,... | collective-permute-start | bytes 1572872 | tf_op jit(solution)/shard_map/ppermute | solution.py:320
  540.8 47.0 %collective-permute-start.29 = (bf16[1,1,1,1,128,1024]{5,4,3,2,1,0:T(8,128)(2,1)}, bf16[1,1,1,1,128,1024]{5,4,3,2,1,0:T(8,128)(2,1)S(1)}, u32[]{:S(2)}, u32[]{:S(2)}) collective-permute-start(bf16[1,1,1,1,128,1024]{5,4,3,2,1,0:T(8,128)(2,1)} %add_convert_fusion.23), channel_id=1, source_target_pairs={{0,8},{1,9},{2,10},{3,11},{4,12},{5,13},{6,14},{7,15},{8,0},{9,1},... | collective-permute-start | bytes 786440 | tf_op jit(solution)/shard_map/ppermute | solution.py:320
  556.9 25.8 %collective-permute-start.26 = (bf16[1,1,1,1,64,2048]{5,4,3,2,1,0:T(8,128)(2,1)}, bf16[1,1,1,1,64,2048]{5,4,3,2,1,0:T(8,128)(2,1)}, u32[]{:S(2)}, u32[]{:S(2)}) collective-permute-start(bf16[1,1,1,1,64,2048]{5,4,3,2,1,0:T(8,128)(2,1)} %add_convert_fusion.26), channel_id=1, source_target_pairs={{0,8},{1,9},{2,10},{3,11},{4,12},{5,13},{6,14},{7,15},{8,0},{9,1},... | collective-permute-start | bytes 786440 | tf_op jit(solution)/shard_map/ppermute | solution.py:320
  576.3 27.8 %all-to-all-start.4 = ((bf16[16,16,1024]{2,1,0:T(8,128)(2,1)}), bf16[16,16,1024]{2,1,0:T(8,128)(2,1)S(1)}, u32[]{:S(2)}, u32[]{:S(2)}) async-start(bf16[16,16,1024]{2,1,0:T(8,128)(2,1)} %get-tuple-element.90), calls=%async_computation.4 | async-start | bytes 1048576 | tf_op jit(solution)/shard_map/all_to_all | solution.py:1100
  583.9 5.7 collective-permute-start.27
  584.0 3.8 copy-start.23
  587.3 28.2 %collective-permute-start.10 = (bf16[3,1024,512]{2,1,0:T(8,128)(2,1)}, bf16[3,1024,512]{2,1,0:T(8,128)(2,1)}, u32[]{:S(2)}, u32[]{:S(2)}) collective-permute-start(bf16[3,1024,512]{2,1,0:T(8,128)(2,1)} %get-tuple-element.92), channel_id=1, source_target_pairs={{0,16},{16,0},{1,17},{17,1},{2,18},{18,2},{3,19},{19,3},{4,20},{20... | collective-permute-start | bytes 9437192 | tf_op jit(solution)/shard_map/ppermute | solution.py:320
  589.6 4.2 collective-permute-start.30
  604.8 7.6 %collective-permute-start.9 = (bf16[16,8,1024]{2,1,0:T(8,128)(2,1)}, bf16[16,8,1024]{2,1,0:T(8,128)(2,1)S(1)}, u32[]{:S(2)}, u32[]{:S(2)}) collective-permute-start(bf16[16,8,1024]{2,1,0:T(8,128)(2,1)} %slice.288), channel_id=1, source_target_pairs={{0,16},{16,0},{1,17},{17,1},{2,18},{18,2},{3,19},{19,3},{4,20},{20... | collective-permute-start | bytes 786440 | tf_op jit(solution)/shard_map/ppermute | solution.py:320
  617.6 2.7 copy-start.18
  618.2 19.9 %collective-permute-start.11 = (bf16[3,2,2,2,1,64,256]{6,5,4,3,2,1,0:T(8,128)(2,1)S(1)}, bf16[3,2,2,2,1,64,256]{6,5,4,3,2,1,0:T(8,128)(2,1)S(1)}, u32[]{:S(2)}, u32[]{:S(2)}) collective-permute-start(bf16[3,2,2,2,1,64,256]{6,5,4,3,2,1,0:T(8,128)(2,1)S(1)} %get-tuple-element.111), channel_id=1, source_target_pairs={{0,1},{1,0},{2,3},{3,2},{4,5},{5,4},{6,7},{7,6},{8,9},{9,8},{10,11... | collective-permute-start | bytes 2359304 | tf_op jit(solution)/shard_map/ppermute | solution.py:320
  620.6 19.7 %collective-permute-start.16 = (bf16[3,2,2,1,2,64,256]{6,5,4,3,2,1,0:T(8,128)(2,1)S(1)}, bf16[3,2,2,1,2,64,256]{6,5,4,3,2,1,0:T(8,128)(2,1)S(1)}, u32[]{:S(2)}, u32[]{:S(2)}) collective-permute-start(bf16[3,2,2,1,2,64,256]{6,5,4,3,2,1,0:T(8,128)(2,1)S(1)} %add_convert_fusion.8), channel_id=1, source_target_pairs={{0,2},{1,3},{2,0},{3,1},{4,6},{5,7},{6,4},{7,5},{8,10},{9,11},{10,... | collective-permute-start | bytes 2359304 | tf_op jit(solution)/shard_map/ppermute | solution.py:320
  638.4 3.7 copy-start.25
  638.4 4.8 copy-start.24
  638.4 4.8 copy-start.26
  638.5 10.6 %collective-permute-start.12 = (bf16[3,2,2,1,1,64,256]{6,5,4,3,2,1,0:T(8,128)(2,1)S(1)}, bf16[3,2,2,1,1,64,256]{6,5,4,3,2,1,0:T(8,128)(2,1)S(1)}, u32[]{:S(2)}, u32[]{:S(2)}) collective-permute-start(bf16[3,2,2,1,1,64,256]{6,5,4,3,2,1,0:T(8,128)(2,1)S(1)} %get-tuple-element.123), channel_id=1, source_target_pairs={{0,2},{1,3},{2,0},{3,1},{4,6},{5,7},{6,4},{7,5},{8,10},{9,11},{10,... | collective-permute-start | bytes 1179656 | tf_op jit(solution)/shard_map/ppermute | solution.py:320
  640.6 11.7 %copy-start.27 = (f32[4096]{0:T(1024)S(1)}, f32[4096]{0:T(1024)}, u32[]{:S(2)}) copy-start(f32[4096]{0:T(1024)} %get-tuple-element.216) | copy-start | bytes 49156
  640.6 10.2 %collective-permute-start.17 = (bf16[3,2,2,1,1,64,256]{6,5,0,4,3,2,1:T(8,128)(2,1)S(1)}, bf16[3,2,2,1,1,64,256]{6,5,0,4,3,2,1:T(8,128)(2,1)S(1)}, u32[]{:S(2)}, u32[]{:S(2)}) collective-permute-start(bf16[3,2,2,1,1,64,256]{6,5,0,4,3,2,1:T(8,128)(2,1)S(1)} %get-tuple-element.133), channel_id=1, source_target_pairs={{0,1},{1,0},{2,3},{3,2},{4,5},{5,4},{6,7},{7,6},{8,9},{9,8},{10,11... | collective-permute-start | bytes 1179656 | tf_op jit(solution)/shard_map/ppermute | solution.py:320
  649.2 8.7 %collective-permute-start.13 = (bf16[3,2,1,1,1,64,256]{6,5,4,3,2,1,0:T(8,128)(2,1)S(1)}, bf16[3,2,1,1,1,64,256]{6,5,4,3,2,1,0:T(8,128)(2,1)S(1)}, u32[]{:S(2)}, u32[]{:S(2)}) collective-permute-start(bf16[3,2,1,1,1,64,256]{6,5,4,3,2,1,0:T(8,128)(2,1)S(1)} %get-tuple-element.129), channel_id=1, source_target_pairs={{0,4},{1,5},{2,6},{3,7},{4,0},{5,1},{6,2},{7,3},{8,12},{9,13},{10,... | collective-permute-start | bytes 589832 | tf_op jit(solution)/shard_map/ppermute | solution.py:320
  650.9 9.2 %collective-permute-start.18 = (bf16[3,2,1,1,1,64,256]{6,5,0,4,3,2,1:T(8,128)(2,1)S(1)}, bf16[3,2,1,1,1,64,256]{6,5,0,4,3,2,1:T(8,128)(2,1)S(1)}, u32[]{:S(2)}, u32[]{:S(2)}) collective-permute-start(bf16[3,2,1,1,1,64,256]{6,5,0,4,3,2,1:T(8,128)(2,1)S(1)} %get-tuple-element.131), channel_id=1, source_target_pairs={{0,4},{1,5},{2,6},{3,7},{4,0},{5,1},{6,2},{7,3},{8,12},{9,13},{10,... | collective-permute-start | bytes 589832 | tf_op jit(solution)/shard_map/ppermute | solution.py:320
  658.0 7.6 %collective-permute-start.14 = (bf16[3,1,1,1,1,64,256]{6,5,4,3,2,1,0:T(8,128)(2,1)S(1)}, bf16[3,1,1,1,1,64,256]{6,5,4,3,2,1,0:T(8,128)(2,1)S(1)}, u32[]{:S(2)}, u32[]{:S(2)}) collective-permute-start(bf16[3,1,1,1,1,64,256]{6,5,4,3,2,1,0:T(8,128)(2,1)S(1)} %add_convert_fusion.40), channel_id=1, source_target_pairs={{0,8},{1,9},{2,10},{3,11},{4,12},{5,13},{6,14},{7,15},{8,0},{9,1},... | collective-permute-start | bytes 294920 | tf_op jit(solution)/shard_map/ppermute | solution.py:320
  660.1 7.6 %collective-permute-start.19 = (bf16[3,1,1,1,1,64,256]{6,5,0,4,3,2,1:T(8,128)(2,1)S(1)}, bf16[3,1,1,1,1,64,256]{6,5,0,4,3,2,1:T(8,128)(2,1)S(1)}, u32[]{:S(2)}, u32[]{:S(2)}) collective-permute-start(bf16[3,1,1,1,1,64,256]{6,5,0,4,3,2,1:T(8,128)(2,1)S(1)} %add_convert_fusion.37), channel_id=1, source_target_pairs={{0,8},{1,9},{2,10},{3,11},{4,12},{5,13},{6,14},{7,15},{8,0},{9,1},... | collective-permute-start | bytes 294920 | tf_op jit(solution)/shard_map/ppermute | solution.py:320
  665.6 2.2 collective-permute-start.15
  667.7 1.4 collective-permute-start.20
  (4 other events, 3.2 us)

commit v4 on v3

--- a/solution.py
+++ b/solution.py
@@ -68,7 +68,7 @@
     return whole(jnp.cos), whole(jnp.sin)
 
 
-def walk_frames(frames, per_device, parts, segments_ref, live_ref, list_ref, visit):
+def walk_frames(frames, per_device, segments_ref, live_ref, list_ref, visit):
     def step(source, held):
         for place in range(per_device):
             frame = source * per_device + place
@@ -76,8 +76,7 @@
             fresh = (frame == 0) | (segments_ref[frame] != segments_ref[before])
             held = jnp.where(fresh, 0, held)
             list_ref[held] = frame
-            if place in parts:
-                visit(source, place, frame, held + 1)
+            visit(source, place, frame, held + 1)
             held = held + jnp.where(live_ref[frame] == 1, 1, 0)
         return held
 
@@ -147,7 +146,7 @@
         mix_ref[source, place] = result.astype(BF16)
         lse_ref[pl.ds(frame, 1), :] = top + jnp.log(total)
 
-    walk_frames(frames, per_device, range(per_device), segments_ref, live_ref, list_ref, visit)
+    walk_frames(frames, per_device, segments_ref, live_ref, list_ref, visit)
 
 
 def whole_spec():
@@ -186,8 +185,7 @@
 
 def attend_back_kernel(
     per_device,
-    part,
-    last,
+    orders,
     segments_ref,
     live_ref,
     x_ref,
@@ -199,10 +197,7 @@
     sin_ref,
     *refs
 ):
-    if last:
-        before_ref, d_query_ref, out_ref, dkv_ref, list_ref = refs
-    else:
-        out_ref, dkv_ref, list_ref = refs
+    out_ref, dkv_ref, list_ref = refs[orders:]
     frames = kv_ref.shape[0]
 
     def clear(frame, carry):
@@ -256,63 +251,46 @@
             d_query,
         )
         d_query = unturn(frame, d_query * (HEAD**-0.5)).astype(BF16)
-        if last:
-            out_ref[source, 2 * per_device + part] = d_query
-        else:
-            out_ref[source] = d_query
-
-    walk_frames(frames, per_device, (part,), segments_ref, live_ref, list_ref, visit)
+        out_ref[source, 2 * per_device + place] = d_query
+
+    walk_frames(frames, per_device, segments_ref, live_ref, list_ref, visit)
 
     def finish(source, carry):
         for place in range(per_device):
             frame = source * per_device + place
-            both = (dkv_ref[frame] + before_ref[frame]).T
+            both = dkv_ref[frame].T
             out_ref[source, place] = unturn(frame, both[:HEAD]).astype(BF16)
             out_ref[source, per_device + place] = both[HEAD:].astype(BF16)
-        for place in range(part):
-            out_ref[source, 2 * per_device + place] = d_query_ref[source]
         return carry
 
-    if last:
-        lax.fori_loop(0, frames // per_device, finish, 0)
-
-
-def attend_back(
-    part, per_device, segments, live, x, kv, wide, lse, d_mix, cosine, sine, before
-):
+    lax.fori_loop(0, frames // per_device, finish, 0)
+
+
+def attend_back(per_device, segments, live, x, kv, wide, lse, d_mix, cosine, sine, orders):
     sources = x.shape[0]
     frames = sources * per_device
-    pairs = sources * 6
-    last = part == per_device - 1
+    pairs = frames * 6
+    orders = [each.reshape(-1, each.shape[-1])[:8, :128] for each in orders]
     args = [segments, live, x, kv, wide, lse, d_mix, cosine, sine]
-    dkv = (frames, PATCHES, 2 * HEAD)
-    lists = pltpu.SMEM((frames,), jnp.int32)
-    if last:
-        args += [before[1], before[0]]
-        outs = jax.ShapeDtypeStruct(x.shape, BF16)
-        out_specs = whole_spec()
-        scratch = [pltpu.VMEM(dkv, F32), lists]
-    else:
-        outs = (
-            jax.ShapeDtypeStruct((sources, HEAD, PATCHES), BF16),
-            jax.ShapeDtypeStruct(dkv, F32),
-        )
-        out_specs = (whole_spec(), whole_spec())
-        scratch = [lists]
     return pl.pallas_call(
-        functools.partial(attend_back_kernel, per_device, part, last),
-        out_shape=outs,
-        in_specs=[scalar_spec(), scalar_spec()] + [whole_spec()] * (len(args) - 2),
-        out_specs=out_specs,
-        scratch_shapes=scratch,
+        functools.partial(attend_back_kernel, per_device, len(orders)),
+        out_shape=jax.ShapeDtypeStruct(x.shape, BF16),
+        in_specs=[scalar_spec(), scalar_spec()]
+        + [whole_spec()] * (len(args) - 2)
+        + [pl.BlockSpec(memory_space=pl.ANY)] * len(orders),
+        out_specs=whole_spec(),
+        scratch_shapes=[
+            pltpu.VMEM((frames, PATCHES, 2 * HEAD), F32),
+            pltpu.SMEM((frames,), jnp.int32),
+        ],
         cost_estimate=pl.CostEstimate(
             flops=pairs * 10 * PATCHES * PATCHES * 256,
             bytes_accessed=x.size * 2 * 5,
             transcendentals=pairs * PATCHES * PATCHES,
         ),
         compiler_params=pltpu.CompilerParams(vmem_limit_bytes=60 << 20),
-        name="attend_back%d" % part,
-    )(*args)
+        name="attend_back",
+    )(*args, *orders)
 
 
 def exchange(value, axis, bit):
@@ -352,9 +330,6 @@
         pieces = [lax.dynamic_slice_in_dim(part, which, 1, axis) for part in self.parts]
         return (pieces[0].astype(F32) + pieces[1].astype(F32)).astype(BF16)
 
-    def hold(self, *earlier):
-        self.parts = [after(part, *earlier) for part in self.parts]
-
     def stage(self):
         bit = self.order.pop(0)
         own_bit = lax.rem(lax.div(self.index, bit), 2)
@@ -367,10 +342,17 @@
         while self.order:
             self.stage()
         own = (self.parts[0].astype(F32) + self.parts[1].astype(F32)).astype(BF16)
-        own = own.reshape(self.lead + self.tail)
-        other = exchange(own, "pack", 1)
-        first = lax.axis_index("pack") == 0
-        return jnp.where(first, own, other), jnp.where(first, other, own)
+        return by_pack(own.reshape(self.lead + self.tail))
+
+
+def by_pack(own):
+    other = exchange(own, "pack", 1)
+    first = lax.axis_index("pack") == 0
+    return jnp.where(first, own, other), jnp.where(first, other, own)
+
+
+def scattered(half):
+    return by_pack(lax.psum_scatter(half, "seq", scatter_dimension=0, tiled=True))
 
 
 def row_sum_direct(term):
@@ -996,13 +978,16 @@
     def out_term(start, size):
         return dot_over(attn_mix, columns_of(d_attn_out, start, size), 1, 0).astype(BF16)
 
-    sums = ()
+    sums = []
     if halves:
-        up_sum = RowSum(mine[2], exchange(theirs[2], "pack", 1), (2, 1, 4, 8))
-        down_sum = RowSum(mine[3], exchange(theirs[3], "pack", 1), (1, 2, 4, 8))
-        out_theirs = exchange(out_term((1 - pack) * (width // 2), width // 2), "pack", 1)
-        out_sum = RowSum(out_term(pack * (width // 2), width // 2), out_theirs, (1, 2, 4, 8))
-        sums = (down_sum, up_sum)
+        half = width // 2
+        out_theirs = exchange(out_term((1 - pack) * half, half), "pack", 1)
+        sums = [
+            mine[3] + exchange(theirs[3], "pack", 1),
+            mine[2] + exchange(theirs[2], "pack", 1),
+            out_term(pack * half, half) + out_theirs,
+        ]
+
     def own_share(row):
         piece = row.shape[0] // seq_count
         return lax.dynamic_slice_in_dim(row, seq_index * piece, piece)
@@ -1055,32 +1040,10 @@
     for part in parts:
         early_done += [part[1], part[3]]
 
-    before = None
-    for part in range(per_device):
-        sends = [each.stage() for each in sums]
-        if halves and part:
-            sends.append(out_sum.stage())
-        result = attend_back(
-            part,
-            per_device,
-            clip_ids,
-            live,
-            x,
-            kv,
-            wide,
-            lse,
-            after(d_mix, *sends),
-            cos_all,
-            sin_all,
-            before,
-        )
-        before = result
-    sends = [each.stage() for each in sums]
-    if halves:
-        sends.append(out_sum.stage())
-    back = to_tokens(after(result, *sends))
-    for each in sums:
-        each.hold(back[0, 0, :8])
+    result = attend_back(
+        per_device, clip_ids, live, x, kv, wide, lse, d_mix, cos_all, sin_all, sums
+    )
+    back = to_tokens(result)
     back = after(back, *early_done)
     which = (1 - pack, pack) if halves else (pack * 0, pack * 0 + 1)
     d_in_theirs, qkv_theirs, bias_theirs = unproject(
@@ -1111,13 +1074,13 @@
             RowSum(qkv_mine[..., :split], came[..., :split], (1, 2, 4, 8)),
             RowSum(qkv_mine[..., split:], came[..., split:], (2, 1, 4, 8)),
         ]
-        down_weight_grad = jnp.concatenate(down_sum.finish(), axis=0).astype(F32)
-        even, odd = up_sum.finish()
+        down_weight_grad = jnp.concatenate(scattered(sums[0]), axis=0).astype(F32)
+        even, odd = scattered(sums[1])
         up_weight_grad = jnp.stack(
             [even.reshape(share, -1, small), odd.reshape(share, -1, small)], axis=2
         ).reshape(share, hidden_units)
         up_weight_grad = up_weight_grad.astype(F32)
-        out_weight_grad = jnp.concatenate(out_sum.finish(), axis=1).astype(F32)
+        out_weight_grad = jnp.concatenate(scattered(sums[2]), axis=1).astype(F32)
         done = [each.finish() for each in qkv_sums]
         qkv_weight_grad = jnp.concatenate(
             [done[0][0], done[1][0], done[0][1], done[1][1]], axis=-1

time: 681 us -> 659 us (0.968)
  other arithmetic: 64.2 us -> 46.8 us
  between operations: 6.1 us -> 18.9 us
  local copies, waits for them, and re-layouts: 49 us -> 59.1 us
  starting transfers between devices: 77.2 us -> 67.4 us
  Pallas kernels: 196 us -> 188 us
  waiting for transfers between devices: 253 us -> 245 us
    ppermute x31 -> x19, waiting for transfers between devices: 177 us -> 21.8 us  [exchange(): lax.ppermute(value, axis, [(source, source ^ bit) for source in range(cou...]
    reduce_scatter x0 -> x3, waiting for transfers between devices: none -> 70.4 us  [scattered(): lax.psum_scatter(half, 'seq', scatter_dimension=0, tiled=True)]
    all_to_all x2, waiting for transfers between devices: 23.4 us -> 69 us  [to_tokens(): return lax.all_to_all(array, 'seq', 0, 0, tiled=True)[:heads]]
    ppermute x31 -> x19, starting transfers between devices: 34.9 us -> 5.24 us  [exchange(): lax.ppermute(value, axis, [(source, source ^ bit) for source in range(cou...]
    convert_element_type x21 -> x9, other arithmetic: 35.9 us -> 8.46 us  [pick(): return (pieces[0].astype(F32) + pieces[1].astype(F32)).astype(BF16)]
    all_to_all x2, waiting for transfers between devices: 52.3 us -> 71.2 us  [to_heads(): return lax.all_to_all(array, 'seq', 0, 0, tiled=True)]
    all_to_all x1, starting transfers between devices: 6.41 us -> 22.6 us  [local(): late_rows = lax.all_to_all(late, 'seq', 0, 0, tiled=True)]
    add x0 -> x2, other arithmetic: none -> 15.4 us  [the longest x1 7.77 us: local(): mine[2] + exchange(theirs[2], 'pack', 1)]
  transfers between devices with their start and end apart: 36 -> 27, of which waited for: 17 -> 15; matrix products, arithmetic and copies ran while one was open for 16% -> 16% of each run, Pallas kernels for 17% -> 17%
where the time goes in v4:
time: 659 us; the launch traced here: 653 us
  waiting for transfers between devices  245 us (37%)
  Pallas kernels  188 us (29%)
  starting transfers between devices  67.4 us (10%)
  local copies, waits for them, and re-layouts  59.1 us (9%)
  other arithmetic  46.8 us (7%)
  matrix products  27.9 us (4%)
  between operations  18.9 us (3%)
    all_to_all x2, waiting for transfers between devices, to_heads(): return lax.all_to_all(array, 'seq', 0, 0, tiled=True)  71.2 us
    reduce_scatter x3, waiting for transfers between devices, scattered(): lax.psum_scatter(half, 'seq', scatter_dimension=0, tiled=True)  70.4 us
    all_to_all x2, waiting for transfers between devices, to_tokens(): return lax.all_to_all(array, 'seq', 0, 0, tiled=True)[:heads]  69 us
    pallas_call x1, Pallas kernels, attend_back(): pl.pallas_call(functools.partial(attend_back_kernel, per_device, len(orde...  58.1 us
    pallas_call x1, Pallas kernels, attend(): pl.pallas_call(functools.partial(attend_kernel, per_device), out_shape=ou...  45.2 us
    pallas_call x2, Pallas kernels, feed(): pl.pallas_call(functools.partial(feed_kernel, before is not None), grid_s...  45.2 us
    all_to_all x2, starting transfers between devices, to_tokens(): return lax.all_to_all(array, 'seq', 0, 0, tiled=True)[:heads]  25.5 us
    all_to_all x1, starting transfers between devices, local(): late_rows = lax.all_to_all(late, 'seq', 0, 0, tiled=True)  22.6 us
  transfers between devices with their start and end apart: 27, of which 15 were waited for; matrix products, arithmetic and copies ran while one was open for 16% of the time, Pallas kernels for 17%

profile of v4, /device:TPU:0, one launch (start us, length us, event | category | flops | bytes accessed | tf_op | source)
XLA Modules:
  0.0 653.0 jit_solution(7174719827265786817)
XLA Ops:
  7.2 1.3 fusion.86
  14.9 2.9 fusion.7
  18.4 2.8 copy-done
  21.2 11.4 %project.1 = (bf16[512,1024]{1,0:T(8,128)(2,1)S(1)}, bf16[16,6,64,256]{3,2,1,0:T(8,128)(2,1)S(1)}) custom-call(bf16[512,1024]{1,0:T(8,128)(2,1)S(1)} %bitcast.144, f32[2,1024]{1,0:T(2,128)S(1)} %get-tuple-element.152.shift_ref, f32[2,1024]{1,0:T(2,128)S(1)} %get-tuple-element.151.scale_ref.refs_3_, bf16[1024,3072]{1,0:T(8,128)(2,1)S(1)} %copy-done, ...), custom_call_target="tpu_custom_call" | custom-call | flops 3221225472 | bytes 11534336 | tf_op jit(solution)/shard_map/project/pallas_call | solution.py:432
  32.6 1.6 copy-done.3
  34.2 8.5 %all-to-all-start = ((bf16[16,6,64,256]{3,2,1,0:T(8,128)(2,1)}), bf16[16,6,64,256]{3,2,1,0:T(8,128)(2,1)}, u32[]{:S(2)}, u32[]{:S(2)}) async-start(bf16[16,6,64,256]{3,2,1,0:T(8,128)(2,1)} %copy-done.3), calls=%async_computation | async-start | bytes 6291456 | tf_op jit(solution)/shard_map/all_to_all | solution.py:905
  42.7 4.7 fusion.2
  47.4 1.2 fusion.13.d_out_ref
  51.4 52.3 %all-to-all-done.x_ref = bf16[16,6,64,256]{3,2,1,0:T(8,128)(2,1)} async-done(((bf16[16,6,64,256]{3,2,1,0:T(8,128)(2,1)}), bf16[16,6,64,256]{3,2,1,0:T(8,128)(2,1)}, u32[]{:S(2)}, u32[]{:S(2)}) %all-to-all-start) | async-done | bytes 3145760 | tf_op jit(solution)/shard_map/all_to_all | solution.py:905
  103.7 45.2 %attend.1 = (bf16[16,2,64,256]{3,2,1,0:T(8,128)(2,1)S(1)}, f32[16,2,64,256]{3,2,1,0:T(8,128)S(1)}, f32[32,256]{1,0:T(8,128)S(1)}, bf16[32,256,128]{2,1,0:T(8,128)(2,1)S(1)}) custom-call(s32[32]{0:T(128)S(1)} %bitcast.153, s32[32]{0:T(128)S(1)} %bitcast.155, bf16[16,6,64,256]{3,2,1,0:T(8,128)(2,1)} %all-to-all-done.x_ref), custom_call_target="tpu_custom_call" | custom-call | flops 12884901888 | bytes 9437184 | tf_op jit(solution)/shard_map/attend/pallas_call | solution.py:170
  149.9 1.3 copy-done.12
  151.2 1.3 copy-done.13
  153.1 15.3 %all-to-all-start.1 = ((bf16[16,2,64,256]{3,2,1,0:T(8,128)(2,1)}), bf16[16,2,64,256]{3,2,1,0:T(8,128)(2,1)}, u32[]{:S(2)}, u32[]{:S(2)}) async-start(bf16[16,2,64,256]{3,2,1,0:T(8,128)(2,1)} %copy-done.6), calls=%async_computation.1 | async-start | bytes 2097152 | tf_op jit(solution)/shard_map/all_to_all | solution.py:908
  172.0 18.0 %all-to-all-done.1 = bf16[16,2,64,256]{3,2,1,0:T(8,128)(2,1)} async-done(((bf16[16,2,64,256]{3,2,1,0:T(8,128)(2,1)}), bf16[16,2,64,256]{3,2,1,0:T(8,128)(2,1)}, u32[]{:S(2)}, u32[]{:S(2)}) %all-to-all-start.1) | async-done | bytes 1048608 | tf_op jit(solution)/shard_map/all_to_all | solution.py:908
  190.0 1.4 fusion.76
  195.4 3.2 fusion.10
  198.6 21.9 %feed0.1 = (f32[512,1024]{1,0:T(8,128)}, f32[512,1024]{1,0:T(8,128)}, bf16[1024,2048]{1,0:T(8,128)(2,1)}, bf16[2048,1024]{1,0:T(8,128)(2,1)}, f32[1,2048]{1,0:T(1,128)}) custom-call(s32[1]{0:T(128)} %bitcast.20.which_ref, bf16[512,1024]{1,0:T(8,128)(2,1)} %get-tuple-element.79.in_ref, bf16[512,1024]{1,0:T(8,128)(2,1)} %fusion.13.d_out_ref, ...), custom_call_target="tpu_custom_call" | custom-call | flops 12884901888 | bytes 25165824 | tf_op jit(solution)/shard_map/feed0/pallas_call | solution.py:538
  220.7 23.3 %feed1.1 = (f32[512,1024]{1,0:T(8,128)}, f32[512,1024]{1,0:T(8,128)}, bf16[1024,2048]{1,0:T(8,128)(2,1)}, bf16[2048,1024]{1,0:T(8,128)(2,1)}, f32[1,2048]{1,0:T(1,128)}) custom-call(s32[1]{0:T(128)} %bitcast.which_ref, bf16[512,1024]{1,0:T(8,128)(2,1)} %get-tuple-element.79.in_ref, bf16[512,1024]{1,0:T(8,128)(2,1)} %fusion.13.d_out_ref, ...), custom_call_target="tpu_custom_call" | custom-call | flops 12884901888 | bytes 25165824 | tf_op jit(solution)/shard_map/feed1/pallas_call | solution.py:538
  244.8 8.2 %middle_back.1 = (f32[512,1024]{1,0:T(8,128)S(1)}, bf16[512,1024]{1,0:T(8,128)(2,1)S(1)}, bf16[512,1024]{1,0:T(8,128)(2,1)}, bf16[16,3,64,256]{3,2,1,0:T(8,128)(2,1)S(1)}) custom-call(f32[512,1024]{1,0:T(8,128)} %get-tuple-element.55.d_in_ref, f32[512,1024]{1,0:T(8,128)} %get-tuple-element.80.middle_ref, bf16[512,1024]{1,0:T(8,128)(2,1)S(1)} %bitcast.146, ...), custom_call_target="tpu_custom_call" | custom-call | flops 1073741824 | bytes 12582912 | tf_op jit(solution)/shard_map/middle_back/pallas_call | solution.py:662
  253.0 1.3 copy-done.4
  256.5 1.7 convolution_convert_fusion
  258.7 2.6 collective-permute-done.2
  261.2 3.1 fusion.15
  264.3 5.3 all-to-all-start.2
  269.7 7.8 %add.314 = bf16[1024,2048]{1,0:T(8,128)(2,1)} add(bf16[1024,2048]{1,0:T(8,128)(2,1)} %get-tuple-element.68, bf16[1024,2048]{1,0:T(8,128)(2,1)} %collective-permute-done.1) | non-fusion elementwise | flops 2097152 | bytes 12582912 | tf_op jit(solution)/shard_map/add | solution.py:987
  277.5 1.3 slice.267.refs_2_
  278.7 1.2 slice.266.refs_1_
  280.0 7.6 %add.313 = bf16[2048,1024]{1,0:T(8,128)(2,1)} add(bf16[2048,1024]{1,0:T(8,128)(2,1)} %get-tuple-element.66, bf16[2048,1024]{1,0:T(8,128)(2,1)} %collective-permute-done) | non-fusion elementwise | flops 2097152 | bytes 12582912 | tf_op jit(solution)/shard_map/add | solution.py:986
  287.6 1.2 slice.265.refs_0_
  288.8 18.9 %all-to-all-done.2.d_mix_ref = bf16[16,3,64,256]{3,2,1,0:T(8,128)(2,1)} async-done(((bf16[16,3,64,256]{3,2,1,0:T(8,128)(2,1)}), bf16[16,3,64,256]{3,2,1,0:T(8,128)(2,1)}, u32[]{:S(2)}, u32[]{:S(2)}) %all-to-all-start.2) | async-done | bytes 1572896 | tf_op jit(solution)/shard_map/all_to_all | solution.py:905
  307.7 58.1 %attend_back.1 = bf16[16,6,64,256]{3,2,1,0:T(8,128)(2,1)} custom-call(s32[32]{0:T(128)} %bitcast.152, s32[32]{0:T(128)} %bitcast.154, bf16[16,6,64,256]{3,2,1,0:T(8,128)(2,1)} %all-to-all-done.x_ref, bf16[32,256,128]{2,1,0:T(8,128)(2,1)} %copy-done.13, f32[16,2,64,256]{3,2,1,0:T(8,128)} %copy-done.12, f32[32,256]{1,0:T(8,128)} %copy-done.14, ...), custom_call_target="tpu_custom_call" | custom-call | flops 32212254720 | bytes 15728640 | tf_op jit(solution)/shard_map/attend_back/pallas_call | solution.py:275
  365.8 10.3 %all-to-all-start.3 = ((bf16[16,6,64,256]{3,2,1,0:T(8,128)(2,1)}), bf16[16,6,64,256]{3,2,1,0:T(8,128)(2,1)}, u32[]{:S(2)}, u32[]{:S(2)}) async-start(bf16[16,6,64,256]{3,2,1,0:T(8,128)(2,1)} %attend_back.1), calls=%async_computation.3 | async-start | bytes 6291456 | tf_op jit(solution)/shard_map/all_to_all | solution.py:908
  379.2 2.6 fusion.79
  382.6 1.5 reshape.460
  384.9 1.5 reshape.459
  388.1 1.4 fusion.21
  389.6 1.9 fusion.25
  391.5 1.3 fusion.72
  397.6 1.4 fusion.19
  399.1 1.9 fusion.23
  401.0 1.5 convolution_add_fusion
  402.6 51.1 %all-to-all-done.3.back_ref = bf16[16,6,64,256]{3,2,1,0:T(8,128)(2,1)} async-done(((bf16[16,6,64,256]{3,2,1,0:T(8,128)(2,1)}), bf16[16,6,64,256]{3,2,1,0:T(8,128)(2,1)}, u32[]{:S(2)}, u32[]{:S(2)}) %all-to-all-start.3) | async-done | bytes 3145760 | tf_op jit(solution)/shard_map/all_to_all | solution.py:908
  453.6 8.2 %unproject0.1 = (f32[512,1024]{1,0:T(8,128)S(1)}, bf16[3,1024,512]{2,1,0:T(8,128)(2,1)}, f32[3,1,512]{2,1,0:T(1,128)S(1)}) custom-call(s32[1]{0:T(128)} %bitcast.20.which_ref, bf16[512,1024]{1,0:T(8,128)(2,1)S(1)} %get-tuple-element.46.in_ref, bf16[16,6,64,256]{3,2,1,0:T(8,128)(2,1)} %all-to-all-done.3.back_ref, bf16[1024,3072]{1,0:T(8,128)(2,1)} %wv_ref.5, ...), custom_call_target="tpu_custom_call" | custom-call | flops 3221225472 | bytes 12582912 | tf_op jit(solution)/shard_map/unproject0/pallas_call | solution.py:820
  461.9 11.2 %unproject1.1 = (bf16[3,1024,512]{2,1,0:T(8,128)(2,1)}, bf16[512,1024]{1,0:T(8,128)(2,1)}, bf16[16,16,1024]{2,1,0:T(8,128)(2,1)}) custom-call(s32[1]{0:T(128)} %bitcast.which_ref, bf16[512,1024]{1,0:T(8,128)(2,1)S(1)} %get-tuple-element.46.in_ref, bf16[16,6,64,256]{3,2,1,0:T(8,128)(2,1)} %all-to-all-done.3.back_ref, bf16[1024,3072]{1,0:T(8,128)(2,1)} %wv_ref.5, ...), custom_call_target="tpu_custom_call" | custom-call | flops 3221225472 | bytes 12582912 | tf_op jit(solution)/shard_map/unproject1/pallas_call | solution.py:820
  473.1 22.6 %all-to-all-start.4 = ((bf16[16,16,1024]{2,1,0:T(8,128)(2,1)}), bf16[16,16,1024]{2,1,0:T(8,128)(2,1)S(1)}, u32[]{:S(2)}, u32[]{:S(2)}) async-start(bf16[16,16,1024]{2,1,0:T(8,128)(2,1)} %get-tuple-element.76), calls=%async_computation.4 | async-start | bytes 1048576 | tf_op jit(solution)/shard_map/all_to_all | solution.py:1063
  497.2 3.2 fusion.74
  500.4 12.8 %all-to-all-done.4 = bf16[16,16,1024]{2,1,0:T(8,128)(2,1)S(1)} async-done(((bf16[16,16,1024]{2,1,0:T(8,128)(2,1)}), bf16[16,16,1024]{2,1,0:T(8,128)(2,1)S(1)}, u32[]{:S(2)}, u32[]{:S(2)}) %all-to-all-start.4) | async-done | bytes 524320 | tf_op jit(solution)/shard_map/all_to_all | solution.py:1063
  519.7 1.8 fusion.39
  527.6 1.2 fusion.41
  529.1 1.3 pad_maximum_fusion.1
  530.8 2.1 fusion.75
  533.0 1.5 add_convert_fusion.3
  539.6 70.4 %reduce-scatter.8.cloned.1.call-done = bf16[128,1024]{1,0:T(8,128)(2,1)} async-done(((bf16[2048,1024]{1,0:T(8,128)(2,1)}), bf16[128,1024]{1,0:T(8,128)(2,1)}) %reduce-scatter.8.cloned.1.call-update) | async-done | bytes 262160 | tf_op jit(solution)/shard_map/reduce_scatter | solution.py:355
  610.2 1.2 copy-done.19
  611.7 2.2 add_convert_fusion.7
  613.9 1.2 constant_dynamic-slice_fusion.1
  617.0 1.8 reshape.482
  619.8 4.7 collective-permute-done.7
  624.5 1.2 add_convert_fusion.11
  626.7 1.2 add_convert_fusion.9
  627.9 1.2 collective-permute-start.13
  630.1 4.1 collective-permute-done.8
  634.3 2.0 collective-permute-done.13
  637.4 5.4 collective-permute-done.9
  (257 shorter events, 59.3 us)
Async XLA Ops:
  14.9 3.5 copy-start.1
  14.9 3.5 copy-start.7
  18.4 2.8 copy-start
  32.6 1.6 copy-start.3
  34.2 8.5 %slice-start = ((f32[6144]{0:T(1024)}), f32[4096]{0:T(1024)S(1)}, s32[]{:S(2)}) async-start(f32[6144]{0:T(1024)} %param.23), calls=%async_computation.11 | async-start | bytes 32768 | tf_op jit(solution)/shard_map/slice | solution.py:915
  34.2 69.4 %all-to-all-start = ((bf16[16,6,64,256]{3,2,1,0:T(8,128)(2,1)}), bf16[16,6,64,256]{3,2,1,0:T(8,128)(2,1)}, u32[]{:S(2)}, u32[]{:S(2)}) async-start(bf16[16,6,64,256]{3,2,1,0:T(8,128)(2,1)} %copy-done.3), calls=%async_computation | async-start | bytes 6291456 | tf_op jit(solution)/shard_map/all_to_all | solution.py:905
  42.7 4.7 copy-start.2
  50.1 53.6 %copy-start.10 = (s32[1,32]{1,0:T(1,128)S(1)}, s32[1,32]{1,0:T(1,128)}, u32[]{:S(2)}) copy-start(s32[1,32]{1,0:T(1,128)} %param.19) | copy-start | bytes 388
  50.1 53.6 %copy-start.11 = (s32[1,32]{1,0:T(1,128)S(1)}, s32[1,32]{1,0:T(1,128)}, u32[]{:S(2)}) copy-start(s32[1,32]{1,0:T(1,128)} %param.20) | copy-start | bytes 388
  148.9 1.0 copy-start.6
  149.9 1.3 copy-start.12
  151.2 1.3 copy-start.13
  153.1 15.5 %copy-start.37 = (s32[1,2]{1,0:T(1,128)S(1)}, s32[1,2]{1,0:T(1,128)}, u32[]{:S(2)}) copy-start(s32[1,2]{1,0:T(1,128)} %param.18) | copy-start | bytes 28
  153.1 36.9 %all-to-all-start.1 = ((bf16[16,2,64,256]{3,2,1,0:T(8,128)(2,1)}), bf16[16,2,64,256]{3,2,1,0:T(8,128)(2,1)}, u32[]{:S(2)}, u32[]{:S(2)}) async-start(bf16[16,2,64,256]{3,2,1,0:T(8,128)(2,1)} %copy-done.6), calls=%async_computation.1 | async-start | bytes 2097152 | tf_op jit(solution)/shard_map/all_to_all | solution.py:908
  168.4 224.4 %reduce-scatter.4.cloned.1.call-start = ((), (), s32[]{:S(2)}) async-start(), calls=%async_computation.8 | async-start | bytes 1114112 | tf_op jit(solution)/shard_map/reduce_scatter | solution.py:355
  190.0 1.9 copy-start.15
  191.4 1.2 copy-start.20
  191.5 1.2 copy-start.23
  220.6 49.1 %collective-permute-start.1 = (bf16[1024,2048]{1,0:T(8,128)(2,1)}, bf16[1024,2048]{1,0:T(8,128)(2,1)}, u32[]{:S(2)}, u32[]{:S(2)}) collective-permute-start(bf16[1024,2048]{1,0:T(8,128)(2,1)} %get-tuple-element.69), channel_id=1, source_target_pairs={{0,16},{16,0},{1,17},{17,1},{2,18},{18,2},{3,19},{19,3},{4,20},{20... | collective-permute-start | bytes 12582920 | tf_op jit(solution)/shard_map/ppermute | solution.py:298
  220.6 23.3 %copy-start.36 = (f32[1,2048]{1,0:T(1,128)S(1)}, f32[1,2048]{1,0:T(1,128)}, u32[]{:S(2)}) copy-start(f32[1,2048]{1,0:T(1,128)} %get-tuple-element.58) | copy-start | bytes 24580
  220.6 24.1 %copy-start.8 = (f32[1024]{0:T(1024)S(1)}, f32[1024]{0:T(1024)}, u32[]{:S(2)}) copy-start(f32[1024]{0:T(1024)} %param.31) | copy-start | bytes 12292
  244.8 11.7 %copy-start.21 = (bf16[16,1,64,256]{3,2,1,0:T(8,128)(2,1)S(1)}, bf16[16,1,64,256]{3,2,1,0:T(8,128)(2,1)}, u32[]{:S(2)}) copy-start(bf16[16,1,64,256]{3,2,1,0:T(8,128)(2,1)} %copy-done.20) | copy-start | bytes 1572868
  244.8 11.7 %copy-start.24 = (bf16[16,1,64,256]{3,2,1,0:T(8,128)(2,1)S(1)}, bf16[16,1,64,256]{3,2,1,0:T(8,128)(2,1)}, u32[]{:S(2)}) copy-start(bf16[16,1,64,256]{3,2,1,0:T(8,128)(2,1)} %copy-done.23) | copy-start | bytes 1572868
  253.0 1.3 copy-start.4
  254.4 1.1 copy-start.5
  255.5 1.0 copy-start.9
  255.5 5.7 copy-start.22
  255.5 5.7 copy-start.25
  258.2 3.1 collective-permute-start.2
  258.6 21.4 %collective-permute-start = (bf16[2048,1024]{1,0:T(8,128)(2,1)}, bf16[2048,1024]{1,0:T(8,128)(2,1)}, u32[]{:S(2)}, u32[]{:S(2)}) collective-permute-start(bf16[2048,1024]{1,0:T(8,128)(2,1)} %get-tuple-element.67), channel_id=1, source_target_pairs={{0,16},{16,0},{1,17},{17,1},{2,18},{18,2},{3,19},{19,3},{4,20},{20... | collective-permute-start | bytes 12582920 | tf_op jit(solution)/shard_map/ppermute | solution.py:298
  264.3 43.4 %all-to-all-start.2 = ((bf16[16,3,64,256]{3,2,1,0:T(8,128)(2,1)}), bf16[16,3,64,256]{3,2,1,0:T(8,128)(2,1)}, u32[]{:S(2)}, u32[]{:S(2)}) async-start(bf16[16,3,64,256]{3,2,1,0:T(8,128)(2,1)} %copy-done.5), calls=%async_computation.2 | async-start | bytes 3145728 | tf_op jit(solution)/shard_map/all_to_all | solution.py:905
  269.6 260.7 %reduce-scatter.6.cloned.1.call-start = ((), (), s32[]{:S(2)}) async-start(), calls=%async_computation.9 | async-start | bytes 4456448 | tf_op jit(solution)/shard_map/reduce_scatter | solution.py:355
  365.8 87.8 %all-to-all-start.3 = ((bf16[16,6,64,256]{3,2,1,0:T(8,128)(2,1)}), bf16[16,6,64,256]{3,2,1,0:T(8,128)(2,1)}, u32[]{:S(2)}, u32[]{:S(2)}) async-start(bf16[16,6,64,256]{3,2,1,0:T(8,128)(2,1)} %attend_back.1), calls=%async_computation.3 | async-start | bytes 6291456 | tf_op jit(solution)/shard_map/all_to_all | solution.py:908
  376.1 234.0 %reduce-scatter.8.cloned.1.call-start = ((), (), s32[]{:S(2)}) async-start(), calls=%async_computation.10 | async-start | bytes 4456448 | tf_op jit(solution)/shard_map/reduce_scatter | solution.py:355
  378.2 15.2 %collective-permute-start.3 = (bf16[16,16,1024]{2,1,0:T(8,128)(2,1)}, bf16[16,16,1024]{2,1,0:T(8,128)(2,1)S(1)}, u32[]{:S(2)}, u32[]{:S(2)}) collective-permute-start(bf16[16,16,1024]{2,1,0:T(8,128)(2,1)} %bitcast.53), channel_id=1, source_target_pairs={{0,16},{16,0},{1,17},{17,1},{2,18},{18,2},{3,19},{19,3},{4,20},{20... | collective-permute-start | bytes 1572872 | tf_op jit(solution)/shard_map/ppermute | solution.py:298
  384.9 4.6 copy-start.26
  389.5 4.4 copy-start.29
  392.8 102.9 %collective-permute-start.16 = (bf16[64,512]{1,0:T(8,128)(2,1)}, bf16[64,512]{1,0:T(8,128)(2,1)S(1)}, u32[]{:S(2)}, u32[]{:S(2)}) collective-permute-start(bf16[64,512]{1,0:T(8,128)(2,1)} %reduce-scatter.4.cloned.1.call-done), channel_id=1, source_target_pairs={{0,16},{16,0},{1,17},{17,1},{2,18},{18,2},{3,19},{19,3},{4,20},{20... | collective-permute-start | bytes 196616 | tf_op jit(solution)/shard_map/ppermute | solution.py:298
  461.9 33.9 %copy-start.34 = (bf16[64,512]{1,0:T(8,128)(2,1)S(1)}, bf16[64,512]{1,0:T(8,128)(2,1)}, u32[]{:S(2)}) copy-start(bf16[64,512]{1,0:T(8,128)(2,1)} %reduce-scatter.4.cloned.1.call-done) | copy-start | bytes 196612
  473.1 40.1 %all-to-all-start.4 = ((bf16[16,16,1024]{2,1,0:T(8,128)(2,1)}), bf16[16,16,1024]{2,1,0:T(8,128)(2,1)S(1)}, u32[]{:S(2)}, u32[]{:S(2)}) async-start(bf16[16,16,1024]{2,1,0:T(8,128)(2,1)} %get-tuple-element.76), calls=%async_computation.4 | async-start | bytes 1048576 | tf_op jit(solution)/shard_map/all_to_all | solution.py:1063
  497.2 33.6 %collective-permute-start.5 = (bf16[3,1024,512]{2,1,0:T(8,128)(2,1)}, bf16[3,1024,512]{2,1,0:T(8,128)(2,1)}, u32[]{:S(2)}, u32[]{:S(2)}) collective-permute-start(bf16[3,1024,512]{2,1,0:T(8,128)(2,1)} %get-tuple-element.78), channel_id=1, source_target_pairs={{0,16},{16,0},{1,17},{17,1},{2,18},{18,2},{3,19},{19,3},{4,20},{20... | collective-permute-start | bytes 9437192 | tf_op jit(solution)/shard_map/ppermute | solution.py:298
  500.4 19.2 %copy-start.30 = (f32[32,64]{1,0:T(8,128)S(1)}, f32[32,64]{1,0:T(8,128)}, u32[]{:S(2)}) copy-start(f32[32,64]{1,0:T(8,128)} %copy-done.29) | copy-start | bytes 24580
  513.9 7.8 %collective-permute-start.4 = (bf16[16,8,1024]{2,1,0:T(8,128)(2,1)}, bf16[16,8,1024]{2,1,0:T(8,128)(2,1)S(1)}, u32[]{:S(2)}, u32[]{:S(2)}) collective-permute-start(bf16[16,8,1024]{2,1,0:T(8,128)(2,1)} %slice.298), channel_id=1, source_target_pairs={{0,16},{16,0},{1,17},{17,1},{2,18},{18,2},{3,19},{19,3},{4,20},{20... | collective-permute-start | bytes 786440 | tf_op jit(solution)/shard_map/ppermute | solution.py:298
  530.3 79.8 %collective-permute-start.17 = (bf16[64,2048]{1,0:T(8,128)(2,1)}, bf16[64,2048]{1,0:T(8,128)(2,1)S(1)}, u32[]{:S(2)}, u32[]{:S(2)}) collective-permute-start(bf16[64,2048]{1,0:T(8,128)(2,1)} %reduce-scatter.6.cloned.1.call-done), channel_id=1, source_target_pairs={{0,16},{16,0},{1,17},{17,1},{2,18},{18,2},{3,19},{19,3},{4,20},{20... | collective-permute-start | bytes 786440 | tf_op jit(solution)/shard_map/ppermute | solution.py:298
  532.9 1.6 copy-start.18
  533.0 2.3 copy-start.16
  534.5 3.5 copy-start.33
  534.5 4.2 copy-start.31
  534.5 4.2 copy-start.32
  534.5 75.6 %copy-start.27 = (bf16[64,2048]{1,0:T(8,128)(2,1)S(1)}, bf16[64,2048]{1,0:T(8,128)(2,1)}, u32[]{:S(2)}) copy-start(bf16[64,2048]{1,0:T(8,128)(2,1)} %reduce-scatter.6.cloned.1.call-done) | copy-start | bytes 786436
  534.5 77.3 %collective-permute-start.6 = (bf16[3,2,2,2,1,64,256]{6,5,4,3,2,1,0:T(8,128)(2,1)}, bf16[3,2,2,2,1,64,256]{6,5,4,3,2,1,0:T(8,128)(2,1)}, u32[]{:S(2)}, u32[]{:S(2)}) collective-permute-start(bf16[3,2,2,2,1,64,256]{6,5,4,3,2,1,0:T(8,128)(2,1)} %get-tuple-element.85), channel_id=1, source_target_pairs={{0,1},{1,0},{2,3},{3,2},{4,5},{5,4},{6,7},{7,6},{8,9},{9,8},{10,11... | collective-permute-start | bytes 2359304 | tf_op jit(solution)/shard_map/ppermute | solution.py:298
  535.2 75.0 %copy-start.17 = (bf16[3,1024,256]{2,1,0:T(8,128)(2,1)S(1)}, bf16[3,1024,256]{2,1,0:T(8,128)(2,1)}, u32[]{:S(2)}) copy-start(bf16[3,1024,256]{2,1,0:T(8,128)(2,1)} %get-tuple-element.87) | copy-start | bytes 4718596
  536.4 77.5 %collective-permute-start.11 = (bf16[3,2,2,1,2,64,256]{6,5,4,3,2,1,0:T(8,128)(2,1)}, bf16[3,2,2,1,2,64,256]{6,5,4,3,2,1,0:T(8,128)(2,1)}, u32[]{:S(2)}, u32[]{:S(2)}) collective-permute-start(bf16[3,2,2,1,2,64,256]{6,5,4,3,2,1,0:T(8,128)(2,1)} %add_convert_fusion), channel_id=1, source_target_pairs={{0,2},{1,3},{2,0},{3,1},{4,6},{5,7},{6,4},{7,5},{8,10},{9,11},{10,... | collective-permute-start | bytes 2359304 | tf_op jit(solution)/shard_map/ppermute | solution.py:298
  610.1 1.4 copy-start.19
  610.1 8.8 %collective-permute-start.18 = (bf16[128,1024]{1,0:T(8,128)(2,1)}, bf16[128,1024]{1,0:T(8,128)(2,1)}, u32[]{:S(2)}, u32[]{:S(2)}) collective-permute-start(bf16[128,1024]{1,0:T(8,128)(2,1)} %reduce-scatter.8.cloned.1.call-done), channel_id=1, source_target_pairs={{0,16},{16,0},{1,17},{17,1},{2,18},{18,2},{3,19},{19,3},{4,20},{20... | collective-permute-start | bytes 786440 | tf_op jit(solution)/shard_map/ppermute | solution.py:298
  613.9 10.6 %collective-permute-start.7 = (bf16[3,2,2,1,1,64,256]{6,5,4,3,2,1,0:T(8,128)(2,1)}, bf16[3,2,2,1,1,64,256]{6,5,4,3,2,1,0:T(8,128)(2,1)}, u32[]{:S(2)}, u32[]{:S(2)}) collective-permute-start(bf16[3,2,2,1,1,64,256]{6,5,4,3,2,1,0:T(8,128)(2,1)} %get-tuple-element.91), channel_id=1, source_target_pairs={{0,2},{1,3},{2,0},{3,1},{4,6},{5,7},{6,4},{7,5},{8,10},{9,11},{10,... | collective-permute-start | bytes 1179656 | tf_op jit(solution)/shard_map/ppermute | solution.py:298
  616.1 10.6 %collective-permute-start.12 = (bf16[3,2,2,1,1,64,256]{6,5,0,4,3,2,1:T(8,128)(2,1)}, bf16[3,2,2,1,1,64,256]{6,5,0,4,3,2,1:T(8,128)(2,1)}, u32[]{:S(2)}, u32[]{:S(2)}) collective-permute-start(bf16[3,2,2,1,1,64,256]{6,5,0,4,3,2,1:T(8,128)(2,1)} %get-tuple-element.99), channel_id=1, source_target_pairs={{0,1},{1,0},{2,3},{3,2},{4,5},{5,4},{6,7},{7,6},{8,9},{9,8},{10,11... | collective-permute-start | bytes 1179656 | tf_op jit(solution)/shard_map/ppermute | solution.py:298
  616.2 2.6 copy-start.28
  625.7 8.6 %collective-permute-start.8 = (bf16[3,2,1,1,1,64,256]{6,5,4,3,2,1,0:T(8,128)(2,1)S(1)}, bf16[3,2,1,1,1,64,256]{6,5,4,3,2,1,0:T(8,128)(2,1)S(1)}, u32[]{:S(2)}, u32[]{:S(2)}) collective-permute-start(bf16[3,2,1,1,1,64,256]{6,5,4,3,2,1,0:T(8,128)(2,1)S(1)} %get-tuple-element.95), channel_id=1, source_target_pairs={{0,4},{1,5},{2,6},{3,7},{4,0},{5,1},{6,2},{7,3},{8,12},{9,13},{10,... | collective-permute-start | bytes 589832 | tf_op jit(solution)/shard_map/ppermute | solution.py:298
  627.9 8.4 %collective-permute-start.13 = (bf16[3,2,1,1,1,64,256]{6,5,0,4,3,2,1:T(8,128)(2,1)S(1)}, bf16[3,2,1,1,1,64,256]{6,5,0,4,3,2,1:T(8,128)(2,1)S(1)}, u32[]{:S(2)}, u32[]{:S(2)}) collective-permute-start(bf16[3,2,1,1,1,64,256]{6,5,0,4,3,2,1:T(8,128)(2,1)S(1)} %get-tuple-element.97), channel_id=1, source_target_pairs={{0,4},{1,5},{2,6},{3,7},{4,0},{5,1},{6,2},{7,3},{8,12},{9,13},{10,... | collective-permute-start | bytes 589832 | tf_op jit(solution)/shard_map/ppermute | solution.py:298
  634.3 8.5 %collective-permute-start.9 = (bf16[3,1,1,1,1,64,256]{6,5,4,3,2,1,0:T(8,128)(2,1)S(1)}, bf16[3,1,1,1,1,64,256]{6,5,4,3,2,1,0:T(8,128)(2,1)S(1)}, u32[]{:S(2)}, u32[]{:S(2)}) collective-permute-start(bf16[3,1,1,1,1,64,256]{6,5,4,3,2,1,0:T(8,128)(2,1)S(1)} %add_convert_fusion.16), channel_id=1, source_target_pairs={{0,8},{1,9},{2,10},{3,11},{4,12},{5,13},{6,14},{7,15},{8,0},{9,1},... | collective-permute-start | bytes 294920 | tf_op jit(solution)/shard_map/ppermute | solution.py:298
  636.4 7.5 %collective-permute-start.14 = (bf16[3,1,1,1,1,64,256]{6,5,0,4,3,2,1:T(8,128)(2,1)S(1)}, bf16[3,1,1,1,1,64,256]{6,5,0,4,3,2,1:T(8,128)(2,1)S(1)}, u32[]{:S(2)}, u32[]{:S(2)}) collective-permute-start(bf16[3,1,1,1,1,64,256]{6,5,0,4,3,2,1:T(8,128)(2,1)S(1)} %add_convert_fusion.13), channel_id=1, source_target_pairs={{0,8},{1,9},{2,10},{3,11},{4,12},{5,13},{6,14},{7,15},{8,0},{9,1},... | collective-permute-start | bytes 294920 | tf_op jit(solution)/shard_map/ppermute | solution.py:298
  642.8 1.4 collective-permute-start.10
  643.9 1.4 collective-permute-start.15
  (2 other events, 1.3 us)
Sparse Core Ops, SparseCore 0:
  264.5 87.5 reduce-scatter.3
  354.3 137.7 reduce-scatter.5
  494.4 115.5 reduce-scatter.7

commit v5 on v3

--- a/solution.py
+++ b/solution.py
@@ -150,6 +150,14 @@
     walk_frames(frames, per_device, range(per_device), segments_ref, live_ref, list_ref, visit)
 
 
+def corners(values):
+    return [each.reshape(-1, each.shape[-1])[:1, :128] for each in values]
+
+
+def unread_spec():
+    return pl.BlockSpec(memory_space=pl.ANY)
+
+
 def whole_spec():
     return pl.BlockSpec(memory_space=pltpu.VMEM)
 
@@ -200,9 +208,8 @@
     *refs
 ):
     if last:
-        before_ref, d_query_ref, out_ref, dkv_ref, list_ref = refs
-    else:
-        out_ref, dkv_ref, list_ref = refs
+        before_ref, d_query_ref = refs[:2]
+    out_ref, dkv_ref, list_ref = refs[-3:]
     frames = kv_ref.shape[0]
 
     def clear(frame, carry):
@@ -278,7 +285,7 @@
 
 
 def attend_back(
-    part, per_device, segments, live, x, kv, wide, lse, d_mix, cosine, sine, before
+    part, per_device, segments, live, x, kv, wide, lse, d_mix, cosine, sine, before, orders
 ):
     sources = x.shape[0]
     frames = sources * per_device
@@ -299,10 +306,12 @@
         )
         out_specs = (whole_spec(), whole_spec())
         scratch = [lists]
+    specs = [scalar_spec(), scalar_spec()] + [whole_spec()] * (len(args) - 2)
+    orders = corners(orders)
     return pl.pallas_call(
         functools.partial(attend_back_kernel, per_device, part, last),
         out_shape=outs,
-        in_specs=[scalar_spec(), scalar_spec()] + [whole_spec()] * (len(args) - 2),
+        in_specs=specs + [unread_spec()] * len(orders),
         out_specs=out_specs,
         scratch_shapes=scratch,
         cost_estimate=pl.CostEstimate(
@@ -312,7 +321,7 @@
         ),
         compiler_params=pltpu.CompilerParams(vmem_limit_bytes=60 << 20),
         name="attend_back%d" % part,
-    )(*args)
+    )(*args, *orders)
 
 
 def exchange(value, axis, bit):
@@ -352,9 +361,6 @@
         pieces = [lax.dynamic_slice_in_dim(part, which, 1, axis) for part in self.parts]
         return (pieces[0].astype(F32) + pieces[1].astype(F32)).astype(BF16)
 
-    def hold(self, *earlier):
-        self.parts = [after(part, *earlier) for part in self.parts]
-
     def stage(self):
         bit = self.order.pop(0)
         own_bit = lax.rem(lax.div(self.index, bit), 2)
@@ -363,14 +369,62 @@
         self.parts = [self.pick(bit, own_bit), came]
         return send
 
+    def tie(self, value):
+        value, *self.parts = lax.optimization_barrier((value, *self.parts))
+        return value
+
     def finish(self):
         while self.order:
             self.stage()
         own = (self.parts[0].astype(F32) + self.parts[1].astype(F32)).astype(BF16)
         own = own.reshape(self.lead + self.tail)
-        other = exchange(own, "pack", 1)
-        first = lax.axis_index("pack") == 0
-        return jnp.where(first, own, other), jnp.where(first, other, own)
+        return own, exchange(own, "pack", 1)
+
+
+def settle_kernel(pack_ref, *refs):
+    ups, downs, outs, firsts, seconds = [refs[2 * nth : 2 * nth + 2] for nth in range(5)]
+    up_ref, down_ref, out_ref, qkv_ref = refs[10:]
+    own_first = pack_ref[0] == 0
+    small = 128
+
+    def of_pack(pack, pair, *index):
+        one, two = pair[0][index].astype(F32), pair[1][index].astype(F32)
+        return jnp.where(own_first, one, two) if pack == 0 else jnp.where(own_first, two, one)
+
+    every = slice(None)
+    for pack in range(2):
+        for group in range(ups[0].shape[1] // small):
+            at = (2 * group + pack) * small
+            columns = slice(group * small, (group + 1) * small)
+            up_ref[:, at : at + small] = of_pack(pack, ups, every, columns)
+        rows = downs[0].shape[0]
+        down_ref[pack * rows : (pack + 1) * rows, :] = of_pack(pack, downs, every, every)
+        columns = outs[0].shape[1]
+        out_ref[:, pack * columns : (pack + 1) * columns] = of_pack(pack, outs, every, every)
+        for kind in range(3):
+            for nth, pair in enumerate((firsts, seconds)):
+                columns = pair[0].shape[2]
+                at = (4 * kind + 2 * pack + nth) * columns
+                qkv_ref[:, at : at + columns] = of_pack(pack, pair, kind, every, every)
+
+
+def settle(pack, *pairs):
+    up, down, out, qkv = pairs[0][0], pairs[1][0], pairs[2][0], pairs[3][0]
+    shapes = (
+        (up.shape[0], 2 * up.shape[1]),
+        (2 * down.shape[0], down.shape[1]),
+        (out.shape[0], 2 * out.shape[1]),
+        (qkv.shape[1], 12 * qkv.shape[2]),
+    )
+    args = [each for pair in pairs for each in pair]
+    return pl.pallas_call(
+        settle_kernel,
+        out_shape=tuple(jax.ShapeDtypeStruct(shape, F32) for shape in shapes),
+        in_specs=[scalar_spec()] + [whole_spec()] * len(args),
+        out_specs=(whole_spec(),) * 4,
+        compiler_params=pltpu.CompilerParams(vmem_limit_bytes=32 << 20),
+        name="settle",
+    )(pack.reshape(1), *args)
 
 
 def row_sum_direct(term):
@@ -719,6 +773,8 @@
 def unproject_kernel(
     per_device, carried, which_ref, in_ref, back_ref, wq_ref, wk_ref, wv_ref, *refs
 ):
+    if not carried:
+        refs = refs[-4:]
     if carried:
         before_ref, hidden_ref, d_middle_ref, scale_ref, bias_theirs_ref = refs[:5]
         d_weight_ref, grad_ref, rows_ref, d_in_ref, d_bias_ref, turned_ref = refs[5:]
@@ -789,7 +845,7 @@
                 rows_ref[target] = late
 
 
-def unproject(per_device, targets, which, attn_in, back, weight, before=None, norm_args=()):
+def unproject(per_device, targets, which, attn_in, back, weight, orders, before=None, norm_args=()):
     tokens, width = attn_in.shape
     heads = width // HEAD
     group = 2
@@ -835,6 +891,9 @@
     else:
         outs = (jax.ShapeDtypeStruct((tokens, width), F32),) + weight_shape
         out_specs = (whole((tokens, width)),) + weight_specs
+        orders = corners(orders)
+        args += orders
+        specs += [unread_spec()] * len(orders)
     return pl.pallas_call(
         functools.partial(unproject_kernel, per_device, before is not None),
         grid_spec=pltpu.PrefetchScalarGridSpec(
@@ -1051,16 +1110,13 @@
         )
     mod_grad_early = functools.reduce(jnp.add, [each[4] for each in parts])
     mod_sum_early = (early_sum[:4] + early_sum[4:8]).reshape(4 * width)
-    early_done = [mod_grad_early, mod_sum_early, out_bias_grad, down_bias_grad, up_bias_grad]
-    for part in parts:
-        early_done += [part[1], part[3]]
-
     before = None
     for part in range(per_device):
-        sends = [each.stage() for each in sums]
+        orders = [each.stage() for each in sums]
         if halves and part:
-            sends.append(out_sum.stage())
-        result = attend_back(
+            before = (out_sum.tie(before[0]), before[1])
+            orders.append(out_sum.stage())
+        before = attend_back(
             part,
             per_device,
             clip_ids,
@@ -1069,22 +1125,21 @@
             kv,
             wide,
             lse,
-            after(d_mix, *sends),
+            d_mix,
             cos_all,
             sin_all,
             before,
-        )
-        before = result
-    sends = [each.stage() for each in sums]
+            orders,
+        )
+    back = to_tokens(before)
+    orders = [each.stage() for each in sums]
     if halves:
-        sends.append(out_sum.stage())
-    back = to_tokens(after(result, *sends))
-    for each in sums:
-        each.hold(back[0, 0, :8])
-    back = after(back, *early_done)
+        orders.append(out_sum.stage())
+        orders.append(out_sum.stage())
+    orders += [mod_grad_early] + [part[3] for part in parts]
     which = (1 - pack, pack) if halves else (pack * 0, pack * 0 + 1)
     d_in_theirs, qkv_theirs, bias_theirs = unproject(
-        per_device, seq_count, which[0], attn_in, back, qkv_weight
+        per_device, seq_count, which[0], attn_in, back, qkv_weight, orders
     )
     qkv_mine, hidden_grad, late = unproject(
         per_device,
@@ -1093,10 +1148,14 @@
         attn_in,
         back,
         qkv_weight,
+        (),
         d_in_theirs,
         (hidden[0], d_middle, attn_scale, bias_theirs),
     )
     hidden_grad = hidden_grad.reshape(1, tokens, width)
+    if halves:
+        for each in (up_sum, down_sum, out_sum):
+            late = each.tie(late)
     late_rows = lax.all_to_all(late, "seq", 0, 0, tiled=True)
 
     def halves_in_order(own, other):
@@ -1111,18 +1170,9 @@
             RowSum(qkv_mine[..., :split], came[..., :split], (1, 2, 4, 8)),
             RowSum(qkv_mine[..., split:], came[..., split:], (2, 1, 4, 8)),
         ]
-        down_weight_grad = jnp.concatenate(down_sum.finish(), axis=0).astype(F32)
-        even, odd = up_sum.finish()
-        up_weight_grad = jnp.stack(
-            [even.reshape(share, -1, small), odd.reshape(share, -1, small)], axis=2
-        ).reshape(share, hidden_units)
-        up_weight_grad = up_weight_grad.astype(F32)
-        out_weight_grad = jnp.concatenate(out_sum.finish(), axis=1).astype(F32)
-        done = [each.finish() for each in qkv_sums]
-        qkv_weight_grad = jnp.concatenate(
-            [done[0][0], done[1][0], done[0][1], done[1][1]], axis=-1
-        )
-        qkv_weight_grad = qkv_weight_grad.transpose(1, 0, 2).reshape(share, 3 * width).astype(F32)
+        up_weight_grad, down_weight_grad, out_weight_grad, qkv_weight_grad = settle(
+            pack, *[each.finish() for each in (up_sum, down_sum, out_sum, *qkv_sums)]
+        )
     else:
         up_weight_grad = row_sum_direct(in_order(mine[2], theirs[2]))
         pairs = [each[3].reshape(-1, small, width) for each in (mine, theirs)]

time: 681 us -> 599 us (0.88)
  waiting for transfers between devices: 253 us -> 194 us
  other arithmetic: 64.2 us -> 50.2 us
    ppermute x31, waiting for transfers between devices: 177 us -> 111 us  [exchange(): lax.ppermute(value, axis, [(source, source ^ bit) for source in range(cou...]
    all_to_all x2, waiting for transfers between devices: 52.3 us -> 63 us  [to_heads(): return lax.all_to_all(array, 'seq', 0, 0, tiled=True)]
    convert_element_type x21 -> x22, other arithmetic: 35.9 us -> 33.4 us  [pick(): return (pieces[0].astype(F32) + pieces[1].astype(F32)).astype(BF16)]
    unnamed x70 -> x106, local copies, waits for them, and re-layouts: 13.9 us -> 15.5 us
  transfers between devices with their start and end apart: 36 -> 36, of which waited for: 17 -> 19; matrix products, arithmetic and copies ran while one was open for 16% -> 15% of each run, Pallas kernels for 17% -> 13%
where the time goes in v5:
time: 599 us; the launch traced here: 590 us
  waiting for transfers between devices  194 us (32%)
  Pallas kernels  192 us (32%)
  starting transfers between devices  76.9 us (13%)
  other arithmetic  50.2 us (8%)
  local copies, waits for them, and re-layouts  47.7 us (8%)
  matrix products  23.1 us (4%)
  between operations  6.13 us (1%)
    ppermute x31, waiting for transfers between devices, exchange(): lax.ppermute(value, axis, [(source, source ^ bit) for source in range(cou...  111 us
    pallas_call x2, Pallas kernels, attend_back(): pl.pallas_call(functools.partial(attend_back_kernel, per_device, part, la...  63.4 us
    all_to_all x2, waiting for transfers between devices, to_heads(): return lax.all_to_all(array, 'seq', 0, 0, tiled=True)  63 us
    pallas_call x2, Pallas kernels, feed(): pl.pallas_call(functools.partial(feed_kernel, before is not None), grid_s...  45.2 us
    pallas_call x1, Pallas kernels, attend(): pl.pallas_call(functools.partial(attend_kernel, per_device), out_shape=ou...  43 us
    convert_element_type x22, other arithmetic, pick(): return (pieces[0].astype(F32) + pieces[1].astype(F32)).astype(BF16)  33.4 us
    ppermute x31, starting transfers between devices, exchange(): lax.ppermute(value, axis, [(source, source ^ bit) for source in range(cou...  33.2 us
    all_to_all x2, starting transfers between devices, to_tokens(): return lax.all_to_all(array, 'seq', 0, 0, tiled=True)[:heads]  22.5 us
  transfers between devices with their start and end apart: 36, of which 19 were waited for; matrix products, arithmetic and copies ran while one was open for 15% of the time, Pallas kernels for 13%

profile of v5, /device:TPU:0, one launch (start us, length us, event | category | flops | bytes accessed | tf_op | source)
XLA Modules:
  0.0 590.2 jit_solution(1122874693111932206)
XLA Ops:
  7.5 2.9 fusion.7
  11.2 2.8 copy-done
  14.0 11.4 %project.1 = (bf16[512,1024]{1,0:T(8,128)(2,1)S(1)}, bf16[16,6,64,256]{3,2,1,0:T(8,128)(2,1)S(1)}) custom-call(bf16[512,1024]{1,0:T(8,128)(2,1)S(1)} %bitcast.149, f32[2,1024]{1,0:T(2,128)S(1)} %get-tuple-element.198.shift_ref, f32[2,1024]{1,0:T(2,128)S(1)} %get-tuple-element.197.scale_ref.refs_3_, bf16[1024,3072]{1,0:T(8,128)(2,1)S(1)} %copy-done, ...), custom_call_target="tpu_custom_call" | custom-call | flops 3221225472 | bytes 11534336 | tf_op jit(solution)/shard_map/project/pallas_call | solution.py:504
  25.4 1.6 copy-done.3
  27.0 8.5 %all-to-all-start = ((bf16[16,6,64,256]{3,2,1,0:T(8,128)(2,1)}), bf16[16,6,64,256]{3,2,1,0:T(8,128)(2,1)}, u32[]{:S(2)}, u32[]{:S(2)}) async-start(bf16[16,6,64,256]{3,2,1,0:T(8,128)(2,1)} %copy-done.3), calls=%async_computation | async-start | bytes 6291456 | tf_op jit(solution)/shard_map/all_to_all | solution.py:982
  35.6 4.7 fusion.2
  44.2 52.2 %all-to-all-done.x_ref = bf16[16,6,64,256]{3,2,1,0:T(8,128)(2,1)} async-done(((bf16[16,6,64,256]{3,2,1,0:T(8,128)(2,1)}), bf16[16,6,64,256]{3,2,1,0:T(8,128)(2,1)}, u32[]{:S(2)}, u32[]{:S(2)}) %all-to-all-start) | async-done | bytes 3145760 | tf_op jit(solution)/shard_map/all_to_all | solution.py:982
  96.5 43.0 %attend.1 = (bf16[16,2,64,256]{3,2,1,0:T(8,128)(2,1)S(1)}, f32[16,2,64,256]{3,2,1,0:T(8,128)S(1)}, f32[32,256]{1,0:T(8,128)S(1)}, bf16[32,256,128]{2,1,0:T(8,128)(2,1)S(1)}) custom-call(s32[32]{0:T(128)S(1)} %bitcast.159, s32[32]{0:T(128)S(1)} %bitcast.162, bf16[16,6,64,256]{3,2,1,0:T(8,128)(2,1)} %all-to-all-done.x_ref), custom_call_target="tpu_custom_call" | custom-call | flops 12884901888 | bytes 9437184 | tf_op jit(solution)/shard_map/attend/pallas_call | solution.py:179
  143.6 15.6 %all-to-all-start.1 = ((bf16[16,2,64,256]{3,2,1,0:T(8,128)(2,1)}), bf16[16,2,64,256]{3,2,1,0:T(8,128)(2,1)}, u32[]{:S(2)}, u32[]{:S(2)}) async-start(bf16[16,2,64,256]{3,2,1,0:T(8,128)(2,1)} %copy-done.6), calls=%async_computation.1 | async-start | bytes 2097152 | tf_op jit(solution)/shard_map/all_to_all | solution.py:985
  163.2 19.5 %all-to-all-done.1 = bf16[16,2,64,256]{3,2,1,0:T(8,128)(2,1)} async-done(((bf16[16,2,64,256]{3,2,1,0:T(8,128)(2,1)}), bf16[16,2,64,256]{3,2,1,0:T(8,128)(2,1)}, u32[]{:S(2)}, u32[]{:S(2)}) %all-to-all-start.1) | async-done | bytes 1048608 | tf_op jit(solution)/shard_map/all_to_all | solution.py:985
  188.1 3.2 fusion.10
  191.3 21.9 %feed0.1 = (f32[512,1024]{1,0:T(8,128)}, f32[512,1024]{1,0:T(8,128)}, bf16[1024,2048]{1,0:T(8,128)(2,1)}, bf16[2048,1024]{1,0:T(8,128)(2,1)}, f32[1,2048]{1,0:T(1,128)}) custom-call(s32[1]{0:T(128)} %bitcast.20.which_ref, bf16[512,1024]{1,0:T(8,128)(2,1)} %get-tuple-element.113.in_ref, bf16[512,1024]{1,0:T(8,128)(2,1)} %fusion.13.d_out_ref, ...), custom_call_target="tpu_custom_call" | custom-call | flops 12884901888 | bytes 25165824 | tf_op jit(solution)/shard_map/feed0/pallas_call | solution.py:610
  213.2 2.3 collective-permute-start.1
  215.6 23.3 %feed1.1 = (f32[512,1024]{1,0:T(8,128)}, f32[512,1024]{1,0:T(8,128)}, bf16[1024,2048]{1,0:T(8,128)(2,1)}, bf16[2048,1024]{1,0:T(8,128)(2,1)}, f32[1,2048]{1,0:T(1,128)}) custom-call(s32[1]{0:T(128)} %bitcast.which_ref.pack_ref, bf16[512,1024]{1,0:T(8,128)(2,1)} %get-tuple-element.113.in_ref, bf16[512,1024]{1,0:T(8,128)(2,1)} %fusion.13.d_out_ref, ...), custom_call_target="tpu_custom_call" | custom-call | flops 12884901888 | bytes 25165824 | tf_op jit(solution)/shard_map/feed1/pallas_call | solution.py:610
  239.7 8.1 %middle_back.1 = (f32[512,1024]{1,0:T(8,128)S(1)}, bf16[512,1024]{1,0:T(8,128)(2,1)S(1)}, bf16[512,1024]{1,0:T(8,128)(2,1)}, bf16[16,3,64,256]{3,2,1,0:T(8,128)(2,1)S(1)}) custom-call(f32[512,1024]{1,0:T(8,128)} %get-tuple-element.72.d_in_ref, f32[512,1024]{1,0:T(8,128)} %get-tuple-element.114.middle_ref, bf16[512,1024]{1,0:T(8,128)(2,1)S(1)} %bitcast.151, ...), custom_call_target="tpu_custom_call" | custom-call | flops 1073741824 | bytes 12582912 | tf_op jit(solution)/shard_map/middle_back/pallas_call | solution.py:734
  251.3 6.8 %all-to-all-start.2 = ((bf16[16,3,64,256]{3,2,1,0:T(8,128)(2,1)}), bf16[16,3,64,256]{3,2,1,0:T(8,128)(2,1)}, u32[]{:S(2)}, u32[]{:S(2)}) async-start(bf16[16,3,64,256]{3,2,1,0:T(8,128)(2,1)} %copy-done.5), calls=%async_computation.2 | async-start | bytes 3145728 | tf_op jit(solution)/shard_map/all_to_all | solution.py:982
  258.1 7.9 %add_convert_fusion = (bf16[2,2,1,2,64,2048]{5,4,3,2,1,0:T(8,128)(2,1)}, bf16[2,2,1,2,64,2048]{5,4,3,2,1,0:T(8,128)(2,1)}) fusion(bf16[2,2,2,2,64,2048]{5,4,3,2,1,0:T(8,128)(2,1)} %bitcast.36, s32[]{:T(128)S(6)} %select_n.97, bf16[2,2,2,2,64,2048]{5,4,3,2,1,0:T(8,128)(2,1)} %bitcast.174, s32[]{:T(128)S(6)} %select_n.93), kind=kLoop, calls=%fused_computation.4 | loop fusion | flops 8388608 | bytes 12582920 | tf_op jit(solution)/shard_map/convert_element_type | solution.py:362
  266.0 2.0 collective-permute-start.4
  268.0 6.5 %add_convert_fusion.1 = (bf16[2,2,2,1,128,1024]{5,4,3,2,1,0:T(8,128)(2,1)}, bf16[2,2,2,1,128,1024]{5,4,3,2,1,0:T(8,128)(2,1)}) fusion(bf16[2,2,2,2,128,1024]{5,4,3,2,1,0:T(8,128)(2,1)} %bitcast.33, s32[]{:T(128)S(6)} %select_n.96, bf16[2,2,2,2,128,1024]{5,4,3,2,1,0:T(8,128)(2,1)S(1)} %bitcast.173, s32[]{:T(128)S(6)} %select_n.92), kind=kLoop, calls=%fused_computation.5 | loop fusion | flops 8388608 | bytes 12582920 | tf_op jit(solution)/shard_map/convert_element_type | solution.py:362
  274.6 1.5 collective-permute-start.3
  276.0 1.7 convolution_convert_fusion
  277.7 1.7 convolution_convert_fusion.1
  281.8 10.7 %all-to-all-done.2.d_mix_ref = bf16[16,3,64,256]{3,2,1,0:T(8,128)(2,1)} async-done(((bf16[16,3,64,256]{3,2,1,0:T(8,128)(2,1)}), bf16[16,3,64,256]{3,2,1,0:T(8,128)(2,1)}, u32[]{:S(2)}, u32[]{:S(2)}) %all-to-all-start.2) | async-done | bytes 1572896 | tf_op jit(solution)/shard_map/all_to_all | solution.py:982
  292.5 28.3 %attend_back0.1 = (bf16[16,64,256]{2,1,0:T(8,128)(2,1)}, f32[32,256,128]{2,1,0:T(8,128)}) custom-call(s32[32]{0:T(128)} %bitcast.156, s32[32]{0:T(128)} %bitcast.160, bf16[16,6,64,256]{3,2,1,0:T(8,128)(2,1)} %all-to-all-done.x_ref, bf16[32,256,128]{2,1,0:T(8,128)(2,1)} %copy-done.14, f32[16,2,64,256]{3,2,1,0:T(8,128)} %copy-done.13, f32[32,256]{1,0:T(8,128)} %copy-done.15, ...), custom_call_target="tpu_custom_call" | custom-call | flops 16106127360 | bytes 15728640 | tf_op jit(solution)/shard_map/attend_back0/pallas_call | solution.py:311
  320.8 2.5 add_convert_fusion.14
  324.0 3.2 add_convert_fusion.4
  327.8 4.3 collective-permute-done.3
  332.2 3.1 add_convert_fusion.5
  336.8 35.1 %attend_back1.1 = bf16[16,6,64,256]{3,2,1,0:T(8,128)(2,1)} custom-call(s32[32]{0:T(128)} %bitcast.157, s32[32]{0:T(128)} %bitcast.161, bf16[16,6,64,256]{3,2,1,0:T(8,128)(2,1)} %all-to-all-done.x_ref, bf16[32,256,128]{2,1,0:T(8,128)(2,1)} %copy-done.14, f32[16,2,64,256]{3,2,1,0:T(8,128)} %copy-done.13, f32[32,256]{1,0:T(8,128)} %copy-done.15, ...), custom_call_target="tpu_custom_call" | custom-call | flops 16106127360 | bytes 15728640 | tf_op jit(solution)/shard_map/attend_back1/pallas_call | solution.py:311
  371.8 6.9 %all-to-all-start.3 = ((bf16[16,6,64,256]{3,2,1,0:T(8,128)(2,1)}), bf16[16,6,64,256]{3,2,1,0:T(8,128)(2,1)}, u32[]{:S(2)}, u32[]{:S(2)}) async-start(bf16[16,6,64,256]{3,2,1,0:T(8,128)(2,1)} %attend_back1.1), calls=%async_computation.3 | async-start | bytes 6291456 | tf_op jit(solution)/shard_map/all_to_all | solution.py:985
  383.2 2.6 fusion.81
  389.7 1.4 fusion.20
  391.2 1.6 fusion.18
  394.1 1.8 collective-permute-start.7
  397.5 1.8 collective-permute-start.5
  399.4 26.4 %collective-permute-done.7 = bf16[2,2,2,1,64,512]{5,4,3,2,1,0:T(8,128)(2,1)S(1)} collective-permute-done((bf16[2,2,2,1,64,512]{5,4,3,2,1,0:T(8,128)(2,1)S(1)}, bf16[2,2,2,1,64,512]{5,4,3,2,1,0:T(8,128)(2,1)S(1)}, u32[]{:S(2)}, u32[]{:S(2)}) %collective-permute-start.7) | collective-permute-done | bytes 524320 | tf_op jit(solution)/shard_map/ppermute | solution.py:329
  425.9 1.8 collective-permute-start.8
  429.1 18.0 %collective-permute-done.8 = bf16[2,2,1,1,64,512]{5,4,3,2,1,0:T(8,128)(2,1)S(1)} collective-permute-done((bf16[2,2,1,1,64,512]{5,4,3,2,1,0:T(8,128)(2,1)S(1)}, bf16[2,2,1,1,64,512]{5,4,3,2,1,0:T(8,128)(2,1)S(1)}, u32[]{:S(2)}, u32[]{:S(2)}) %collective-permute-start.8) | collective-permute-done | bytes 262176 | tf_op jit(solution)/shard_map/ppermute | solution.py:329
  447.8 3.3 collective-permute-start.12
  451.8 4.0 collective-permute-done.6
  455.7 1.4 add_convert_fusion.13
  457.2 1.7 collective-permute-start.10
  462.0 8.2 %unproject0.1 = (f32[512,1024]{1,0:T(8,128)S(1)}, bf16[3,1024,512]{2,1,0:T(8,128)(2,1)}, f32[3,1,512]{2,1,0:T(1,128)S(1)}) custom-call(s32[1]{0:T(128)} %bitcast.20.which_ref, bf16[512,1024]{1,0:T(8,128)(2,1)S(1)} %get-tuple-element.63.in_ref, bf16[16,6,64,256]{3,2,1,0:T(8,128)(2,1)} %all-to-all-done.3.back_ref, bf16[1024,3072]{1,0:T(8,128)(2,1)} %wv_ref.5, ...), custom_call_target="tpu_custom_call" | custom-call | flops 3221225472 | bytes 12582912 | tf_op jit(solution)/shard_map/unproject0/pallas_call | solution.py:897
  470.3 11.1 %unproject1.1 = (bf16[3,1024,512]{2,1,0:T(8,128)(2,1)}, bf16[512,1024]{1,0:T(8,128)(2,1)}, bf16[16,16,1024]{2,1,0:T(8,128)(2,1)}) custom-call(s32[1]{0:T(128)} %bitcast.which_ref.pack_ref, bf16[512,1024]{1,0:T(8,128)(2,1)S(1)} %get-tuple-element.63.in_ref, bf16[16,6,64,256]{3,2,1,0:T(8,128)(2,1)} %all-to-all-done.3.back_ref, bf16[1024,3072]{1,0:T(8,128)(2,1)} %wv_ref.5, ...), custom_call_target="tpu_custom_call" | custom-call | flops 3221225472 | bytes 12582912 | tf_op jit(solution)/shard_map/unproject1/pallas_call | solution.py:897
  481.7 6.0 %all-to-all-start.4 = ((bf16[16,16,1024]{2,1,0:T(8,128)(2,1)}), bf16[16,16,1024]{2,1,0:T(8,128)(2,1)S(1)}, u32[]{:S(2)}, u32[]{:S(2)}) async-start(bf16[16,16,1024]{2,1,0:T(8,128)(2,1)} %get-tuple-element.100), calls=%async_computation.4 | async-start | bytes 1048576 | tf_op jit(solution)/shard_map/all_to_all | solution.py:1159
  487.7 2.1 fusion.76
  491.3 3.0 collective-permute-start.18
  497.6 2.9 collective-permute-start.14
  500.5 15.6 %collective-permute-done.18 = bf16[1,1,1,1,64,512]{5,4,3,2,1,0:T(8,128)(2,1)S(1)} collective-permute-done((bf16[1,1,1,1,64,512]{5,4,3,2,1,0:T(8,128)(2,1)S(1)}, bf16[1,1,1,1,64,512]{5,4,3,2,1,0:T(8,128)(2,1)S(1)}, u32[]{:S(2)}, u32[]{:S(2)}) %collective-permute-start.18) | collective-permute-done | bytes 65568 | tf_op jit(solution)/shard_map/ppermute | solution.py:329
  516.3 5.5 collective-permute-done.16
  522.9 3.0 collective-permute-done.14
  529.6 1.8 fusion.47
  534.0 2.1 fusion.77
  537.5 1.5 collective-permute-start.26
  539.4 1.5 collective-permute-start.21
  541.5 15.5 %collective-permute-done.26 = bf16[3,2,2,1,2,64,256]{6,5,0,4,3,2,1:T(8,128)(2,1)S(1)} collective-permute-done((bf16[3,2,2,1,2,64,256]{6,5,0,4,3,2,1:T(8,128)(2,1)S(1)}, bf16[3,2,2,1,2,64,256]{6,5,0,4,3,2,1:T(8,128)(2,1)S(1)}, u32[]{:S(2)}, u32[]{:S(2)}) %collective-permute-start.26) | collective-permute-done | bytes 786464 | tf_op jit(solution)/shard_map/ppermute | solution.py:329
  558.0 1.5 collective-permute-start.27
  560.5 1.5 collective-permute-start.22
  563.8 4.7 collective-permute-done.27
  573.0 5.0 collective-permute-done.28
  578.1 2.1 collective-permute-done.23
  581.1 3.3 collective-permute-done.29
  584.5 2.3 collective-permute-done.24
  588.2 1.8 settle.1
  (303 shorter events, 73.4 us)
Async XLA Ops:
  7.4 3.0 copy-start.11
  7.4 3.7 copy-start.1
  7.5 3.7 copy-start.7
  27.0 8.5 %slice-start = ((f32[6144]{0:T(1024)}), f32[4096]{0:T(1024)S(1)}, s32[]{:S(2)}) async-start(f32[6144]{0:T(1024)} %param.23), calls=%async_computation.5 | async-start | bytes 32768 | tf_op jit(solution)/shard_map/slice | solution.py:992
  27.0 69.4 %all-to-all-start = ((bf16[16,6,64,256]{3,2,1,0:T(8,128)(2,1)}), bf16[16,6,64,256]{3,2,1,0:T(8,128)(2,1)}, u32[]{:S(2)}, u32[]{:S(2)}) async-start(bf16[16,6,64,256]{3,2,1,0:T(8,128)(2,1)} %copy-done.3), calls=%async_computation | async-start | bytes 6291456 | tf_op jit(solution)/shard_map/all_to_all | solution.py:982
  35.6 4.7 copy-start.2
  42.9 53.6 %copy-start.12 = (s32[1,32]{1,0:T(1,128)S(1)}, s32[1,32]{1,0:T(1,128)}, u32[]{:S(2)}) copy-start(s32[1,32]{1,0:T(1,128)} %param.20) | copy-start | bytes 388
  143.6 15.6 %copy-start.48 = (s32[1,2]{1,0:T(1,128)S(1)}, s32[1,2]{1,0:T(1,128)}, u32[]{:S(2)}) copy-start(s32[1,2]{1,0:T(1,128)} %param.18) | copy-start | bytes 28
  143.6 39.0 %all-to-all-start.1 = ((bf16[16,2,64,256]{3,2,1,0:T(8,128)(2,1)}), bf16[16,2,64,256]{3,2,1,0:T(8,128)(2,1)}, u32[]{:S(2)}, u32[]{:S(2)}) async-start(bf16[16,2,64,256]{3,2,1,0:T(8,128)(2,1)} %copy-done.6), calls=%async_computation.1 | async-start | bytes 2097152 | tf_op jit(solution)/shard_map/all_to_all | solution.py:985
  213.2 44.9 %collective-permute-start.1 = (bf16[1024,2048]{1,0:T(8,128)(2,1)}, bf16[1024,2048]{1,0:T(8,128)(2,1)}, u32[]{:S(2)}, u32[]{:S(2)}) collective-permute-start(bf16[1024,2048]{1,0:T(8,128)(2,1)} %get-tuple-element.86), channel_id=1, source_target_pairs={{0,16},{16,0},{1,17},{17,1},{2,18},{18,2},{3,19},{19,3},{4,20},{20... | collective-permute-start | bytes 12582920 | tf_op jit(solution)/shard_map/ppermute | solution.py:329
  215.5 52.5 %collective-permute-start = (bf16[2048,1024]{1,0:T(8,128)(2,1)}, bf16[2048,1024]{1,0:T(8,128)(2,1)}, u32[]{:S(2)}, u32[]{:S(2)}) collective-permute-start(bf16[2048,1024]{1,0:T(8,128)(2,1)} %get-tuple-element.84), channel_id=1, source_target_pairs={{0,16},{16,0},{1,17},{17,1},{2,18},{18,2},{3,19},{19,3},{4,20},{20... | collective-permute-start | bytes 12582920 | tf_op jit(solution)/shard_map/ppermute | solution.py:329
  215.6 23.3 %copy-start.47 = (f32[1,2048]{1,0:T(1,128)S(1)}, f32[1,2048]{1,0:T(1,128)}, u32[]{:S(2)}) copy-start(f32[1,2048]{1,0:T(1,128)} %get-tuple-element.75) | copy-start | bytes 24580
  215.6 24.1 %copy-start.8 = (f32[1024]{0:T(1024)S(1)}, f32[1024]{0:T(1024)}, u32[]{:S(2)}) copy-start(f32[1024]{0:T(1024)} %param.31) | copy-start | bytes 12292
  251.3 41.2 %all-to-all-start.2 = ((bf16[16,3,64,256]{3,2,1,0:T(8,128)(2,1)}), bf16[16,3,64,256]{3,2,1,0:T(8,128)(2,1)}, u32[]{:S(2)}, u32[]{:S(2)}) async-start(bf16[16,3,64,256]{3,2,1,0:T(8,128)(2,1)} %copy-done.5), calls=%async_computation.2 | async-start | bytes 3145728 | tf_op jit(solution)/shard_map/all_to_all | solution.py:982
  258.1 9.9 %copy-start.19 = (bf16[2048,1024]{1,0:T(8,128)(2,1)S(1)}, bf16[2048,1024]{1,0:T(8,128)(2,1)}, u32[]{:S(2)}) copy-start(bf16[2048,1024]{1,0:T(8,128)(2,1)} %get-tuple-element.83) | copy-start | bytes 12582916
  266.0 57.8 %collective-permute-start.4 = (bf16[2,2,1,2,64,2048]{5,4,3,2,1,0:T(8,128)(2,1)}, bf16[2,2,1,2,64,2048]{5,4,3,2,1,0:T(8,128)(2,1)}, u32[]{:S(2)}, u32[]{:S(2)}) collective-permute-start(bf16[2,2,1,2,64,2048]{5,4,3,2,1,0:T(8,128)(2,1)} %get-tuple-element.117), channel_id=1, source_target_pairs={{0,2},{1,3},{2,0},{3,1},{4,6},{5,7},{6,4},{7,5},{8,10},{9,11},{10,... | collective-permute-start | bytes 6291464 | tf_op jit(solution)/shard_map/ppermute | solution.py:329
  268.0 8.0 %copy-start.10 = (bf16[512,1024]{1,0:T(8,128)(2,1)S(1)}, bf16[512,1024]{1,0:T(8,128)(2,1)}, u32[]{:S(2)}) copy-start(bf16[512,1024]{1,0:T(8,128)(2,1)} %copy-done.9) | copy-start | bytes 3145732
  268.0 8.0 %copy-start.27 = (bf16[16,1,64,256]{3,2,1,0:T(8,128)(2,1)S(1)}, bf16[16,1,64,256]{3,2,1,0:T(8,128)(2,1)}, u32[]{:S(2)}) copy-start(bf16[16,1,64,256]{3,2,1,0:T(8,128)(2,1)} %copy-done.26) | copy-start | bytes 1572868
  268.0 8.0 %copy-start.29 = (bf16[16,1,64,256]{3,2,1,0:T(8,128)(2,1)S(1)}, bf16[16,1,64,256]{3,2,1,0:T(8,128)(2,1)}, u32[]{:S(2)}) copy-start(bf16[16,1,64,256]{3,2,1,0:T(8,128)(2,1)} %copy-done.28) | copy-start | bytes 1572868
  274.6 57.6 %collective-permute-start.3 = (bf16[2,2,2,1,128,1024]{5,4,3,2,1,0:T(8,128)(2,1)}, bf16[2,2,2,1,128,1024]{5,4,3,2,1,0:T(8,128)(2,1)}, u32[]{:S(2)}, u32[]{:S(2)}) collective-permute-start(bf16[2,2,2,1,128,1024]{5,4,3,2,1,0:T(8,128)(2,1)} %get-tuple-element.119), channel_id=1, source_target_pairs={{0,1},{1,0},{2,3},{3,2},{4,5},{5,4},{6,7},{7,6},{8,9},{9,8},{10,11... | collective-permute-start | bytes 6291464 | tf_op jit(solution)/shard_map/ppermute | solution.py:329
  277.7 43.0 %collective-permute-start.2 = (bf16[1024,512]{1,0:T(8,128)(2,1)}, bf16[1024,512]{1,0:T(8,128)(2,1)S(1)}, u32[]{:S(2)}, u32[]{:S(2)}) collective-permute-start(bf16[1024,512]{1,0:T(8,128)(2,1)} %convolution_convert_fusion), channel_id=1, source_target_pairs={{0,16},{16,0},{1,17},{17,1},{2,18},{18,2},{3,19},{19,3},{4,20},{20... | collective-permute-start | bytes 3145736 | tf_op jit(solution)/shard_map/ppermute | solution.py:329
  320.8 3.3 copy-start.17
  324.0 8.1 %copy-start.18 = (bf16[2,2,2,1,128,1024]{5,4,3,2,1,0:T(8,128)(2,1)S(1)}, bf16[2,2,2,1,128,1024]{5,4,3,2,1,0:T(8,128)(2,1)}, u32[]{:S(2)}) copy-start(bf16[2,2,2,1,128,1024]{5,4,3,2,1,0:T(8,128)(2,1)} %get-tuple-element.118) | copy-start | bytes 6291460
  327.3 8.0 %copy-start.35 = (bf16[2,2,1,1,64,2048]{5,4,3,2,1,0:T(8,128)(2,1)}, bf16[2,2,1,1,64,2048]{5,4,3,2,1,0:T(8,128)(2,1)S(1)}, u32[]{:S(2)}) copy-start(bf16[2,2,1,1,64,2048]{5,4,3,2,1,0:T(8,128)(2,1)S(1)} %get-tuple-element.121) | copy-start | bytes 3145732
  371.8 90.2 %all-to-all-start.3 = ((bf16[16,6,64,256]{3,2,1,0:T(8,128)(2,1)}), bf16[16,6,64,256]{3,2,1,0:T(8,128)(2,1)}, u32[]{:S(2)}, u32[]{:S(2)}) async-start(bf16[16,6,64,256]{3,2,1,0:T(8,128)(2,1)} %attend_back1.1), calls=%async_computation.3 | async-start | bytes 6291456 | tf_op jit(solution)/shard_map/all_to_all | solution.py:985
  380.7 7.2 %collective-permute-start.9 = (bf16[16,16,1024]{2,1,0:T(8,128)(2,1)}, bf16[16,16,1024]{2,1,0:T(8,128)(2,1)S(1)}, u32[]{:S(2)}, u32[]{:S(2)}) collective-permute-start(bf16[16,16,1024]{2,1,0:T(8,128)(2,1)} %bitcast.70), channel_id=1, source_target_pairs={{0,16},{16,0},{1,17},{17,1},{2,18},{18,2},{3,19},{19,3},{4,20},{20... | collective-permute-start | bytes 1572872 | tf_op jit(solution)/shard_map/ppermute | solution.py:329
  391.2 4.7 copy-start.36
  393.4 4.1 copy-start.34
  393.4 32.4 %copy-start.30 = (bf16[2,2,2,1,64,512]{5,4,3,2,1,0:T(8,128)(2,1)S(1)}, bf16[2,2,2,1,64,512]{5,4,3,2,1,0:T(8,128)(2,1)}, u32[]{:S(2)}) copy-start(bf16[2,2,2,1,64,512]{5,4,3,2,1,0:T(8,128)(2,1)} %get-tuple-element.134) | copy-start | bytes 1572868
  394.0 61.7 %copy-start.21 = (bf16[2,2,1,1,64,2048]{5,4,3,2,1,0:T(8,128)(2,1)S(1)}, bf16[2,2,1,1,64,2048]{5,4,3,2,1,0:T(8,128)(2,1)}, u32[]{:S(2)}) copy-start(bf16[2,2,1,1,64,2048]{5,4,3,2,1,0:T(8,128)(2,1)} %get-tuple-element.120) | copy-start | bytes 3145732
  394.1 31.7 %collective-permute-start.7 = (bf16[2,2,2,1,64,512]{5,4,3,2,1,0:T(8,128)(2,1)S(1)}, bf16[2,2,2,1,64,512]{5,4,3,2,1,0:T(8,128)(2,1)S(1)}, u32[]{:S(2)}, u32[]{:S(2)}) collective-permute-start(bf16[2,2,2,1,64,512]{5,4,3,2,1,0:T(8,128)(2,1)S(1)} %copy-done.38), channel_id=1, source_target_pairs={{0,1},{1,0},{2,3},{3,2},{4,5},{5,4},{6,7},{7,6},{8,9},{9,8},{10,11... | collective-permute-start | bytes 1572872 | tf_op jit(solution)/shard_map/ppermute | solution.py:329
  395.9 59.8 %collective-permute-start.6 = (bf16[2,2,1,1,64,2048]{5,4,3,2,1,0:T(8,128)(2,1)S(1)}, bf16[2,2,1,1,64,2048]{5,4,3,2,1,0:T(8,128)(2,1)S(1)}, u32[]{:S(2)}, u32[]{:S(2)}) collective-permute-start(bf16[2,2,1,1,64,2048]{5,4,3,2,1,0:T(8,128)(2,1)S(1)} %copy-done.36), channel_id=1, source_target_pairs={{0,1},{1,0},{2,3},{3,2},{4,5},{5,4},{6,7},{7,6},{8,9},{9,8},{10,11... | collective-permute-start | bytes 3145736 | tf_op jit(solution)/shard_map/ppermute | solution.py:329
  397.5 31.6 %copy-start.39 = (f32[32,64]{1,0:T(8,128)}, f32[32,64]{1,0:T(8,128)S(1)}, u32[]{:S(2)}) copy-start(f32[32,64]{1,0:T(8,128)S(1)} %fusion.22) | copy-start | bytes 24580
  397.5 62.1 %collective-permute-start.5 = (bf16[2,2,1,1,128,1024]{5,4,3,2,1,0:T(8,128)(2,1)S(1)}, bf16[2,2,1,1,128,1024]{5,4,3,2,1,0:T(8,128)(2,1)S(1)}, u32[]{:S(2)}, u32[]{:S(2)}) collective-permute-start(bf16[2,2,1,1,128,1024]{5,4,3,2,1,0:T(8,128)(2,1)S(1)} %copy-done.34), channel_id=1, source_target_pairs={{0,2},{1,3},{2,0},{3,1},{4,6},{5,7},{6,4},{7,5},{8,10},{9,11},{10,... | collective-permute-start | bytes 3145736 | tf_op jit(solution)/shard_map/ppermute | solution.py:329
  425.9 33.7 %copy-start.20 = (bf16[2,2,1,1,128,1024]{5,4,3,2,1,0:T(8,128)(2,1)S(1)}, bf16[2,2,1,1,128,1024]{5,4,3,2,1,0:T(8,128)(2,1)}, u32[]{:S(2)}) copy-start(bf16[2,2,1,1,128,1024]{5,4,3,2,1,0:T(8,128)(2,1)} %get-tuple-element.122) | copy-start | bytes 3145732
  425.9 21.1 %collective-permute-start.8 = (bf16[2,2,1,1,64,512]{5,4,3,2,1,0:T(8,128)(2,1)S(1)}, bf16[2,2,1,1,64,512]{5,4,3,2,1,0:T(8,128)(2,1)S(1)}, u32[]{:S(2)}, u32[]{:S(2)}) collective-permute-start(bf16[2,2,1,1,64,512]{5,4,3,2,1,0:T(8,128)(2,1)S(1)} %get-tuple-element.149), channel_id=1, source_target_pairs={{0,2},{1,3},{2,0},{3,1},{4,6},{5,7},{6,4},{7,5},{8,10},{9,11},{10,... | collective-permute-start | bytes 786440 | tf_op jit(solution)/shard_map/ppermute | solution.py:329
  447.8 33.9 %collective-permute-start.12 = (bf16[2,1,1,1,64,512]{5,4,3,2,1,0:T(8,128)(2,1)}, bf16[2,1,1,1,64,512]{5,4,3,2,1,0:T(8,128)(2,1)S(1)}, u32[]{:S(2)}, u32[]{:S(2)}) collective-permute-start(bf16[2,1,1,1,64,512]{5,4,3,2,1,0:T(8,128)(2,1)} %get-tuple-element.161), channel_id=1, source_target_pairs={{0,4},{1,5},{2,6},{3,7},{4,0},{5,1},{6,2},{7,3},{8,12},{9,13},{10,... | collective-permute-start | bytes 393224 | tf_op jit(solution)/shard_map/ppermute | solution.py:329
  457.2 24.3 %collective-permute-start.10 = (bf16[2,1,1,1,64,2048]{5,4,3,2,1,0:T(8,128)(2,1)}, bf16[2,1,1,1,64,2048]{5,4,3,2,1,0:T(8,128)(2,1)}, u32[]{:S(2)}, u32[]{:S(2)}) collective-permute-start(bf16[2,1,1,1,64,2048]{5,4,3,2,1,0:T(8,128)(2,1)} %get-tuple-element.133), channel_id=1, source_target_pairs={{0,4},{1,5},{2,6},{3,7},{4,0},{5,1},{6,2},{7,3},{8,12},{9,13},{10,... | collective-permute-start | bytes 1572872 | tf_op jit(solution)/shard_map/ppermute | solution.py:329
  461.0 20.7 %collective-permute-start.11 = (bf16[2,1,1,1,128,1024]{5,4,3,2,1,0:T(8,128)(2,1)}, bf16[2,1,1,1,128,1024]{5,4,3,2,1,0:T(8,128)(2,1)}, u32[]{:S(2)}, u32[]{:S(2)}) collective-permute-start(bf16[2,1,1,1,128,1024]{5,4,3,2,1,0:T(8,128)(2,1)} %get-tuple-element.131), channel_id=1, source_target_pairs={{0,4},{1,5},{2,6},{3,7},{4,0},{5,1},{6,2},{7,3},{8,12},{9,13},{10,... | collective-permute-start | bytes 1572872 | tf_op jit(solution)/shard_map/ppermute | solution.py:329
  481.7 45.4 %all-to-all-start.4 = ((bf16[16,16,1024]{2,1,0:T(8,128)(2,1)}), bf16[16,16,1024]{2,1,0:T(8,128)(2,1)S(1)}, u32[]{:S(2)}, u32[]{:S(2)}) async-start(bf16[16,16,1024]{2,1,0:T(8,128)(2,1)} %get-tuple-element.100), calls=%async_computation.4 | async-start | bytes 1048576 | tf_op jit(solution)/shard_map/all_to_all | solution.py:1159
  489.8 4.5 copy-start.32
  489.8 5.6 copy-start.31
  491.2 42.7 %collective-permute-start.20 = (bf16[3,1024,512]{2,1,0:T(8,128)(2,1)}, bf16[3,1024,512]{2,1,0:T(8,128)(2,1)}, u32[]{:S(2)}, u32[]{:S(2)}) collective-permute-start(bf16[3,1024,512]{2,1,0:T(8,128)(2,1)} %get-tuple-element.108), channel_id=1, source_target_pairs={{0,16},{16,0},{1,17},{17,1},{2,18},{18,2},{3,19},{19,3},{4,20},{20... | collective-permute-start | bytes 9437192 | tf_op jit(solution)/shard_map/ppermute | solution.py:329
  491.3 24.9 %collective-permute-start.18 = (bf16[1,1,1,1,64,512]{5,4,3,2,1,0:T(8,128)(2,1)S(1)}, bf16[1,1,1,1,64,512]{5,4,3,2,1,0:T(8,128)(2,1)S(1)}, u32[]{:S(2)}, u32[]{:S(2)}) collective-permute-start(bf16[1,1,1,1,64,512]{5,4,3,2,1,0:T(8,128)(2,1)S(1)} %add_convert_fusion.43), channel_id=1, source_target_pairs={{0,8},{1,9},{2,10},{3,11},{4,12},{5,13},{6,14},{7,15},{8,0},{9,1},... | collective-permute-start | bytes 196616 | tf_op jit(solution)/shard_map/ppermute | solution.py:329
  495.3 26.5 %collective-permute-start.16 = (bf16[1,1,1,1,128,1024]{5,4,3,2,1,0:T(8,128)(2,1)S(1)}, bf16[1,1,1,1,128,1024]{5,4,3,2,1,0:T(8,128)(2,1)S(1)}, u32[]{:S(2)}, u32[]{:S(2)}) collective-permute-start(bf16[1,1,1,1,128,1024]{5,4,3,2,1,0:T(8,128)(2,1)S(1)} %add_convert_fusion.23), channel_id=1, source_target_pairs={{0,8},{1,9},{2,10},{3,11},{4,12},{5,13},{6,14},{7,15},{8,0},{9,1},... | collective-permute-start | bytes 786440 | tf_op jit(solution)/shard_map/ppermute | solution.py:329
  497.6 28.3 %collective-permute-start.14 = (bf16[1,1,1,1,64,2048]{5,4,3,2,1,0:T(8,128)(2,1)S(1)}, bf16[1,1,1,1,64,2048]{5,4,3,2,1,0:T(8,128)(2,1)S(1)}, u32[]{:S(2)}, u32[]{:S(2)}) collective-permute-start(bf16[1,1,1,1,64,2048]{5,4,3,2,1,0:T(8,128)(2,1)S(1)} %add_convert_fusion.26), channel_id=1, source_target_pairs={{0,8},{1,9},{2,10},{3,11},{4,12},{5,13},{6,14},{7,15},{8,0},{9,1},... | collective-permute-start | bytes 786440 | tf_op jit(solution)/shard_map/ppermute | solution.py:329
  516.2 13.4 %copy-start.42 = (f32[32,64]{1,0:T(8,128)S(1)}, f32[32,64]{1,0:T(8,128)}, u32[]{:S(2)}) copy-start(f32[32,64]{1,0:T(8,128)} %copy-done.41) | copy-start | bytes 24580
  516.2 71.4 %collective-permute-start.19 = (bf16[64,512]{1,0:T(8,128)(2,1)S(1)}, bf16[64,512]{1,0:T(8,128)(2,1)S(1)}, u32[]{:S(2)}, u32[]{:S(2)}) collective-permute-start(bf16[64,512]{1,0:T(8,128)(2,1)S(1)} %fusion.36.refs_4_), channel_id=1, source_target_pairs={{0,16},{16,0},{1,17},{17,1},{2,18},{18,2},{3,19},{19,3},{4,20},{20... | collective-permute-start | bytes 196616 | tf_op jit(solution)/shard_map/ppermute | solution.py:329
  522.9 64.8 %collective-permute-start.17 = (bf16[128,1024]{1,0:T(8,128)(2,1)S(1)}, bf16[128,1024]{1,0:T(8,128)(2,1)S(1)}, u32[]{:S(2)}, u32[]{:S(2)}) collective-permute-start(bf16[128,1024]{1,0:T(8,128)(2,1)S(1)} %fusion.27.refs_2_), channel_id=1, source_target_pairs={{0,16},{16,0},{1,17},{17,1},{2,18},{18,2},{3,19},{19,3},{4,20},{20... | collective-permute-start | bytes 786440 | tf_op jit(solution)/shard_map/ppermute | solution.py:329
  527.0 60.6 %collective-permute-start.15 = (bf16[64,2048]{1,0:T(8,128)(2,1)S(1)}, bf16[64,2048]{1,0:T(8,128)(2,1)S(1)}, u32[]{:S(2)}, u32[]{:S(2)}) collective-permute-start(bf16[64,2048]{1,0:T(8,128)(2,1)S(1)} %fusion.26.refs_0_), channel_id=1, source_target_pairs={{0,16},{16,0},{1,17},{17,1},{2,18},{18,2},{3,19},{19,3},{4,20},{20... | collective-permute-start | bytes 786440 | tf_op jit(solution)/shard_map/ppermute | solution.py:329
  527.8 3.9 collective-permute-start.13
  537.5 19.5 %collective-permute-start.26 = (bf16[3,2,2,1,2,64,256]{6,5,0,4,3,2,1:T(8,128)(2,1)S(1)}, bf16[3,2,2,1,2,64,256]{6,5,0,4,3,2,1:T(8,128)(2,1)S(1)}, u32[]{:S(2)}, u32[]{:S(2)}) collective-permute-start(bf16[3,2,2,1,2,64,256]{6,5,0,4,3,2,1:T(8,128)(2,1)S(1)} %add_convert_fusion.8), channel_id=1, source_target_pairs={{0,2},{1,3},{2,0},{3,1},{4,6},{5,7},{6,4},{7,5},{8,10},{9,11},{10,... | collective-permute-start | bytes 2359304 | tf_op jit(solution)/shard_map/ppermute | solution.py:329
  539.4 20.1 %collective-permute-start.21 = (bf16[3,2,2,2,1,64,256]{6,5,0,4,3,2,1:T(8,128)(2,1)S(1)}, bf16[3,2,2,2,1,64,256]{6,5,0,4,3,2,1:T(8,128)(2,1)S(1)}, u32[]{:S(2)}, u32[]{:S(2)}) collective-permute-start(bf16[3,2,2,2,1,64,256]{6,5,0,4,3,2,1:T(8,128)(2,1)S(1)} %add_convert_fusion.10), channel_id=1, source_target_pairs={{0,1},{1,0},{2,3},{3,2},{4,5},{5,4},{6,7},{7,6},{8,9},{9,8},{10,11... | collective-permute-start | bytes 2359304 | tf_op jit(solution)/shard_map/ppermute | solution.py:329
  541.5 21.1 %copy-start.40 = (f32[32,64]{1,0:T(8,128)S(1)}, f32[32,64]{1,0:T(8,128)}, u32[]{:S(2)}) copy-start(f32[32,64]{1,0:T(8,128)} %copy-done.39) | copy-start | bytes 24580
  558.0 13.9 %copy-start.43 = (f32[32,64]{1,0:T(8,128)S(1)}, f32[32,64]{1,0:T(8,128)}, u32[]{:S(2)}) copy-start(f32[32,64]{1,0:T(8,128)} %fusion.47) | copy-start | bytes 24580
  558.0 10.5 %collective-permute-start.27 = (bf16[3,2,2,1,1,64,256]{6,5,0,4,3,2,1:T(8,128)(2,1)}, bf16[3,2,2,1,1,64,256]{6,5,0,4,3,2,1:T(8,128)(2,1)}, u32[]{:S(2)}, u32[]{:S(2)}) collective-permute-start(bf16[3,2,2,1,1,64,256]{6,5,0,4,3,2,1:T(8,128)(2,1)} %get-tuple-element.137), channel_id=1, source_target_pairs={{0,1},{1,0},{2,3},{3,2},{4,5},{5,4},{6,7},{7,6},{8,9},{9,8},{10,11... | collective-permute-start | bytes 1179656 | tf_op jit(solution)/shard_map/ppermute | solution.py:329
  560.5 10.1 %collective-permute-start.22 = (bf16[3,2,2,1,1,64,256]{6,5,0,4,3,2,1:T(8,128)(2,1)}, bf16[3,2,2,1,1,64,256]{6,5,0,4,3,2,1:T(8,128)(2,1)S(1)}, u32[]{:S(2)}, u32[]{:S(2)}) collective-permute-start(bf16[3,2,2,1,1,64,256]{6,5,0,4,3,2,1:T(8,128)(2,1)} %get-tuple-element.143), channel_id=1, source_target_pairs={{0,2},{1,3},{2,0},{3,1},{4,6},{5,7},{6,4},{7,5},{8,10},{9,11},{10,... | collective-permute-start | bytes 1179656 | tf_op jit(solution)/shard_map/ppermute | solution.py:329
  563.8 23.1 %copy-start.45 = (f32[4096]{0:T(1024)S(1)}, f32[4096]{0:T(1024)}, u32[]{:S(2)}) copy-start(f32[4096]{0:T(1024)} %get-tuple-element.226) | copy-start | bytes 49156
  569.7 8.3 %collective-permute-start.28 = (bf16[3,2,1,1,1,64,256]{6,5,0,4,3,2,1:T(8,128)(2,1)S(1)}, bf16[3,2,1,1,1,64,256]{6,5,0,4,3,2,1:T(8,128)(2,1)S(1)}, u32[]{:S(2)}, u32[]{:S(2)}) collective-permute-start(bf16[3,2,1,1,1,64,256]{6,5,0,4,3,2,1:T(8,128)(2,1)S(1)} %get-tuple-element.153), channel_id=1, source_target_pairs={{0,4},{1,5},{2,6},{3,7},{4,0},{5,1},{6,2},{7,3},{8,12},{9,13},{10,... | collective-permute-start | bytes 589832 | tf_op jit(solution)/shard_map/ppermute | solution.py:329
  570.7 9.4 %collective-permute-start.23 = (bf16[3,2,1,1,1,64,256]{6,5,0,4,3,2,1:T(8,128)(2,1)S(1)}, bf16[3,2,1,1,1,64,256]{6,5,0,4,3,2,1:T(8,128)(2,1)S(1)}, u32[]{:S(2)}, u32[]{:S(2)}) collective-permute-start(bf16[3,2,1,1,1,64,256]{6,5,0,4,3,2,1:T(8,128)(2,1)S(1)} %get-tuple-element.155), channel_id=1, source_target_pairs={{0,4},{1,5},{2,6},{3,7},{4,0},{5,1},{6,2},{7,3},{8,12},{9,13},{10,... | collective-permute-start | bytes 589832 | tf_op jit(solution)/shard_map/ppermute | solution.py:329
  578.0 6.3 %collective-permute-start.29 = (bf16[3,1,1,1,1,64,256]{6,5,0,4,3,2,1:T(8,128)(2,1)S(1)}, bf16[3,1,1,1,1,64,256]{6,5,0,4,3,2,1:T(8,128)(2,1)S(1)}, u32[]{:S(2)}, u32[]{:S(2)}) collective-permute-start(bf16[3,1,1,1,1,64,256]{6,5,0,4,3,2,1:T(8,128)(2,1)S(1)} %add_convert_fusion.37), channel_id=1, source_target_pairs={{0,8},{1,9},{2,10},{3,11},{4,12},{5,13},{6,14},{7,15},{8,0},{9,1},... | collective-permute-start | bytes 294920 | tf_op jit(solution)/shard_map/ppermute | solution.py:329
  580.2 6.6 %collective-permute-start.24 = (bf16[3,1,1,1,1,64,256]{6,5,0,4,3,2,1:T(8,128)(2,1)S(1)}, bf16[3,1,1,1,1,64,256]{6,5,0,4,3,2,1:T(8,128)(2,1)S(1)}, u32[]{:S(2)}, u32[]{:S(2)}) collective-permute-start(bf16[3,1,1,1,1,64,256]{6,5,0,4,3,2,1:T(8,128)(2,1)S(1)} %add_convert_fusion.40), channel_id=1, source_target_pairs={{0,8},{1,9},{2,10},{3,11},{4,12},{5,13},{6,14},{7,15},{8,0},{9,1},... | collective-permute-start | bytes 294920 | tf_op jit(solution)/shard_map/ppermute | solution.py:329
  584.4 3.2 collective-permute-start.30
  586.8 1.4 collective-permute-start.25
  (22 other events, 31.1 us)

commit v6 on v5

--- a/solution.py
+++ b/solution.py
@@ -361,10 +361,12 @@
         pieces = [lax.dynamic_slice_in_dim(part, which, 1, axis) for part in self.parts]
         return (pieces[0].astype(F32) + pieces[1].astype(F32)).astype(BF16)
 
-    def stage(self):
+    def stage(self, later=()):
         bit = self.order.pop(0)
         own_bit = lax.rem(lax.div(self.index, bit), 2)
         send = self.pick(bit, 1 - own_bit)
+        for each in later:
+            send = each.tie(send)
         came = exchange(send, "seq", bit)
         self.parts = [self.pick(bit, own_bit), came]
         return send
@@ -1153,9 +1155,6 @@
         (hidden[0], d_middle, attn_scale, bias_theirs),
     )
     hidden_grad = hidden_grad.reshape(1, tokens, width)
-    if halves:
-        for each in (up_sum, down_sum, out_sum):
-            late = each.tie(late)
     late_rows = lax.all_to_all(late, "seq", 0, 0, tiled=True)
 
     def halves_in_order(own, other):
@@ -1170,6 +1169,8 @@
             RowSum(qkv_mine[..., :split], came[..., :split], (1, 2, 4, 8)),
             RowSum(qkv_mine[..., split:], came[..., split:], (2, 1, 4, 8)),
         ]
+        for each in qkv_sums:
+            each.stage((up_sum, down_sum, out_sum))
         up_weight_grad, down_weight_grad, out_weight_grad, qkv_weight_grad = settle(
             pack, *[each.finish() for each in (up_sum, down_sum, out_sum, *qkv_sums)]
         )

time: 599 us -> 583 us (0.973)
  waiting for transfers between devices: 194 us -> 164 us
  Pallas kernels: 192 us -> 211 us
    ppermute x31, waiting for transfers between devices: 111 us -> 84.3 us  [exchange(): lax.ppermute(value, axis, [(source, source ^ bit) for source in range(cou...]
    pallas_call x2, Pallas kernels: 63.4 us -> 73.9 us  [attend_back(): pl.pallas_call(functools.partial(attend_back_kernel, per_device, part, la...]
    pallas_call x1, Pallas kernels: 43 us -> 51.1 us  [attend(): pl.pallas_call(functools.partial(attend_kernel, per_device), out_shape=ou...]
    all_to_all x2, waiting for transfers between devices: 19.5 us -> 11.7 us  [to_tokens(): return lax.all_to_all(array, 'seq', 0, 0, tiled=True)[:heads]]
    unnamed x106 -> x112, local copies, waits for them, and re-layouts: 15.5 us -> 16.9 us
  transfers between devices with their start and end apart: 36 -> 36, of which waited for: 19 -> 19; matrix products, arithmetic and copies ran while one was open for 15% -> 14% of each run, Pallas kernels for 13% -> 11%
where the time goes in v6:
time: 583 us; the launch traced here: 574 us
  Pallas kernels  211 us (36%)
  waiting for transfers between devices  164 us (28%)
  starting transfers between devices  76.2 us (13%)
  local copies, waits for them, and re-layouts  47.2 us (8%)
  other arithmetic  46.7 us (8%)
  matrix products  22.5 us (4%)
  between operations  6.21 us (1%)
    ppermute x31, waiting for transfers between devices, exchange(): lax.ppermute(value, axis, [(source, source ^ bit) for source in range(cou...  84.3 us
    pallas_call x2, Pallas kernels, attend_back(): pl.pallas_call(functools.partial(attend_back_kernel, per_device, part, la...  73.9 us
    all_to_all x2, waiting for transfers between devices, to_heads(): return lax.all_to_all(array, 'seq', 0, 0, tiled=True)  62.9 us
    pallas_call x1, Pallas kernels, attend(): pl.pallas_call(functools.partial(attend_kernel, per_device), out_shape=ou...  51.1 us
    pallas_call x2, Pallas kernels, feed(): pl.pallas_call(functools.partial(feed_kernel, before is not None), grid_s...  45.2 us
    convert_element_type x22, other arithmetic, pick(): return (pieces[0].astype(F32) + pieces[1].astype(F32)).astype(BF16)  29.8 us
    ppermute x31, starting transfers between devices, exchange(): lax.ppermute(value, axis, [(source, source ^ bit) for source in range(cou...  28.7 us
    all_to_all x2, starting transfers between devices, to_tokens(): return lax.all_to_all(array, 'seq', 0, 0, tiled=True)[:heads]  24 us
  transfers between devices with their start and end apart: 36, of which 19 were waited for; matrix products, arithmetic and copies ran while one was open for 14% of the time, Pallas kernels for 11%

profile of v6, /device:TPU:0, one launch (start us, length us, event | category | flops | bytes accessed | tf_op | source)
XLA Modules:
  0.0 574.0 jit_solution(12991691671242418710)
XLA Ops:
  7.5 2.9 fusion.7
  11.2 2.8 copy-done
  14.0 11.4 %project.1 = (bf16[512,1024]{1,0:T(8,128)(2,1)S(1)}, bf16[16,6,64,256]{3,2,1,0:T(8,128)(2,1)S(1)}) custom-call(bf16[512,1024]{1,0:T(8,128)(2,1)S(1)} %bitcast.149, f32[2,1024]{1,0:T(2,128)S(1)} %get-tuple-element.216.shift_ref, f32[2,1024]{1,0:T(2,128)S(1)} %get-tuple-element.215.scale_ref.refs_3_, bf16[1024,3072]{1,0:T(8,128)(2,1)S(1)} %copy-done, ...), custom_call_target="tpu_custom_call" | custom-call | flops 3221225472 | bytes 11534336 | tf_op jit(solution)/shard_map/project/pallas_call | solution.py:506
  25.4 1.6 copy-done.3
  27.0 8.5 %all-to-all-start = ((bf16[16,6,64,256]{3,2,1,0:T(8,128)(2,1)}), bf16[16,6,64,256]{3,2,1,0:T(8,128)(2,1)}, u32[]{:S(2)}, u32[]{:S(2)}) async-start(bf16[16,6,64,256]{3,2,1,0:T(8,128)(2,1)} %copy-done.3), calls=%async_computation | async-start | bytes 6291456 | tf_op jit(solution)/shard_map/all_to_all | solution.py:984
  35.6 4.7 fusion.2
  44.2 52.2 %all-to-all-done.x_ref = bf16[16,6,64,256]{3,2,1,0:T(8,128)(2,1)} async-done(((bf16[16,6,64,256]{3,2,1,0:T(8,128)(2,1)}), bf16[16,6,64,256]{3,2,1,0:T(8,128)(2,1)}, u32[]{:S(2)}, u32[]{:S(2)}) %all-to-all-start) | async-done | bytes 3145760 | tf_op jit(solution)/shard_map/all_to_all | solution.py:984
  96.5 51.1 %attend.1 = (bf16[16,2,64,256]{3,2,1,0:T(8,128)(2,1)S(1)}, f32[16,2,64,256]{3,2,1,0:T(8,128)S(1)}, f32[32,256]{1,0:T(8,128)S(1)}, bf16[32,256,128]{2,1,0:T(8,128)(2,1)S(1)}) custom-call(s32[32]{0:T(128)S(1)} %bitcast.159, s32[32]{0:T(128)S(1)} %bitcast.162, bf16[16,6,64,256]{3,2,1,0:T(8,128)(2,1)} %all-to-all-done.x_ref), custom_call_target="tpu_custom_call" | custom-call | flops 12884901888 | bytes 9437184 | tf_op jit(solution)/shard_map/attend/pallas_call | solution.py:179
  148.6 1.3 copy-done.13
  151.8 15.6 %all-to-all-start.1 = ((bf16[16,2,64,256]{3,2,1,0:T(8,128)(2,1)}), bf16[16,2,64,256]{3,2,1,0:T(8,128)(2,1)}, u32[]{:S(2)}, u32[]{:S(2)}) async-start(bf16[16,2,64,256]{3,2,1,0:T(8,128)(2,1)} %copy-done.6), calls=%async_computation.1 | async-start | bytes 2097152 | tf_op jit(solution)/shard_map/all_to_all | solution.py:987
  171.4 11.7 %all-to-all-done.1 = bf16[16,2,64,256]{3,2,1,0:T(8,128)(2,1)} async-done(((bf16[16,2,64,256]{3,2,1,0:T(8,128)(2,1)}), bf16[16,2,64,256]{3,2,1,0:T(8,128)(2,1)}, u32[]{:S(2)}, u32[]{:S(2)}) %all-to-all-start.1) | async-done | bytes 1048608 | tf_op jit(solution)/shard_map/all_to_all | solution.py:987
  183.1 1.4 fusion.78
  188.5 3.2 fusion.10
  191.7 21.9 %feed0.1 = (f32[512,1024]{1,0:T(8,128)}, f32[512,1024]{1,0:T(8,128)}, bf16[1024,2048]{1,0:T(8,128)(2,1)}, bf16[2048,1024]{1,0:T(8,128)(2,1)}, f32[1,2048]{1,0:T(1,128)}) custom-call(s32[1]{0:T(128)} %bitcast.20.which_ref, bf16[512,1024]{1,0:T(8,128)(2,1)} %get-tuple-element.131.in_ref, bf16[512,1024]{1,0:T(8,128)(2,1)} %fusion.13.d_out_ref, ...), custom_call_target="tpu_custom_call" | custom-call | flops 12884901888 | bytes 25165824 | tf_op jit(solution)/shard_map/feed0/pallas_call | solution.py:612
  214.3 23.2 %feed1.1 = (f32[512,1024]{1,0:T(8,128)}, f32[512,1024]{1,0:T(8,128)}, bf16[1024,2048]{1,0:T(8,128)(2,1)}, bf16[2048,1024]{1,0:T(8,128)(2,1)}, f32[1,2048]{1,0:T(1,128)}) custom-call(s32[1]{0:T(128)} %bitcast.which_ref.pack_ref, bf16[512,1024]{1,0:T(8,128)(2,1)} %get-tuple-element.131.in_ref, bf16[512,1024]{1,0:T(8,128)(2,1)} %fusion.13.d_out_ref, ...), custom_call_target="tpu_custom_call" | custom-call | flops 12884901888 | bytes 25165824 | tf_op jit(solution)/shard_map/feed1/pallas_call | solution.py:612
  238.4 8.1 %middle_back.1 = (f32[512,1024]{1,0:T(8,128)S(1)}, bf16[512,1024]{1,0:T(8,128)(2,1)S(1)}, bf16[512,1024]{1,0:T(8,128)(2,1)}, bf16[16,3,64,256]{3,2,1,0:T(8,128)(2,1)S(1)}) custom-call(f32[512,1024]{1,0:T(8,128)} %get-tuple-element.81.d_in_ref, f32[512,1024]{1,0:T(8,128)} %get-tuple-element.132.middle_ref, bf16[512,1024]{1,0:T(8,128)(2,1)S(1)} %bitcast.151, ...), custom_call_target="tpu_custom_call" | custom-call | flops 1073741824 | bytes 12582912 | tf_op jit(solution)/shard_map/middle_back/pallas_call | solution.py:736
  246.5 1.3 copy-done.4
  250.0 5.8 %all-to-all-start.2 = ((bf16[16,3,64,256]{3,2,1,0:T(8,128)(2,1)}), bf16[16,3,64,256]{3,2,1,0:T(8,128)(2,1)}, u32[]{:S(2)}, u32[]{:S(2)}) async-start(bf16[16,3,64,256]{3,2,1,0:T(8,128)(2,1)} %copy-done.5), calls=%async_computation.2 | async-start | bytes 3145728 | tf_op jit(solution)/shard_map/all_to_all | solution.py:984
  255.8 7.9 %add_convert_fusion = (bf16[2,2,1,2,64,2048]{5,4,3,2,1,0:T(8,128)(2,1)}, bf16[2,2,1,2,64,2048]{5,4,3,2,1,0:T(8,128)(2,1)}) fusion(bf16[2,2,2,2,64,2048]{5,4,3,2,1,0:T(8,128)(2,1)} %bitcast.36, s32[]{:T(128)S(6)} %select_n.97, bf16[2,2,2,2,64,2048]{5,4,3,2,1,0:T(8,128)(2,1)} %bitcast.174, s32[]{:T(128)S(6)} %select_n.93), kind=kLoop, calls=%fused_computation.4 | loop fusion | flops 8388608 | bytes 12582920 | tf_op jit(solution)/shard_map/convert_element_type | solution.py:362
  263.7 2.0 collective-permute-start.4
  265.7 6.5 %add_convert_fusion.1 = (bf16[2,2,2,1,128,1024]{5,4,3,2,1,0:T(8,128)(2,1)}, bf16[2,2,2,1,128,1024]{5,4,3,2,1,0:T(8,128)(2,1)}) fusion(bf16[2,2,2,2,128,1024]{5,4,3,2,1,0:T(8,128)(2,1)} %bitcast.33, s32[]{:T(128)S(6)} %select_n.96, bf16[2,2,2,2,128,1024]{5,4,3,2,1,0:T(8,128)(2,1)S(1)} %bitcast.173, s32[]{:T(128)S(6)} %select_n.92), kind=kLoop, calls=%fused_computation.5 | loop fusion | flops 8388608 | bytes 12582920 | tf_op jit(solution)/shard_map/convert_element_type | solution.py:362
  272.2 1.5 collective-permute-start.3
  273.7 1.7 convolution_convert_fusion
  275.4 1.7 convolution_convert_fusion.1
  279.4 10.6 %all-to-all-done.2.d_mix_ref = bf16[16,3,64,256]{3,2,1,0:T(8,128)(2,1)} async-done(((bf16[16,3,64,256]{3,2,1,0:T(8,128)(2,1)}), bf16[16,3,64,256]{3,2,1,0:T(8,128)(2,1)}, u32[]{:S(2)}, u32[]{:S(2)}) %all-to-all-start.2) | async-done | bytes 1572896 | tf_op jit(solution)/shard_map/all_to_all | solution.py:984
  290.0 33.7 %attend_back0.1 = (bf16[16,64,256]{2,1,0:T(8,128)(2,1)}, f32[32,256,128]{2,1,0:T(8,128)}) custom-call(s32[32]{0:T(128)} %bitcast.156, s32[32]{0:T(128)} %bitcast.160, bf16[16,6,64,256]{3,2,1,0:T(8,128)(2,1)} %all-to-all-done.x_ref, bf16[32,256,128]{2,1,0:T(8,128)(2,1)} %copy-done.14, f32[16,2,64,256]{3,2,1,0:T(8,128)} %copy-done.13, f32[32,256]{1,0:T(8,128)} %copy-done.15, ...), custom_call_target="tpu_custom_call" | custom-call | flops 16106127360 | bytes 15728640 | tf_op jit(solution)/shard_map/attend_back0/pallas_call | solution.py:311
  323.8 2.5 add_convert_fusion.14
  327.1 3.2 add_convert_fusion.4
  330.8 3.1 add_convert_fusion.5
  335.4 40.2 %attend_back1.1 = bf16[16,6,64,256]{3,2,1,0:T(8,128)(2,1)} custom-call(s32[32]{0:T(128)} %bitcast.157, s32[32]{0:T(128)} %bitcast.161, bf16[16,6,64,256]{3,2,1,0:T(8,128)(2,1)} %all-to-all-done.x_ref, bf16[32,256,128]{2,1,0:T(8,128)(2,1)} %copy-done.14, f32[16,2,64,256]{3,2,1,0:T(8,128)} %copy-done.13, f32[32,256]{1,0:T(8,128)} %copy-done.15, ...), custom_call_target="tpu_custom_call" | custom-call | flops 16106127360 | bytes 15728640 | tf_op jit(solution)/shard_map/attend_back1/pallas_call | solution.py:311
  375.6 8.4 %all-to-all-start.3 = ((bf16[16,6,64,256]{3,2,1,0:T(8,128)(2,1)}), bf16[16,6,64,256]{3,2,1,0:T(8,128)(2,1)}, u32[]{:S(2)}, u32[]{:S(2)}) async-start(bf16[16,6,64,256]{3,2,1,0:T(8,128)(2,1)} %attend_back1.1), calls=%async_computation.3 | async-start | bytes 6291456 | tf_op jit(solution)/shard_map/all_to_all | solution.py:987
  387.2 2.6 fusion.81
  395.7 1.4 fusion.20
  397.1 1.4 fusion.18
  398.6 1.4 fusion.22
  400.7 2.1 collective-permute-start.7
  403.8 1.5 collective-permute-start.5
  405.9 19.7 %collective-permute-done.7 = bf16[2,2,2,1,64,512]{5,4,3,2,1,0:T(8,128)(2,1)S(1)} collective-permute-done((bf16[2,2,2,1,64,512]{5,4,3,2,1,0:T(8,128)(2,1)S(1)}, bf16[2,2,2,1,64,512]{5,4,3,2,1,0:T(8,128)(2,1)S(1)}, u32[]{:S(2)}, u32[]{:S(2)}) %collective-permute-start.7) | collective-permute-done | bytes 524320 | tf_op jit(solution)/shard_map/ppermute | solution.py:329
  426.7 19.3 %collective-permute-done.8 = bf16[2,2,1,1,64,512]{5,4,3,2,1,0:T(8,128)(2,1)S(1)} collective-permute-done((bf16[2,2,1,1,64,512]{5,4,3,2,1,0:T(8,128)(2,1)S(1)}, bf16[2,2,1,1,64,512]{5,4,3,2,1,0:T(8,128)(2,1)S(1)}, u32[]{:S(2)}, u32[]{:S(2)}) %collective-permute-start.8) | collective-permute-done | bytes 262176 | tf_op jit(solution)/shard_map/ppermute | solution.py:329
  446.0 8.8 %collective-permute-done.6 = bf16[2,2,1,1,64,2048]{5,4,3,2,1,0:T(8,128)(2,1)S(1)} collective-permute-done((bf16[2,2,1,1,64,2048]{5,4,3,2,1,0:T(8,128)(2,1)S(1)}, bf16[2,2,1,1,64,2048]{5,4,3,2,1,0:T(8,128)(2,1)S(1)}, u32[]{:S(2)}, u32[]{:S(2)}) %collective-permute-start.6) | collective-permute-done | bytes 1048608 | tf_op jit(solution)/shard_map/ppermute | solution.py:329
  458.0 8.2 %unproject0.1 = (f32[512,1024]{1,0:T(8,128)S(1)}, bf16[3,1024,512]{2,1,0:T(8,128)(2,1)}, f32[3,1,512]{2,1,0:T(1,128)S(1)}) custom-call(s32[1]{0:T(128)} %bitcast.20.which_ref, bf16[512,1024]{1,0:T(8,128)(2,1)S(1)} %get-tuple-element.72.in_ref, bf16[16,6,64,256]{3,2,1,0:T(8,128)(2,1)} %all-to-all-done.3.back_ref, bf16[1024,3072]{1,0:T(8,128)(2,1)} %wv_ref.5, ...), custom_call_target="tpu_custom_call" | custom-call | flops 3221225472 | bytes 12582912 | tf_op jit(solution)/shard_map/unproject0/pallas_call | solution.py:899
  466.3 11.1 %unproject1.1 = (bf16[3,1024,512]{2,1,0:T(8,128)(2,1)}, bf16[512,1024]{1,0:T(8,128)(2,1)}, bf16[16,16,1024]{2,1,0:T(8,128)(2,1)}) custom-call(s32[1]{0:T(128)} %bitcast.which_ref.pack_ref, bf16[512,1024]{1,0:T(8,128)(2,1)S(1)} %get-tuple-element.72.in_ref, bf16[16,6,64,256]{3,2,1,0:T(8,128)(2,1)} %all-to-all-done.3.back_ref, bf16[1024,3072]{1,0:T(8,128)(2,1)} %wv_ref.5, ...), custom_call_target="tpu_custom_call" | custom-call | flops 3221225472 | bytes 12582912 | tf_op jit(solution)/shard_map/unproject1/pallas_call | solution.py:899
  477.4 9.2 %all-to-all-start.4 = ((bf16[16,16,1024]{2,1,0:T(8,128)(2,1)}), bf16[16,16,1024]{2,1,0:T(8,128)(2,1)S(1)}, u32[]{:S(2)}, u32[]{:S(2)}) async-start(bf16[16,16,1024]{2,1,0:T(8,128)(2,1)} %get-tuple-element.106), calls=%async_computation.4 | async-start | bytes 1048576 | tf_op jit(solution)/shard_map/all_to_all | solution.py:1158
  487.4 2.1 collective-permute-start.18
  489.5 1.9 collective-permute-start.15
  491.5 2.1 fusion.76
  493.6 1.4 constant_dynamic-slice_fusion
  496.2 5.4 all-to-all-done.4
  509.1 2.1 fusion.77
  512.7 10.3 %collective-permute-done.15 = bf16[2,1,1,1,128,1024]{5,4,3,2,1,0:T(8,128)(2,1)} collective-permute-done((bf16[2,1,1,1,128,1024]{5,4,3,2,1,0:T(8,128)(2,1)}, bf16[2,1,1,1,128,1024]{5,4,3,2,1,0:T(8,128)(2,1)}, u32[]{:S(2)}, u32[]{:S(2)}) %collective-permute-start.15) | collective-permute-done | bytes 524320 | tf_op jit(solution)/shard_map/ppermute | solution.py:329
  523.5 1.5 collective-permute-start.26
  525.0 1.5 collective-permute-start.21
  526.5 2.5 collective-permute-start.19
  531.6 2.5 collective-permute-start.13
  534.6 7.5 %collective-permute-done.26 = bf16[3,2,2,1,2,64,256]{6,5,0,4,3,2,1:T(8,128)(2,1)S(1)} collective-permute-done((bf16[3,2,2,1,2,64,256]{6,5,0,4,3,2,1:T(8,128)(2,1)S(1)}, bf16[3,2,2,1,2,64,256]{6,5,0,4,3,2,1:T(8,128)(2,1)S(1)}, u32[]{:S(2)}, u32[]{:S(2)}) %collective-permute-start.26) | collective-permute-done | bytes 786464 | tf_op jit(solution)/shard_map/ppermute | solution.py:329
  542.4 1.5 collective-permute-start.27
  544.2 1.5 collective-permute-start.22
  545.9 4.1 collective-permute-done.16
  556.1 3.7 collective-permute-done.28
  559.8 2.3 collective-permute-start.29
  562.1 2.6 collective-permute-done.23
  565.1 2.9 collective-permute-done.29
  568.2 2.5 collective-permute-done.24
  572.0 1.8 settle.1
  (309 shorter events, 65.6 us)
Async XLA Ops:
  7.4 3.7 copy-start.1
  7.5 3.7 copy-start.7
  27.0 8.5 %slice-start = ((f32[6144]{0:T(1024)}), f32[4096]{0:T(1024)S(1)}, s32[]{:S(2)}) async-start(f32[6144]{0:T(1024)} %param.23), calls=%async_computation.5 | async-start | bytes 32768 | tf_op jit(solution)/shard_map/slice | solution.py:994
  27.0 69.4 %all-to-all-start = ((bf16[16,6,64,256]{3,2,1,0:T(8,128)(2,1)}), bf16[16,6,64,256]{3,2,1,0:T(8,128)(2,1)}, u32[]{:S(2)}, u32[]{:S(2)}) async-start(bf16[16,6,64,256]{3,2,1,0:T(8,128)(2,1)} %copy-done.3), calls=%async_computation | async-start | bytes 6291456 | tf_op jit(solution)/shard_map/all_to_all | solution.py:984
  35.6 4.7 copy-start.2
  42.9 53.6 %copy-start.12 = (s32[1,32]{1,0:T(1,128)S(1)}, s32[1,32]{1,0:T(1,128)}, u32[]{:S(2)}) copy-start(s32[1,32]{1,0:T(1,128)} %param.20) | copy-start | bytes 388
  151.8 15.6 %copy-start.51 = (s32[1,2]{1,0:T(1,128)S(1)}, s32[1,2]{1,0:T(1,128)}, u32[]{:S(2)}) copy-start(s32[1,2]{1,0:T(1,128)} %param.18) | copy-start | bytes 28
  151.8 31.3 %all-to-all-start.1 = ((bf16[16,2,64,256]{3,2,1,0:T(8,128)(2,1)}), bf16[16,2,64,256]{3,2,1,0:T(8,128)(2,1)}, u32[]{:S(2)}, u32[]{:S(2)}) async-start(bf16[16,2,64,256]{3,2,1,0:T(8,128)(2,1)} %copy-done.6), calls=%async_computation.1 | async-start | bytes 2097152 | tf_op jit(solution)/shard_map/all_to_all | solution.py:987
  213.6 42.1 %collective-permute-start.1 = (bf16[1024,2048]{1,0:T(8,128)(2,1)}, bf16[1024,2048]{1,0:T(8,128)(2,1)}, u32[]{:S(2)}, u32[]{:S(2)}) collective-permute-start(bf16[1024,2048]{1,0:T(8,128)(2,1)} %get-tuple-element.95), channel_id=1, source_target_pairs={{0,16},{16,0},{1,17},{17,1},{2,18},{18,2},{3,19},{19,3},{4,20},{20... | collective-permute-start | bytes 12582920 | tf_op jit(solution)/shard_map/ppermute | solution.py:329
  213.7 52.0 %collective-permute-start = (bf16[2048,1024]{1,0:T(8,128)(2,1)}, bf16[2048,1024]{1,0:T(8,128)(2,1)}, u32[]{:S(2)}, u32[]{:S(2)}) collective-permute-start(bf16[2048,1024]{1,0:T(8,128)(2,1)} %get-tuple-element.93), channel_id=1, source_target_pairs={{0,16},{16,0},{1,17},{17,1},{2,18},{18,2},{3,19},{19,3},{4,20},{20... | collective-permute-start | bytes 12582920 | tf_op jit(solution)/shard_map/ppermute | solution.py:329
  214.3 23.2 %copy-start.50 = (f32[1,2048]{1,0:T(1,128)S(1)}, f32[1,2048]{1,0:T(1,128)}, u32[]{:S(2)}) copy-start(f32[1,2048]{1,0:T(1,128)} %get-tuple-element.84) | copy-start | bytes 24580
  214.3 24.1 %copy-start.8 = (f32[1024]{0:T(1024)S(1)}, f32[1024]{0:T(1024)}, u32[]{:S(2)}) copy-start(f32[1024]{0:T(1024)} %param.31) | copy-start | bytes 12292
  250.0 40.1 %all-to-all-start.2 = ((bf16[16,3,64,256]{3,2,1,0:T(8,128)(2,1)}), bf16[16,3,64,256]{3,2,1,0:T(8,128)(2,1)}, u32[]{:S(2)}, u32[]{:S(2)}) async-start(bf16[16,3,64,256]{3,2,1,0:T(8,128)(2,1)} %copy-done.5), calls=%async_computation.2 | async-start | bytes 3145728 | tf_op jit(solution)/shard_map/all_to_all | solution.py:984
  255.7 9.9 %copy-start.19 = (bf16[2048,1024]{1,0:T(8,128)(2,1)S(1)}, bf16[2048,1024]{1,0:T(8,128)(2,1)}, u32[]{:S(2)}) copy-start(bf16[2048,1024]{1,0:T(8,128)(2,1)} %get-tuple-element.92) | copy-start | bytes 12582916
  263.7 63.1 %collective-permute-start.4 = (bf16[2,2,1,2,64,2048]{5,4,3,2,1,0:T(8,128)(2,1)}, bf16[2,2,1,2,64,2048]{5,4,3,2,1,0:T(8,128)(2,1)}, u32[]{:S(2)}, u32[]{:S(2)}) collective-permute-start(bf16[2,2,1,2,64,2048]{5,4,3,2,1,0:T(8,128)(2,1)} %get-tuple-element.135), channel_id=1, source_target_pairs={{0,2},{1,3},{2,0},{3,1},{4,6},{5,7},{6,4},{7,5},{8,10},{9,11},{10,... | collective-permute-start | bytes 6291464 | tf_op jit(solution)/shard_map/ppermute | solution.py:329
  265.7 8.0 %copy-start.10 = (bf16[512,1024]{1,0:T(8,128)(2,1)S(1)}, bf16[512,1024]{1,0:T(8,128)(2,1)}, u32[]{:S(2)}) copy-start(bf16[512,1024]{1,0:T(8,128)(2,1)} %copy-done.9) | copy-start | bytes 3145732
  265.7 8.0 %copy-start.29 = (bf16[16,1,64,256]{3,2,1,0:T(8,128)(2,1)S(1)}, bf16[16,1,64,256]{3,2,1,0:T(8,128)(2,1)}, u32[]{:S(2)}) copy-start(bf16[16,1,64,256]{3,2,1,0:T(8,128)(2,1)} %copy-done.28) | copy-start | bytes 1572868
  265.7 8.0 %copy-start.31 = (bf16[16,1,64,256]{3,2,1,0:T(8,128)(2,1)S(1)}, bf16[16,1,64,256]{3,2,1,0:T(8,128)(2,1)}, u32[]{:S(2)}) copy-start(bf16[16,1,64,256]{3,2,1,0:T(8,128)(2,1)} %copy-done.30) | copy-start | bytes 1572868
  272.2 58.6 %collective-permute-start.3 = (bf16[2,2,2,1,128,1024]{5,4,3,2,1,0:T(8,128)(2,1)}, bf16[2,2,2,1,128,1024]{5,4,3,2,1,0:T(8,128)(2,1)}, u32[]{:S(2)}, u32[]{:S(2)}) collective-permute-start(bf16[2,2,2,1,128,1024]{5,4,3,2,1,0:T(8,128)(2,1)} %get-tuple-element.137), channel_id=1, source_target_pairs={{0,1},{1,0},{2,3},{3,2},{4,5},{5,4},{6,7},{7,6},{8,9},{9,8},{10,11... | collective-permute-start | bytes 6291464 | tf_op jit(solution)/shard_map/ppermute | solution.py:329
  275.4 48.4 %collective-permute-start.2 = (bf16[1024,512]{1,0:T(8,128)(2,1)}, bf16[1024,512]{1,0:T(8,128)(2,1)S(1)}, u32[]{:S(2)}, u32[]{:S(2)}) collective-permute-start(bf16[1024,512]{1,0:T(8,128)(2,1)} %convolution_convert_fusion), channel_id=1, source_target_pairs={{0,16},{16,0},{1,17},{17,1},{2,18},{18,2},{3,19},{19,3},{4,20},{20... | collective-permute-start | bytes 3145736 | tf_op jit(solution)/shard_map/ppermute | solution.py:329
  327.1 3.8 copy-start.18
  330.3 3.7 copy-start.35
  375.6 82.4 %all-to-all-start.3 = ((bf16[16,6,64,256]{3,2,1,0:T(8,128)(2,1)}), bf16[16,6,64,256]{3,2,1,0:T(8,128)(2,1)}, u32[]{:S(2)}, u32[]{:S(2)}) async-start(bf16[16,6,64,256]{3,2,1,0:T(8,128)(2,1)} %attend_back1.1), calls=%async_computation.3 | async-start | bytes 6291456 | tf_op jit(solution)/shard_map/all_to_all | solution.py:987
  386.0 6.6 %collective-permute-start.9 = (bf16[16,16,1024]{2,1,0:T(8,128)(2,1)}, bf16[16,16,1024]{2,1,0:T(8,128)(2,1)S(1)}, u32[]{:S(2)}, u32[]{:S(2)}) collective-permute-start(bf16[16,16,1024]{2,1,0:T(8,128)(2,1)} %bitcast.70), channel_id=1, source_target_pairs={{0,16},{16,0},{1,17},{17,1},{2,18},{18,2},{3,19},{19,3},{4,20},{20... | collective-permute-start | bytes 1572872 | tf_op jit(solution)/shard_map/ppermute | solution.py:329
  392.6 7.4 %copy-start.26 = (bf16[16,16,1024]{2,1,0:T(8,128)(2,1)}, bf16[16,16,1024]{2,1,0:T(8,128)(2,1)S(1)}, u32[]{:S(2)}) copy-start(bf16[16,16,1024]{2,1,0:T(8,128)(2,1)S(1)} %collective-permute-done.9) | copy-start | bytes 1572868
  400.0 26.0 %copy-start.46 = (f32[32,64]{1,0:T(8,128)}, f32[32,64]{1,0:T(8,128)S(1)}, u32[]{:S(2)}) copy-start(f32[32,64]{1,0:T(8,128)S(1)} %fusion.22) | copy-start | bytes 24580
  400.0 3.8 copy-start.38
  400.0 25.6 %copy-start.33 = (bf16[2,2,2,1,64,512]{5,4,3,2,1,0:T(8,128)(2,1)S(1)}, bf16[2,2,2,1,64,512]{5,4,3,2,1,0:T(8,128)(2,1)}, u32[]{:S(2)}) copy-start(bf16[2,2,2,1,64,512]{5,4,3,2,1,0:T(8,128)(2,1)} %get-tuple-element.152) | copy-start | bytes 1572868
  400.7 54.0 %copy-start.20 = (bf16[2,2,1,1,64,2048]{5,4,3,2,1,0:T(8,128)(2,1)S(1)}, bf16[2,2,1,1,64,2048]{5,4,3,2,1,0:T(8,128)(2,1)}, u32[]{:S(2)}) copy-start(bf16[2,2,1,1,64,2048]{5,4,3,2,1,0:T(8,128)(2,1)} %get-tuple-element.138) | copy-start | bytes 3145732
  400.7 24.9 %collective-permute-start.7 = (bf16[2,2,2,1,64,512]{5,4,3,2,1,0:T(8,128)(2,1)S(1)}, bf16[2,2,2,1,64,512]{5,4,3,2,1,0:T(8,128)(2,1)S(1)}, u32[]{:S(2)}, u32[]{:S(2)}) collective-permute-start(bf16[2,2,2,1,64,512]{5,4,3,2,1,0:T(8,128)(2,1)S(1)} %copy-done.40), channel_id=1, source_target_pairs={{0,1},{1,0},{2,3},{3,2},{4,5},{5,4},{6,7},{7,6},{8,9},{9,8},{10,11... | collective-permute-start | bytes 1572872 | tf_op jit(solution)/shard_map/ppermute | solution.py:329
  402.9 51.8 %collective-permute-start.6 = (bf16[2,2,1,1,64,2048]{5,4,3,2,1,0:T(8,128)(2,1)S(1)}, bf16[2,2,1,1,64,2048]{5,4,3,2,1,0:T(8,128)(2,1)S(1)}, u32[]{:S(2)}, u32[]{:S(2)}) collective-permute-start(bf16[2,2,1,1,64,2048]{5,4,3,2,1,0:T(8,128)(2,1)S(1)} %copy-done.36), channel_id=1, source_target_pairs={{0,1},{1,0},{2,3},{3,2},{4,5},{5,4},{6,7},{7,6},{8,9},{9,8},{10,11... | collective-permute-start | bytes 3145736 | tf_op jit(solution)/shard_map/ppermute | solution.py:329
  403.8 52.2 %collective-permute-start.5 = (bf16[2,2,1,1,128,1024]{5,4,3,2,1,0:T(8,128)(2,1)S(1)}, bf16[2,2,1,1,128,1024]{5,4,3,2,1,0:T(8,128)(2,1)S(1)}, u32[]{:S(2)}, u32[]{:S(2)}) collective-permute-start(bf16[2,2,1,1,128,1024]{5,4,3,2,1,0:T(8,128)(2,1)S(1)} %copy-done.38), channel_id=1, source_target_pairs={{0,2},{1,3},{2,0},{3,1},{4,6},{5,7},{6,4},{7,5},{8,10},{9,11},{10,... | collective-permute-start | bytes 3145736 | tf_op jit(solution)/shard_map/ppermute | solution.py:329
  425.8 30.2 %copy-start.21 = (bf16[2,2,1,1,128,1024]{5,4,3,2,1,0:T(8,128)(2,1)S(1)}, bf16[2,2,1,1,128,1024]{5,4,3,2,1,0:T(8,128)(2,1)}, u32[]{:S(2)}) copy-start(bf16[2,2,1,1,128,1024]{5,4,3,2,1,0:T(8,128)(2,1)} %get-tuple-element.140) | copy-start | bytes 3145732
  425.8 20.1 %collective-permute-start.8 = (bf16[2,2,1,1,64,512]{5,4,3,2,1,0:T(8,128)(2,1)S(1)}, bf16[2,2,1,1,64,512]{5,4,3,2,1,0:T(8,128)(2,1)S(1)}, u32[]{:S(2)}, u32[]{:S(2)}) collective-permute-start(bf16[2,2,1,1,64,512]{5,4,3,2,1,0:T(8,128)(2,1)S(1)} %get-tuple-element.167), channel_id=1, source_target_pairs={{0,2},{1,3},{2,0},{3,1},{4,6},{5,7},{6,4},{7,5},{8,10},{9,11},{10,... | collective-permute-start | bytes 786440 | tf_op jit(solution)/shard_map/ppermute | solution.py:329
  446.0 8.8 %copy-start.43 = (bf16[2,1,1,1,64,512]{5,4,3,2,1,0:T(8,128)(2,1)}, bf16[2,1,1,1,64,512]{5,4,3,2,1,0:T(8,128)(2,1)S(1)}, u32[]{:S(2)}) copy-start(bf16[2,1,1,1,64,512]{5,4,3,2,1,0:T(8,128)(2,1)S(1)} %get-tuple-element.175) | copy-start | bytes 393220
  477.4 24.2 %all-to-all-start.4 = ((bf16[16,16,1024]{2,1,0:T(8,128)(2,1)}), bf16[16,16,1024]{2,1,0:T(8,128)(2,1)S(1)}, u32[]{:S(2)}, u32[]{:S(2)}) async-start(bf16[16,16,1024]{2,1,0:T(8,128)(2,1)} %get-tuple-element.106), calls=%async_computation.4 | async-start | bytes 1048576 | tf_op jit(solution)/shard_map/all_to_all | solution.py:1158
  487.4 35.8 %collective-permute-start.18 = (bf16[2,1,1,1,64,512]{5,4,3,2,1,0:T(8,128)(2,1)}, bf16[2,1,1,1,64,512]{5,4,3,2,1,0:T(8,128)(2,1)S(1)}, u32[]{:S(2)}, u32[]{:S(2)}) collective-permute-start(bf16[2,1,1,1,64,512]{5,4,3,2,1,0:T(8,128)(2,1)} %copy-done.43), channel_id=1, source_target_pairs={{0,4},{1,5},{2,6},{3,7},{4,0},{5,1},{6,2},{7,3},{8,12},{9,13},{10,... | collective-permute-start | bytes 393224 | tf_op jit(solution)/shard_map/ppermute | solution.py:329
  489.5 23.3 %collective-permute-start.12 = (bf16[2,1,1,1,64,2048]{5,4,3,2,1,0:T(8,128)(2,1)}, bf16[2,1,1,1,64,2048]{5,4,3,2,1,0:T(8,128)(2,1)}, u32[]{:S(2)}, u32[]{:S(2)}) collective-permute-start(bf16[2,1,1,1,64,2048]{5,4,3,2,1,0:T(8,128)(2,1)} %copy-done.41), channel_id=1, source_target_pairs={{0,4},{1,5},{2,6},{3,7},{4,0},{5,1},{6,2},{7,3},{8,12},{9,13},{10,... | collective-permute-start | bytes 1572872 | tf_op jit(solution)/shard_map/ppermute | solution.py:329
  489.5 33.5 %collective-permute-start.15 = (bf16[2,1,1,1,128,1024]{5,4,3,2,1,0:T(8,128)(2,1)}, bf16[2,1,1,1,128,1024]{5,4,3,2,1,0:T(8,128)(2,1)}, u32[]{:S(2)}, u32[]{:S(2)}) collective-permute-start(bf16[2,1,1,1,128,1024]{5,4,3,2,1,0:T(8,128)(2,1)} %copy-done.42), channel_id=1, source_target_pairs={{0,4},{1,5},{2,6},{3,7},{4,0},{5,1},{6,2},{7,3},{8,12},{9,13},{10,... | collective-permute-start | bytes 1572872 | tf_op jit(solution)/shard_map/ppermute | solution.py:329
  491.5 17.6 %collective-permute-start.11 = (bf16[3,1024,512]{2,1,0:T(8,128)(2,1)}, bf16[3,1024,512]{2,1,0:T(8,128)(2,1)}, u32[]{:S(2)}, u32[]{:S(2)}) collective-permute-start(bf16[3,1024,512]{2,1,0:T(8,128)(2,1)} %get-tuple-element.108), channel_id=1, source_target_pairs={{0,16},{16,0},{1,17},{17,1},{2,18},{18,2},{3,19},{19,3},{4,20},{20... | collective-permute-start | bytes 9437192 | tf_op jit(solution)/shard_map/ppermute | solution.py:329
  495.0 7.4 %copy-start.45 = (f32[32,64]{1,0:T(8,128)S(1)}, f32[32,64]{1,0:T(8,128)}, u32[]{:S(2)}) copy-start(f32[32,64]{1,0:T(8,128)} %copy-done.44) | copy-start | bytes 24580
  501.7 2.3 collective-permute-start.10
  512.6 10.6 %copy-start.24 = (bf16[3,2,2,1,2,64,256]{6,5,4,3,2,1,0:T(8,128)(2,1)S(1)}, bf16[3,2,2,1,2,64,256]{6,5,4,3,2,1,0:T(8,128)(2,1)}, u32[]{:S(2)}) copy-start(bf16[3,2,2,1,2,64,256]{6,5,4,3,2,1,0:T(8,128)(2,1)} %get-tuple-element.157) | copy-start | bytes 2359300
  523.0 6.0 %copy-start.34 = (bf16[2,1,1,1,128,1024]{5,4,3,2,1,0:T(8,128)(2,1)S(1)}, bf16[2,1,1,1,128,1024]{5,4,3,2,1,0:T(8,128)(2,1)}, u32[]{:S(2)}) copy-start(bf16[2,1,1,1,128,1024]{5,4,3,2,1,0:T(8,128)(2,1)} %get-tuple-element.117) | copy-start | bytes 1572868
  523.2 7.4 %copy-start.32 = (bf16[2,1,1,1,64,2048]{5,4,3,2,1,0:T(8,128)(2,1)S(1)}, bf16[2,1,1,1,64,2048]{5,4,3,2,1,0:T(8,128)(2,1)}, u32[]{:S(2)}) copy-start(bf16[2,1,1,1,64,2048]{5,4,3,2,1,0:T(8,128)(2,1)} %get-tuple-element.111) | copy-start | bytes 1572868
  523.2 10.9 %copy-start.22 = (bf16[3,2,2,1,2,64,256]{6,5,4,3,2,1,0:T(8,128)(2,1)S(1)}, bf16[3,2,2,1,2,64,256]{6,5,4,3,2,1,0:T(8,128)(2,1)}, u32[]{:S(2)}) copy-start(bf16[3,2,2,1,2,64,256]{6,5,4,3,2,1,0:T(8,128)(2,1)} %get-tuple-element.156) | copy-start | bytes 2359300
  523.5 10.8 %copy-start.23 = (bf16[3,2,2,2,1,64,256]{6,5,4,3,2,1,0:T(8,128)(2,1)S(1)}, bf16[3,2,2,2,1,64,256]{6,5,4,3,2,1,0:T(8,128)(2,1)}, u32[]{:S(2)}) copy-start(bf16[3,2,2,2,1,64,256]{6,5,4,3,2,1,0:T(8,128)(2,1)} %get-tuple-element.162) | copy-start | bytes 2359300
  523.5 18.6 %collective-permute-start.26 = (bf16[3,2,2,1,2,64,256]{6,5,0,4,3,2,1:T(8,128)(2,1)S(1)}, bf16[3,2,2,1,2,64,256]{6,5,0,4,3,2,1:T(8,128)(2,1)S(1)}, u32[]{:S(2)}, u32[]{:S(2)}) collective-permute-start(bf16[3,2,2,1,2,64,256]{6,5,0,4,3,2,1:T(8,128)(2,1)S(1)} %add_convert_fusion.11), channel_id=1, source_target_pairs={{0,2},{1,3},{2,0},{3,1},{4,6},{5,7},{6,4},{7,5},{8,10},{9,11},{10,... | collective-permute-start | bytes 2359304 | tf_op jit(solution)/shard_map/ppermute | solution.py:329
  525.0 18.9 %collective-permute-start.21 = (bf16[3,2,2,2,1,64,256]{6,5,0,4,3,2,1:T(8,128)(2,1)S(1)}, bf16[3,2,2,2,1,64,256]{6,5,0,4,3,2,1:T(8,128)(2,1)S(1)}, u32[]{:S(2)}, u32[]{:S(2)}) collective-permute-start(bf16[3,2,2,2,1,64,256]{6,5,0,4,3,2,1:T(8,128)(2,1)S(1)} %add_convert_fusion.10), channel_id=1, source_target_pairs={{0,1},{1,0},{2,3},{3,2},{4,5},{5,4},{6,7},{7,6},{8,9},{9,8},{10,11... | collective-permute-start | bytes 2359304 | tf_op jit(solution)/shard_map/ppermute | solution.py:329
  526.5 19.2 %collective-permute-start.19 = (bf16[1,1,1,1,64,512]{5,4,3,2,1,0:T(8,128)(2,1)S(1)}, bf16[1,1,1,1,64,512]{5,4,3,2,1,0:T(8,128)(2,1)S(1)}, u32[]{:S(2)}, u32[]{:S(2)}) collective-permute-start(bf16[1,1,1,1,64,512]{5,4,3,2,1,0:T(8,128)(2,1)S(1)} %add_convert_fusion.43), channel_id=1, source_target_pairs={{0,8},{1,9},{2,10},{3,11},{4,12},{5,13},{6,14},{7,15},{8,0},{9,1},... | collective-permute-start | bytes 196616 | tf_op jit(solution)/shard_map/ppermute | solution.py:329
  530.0 19.9 %collective-permute-start.16 = (bf16[1,1,1,1,128,1024]{5,4,3,2,1,0:T(8,128)(2,1)S(1)}, bf16[1,1,1,1,128,1024]{5,4,3,2,1,0:T(8,128)(2,1)S(1)}, u32[]{:S(2)}, u32[]{:S(2)}) collective-permute-start(bf16[1,1,1,1,128,1024]{5,4,3,2,1,0:T(8,128)(2,1)S(1)} %add_convert_fusion.23), channel_id=1, source_target_pairs={{0,8},{1,9},{2,10},{3,11},{4,12},{5,13},{6,14},{7,15},{8,0},{9,1},... | collective-permute-start | bytes 786440 | tf_op jit(solution)/shard_map/ppermute | solution.py:329
  531.6 23.3 %collective-permute-start.13 = (bf16[1,1,1,1,64,2048]{5,4,3,2,1,0:T(8,128)(2,1)S(1)}, bf16[1,1,1,1,64,2048]{5,4,3,2,1,0:T(8,128)(2,1)S(1)}, u32[]{:S(2)}, u32[]{:S(2)}) collective-permute-start(bf16[1,1,1,1,64,2048]{5,4,3,2,1,0:T(8,128)(2,1)S(1)} %add_convert_fusion.26), channel_id=1, source_target_pairs={{0,8},{1,9},{2,10},{3,11},{4,12},{5,13},{6,14},{7,15},{8,0},{9,1},... | collective-permute-start | bytes 786440 | tf_op jit(solution)/shard_map/ppermute | solution.py:329
  542.4 9.4 %collective-permute-start.27 = (bf16[3,2,2,1,1,64,256]{6,5,0,4,3,2,1:T(8,128)(2,1)S(1)}, bf16[3,2,2,1,1,64,256]{6,5,0,4,3,2,1:T(8,128)(2,1)S(1)}, u32[]{:S(2)}, u32[]{:S(2)}) collective-permute-start(bf16[3,2,2,1,1,64,256]{6,5,0,4,3,2,1:T(8,128)(2,1)S(1)} %get-tuple-element.155), channel_id=1, source_target_pairs={{0,1},{1,0},{2,3},{3,2},{4,5},{5,4},{6,7},{7,6},{8,9},{9,8},{10,11... | collective-permute-start | bytes 1179656 | tf_op jit(solution)/shard_map/ppermute | solution.py:329
  544.2 9.1 %collective-permute-start.22 = (bf16[3,2,2,1,1,64,256]{6,5,0,4,3,2,1:T(8,128)(2,1)S(1)}, bf16[3,2,2,1,1,64,256]{6,5,0,4,3,2,1:T(8,128)(2,1)S(1)}, u32[]{:S(2)}, u32[]{:S(2)}) collective-permute-start(bf16[3,2,2,1,1,64,256]{6,5,0,4,3,2,1:T(8,128)(2,1)S(1)} %get-tuple-element.161), channel_id=1, source_target_pairs={{0,2},{1,3},{2,0},{3,1},{4,6},{5,7},{6,4},{7,5},{8,10},{9,11},{10,... | collective-permute-start | bytes 1179656 | tf_op jit(solution)/shard_map/ppermute | solution.py:329
  545.8 25.7 %collective-permute-start.20 = (bf16[64,512]{1,0:T(8,128)(2,1)S(1)}, bf16[64,512]{1,0:T(8,128)(2,1)S(1)}, u32[]{:S(2)}, u32[]{:S(2)}) collective-permute-start(bf16[64,512]{1,0:T(8,128)(2,1)S(1)} %fusion.36.refs_4_), channel_id=1, source_target_pairs={{0,16},{16,0},{1,17},{17,1},{2,18},{18,2},{3,19},{19,3},{4,20},{20... | collective-permute-start | bytes 196616 | tf_op jit(solution)/shard_map/ppermute | solution.py:329
  551.0 20.5 %collective-permute-start.17 = (bf16[128,1024]{1,0:T(8,128)(2,1)S(1)}, bf16[128,1024]{1,0:T(8,128)(2,1)S(1)}, u32[]{:S(2)}, u32[]{:S(2)}) collective-permute-start(bf16[128,1024]{1,0:T(8,128)(2,1)S(1)} %fusion.27.refs_2_), channel_id=1, source_target_pairs={{0,16},{16,0},{1,17},{17,1},{2,18},{18,2},{3,19},{19,3},{4,20},{20... | collective-permute-start | bytes 786440 | tf_op jit(solution)/shard_map/ppermute | solution.py:329
  551.9 18.9 %copy-start.48 = (f32[4096]{0:T(1024)S(1)}, f32[4096]{0:T(1024)}, u32[]{:S(2)}) copy-start(f32[4096]{0:T(1024)} %get-tuple-element.244) | copy-start | bytes 49156
  551.9 7.8 %collective-permute-start.28 = (bf16[3,2,1,1,1,64,256]{6,5,0,4,3,2,1:T(8,128)(2,1)S(1)}, bf16[3,2,1,1,1,64,256]{6,5,0,4,3,2,1:T(8,128)(2,1)S(1)}, u32[]{:S(2)}, u32[]{:S(2)}) collective-permute-start(bf16[3,2,1,1,1,64,256]{6,5,0,4,3,2,1:T(8,128)(2,1)S(1)} %get-tuple-element.171), channel_id=1, source_target_pairs={{0,4},{1,5},{2,6},{3,7},{4,0},{5,1},{6,2},{7,3},{8,12},{9,13},{10,... | collective-permute-start | bytes 589832 | tf_op jit(solution)/shard_map/ppermute | solution.py:329
  553.4 11.2 %collective-permute-start.23 = (bf16[3,2,1,1,1,64,256]{6,5,0,4,3,2,1:T(8,128)(2,1)S(1)}, bf16[3,2,1,1,1,64,256]{6,5,0,4,3,2,1:T(8,128)(2,1)S(1)}, u32[]{:S(2)}, u32[]{:S(2)}) collective-permute-start(bf16[3,2,1,1,1,64,256]{6,5,0,4,3,2,1:T(8,128)(2,1)S(1)} %get-tuple-element.173), channel_id=1, source_target_pairs={{0,4},{1,5},{2,6},{3,7},{4,0},{5,1},{6,2},{7,3},{8,12},{9,13},{10,... | collective-permute-start | bytes 589832 | tf_op jit(solution)/shard_map/ppermute | solution.py:329
  556.0 15.4 %collective-permute-start.14 = (bf16[64,2048]{1,0:T(8,128)(2,1)S(1)}, bf16[64,2048]{1,0:T(8,128)(2,1)S(1)}, u32[]{:S(2)}, u32[]{:S(2)}) collective-permute-start(bf16[64,2048]{1,0:T(8,128)(2,1)S(1)} %fusion.26.refs_0_), channel_id=1, source_target_pairs={{0,16},{16,0},{1,17},{17,1},{2,18},{18,2},{3,19},{19,3},{4,20},{20... | collective-permute-start | bytes 786440 | tf_op jit(solution)/shard_map/ppermute | solution.py:329
  559.8 8.3 %collective-permute-start.29 = (bf16[3,1,1,1,1,64,256]{6,5,0,4,3,2,1:T(8,128)(2,1)S(1)}, bf16[3,1,1,1,1,64,256]{6,5,0,4,3,2,1:T(8,128)(2,1)S(1)}, u32[]{:S(2)}, u32[]{:S(2)}) collective-permute-start(bf16[3,1,1,1,1,64,256]{6,5,0,4,3,2,1:T(8,128)(2,1)S(1)} %add_convert_fusion.37), channel_id=1, source_target_pairs={{0,8},{1,9},{2,10},{3,11},{4,12},{5,13},{6,14},{7,15},{8,0},{9,1},... | collective-permute-start | bytes 294920 | tf_op jit(solution)/shard_map/ppermute | solution.py:329
  564.7 5.9 %collective-permute-start.24 = (bf16[3,1,1,1,1,64,256]{6,5,0,4,3,2,1:T(8,128)(2,1)S(1)}, bf16[3,1,1,1,1,64,256]{6,5,0,4,3,2,1:T(8,128)(2,1)S(1)}, u32[]{:S(2)}, u32[]{:S(2)}) collective-permute-start(bf16[3,1,1,1,1,64,256]{6,5,0,4,3,2,1:T(8,128)(2,1)S(1)} %add_convert_fusion.40), channel_id=1, source_target_pairs={{0,8},{1,9},{2,10},{3,11},{4,12},{5,13},{6,14},{7,15},{8,0},{9,1},... | collective-permute-start | bytes 294920 | tf_op jit(solution)/shard_map/ppermute | solution.py:329
  568.1 3.3 collective-permute-start.30
  570.7 1.4 collective-permute-start.25
  (25 other events, 40.0 us)

commit v7 on v6

--- a/solution.py
+++ b/solution.py
@@ -68,7 +68,7 @@
     return whole(jnp.cos), whole(jnp.sin)
 
 
-def walk_frames(frames, per_device, parts, segments_ref, live_ref, list_ref, visit):
+def walk_frames(frames, per_device, segments_ref, live_ref, list_ref, visit):
     def step(source, held):
         for place in range(per_device):
             frame = source * per_device + place
@@ -76,8 +76,7 @@
             fresh = (frame == 0) | (segments_ref[frame] != segments_ref[before])
             held = jnp.where(fresh, 0, held)
             list_ref[held] = frame
-            if place in parts:
-                visit(source, place, frame, held + 1)
+            visit(source, place, frame, held + 1)
             held = held + jnp.where(live_ref[frame] == 1, 1, 0)
         return held
 
@@ -92,7 +91,7 @@
             both = jnp.concatenate(
                 [x_ref[source, place], x_ref[source, per_device + place]], axis=0
             )
-            kv_ref[source * per_device + place] = both.astype(F32).T.astype(BF16)
+            kv_ref[source * per_device + place] = both.T
         return carry
 
     lax.fori_loop(0, frames // per_device, turn, 0)
@@ -132,6 +131,12 @@
         carry = join([frame], None)
         carry = lax.fori_loop(
             0,
+            lax.div(others, 4),
+            lambda index, state: join([list_ref[4 * index + nth] for nth in range(4)], state),
+            carry,
+        )
+        carry = lax.fori_loop(
+            lax.div(others, 4) * 2,
             lax.div(others, 2),
             lambda index, state: join([list_ref[2 * index], list_ref[2 * index + 1]], state),
             carry,
@@ -147,7 +152,7 @@
         mix_ref[source, place] = result.astype(BF16)
         lse_ref[pl.ds(frame, 1), :] = top + jnp.log(total)
 
-    walk_frames(frames, per_device, range(per_device), segments_ref, live_ref, list_ref, visit)
+    walk_frames(frames, per_device, segments_ref, live_ref, list_ref, visit)
 
 
 def corners(values):
@@ -194,8 +199,6 @@
 
 def attend_back_kernel(
     per_device,
-    part,
-    last,
     segments_ref,
     live_ref,
     x_ref,
@@ -207,16 +210,8 @@
     sin_ref,
     *refs
 ):
-    if last:
-        before_ref, d_query_ref = refs[:2]
     out_ref, dkv_ref, list_ref = refs[-3:]
     frames = kv_ref.shape[0]
-
-    def clear(frame, carry):
-        dkv_ref[frame] = jnp.zeros((PATCHES, 2 * HEAD), F32)
-        return carry
-
-    lax.fori_loop(0, frames, clear, 0)
 
     def unturn(frame, values):
         lower = values[:HALF]
@@ -231,96 +226,85 @@
         blank = jnp.zeros_like(query)
         query_side = jnp.concatenate([query, blank], axis=0)
         d_mix_side = jnp.concatenate([blank, d_mix], axis=0)
+        turned = jnp.concatenate([query, d_mix], axis=0).T
+        first = lax.broadcasted_iota(jnp.int32, turned.shape, 1) < HEAD
+        nothing = jnp.zeros_like(turned)
         both = jnp.concatenate(
-            [query_side.astype(F32).T.astype(BF16), d_mix_side.astype(F32).T.astype(BF16)], axis=0
+            [jnp.where(first, turned, nothing), jnp.where(first, nothing, turned)], axis=0
         )
         lse = lse_ref[pl.ds(frame, 1), :]
         delta = jnp.sum(d_mix.astype(F32) * wide_ref[source, place], axis=0, keepdims=True)
 
-        def block(other):
+        def block(other, own=False):
             key_value = kv_ref[other]
             scores = jnp.dot(key_value, query_side, preferred_element_type=F32)
             d_weights = jnp.dot(key_value, d_mix_side, preferred_element_type=F32)
             weights = jnp.exp(scores - lse)
             d_scores = (weights * (d_weights - delta)).astype(BF16)
             sides = jnp.concatenate([d_scores, weights.astype(BF16)], axis=1)
-            dkv_ref[other] += jnp.dot(sides, both, preferred_element_type=F32)
+            d_both = jnp.dot(sides, both, preferred_element_type=F32)
+            if own:
+                dkv_ref[other] = d_both
+            else:
+                dkv_ref[other] += d_both
             key = x_ref[lax.div(other, per_device), lax.rem(other, per_device)]
             return jnp.dot(key, d_scores, preferred_element_type=F32)
 
+        others = count - 1
+        d_query = block(frame, True)
         d_query = lax.fori_loop(
             0,
-            lax.div(count, 2),
+            lax.div(others, 2),
             lambda index, state: state
             + block(list_ref[2 * index])
             + block(list_ref[2 * index + 1]),
-            jnp.zeros((HEAD, PATCHES), F32),
+            d_query,
         )
         d_query = lax.fori_loop(
             0,
-            lax.rem(count, 2),
-            lambda unused, state: state + block(list_ref[count - 1]),
+            lax.rem(others, 2),
+            lambda unused, state: state + block(list_ref[others - 1]),
             d_query,
         )
         d_query = unturn(frame, d_query * (HEAD**-0.5)).astype(BF16)
-        if last:
-            out_ref[source, 2 * per_device + part] = d_query
-        else:
-            out_ref[source] = d_query
-
-    walk_frames(frames, per_device, (part,), segments_ref, live_ref, list_ref, visit)
+        out_ref[source, 2 * per_device + place] = d_query
+
+    walk_frames(frames, per_device, segments_ref, live_ref, list_ref, visit)
 
     def finish(source, carry):
         for place in range(per_device):
             frame = source * per_device + place
-            both = (dkv_ref[frame] + before_ref[frame]).T
+            both = dkv_ref[frame].T
             out_ref[source, place] = unturn(frame, both[:HEAD]).astype(BF16)
             out_ref[source, per_device + place] = both[HEAD:].astype(BF16)
-        for place in range(part):
-            out_ref[source, 2 * per_device + place] = d_query_ref[source]
         return carry
 
-    if last:
-        lax.fori_loop(0, frames // per_device, finish, 0)
-
-
-def attend_back(
-    part, per_device, segments, live, x, kv, wide, lse, d_mix, cosine, sine, before, orders
-):
+    lax.fori_loop(0, frames // per_device, finish, 0)
+
+
+def attend_back(per_device, segments, live, x, kv, wide, lse, d_mix, cosine, sine, orders):
     sources = x.shape[0]
     frames = sources * per_device
-    pairs = sources * 6
-    last = part == per_device - 1
+    pairs = frames * 6
     args = [segments, live, x, kv, wide, lse, d_mix, cosine, sine]
-    dkv = (frames, PATCHES, 2 * HEAD)
-    lists = pltpu.SMEM((frames,), jnp.int32)
-    if last:
-        args += [before[1], before[0]]
-        outs = jax.ShapeDtypeStruct(x.shape, BF16)
-        out_specs = whole_spec()
-        scratch = [pltpu.VMEM(dkv, F32), lists]
-    else:
-        outs = (
-            jax.ShapeDtypeStruct((sources, HEAD, PATCHES), BF16),
-            jax.ShapeDtypeStruct(dkv, F32),
-        )
-        out_specs = (whole_spec(), whole_spec())
-        scratch = [lists]
     specs = [scalar_spec(), scalar_spec()] + [whole_spec()] * (len(args) - 2)
     orders = corners(orders)
     return pl.pallas_call(
-        functools.partial(attend_back_kernel, per_device, part, last),
-        out_shape=outs,
+        functools.partial(attend_back_kernel, per_device),
+        out_shape=jax.ShapeDtypeStruct(x.shape, BF16),
         in_specs=specs + [unread_spec()] * len(orders),
-        out_specs=out_specs,
-        scratch_shapes=scratch,
+        out_specs=whole_spec(),
+        scratch_shapes=[
+            pltpu.VMEM((frames, PATCHES, 2 * HEAD), F32),
+            pltpu.SMEM((frames,), jnp.int32),
+        ],
         cost_estimate=pl.CostEstimate(
             flops=pairs * 10 * PATCHES * PATCHES * 256,
             bytes_accessed=x.size * 2 * 5,
             transcendentals=pairs * PATCHES * PATCHES,
         ),
         compiler_params=pltpu.CompilerParams(vmem_limit_bytes=60 << 20),
-        name="attend_back%d" % part,
+        name="attend_back",
     )(*args, *orders)
 
 
@@ -1112,32 +1096,20 @@
         )
     mod_grad_early = functools.reduce(jnp.add, [each[4] for each in parts])
     mod_sum_early = (early_sum[:4] + early_sum[4:8]).reshape(4 * width)
-    before = None
-    for part in range(per_device):
-        orders = [each.stage() for each in sums]
-        if halves and part:
-            before = (out_sum.tie(before[0]), before[1])
-            orders.append(out_sum.stage())
-        before = attend_back(
-            part,
-            per_device,
-            clip_ids,
-            live,
-            x,
-            kv,
-            wide,
-            lse,
-            d_mix,
-            cos_all,
-            sin_all,
-            before,
-            orders,
-        )
-    back = to_tokens(before)
     orders = [each.stage() for each in sums]
+    result = attend_back(
+        per_device, clip_ids, live, x, kv, wide, lse, d_mix, cos_all, sin_all, orders
+    )
     if halves:
-        orders.append(out_sum.stage())
-        orders.append(out_sum.stage())
+        for each in sums:
+            result = each.tie(result)
+        result = out_sum.tie(result)
+    back = to_tokens(result)
+    orders = []
+    if halves:
+        for each in (up_sum, down_sum, out_sum):
+            each.stage()
+        orders = [each.stage() for each in (up_sum, down_sum, out_sum)]
     orders += [mod_grad_early] + [part[3] for part in parts]
     which = (1 - pack, pack) if halves else (pack * 0, pack * 0 + 1)
     d_in_theirs, qkv_theirs, bias_theirs = unproject(

time: 583 us -> 580 us (level)
  waiting for transfers between devices: 164 us -> 201 us
  Pallas kernels: 211 us -> 181 us
  starting transfers between devices: 76.2 us -> 68 us
    pallas_call x2 -> x1, Pallas kernels: 73.9 us -> 54.3 us  [attend_back(): pl.pallas_call(functools.partial(attend_back_kernel, per_device), out_sha...]
    all_to_all x2, waiting for transfers between devices: 62.9 us -> 81.7 us  [to_heads(): return lax.all_to_all(array, 'seq', 0, 0, tiled=True)]
    pallas_call x1, Pallas kernels: 51.1 us -> 40.5 us  [attend(): pl.pallas_call(functools.partial(attend_kernel, per_device), out_shape=ou...]
    all_to_all x2, waiting for transfers between devices: 11.7 us -> 21.2 us  [to_tokens(): return lax.all_to_all(array, 'seq', 0, 0, tiled=True)[:heads]]
    ppermute x31, waiting for transfers between devices: 84.3 us -> 92.1 us  [exchange(): lax.ppermute(value, axis, [(source, source ^ bit) for source in range(cou...]
    unnamed x112 -> x90, local copies, waits for them, and re-layouts: 16.9 us -> 15.9 us
  transfers between devices with their start and end apart: 36 -> 36, of which waited for: 19 -> 12; matrix products, arithmetic and copies ran while one was open for 14% -> 15% of each run, Pallas kernels for 11% -> 15%
where the time goes in v7:
time: 580 us; the launch traced here: 575 us
  waiting for transfers between devices  201 us (35%)
  Pallas kernels  181 us (31%)
  starting transfers between devices  68 us (12%)
  local copies, waits for them, and re-layouts  47.6 us (8%)
  other arithmetic  45.2 us (8%)
  matrix products  26.4 us (5%)
  between operations  6.13 us (1%)
    ppermute x31, waiting for transfers between devices, exchange(): lax.ppermute(value, axis, [(source, source ^ bit) for source in range(cou...  92.1 us
    all_to_all x2, waiting for transfers between devices, to_heads(): return lax.all_to_all(array, 'seq', 0, 0, tiled=True)  81.7 us
    pallas_call x1, Pallas kernels, attend_back(): pl.pallas_call(functools.partial(attend_back_kernel, per_device), out_sha...  54.3 us
    pallas_call x2, Pallas kernels, feed(): pl.pallas_call(functools.partial(feed_kernel, before is not None), grid_s...  45.1 us
    pallas_call x1, Pallas kernels, attend(): pl.pallas_call(functools.partial(attend_kernel, per_device), out_shape=ou...  40.5 us
    convert_element_type x22, other arithmetic, pick(): return (pieces[0].astype(F32) + pieces[1].astype(F32)).astype(BF16)  27.9 us
    ppermute x31, starting transfers between devices, exchange(): lax.ppermute(value, axis, [(source, source ^ bit) for source in range(cou...  25.4 us
    all_to_all x2, starting transfers between devices, to_tokens(): return lax.all_to_all(array, 'seq', 0, 0, tiled=True)[:heads]  22.2 us
  transfers between devices with their start and end apart: 36, of which 12 were waited for; matrix products, arithmetic and copies ran while one was open for 15% of the time, Pallas kernels for 15%

profile of v7, /device:TPU:0, one launch (start us, length us, event | category | flops | bytes accessed | tf_op | source)
XLA Modules:
  0.0 575.1 jit_solution(17885076125012936839)
XLA Ops:
  0.6 1.3 fusion.88
  7.5 2.9 fusion.7
  11.2 2.8 copy-done
  14.0 11.4 %project.1 = (bf16[512,1024]{1,0:T(8,128)(2,1)S(1)}, bf16[16,6,64,256]{3,2,1,0:T(8,128)(2,1)S(1)}) custom-call(bf16[512,1024]{1,0:T(8,128)(2,1)S(1)} %bitcast.145, f32[2,1024]{1,0:T(2,128)S(1)} %get-tuple-element.224.shift_ref, f32[2,1024]{1,0:T(2,128)S(1)} %get-tuple-element.223.scale_ref.refs_3_, bf16[1024,3072]{1,0:T(8,128)(2,1)S(1)} %copy-done, ...), custom_call_target="tpu_custom_call" | custom-call | flops 3221225472 | bytes 11534336 | tf_op jit(solution)/shard_map/project/pallas_call | solution.py:490
  25.4 1.6 copy-done.3
  27.0 8.5 %all-to-all-start = ((bf16[16,6,64,256]{3,2,1,0:T(8,128)(2,1)}), bf16[16,6,64,256]{3,2,1,0:T(8,128)(2,1)}, u32[]{:S(2)}, u32[]{:S(2)}) async-start(bf16[16,6,64,256]{3,2,1,0:T(8,128)(2,1)} %copy-done.3), calls=%async_computation | async-start | bytes 6291456 | tf_op jit(solution)/shard_map/all_to_all | solution.py:968
  35.6 4.7 fusion.2
  44.2 52.2 %all-to-all-done.x_ref = bf16[16,6,64,256]{3,2,1,0:T(8,128)(2,1)} async-done(((bf16[16,6,64,256]{3,2,1,0:T(8,128)(2,1)}), bf16[16,6,64,256]{3,2,1,0:T(8,128)(2,1)}, u32[]{:S(2)}, u32[]{:S(2)}) %all-to-all-start) | async-done | bytes 3145760 | tf_op jit(solution)/shard_map/all_to_all | solution.py:968
  96.5 40.5 %attend.1 = (bf16[16,2,64,256]{3,2,1,0:T(8,128)(2,1)S(1)}, f32[16,2,64,256]{3,2,1,0:T(8,128)S(1)}, f32[32,256]{1,0:T(8,128)S(1)}, bf16[32,256,128]{2,1,0:T(8,128)(2,1)S(1)}) custom-call(s32[32]{0:T(128)S(1)} %bitcast.154, s32[32]{0:T(128)S(1)} %bitcast.156, bf16[16,6,64,256]{3,2,1,0:T(8,128)(2,1)} %all-to-all-done.x_ref), custom_call_target="tpu_custom_call" | custom-call | flops 12884901888 | bytes 9437184 | tf_op jit(solution)/shard_map/attend/pallas_call | solution.py:184
  137.9 1.3 copy-done.13
  139.3 1.3 copy-done.14
  141.2 15.5 %all-to-all-start.1 = ((bf16[16,2,64,256]{3,2,1,0:T(8,128)(2,1)}), bf16[16,2,64,256]{3,2,1,0:T(8,128)(2,1)}, u32[]{:S(2)}, u32[]{:S(2)}) async-start(bf16[16,2,64,256]{3,2,1,0:T(8,128)(2,1)} %copy-done.6), calls=%async_computation.1 | async-start | bytes 2097152 | tf_op jit(solution)/shard_map/all_to_all | solution.py:971
  160.7 21.2 %all-to-all-done.1 = bf16[16,2,64,256]{3,2,1,0:T(8,128)(2,1)} async-done(((bf16[16,2,64,256]{3,2,1,0:T(8,128)(2,1)}), bf16[16,2,64,256]{3,2,1,0:T(8,128)(2,1)}, u32[]{:S(2)}, u32[]{:S(2)}) %all-to-all-start.1) | async-done | bytes 1048608 | tf_op jit(solution)/shard_map/all_to_all | solution.py:971
  181.8 1.4 fusion.78
  187.2 3.2 fusion.10
  190.4 21.9 %feed0.1 = (f32[512,1024]{1,0:T(8,128)}, f32[512,1024]{1,0:T(8,128)}, bf16[1024,2048]{1,0:T(8,128)(2,1)}, bf16[2048,1024]{1,0:T(8,128)(2,1)}, f32[1,2048]{1,0:T(1,128)}) custom-call(s32[1]{0:T(128)} %bitcast.20.which_ref, bf16[512,1024]{1,0:T(8,128)(2,1)} %get-tuple-element.139.in_ref, bf16[512,1024]{1,0:T(8,128)(2,1)} %fusion.13.d_out_ref, ...), custom_call_target="tpu_custom_call" | custom-call | flops 12884901888 | bytes 25165824 | tf_op jit(solution)/shard_map/feed0/pallas_call | solution.py:596
  212.9 23.2 %feed1.1 = (f32[512,1024]{1,0:T(8,128)}, f32[512,1024]{1,0:T(8,128)}, bf16[1024,2048]{1,0:T(8,128)(2,1)}, bf16[2048,1024]{1,0:T(8,128)(2,1)}, f32[1,2048]{1,0:T(1,128)}) custom-call(s32[1]{0:T(128)} %bitcast.which_ref.pack_ref, bf16[512,1024]{1,0:T(8,128)(2,1)} %get-tuple-element.139.in_ref, bf16[512,1024]{1,0:T(8,128)(2,1)} %fusion.13.d_out_ref, ...), custom_call_target="tpu_custom_call" | custom-call | flops 12884901888 | bytes 25165824 | tf_op jit(solution)/shard_map/feed1/pallas_call | solution.py:596
  236.9 8.1 %middle_back.1 = (f32[512,1024]{1,0:T(8,128)S(1)}, bf16[512,1024]{1,0:T(8,128)(2,1)S(1)}, bf16[512,1024]{1,0:T(8,128)(2,1)}, bf16[16,3,64,256]{3,2,1,0:T(8,128)(2,1)S(1)}) custom-call(f32[512,1024]{1,0:T(8,128)} %get-tuple-element.85.d_in_ref, f32[512,1024]{1,0:T(8,128)} %get-tuple-element.140.middle_ref, bf16[512,1024]{1,0:T(8,128)(2,1)S(1)} %bitcast.147, ...), custom_call_target="tpu_custom_call" | custom-call | flops 1073741824 | bytes 12582912 | tf_op jit(solution)/shard_map/middle_back/pallas_call | solution.py:720
  248.5 7.2 %all-to-all-start.2 = ((bf16[16,3,64,256]{3,2,1,0:T(8,128)(2,1)}), bf16[16,3,64,256]{3,2,1,0:T(8,128)(2,1)}, u32[]{:S(2)}, u32[]{:S(2)}) async-start(bf16[16,3,64,256]{3,2,1,0:T(8,128)(2,1)} %copy-done.5), calls=%async_computation.2 | async-start | bytes 3145728 | tf_op jit(solution)/shard_map/all_to_all | solution.py:968
  255.8 3.0 convolution_convert_fusion
  258.7 1.7 convolution_convert_fusion.1
  260.4 29.5 %all-to-all-done.2.d_mix_ref = bf16[16,3,64,256]{3,2,1,0:T(8,128)(2,1)} async-done(((bf16[16,3,64,256]{3,2,1,0:T(8,128)(2,1)}), bf16[16,3,64,256]{3,2,1,0:T(8,128)(2,1)}, u32[]{:S(2)}, u32[]{:S(2)}) %all-to-all-start.2) | async-done | bytes 1572896 | tf_op jit(solution)/shard_map/all_to_all | solution.py:968
  292.9 7.9 %add_convert_fusion = (bf16[2,2,1,2,64,2048]{5,4,3,2,1,0:T(8,128)(2,1)}, bf16[2,2,1,2,64,2048]{5,4,3,2,1,0:T(8,128)(2,1)}) fusion(bf16[2,2,2,2,64,2048]{5,4,3,2,1,0:T(8,128)(2,1)} %bitcast.36, s32[]{:T(128)S(6)} %select_n.95, bf16[2,2,2,2,64,2048]{5,4,3,2,1,0:T(8,128)(2,1)} %bitcast.168, s32[]{:T(128)S(6)} %select_n.93), kind=kLoop, calls=%fused_computation.4 | loop fusion | flops 8388608 | bytes 12582920 | tf_op jit(solution)/shard_map/convert_element_type | solution.py:346
  300.9 2.7 collective-permute-start.3
  304.8 6.4 %add_convert_fusion.1 = (bf16[2,2,2,1,128,1024]{5,4,3,2,1,0:T(8,128)(2,1)}, bf16[2,2,2,1,128,1024]{5,4,3,2,1,0:T(8,128)(2,1)}) fusion(bf16[2,2,2,2,128,1024]{5,4,3,2,1,0:T(8,128)(2,1)} %bitcast.33, s32[]{:T(128)S(6)} %select_n.94, bf16[2,2,2,2,128,1024]{5,4,3,2,1,0:T(8,128)(2,1)S(1)} %bitcast.167, s32[]{:T(128)S(6)} %select_n.92), kind=kLoop, calls=%fused_computation.5 | loop fusion | flops 8388608 | bytes 12582920 | tf_op jit(solution)/shard_map/convert_element_type | solution.py:346
  313.4 54.3 %attend_back.1 = bf16[16,6,64,256]{3,2,1,0:T(8,128)(2,1)} custom-call(s32[32]{0:T(128)} %bitcast.152, s32[32]{0:T(128)} %bitcast.155, bf16[16,6,64,256]{3,2,1,0:T(8,128)(2,1)} %all-to-all-done.x_ref, bf16[32,256,128]{2,1,0:T(8,128)(2,1)} %copy-done.14, f32[16,2,64,256]{3,2,1,0:T(8,128)} %copy-done.13, f32[32,256]{1,0:T(8,128)} %copy-done.15, ...), custom_call_target="tpu_custom_call" | custom-call | flops 32212254720 | bytes 15728640 | tf_op jit(solution)/shard_map/attend_back/pallas_call | solution.py:292
  367.7 6.7 %all-to-all-start.3 = ((bf16[16,6,64,256]{3,2,1,0:T(8,128)(2,1)}), bf16[16,6,64,256]{3,2,1,0:T(8,128)(2,1)}, u32[]{:S(2)}, u32[]{:S(2)}) async-start(bf16[16,6,64,256]{3,2,1,0:T(8,128)(2,1)} %attend_back.1), calls=%async_computation.3 | async-start | bytes 6291456 | tf_op jit(solution)/shard_map/all_to_all | solution.py:971
  374.6 2.6 fusion.81
  377.9 1.3 fusion.24
  381.1 1.4 fusion.20
  382.5 1.4 fusion.18
  384.0 1.5 fusion.22
  386.2 2.4 add_convert_fusion.5
  388.6 2.1 collective-permute-start.6
  390.7 2.2 add_convert_fusion.7
  392.9 1.5 collective-permute-start.5
  394.5 1.5 add_convert_fusion.15
  398.0 57.4 %collective-permute-done.7 = bf16[2,2,2,1,64,512]{5,4,3,2,1,0:T(8,128)(2,1)S(1)} collective-permute-done((bf16[2,2,2,1,64,512]{5,4,3,2,1,0:T(8,128)(2,1)S(1)}, bf16[2,2,2,1,64,512]{5,4,3,2,1,0:T(8,128)(2,1)S(1)}, u32[]{:S(2)}, u32[]{:S(2)}) %collective-permute-start.7) | collective-permute-done | bytes 524320 | tf_op jit(solution)/shard_map/ppermute | solution.py:313
  458.7 8.3 %unproject0.1 = (f32[512,1024]{1,0:T(8,128)S(1)}, bf16[3,1024,512]{2,1,0:T(8,128)(2,1)}, f32[3,1,512]{2,1,0:T(1,128)S(1)}) custom-call(s32[1]{0:T(128)} %bitcast.20.which_ref, bf16[512,1024]{1,0:T(8,128)(2,1)S(1)} %get-tuple-element.76.in_ref, bf16[16,6,64,256]{3,2,1,0:T(8,128)(2,1)} %all-to-all-done.3.back_ref, bf16[1024,3072]{1,0:T(8,128)(2,1)} %wv_ref.5, ...), custom_call_target="tpu_custom_call" | custom-call | flops 3221225472 | bytes 12582912 | tf_op jit(solution)/shard_map/unproject0/pallas_call | solution.py:883
  466.9 11.3 %unproject1.1 = (bf16[3,1024,512]{2,1,0:T(8,128)(2,1)}, bf16[512,1024]{1,0:T(8,128)(2,1)}, bf16[16,16,1024]{2,1,0:T(8,128)(2,1)}) custom-call(s32[1]{0:T(128)} %bitcast.which_ref.pack_ref, bf16[512,1024]{1,0:T(8,128)(2,1)S(1)} %get-tuple-element.76.in_ref, bf16[16,6,64,256]{3,2,1,0:T(8,128)(2,1)} %all-to-all-done.3.back_ref, bf16[1024,3072]{1,0:T(8,128)(2,1)} %wv_ref.5, ...), custom_call_target="tpu_custom_call" | custom-call | flops 3221225472 | bytes 12582912 | tf_op jit(solution)/shard_map/unproject1/pallas_call | solution.py:883
  478.3 4.7 all-to-all-start.4
  483.7 1.9 collective-permute-start.17
  485.6 1.5 collective-permute-start.11
  487.6 2.1 fusion.76
  491.8 6.1 %all-to-all-done.4 = bf16[16,16,1024]{2,1,0:T(8,128)(2,1)} async-done(((bf16[16,16,1024]{2,1,0:T(8,128)(2,1)}), bf16[16,16,1024]{2,1,0:T(8,128)(2,1)}, u32[]{:S(2)}, u32[]{:S(2)}) %all-to-all-start.4) | async-done | bytes 524320 | tf_op jit(solution)/shard_map/all_to_all | solution.py:1130
  497.9 1.7 slice.318
  499.6 1.6 fusion.79
  501.6 1.8 fusion.47
  506.9 1.3 dynamic_slice.368
  510.5 1.3 convolution_add_fusion.1
  513.1 2.1 fusion.77
  518.0 1.4 collective-permute-start.26
  523.3 1.5 collective-permute-start.15
  525.8 1.5 collective-permute-start.12
  527.9 1.5 collective-permute-start.19
  529.5 8.5 %collective-permute-done.26 = bf16[3,2,2,1,2,64,256]{6,5,0,4,3,2,1:T(8,128)(2,1)S(1)} collective-permute-done((bf16[3,2,2,1,2,64,256]{6,5,0,4,3,2,1:T(8,128)(2,1)S(1)}, bf16[3,2,2,1,2,64,256]{6,5,0,4,3,2,1:T(8,128)(2,1)S(1)}, u32[]{:S(2)}, u32[]{:S(2)}) %collective-permute-start.26) | collective-permute-done | bytes 786464 | tf_op jit(solution)/shard_map/ppermute | solution.py:313
  538.3 1.5 collective-permute-start.27
  540.6 11.1 %collective-permute-done.19 = bf16[1,1,1,1,64,512]{5,4,3,2,1,0:T(8,128)(2,1)S(1)} collective-permute-done((bf16[1,1,1,1,64,512]{5,4,3,2,1,0:T(8,128)(2,1)S(1)}, bf16[1,1,1,1,64,512]{5,4,3,2,1,0:T(8,128)(2,1)S(1)}, u32[]{:S(2)}, u32[]{:S(2)}) %collective-permute-start.19) | collective-permute-done | bytes 65568 | tf_op jit(solution)/shard_map/ppermute | solution.py:313
  553.8 2.1 collective-permute-start.23
  557.0 4.4 collective-permute-done.28
  561.6 4.2 collective-permute-done.23
  565.9 1.7 collective-permute-done.29
  567.7 4.1 collective-permute-done.24
  573.2 1.8 settle.1
  (282 shorter events, 60.2 us)
Async XLA Ops:
  7.4 3.0 copy-start.11
  7.4 3.7 copy-start.1
  7.5 3.7 copy-start.7
  11.2 2.8 copy-start
  25.4 1.6 copy-start.3
  27.0 8.5 %slice-start = ((f32[6144]{0:T(1024)}), f32[4096]{0:T(1024)S(1)}, s32[]{:S(2)}) async-start(f32[6144]{0:T(1024)} %param.23), calls=%async_computation.5 | async-start | bytes 32768 | tf_op jit(solution)/shard_map/slice | solution.py:978
  27.0 69.5 %all-to-all-start = ((bf16[16,6,64,256]{3,2,1,0:T(8,128)(2,1)}), bf16[16,6,64,256]{3,2,1,0:T(8,128)(2,1)}, u32[]{:S(2)}, u32[]{:S(2)}) async-start(bf16[16,6,64,256]{3,2,1,0:T(8,128)(2,1)} %copy-done.3), calls=%async_computation | async-start | bytes 6291456 | tf_op jit(solution)/shard_map/all_to_all | solution.py:968
  35.5 4.7 copy-start.2
  42.9 53.6 %copy-start.12 = (s32[1,32]{1,0:T(1,128)S(1)}, s32[1,32]{1,0:T(1,128)}, u32[]{:S(2)}) copy-start(s32[1,32]{1,0:T(1,128)} %param.20) | copy-start | bytes 388
  141.2 15.5 %copy-start.40 = (s32[1,2]{1,0:T(1,128)S(1)}, s32[1,2]{1,0:T(1,128)}, u32[]{:S(2)}) copy-start(s32[1,2]{1,0:T(1,128)} %param.18) | copy-start | bytes 28
  141.2 40.6 %all-to-all-start.1 = ((bf16[16,2,64,256]{3,2,1,0:T(8,128)(2,1)}), bf16[16,2,64,256]{3,2,1,0:T(8,128)(2,1)}, u32[]{:S(2)}, u32[]{:S(2)}) async-start(bf16[16,2,64,256]{3,2,1,0:T(8,128)(2,1)} %copy-done.6), calls=%async_computation.1 | async-start | bytes 2097152 | tf_op jit(solution)/shard_map/all_to_all | solution.py:971
  181.8 1.9 copy-start.16
  212.3 80.6 %collective-permute-start.1 = (bf16[1024,2048]{1,0:T(8,128)(2,1)}, bf16[1024,2048]{1,0:T(8,128)(2,1)}, u32[]{:S(2)}, u32[]{:S(2)}) collective-permute-start(bf16[1024,2048]{1,0:T(8,128)(2,1)} %get-tuple-element.99), channel_id=1, source_target_pairs={{0,16},{16,0},{1,17},{17,1},{2,18},{18,2},{3,19},{19,3},{4,20},{20... | collective-permute-start | bytes 12582920 | tf_op jit(solution)/shard_map/ppermute | solution.py:313
  212.4 92.4 %collective-permute-start = (bf16[2048,1024]{1,0:T(8,128)(2,1)}, bf16[2048,1024]{1,0:T(8,128)(2,1)}, u32[]{:S(2)}, u32[]{:S(2)}) collective-permute-start(bf16[2048,1024]{1,0:T(8,128)(2,1)} %get-tuple-element.97), channel_id=1, source_target_pairs={{0,16},{16,0},{1,17},{17,1},{2,18},{18,2},{3,19},{19,3},{4,20},{20... | collective-permute-start | bytes 12582920 | tf_op jit(solution)/shard_map/ppermute | solution.py:313
  212.9 23.2 %copy-start.37 = (f32[1,2048]{1,0:T(1,128)S(1)}, f32[1,2048]{1,0:T(1,128)}, u32[]{:S(2)}) copy-start(f32[1,2048]{1,0:T(1,128)} %get-tuple-element.88) | copy-start | bytes 24580
  212.9 24.1 %copy-start.8 = (f32[1024]{0:T(1024)S(1)}, f32[1024]{0:T(1024)}, u32[]{:S(2)}) copy-start(f32[1024]{0:T(1024)} %param.31) | copy-start | bytes 12292
  248.5 7.3 %copy-start.10 = (bf16[512,1024]{1,0:T(8,128)(2,1)S(1)}, bf16[512,1024]{1,0:T(8,128)(2,1)}, u32[]{:S(2)}) copy-start(bf16[512,1024]{1,0:T(8,128)(2,1)} %copy-done.9) | copy-start | bytes 3145732
  248.5 41.4 %all-to-all-start.2 = ((bf16[16,3,64,256]{3,2,1,0:T(8,128)(2,1)}), bf16[16,3,64,256]{3,2,1,0:T(8,128)(2,1)}, u32[]{:S(2)}, u32[]{:S(2)}) async-start(bf16[16,3,64,256]{3,2,1,0:T(8,128)(2,1)} %copy-done.5), calls=%async_computation.2 | async-start | bytes 3145728 | tf_op jit(solution)/shard_map/all_to_all | solution.py:968
  255.7 3.0 copy-start.23
  255.7 3.0 copy-start.25
  258.7 108.9 %collective-permute-start.4 = (bf16[1024,512]{1,0:T(8,128)(2,1)}, bf16[1024,512]{1,0:T(8,128)(2,1)}, u32[]{:S(2)}, u32[]{:S(2)}) collective-permute-start(bf16[1024,512]{1,0:T(8,128)(2,1)} %convolution_convert_fusion), channel_id=1, source_target_pairs={{0,16},{16,0},{1,17},{17,1},{2,18},{18,2},{3,19},{19,3},{4,20},{20... | collective-permute-start | bytes 3145736 | tf_op jit(solution)/shard_map/ppermute | solution.py:313
  291.8 87.5 %collective-permute-start.8 = (bf16[16,16,1024]{2,1,0:T(8,128)(2,1)}, bf16[16,16,1024]{2,1,0:T(8,128)(2,1)S(1)}, u32[]{:S(2)}, u32[]{:S(2)}) collective-permute-start(bf16[16,16,1024]{2,1,0:T(8,128)(2,1)} %bitcast.66), channel_id=1, source_target_pairs={{0,16},{16,0},{1,17},{17,1},{2,18},{18,2},{3,19},{19,3},{4,20},{20... | collective-permute-start | bytes 1572872 | tf_op jit(solution)/shard_map/ppermute | solution.py:313
  292.9 11.9 %copy-start.19 = (bf16[2048,1024]{1,0:T(8,128)(2,1)S(1)}, bf16[2048,1024]{1,0:T(8,128)(2,1)}, u32[]{:S(2)}) copy-start(bf16[2048,1024]{1,0:T(8,128)(2,1)} %get-tuple-element.96) | copy-start | bytes 12582916
  300.9 66.8 %collective-permute-start.3 = (bf16[2,2,1,2,64,2048]{5,4,3,2,1,0:T(8,128)(2,1)}, bf16[2,2,1,2,64,2048]{5,4,3,2,1,0:T(8,128)(2,1)}, u32[]{:S(2)}, u32[]{:S(2)}) collective-permute-start(bf16[2,2,1,2,64,2048]{5,4,3,2,1,0:T(8,128)(2,1)} %get-tuple-element.143), channel_id=1, source_target_pairs={{0,2},{1,3},{2,0},{3,1},{4,6},{5,7},{6,4},{7,5},{8,10},{9,11},{10,... | collective-permute-start | bytes 6291464 | tf_op jit(solution)/shard_map/ppermute | solution.py:313
  311.1 56.5 %collective-permute-start.2 = (bf16[2,2,2,1,128,1024]{5,4,3,2,1,0:T(8,128)(2,1)}, bf16[2,2,2,1,128,1024]{5,4,3,2,1,0:T(8,128)(2,1)}, u32[]{:S(2)}, u32[]{:S(2)}) collective-permute-start(bf16[2,2,2,1,128,1024]{5,4,3,2,1,0:T(8,128)(2,1)} %get-tuple-element.145), channel_id=1, source_target_pairs={{0,1},{1,0},{2,3},{3,2},{4,5},{5,4},{6,7},{7,6},{8,9},{9,8},{10,11... | collective-permute-start | bytes 6291464 | tf_op jit(solution)/shard_map/ppermute | solution.py:313
  367.7 91.0 %all-to-all-start.3 = ((bf16[16,6,64,256]{3,2,1,0:T(8,128)(2,1)}), bf16[16,6,64,256]{3,2,1,0:T(8,128)(2,1)}, u32[]{:S(2)}, u32[]{:S(2)}) async-start(bf16[16,6,64,256]{3,2,1,0:T(8,128)(2,1)} %attend_back.1), calls=%async_computation.3 | async-start | bytes 6291456 | tf_op jit(solution)/shard_map/all_to_all | solution.py:971
  379.3 1.3 copy-start.32
  381.1 1.5 copy-start.38
  384.0 2.2 copy-start.18
  386.2 4.5 copy-start.17
  388.6 5.9 %copy-start.28 = (bf16[1024,512]{1,0:T(8,128)(2,1)S(1)}, bf16[1024,512]{1,0:T(8,128)(2,1)}, u32[]{:S(2)}) copy-start(bf16[1024,512]{1,0:T(8,128)(2,1)} %convolution_convert_fusion.1) | copy-start | bytes 3145732
  388.6 66.9 %collective-permute-start.6 = (bf16[2,2,1,1,128,1024]{5,4,3,2,1,0:T(8,128)(2,1)S(1)}, bf16[2,2,1,1,128,1024]{5,4,3,2,1,0:T(8,128)(2,1)S(1)}, u32[]{:S(2)}, u32[]{:S(2)}) collective-permute-start(bf16[2,2,1,1,128,1024]{5,4,3,2,1,0:T(8,128)(2,1)S(1)} %get-tuple-element.147), channel_id=1, source_target_pairs={{0,2},{1,3},{2,0},{3,1},{4,6},{5,7},{6,4},{7,5},{8,10},{9,11},{10,... | collective-permute-start | bytes 3145736 | tf_op jit(solution)/shard_map/ppermute | solution.py:313
  392.9 63.8 %collective-permute-start.5 = (bf16[2,2,1,1,64,2048]{5,4,3,2,1,0:T(8,128)(2,1)S(1)}, bf16[2,2,1,1,64,2048]{5,4,3,2,1,0:T(8,128)(2,1)S(1)}, u32[]{:S(2)}, u32[]{:S(2)}) collective-permute-start(bf16[2,2,1,1,64,2048]{5,4,3,2,1,0:T(8,128)(2,1)S(1)} %get-tuple-element.149), channel_id=1, source_target_pairs={{0,1},{1,0},{2,3},{3,2},{4,5},{5,4},{6,7},{7,6},{8,9},{9,8},{10,11... | collective-permute-start | bytes 3145736 | tf_op jit(solution)/shard_map/ppermute | solution.py:313
  396.0 59.3 %collective-permute-start.7 = (bf16[2,2,2,1,64,512]{5,4,3,2,1,0:T(8,128)(2,1)S(1)}, bf16[2,2,2,1,64,512]{5,4,3,2,1,0:T(8,128)(2,1)S(1)}, u32[]{:S(2)}, u32[]{:S(2)}) collective-permute-start(bf16[2,2,2,1,64,512]{5,4,3,2,1,0:T(8,128)(2,1)S(1)} %get-tuple-element.161), channel_id=1, source_target_pairs={{0,1},{1,0},{2,3},{3,2},{4,5},{5,4},{6,7},{7,6},{8,9},{9,8},{10,11... | collective-permute-start | bytes 1572872 | tf_op jit(solution)/shard_map/ppermute | solution.py:313
  455.5 2.4 copy-start.31
  466.9 16.6 %copy-start.39 = (s32[32]{0:T(128)S(1)}, s32[32]{0:T(128)}, u32[]{:S(2)}) copy-start(s32[32]{0:T(128)} %copy-done.38) | copy-start | bytes 388
  478.3 19.6 %all-to-all-start.4 = ((bf16[16,16,1024]{2,1,0:T(8,128)(2,1)}), bf16[16,16,1024]{2,1,0:T(8,128)(2,1)}, u32[]{:S(2)}, u32[]{:S(2)}) async-start(bf16[16,16,1024]{2,1,0:T(8,128)(2,1)} %get-tuple-element.114), calls=%async_computation.4 | async-start | bytes 1048576 | tf_op jit(solution)/shard_map/all_to_all | solution.py:1130
  483.7 33.1 %collective-permute-start.17 = (bf16[2,2,1,1,64,512]{5,4,3,2,1,0:T(8,128)(2,1)}, bf16[2,2,1,1,64,512]{5,4,3,2,1,0:T(8,128)(2,1)}, u32[]{:S(2)}, u32[]{:S(2)}) collective-permute-start(bf16[2,2,1,1,64,512]{5,4,3,2,1,0:T(8,128)(2,1)} %copy-done.31), channel_id=1, source_target_pairs={{0,2},{1,3},{2,0},{3,1},{4,6},{5,7},{6,4},{7,5},{8,10},{9,11},{10,... | collective-permute-start | bytes 786440 | tf_op jit(solution)/shard_map/ppermute | solution.py:313
  485.6 31.0 %collective-permute-start.11 = (bf16[2,1,1,1,64,2048]{5,4,3,2,1,0:T(8,128)(2,1)}, bf16[2,1,1,1,64,2048]{5,4,3,2,1,0:T(8,128)(2,1)}, u32[]{:S(2)}, u32[]{:S(2)}) collective-permute-start(bf16[2,1,1,1,64,2048]{5,4,3,2,1,0:T(8,128)(2,1)} %copy-done.30), channel_id=1, source_target_pairs={{0,4},{1,5},{2,6},{3,7},{4,0},{5,1},{6,2},{7,3},{8,12},{9,13},{10,... | collective-permute-start | bytes 1572872 | tf_op jit(solution)/shard_map/ppermute | solution.py:313
  487.1 29.5 %collective-permute-start.14 = (bf16[2,1,1,1,128,1024]{5,4,3,2,1,0:T(8,128)(2,1)}, bf16[2,1,1,1,128,1024]{5,4,3,2,1,0:T(8,128)(2,1)}, u32[]{:S(2)}, u32[]{:S(2)}) collective-permute-start(bf16[2,1,1,1,128,1024]{5,4,3,2,1,0:T(8,128)(2,1)} %copy-done.29), channel_id=1, source_target_pairs={{0,4},{1,5},{2,6},{3,7},{4,0},{5,1},{6,2},{7,3},{8,12},{9,13},{10,... | collective-permute-start | bytes 1572872 | tf_op jit(solution)/shard_map/ppermute | solution.py:313
  487.6 25.4 %collective-permute-start.10 = (bf16[3,1024,512]{2,1,0:T(8,128)(2,1)}, bf16[3,1024,512]{2,1,0:T(8,128)(2,1)}, u32[]{:S(2)}, u32[]{:S(2)}) collective-permute-start(bf16[3,1024,512]{2,1,0:T(8,128)(2,1)} %get-tuple-element.116), channel_id=1, source_target_pairs={{0,16},{16,0},{1,17},{17,1},{2,18},{18,2},{3,19},{19,3},{4,20},{20... | collective-permute-start | bytes 9437192 | tf_op jit(solution)/shard_map/ppermute | solution.py:313
  490.7 10.9 %copy-start.33 = (f32[32,64]{1,0:T(8,128)S(1)}, f32[32,64]{1,0:T(8,128)}, u32[]{:S(2)}) copy-start(f32[32,64]{1,0:T(8,128)} %copy-done.32) | copy-start | bytes 24580
  499.5 6.0 %collective-permute-start.9 = (bf16[16,8,1024]{2,1,0:T(8,128)(2,1)}, bf16[16,8,1024]{2,1,0:T(8,128)(2,1)S(1)}, u32[]{:S(2)}, u32[]{:S(2)}) collective-permute-start(bf16[16,8,1024]{2,1,0:T(8,128)(2,1)} %slice.318), channel_id=1, source_target_pairs={{0,16},{16,0},{1,17},{17,1},{2,18},{18,2},{3,19},{19,3},{4,20},{20... | collective-permute-start | bytes 786440 | tf_op jit(solution)/shard_map/ppermute | solution.py:313
  503.4 6.1 %copy-start.34 = (f32[32,64]{1,0:T(8,128)S(1)}, f32[32,64]{1,0:T(8,128)}, u32[]{:S(2)}) copy-start(f32[32,64]{1,0:T(8,128)} %fusion.47) | copy-start | bytes 24580
  516.7 5.5 copy-start.27
  516.7 8.1 %copy-start.26 = (bf16[2,1,1,1,64,2048]{5,4,3,2,1,0:T(8,128)(2,1)S(1)}, bf16[2,1,1,1,64,2048]{5,4,3,2,1,0:T(8,128)(2,1)}, u32[]{:S(2)}) copy-start(bf16[2,1,1,1,64,2048]{5,4,3,2,1,0:T(8,128)(2,1)} %get-tuple-element.119) | copy-start | bytes 1572868
  518.0 20.0 %collective-permute-start.26 = (bf16[3,2,2,1,2,64,256]{6,5,0,4,3,2,1:T(8,128)(2,1)S(1)}, bf16[3,2,2,1,2,64,256]{6,5,0,4,3,2,1:T(8,128)(2,1)S(1)}, u32[]{:S(2)}, u32[]{:S(2)}) collective-permute-start(bf16[3,2,2,1,2,64,256]{6,5,0,4,3,2,1:T(8,128)(2,1)S(1)} %add_convert_fusion.11), channel_id=1, source_target_pairs={{0,2},{1,3},{2,0},{3,1},{4,6},{5,7},{6,4},{7,5},{8,10},{9,11},{10,... | collective-permute-start | bytes 2359304 | tf_op jit(solution)/shard_map/ppermute | solution.py:313
  519.4 20.3 %collective-permute-start.21 = (bf16[3,2,2,2,1,64,256]{6,5,0,4,3,2,1:T(8,128)(2,1)S(1)}, bf16[3,2,2,2,1,64,256]{6,5,0,4,3,2,1:T(8,128)(2,1)S(1)}, u32[]{:S(2)}, u32[]{:S(2)}) collective-permute-start(bf16[3,2,2,2,1,64,256]{6,5,0,4,3,2,1:T(8,128)(2,1)S(1)} %add_convert_fusion.10), channel_id=1, source_target_pairs={{0,1},{1,0},{2,3},{3,2},{4,5},{5,4},{6,7},{7,6},{8,9},{9,8},{10,11... | collective-permute-start | bytes 2359304 | tf_op jit(solution)/shard_map/ppermute | solution.py:313
  521.0 6.9 %collective-permute-start.18 = (bf16[2,1,1,1,64,512]{5,4,3,2,1,0:T(8,128)(2,1)S(1)}, bf16[2,1,1,1,64,512]{5,4,3,2,1,0:T(8,128)(2,1)S(1)}, u32[]{:S(2)}, u32[]{:S(2)}) collective-permute-start(bf16[2,1,1,1,64,512]{5,4,3,2,1,0:T(8,128)(2,1)S(1)} %get-tuple-element.183), channel_id=1, source_target_pairs={{0,4},{1,5},{2,6},{3,7},{4,0},{5,1},{6,2},{7,3},{8,12},{9,13},{10,... | collective-permute-start | bytes 393224 | tf_op jit(solution)/shard_map/ppermute | solution.py:313
  523.3 28.6 %collective-permute-start.15 = (bf16[1,1,1,1,128,1024]{5,4,3,2,1,0:T(8,128)(2,1)S(1)}, bf16[1,1,1,1,128,1024]{5,4,3,2,1,0:T(8,128)(2,1)S(1)}, u32[]{:S(2)}, u32[]{:S(2)}) collective-permute-start(bf16[1,1,1,1,128,1024]{5,4,3,2,1,0:T(8,128)(2,1)S(1)} %add_convert_fusion.24), channel_id=1, source_target_pairs={{0,8},{1,9},{2,10},{3,11},{4,12},{5,13},{6,14},{7,15},{8,0},{9,1},... | collective-permute-start | bytes 786440 | tf_op jit(solution)/shard_map/ppermute | solution.py:313
  525.8 30.1 %collective-permute-start.12 = (bf16[1,1,1,1,64,2048]{5,4,3,2,1,0:T(8,128)(2,1)S(1)}, bf16[1,1,1,1,64,2048]{5,4,3,2,1,0:T(8,128)(2,1)S(1)}, u32[]{:S(2)}, u32[]{:S(2)}) collective-permute-start(bf16[1,1,1,1,64,2048]{5,4,3,2,1,0:T(8,128)(2,1)S(1)} %add_convert_fusion.27), channel_id=1, source_target_pairs={{0,8},{1,9},{2,10},{3,11},{4,12},{5,13},{6,14},{7,15},{8,0},{9,1},... | collective-permute-start | bytes 786440 | tf_op jit(solution)/shard_map/ppermute | solution.py:313
  527.9 23.8 %collective-permute-start.19 = (bf16[1,1,1,1,64,512]{5,4,3,2,1,0:T(8,128)(2,1)S(1)}, bf16[1,1,1,1,64,512]{5,4,3,2,1,0:T(8,128)(2,1)S(1)}, u32[]{:S(2)}, u32[]{:S(2)}) collective-permute-start(bf16[1,1,1,1,64,512]{5,4,3,2,1,0:T(8,128)(2,1)S(1)} %add_convert_fusion.43), channel_id=1, source_target_pairs={{0,8},{1,9},{2,10},{3,11},{4,12},{5,13},{6,14},{7,15},{8,0},{9,1},... | collective-permute-start | bytes 196616 | tf_op jit(solution)/shard_map/ppermute | solution.py:313
  538.3 15.2 %collective-permute-start.27 = (bf16[3,2,2,1,1,64,256]{6,5,0,4,3,2,1:T(8,128)(2,1)S(1)}, bf16[3,2,2,1,1,64,256]{6,5,0,4,3,2,1:T(8,128)(2,1)S(1)}, u32[]{:S(2)}, u32[]{:S(2)}) collective-permute-start(bf16[3,2,2,1,1,64,256]{6,5,0,4,3,2,1:T(8,128)(2,1)S(1)} %get-tuple-element.163), channel_id=1, source_target_pairs={{0,1},{1,0},{2,3},{3,2},{4,5},{5,4},{6,7},{7,6},{8,9},{9,8},{10,11... | collective-permute-start | bytes 1179656 | tf_op jit(solution)/shard_map/ppermute | solution.py:313
  540.0 13.7 %collective-permute-start.22 = (bf16[3,2,2,1,1,64,256]{6,5,0,4,3,2,1:T(8,128)(2,1)S(1)}, bf16[3,2,2,1,1,64,256]{6,5,0,4,3,2,1:T(8,128)(2,1)S(1)}, u32[]{:S(2)}, u32[]{:S(2)}) collective-permute-start(bf16[3,2,2,1,1,64,256]{6,5,0,4,3,2,1:T(8,128)(2,1)S(1)} %get-tuple-element.169), channel_id=1, source_target_pairs={{0,2},{1,3},{2,0},{3,1},{4,6},{5,7},{6,4},{7,5},{8,10},{9,11},{10,... | collective-permute-start | bytes 1179656 | tf_op jit(solution)/shard_map/ppermute | solution.py:313
  551.8 20.8 %collective-permute-start.20 = (bf16[64,512]{1,0:T(8,128)(2,1)S(1)}, bf16[64,512]{1,0:T(8,128)(2,1)S(1)}, u32[]{:S(2)}, u32[]{:S(2)}) collective-permute-start(bf16[64,512]{1,0:T(8,128)(2,1)S(1)} %fusion.36.refs_4_), channel_id=1, source_target_pairs={{0,16},{16,0},{1,17},{17,1},{2,18},{18,2},{3,19},{19,3},{4,20},{20... | collective-permute-start | bytes 196616 | tf_op jit(solution)/shard_map/ppermute | solution.py:313
  552.9 19.6 %collective-permute-start.16 = (bf16[128,1024]{1,0:T(8,128)(2,1)S(1)}, bf16[128,1024]{1,0:T(8,128)(2,1)S(1)}, u32[]{:S(2)}, u32[]{:S(2)}) collective-permute-start(bf16[128,1024]{1,0:T(8,128)(2,1)S(1)} %fusion.27.refs_2_), channel_id=1, source_target_pairs={{0,16},{16,0},{1,17},{17,1},{2,18},{18,2},{3,19},{19,3},{4,20},{20... | collective-permute-start | bytes 786440 | tf_op jit(solution)/shard_map/ppermute | solution.py:313
  553.6 18.3 %copy-start.35 = (f32[4096]{0:T(1024)S(1)}, f32[4096]{0:T(1024)}, u32[]{:S(2)}) copy-start(f32[4096]{0:T(1024)} %get-tuple-element.252) | copy-start | bytes 49156
  553.6 7.8 %collective-permute-start.28 = (bf16[3,2,1,1,1,64,256]{6,5,0,4,3,2,1:T(8,128)(2,1)S(1)}, bf16[3,2,1,1,1,64,256]{6,5,0,4,3,2,1:T(8,128)(2,1)S(1)}, u32[]{:S(2)}, u32[]{:S(2)}) collective-permute-start(bf16[3,2,1,1,1,64,256]{6,5,0,4,3,2,1:T(8,128)(2,1)S(1)} %get-tuple-element.179), channel_id=1, source_target_pairs={{0,4},{1,5},{2,6},{3,7},{4,0},{5,1},{6,2},{7,3},{8,12},{9,13},{10,... | collective-permute-start | bytes 589832 | tf_op jit(solution)/shard_map/ppermute | solution.py:313
  553.8 12.0 %collective-permute-start.23 = (bf16[3,2,1,1,1,64,256]{6,5,0,4,3,2,1:T(8,128)(2,1)S(1)}, bf16[3,2,1,1,1,64,256]{6,5,0,4,3,2,1:T(8,128)(2,1)S(1)}, u32[]{:S(2)}, u32[]{:S(2)}) collective-permute-start(bf16[3,2,1,1,1,64,256]{6,5,0,4,3,2,1:T(8,128)(2,1)S(1)} %get-tuple-element.181), channel_id=1, source_target_pairs={{0,4},{1,5},{2,6},{3,7},{4,0},{5,1},{6,2},{7,3},{8,12},{9,13},{10,... | collective-permute-start | bytes 589832 | tf_op jit(solution)/shard_map/ppermute | solution.py:313
  557.0 15.6 %collective-permute-start.13 = (bf16[64,2048]{1,0:T(8,128)(2,1)S(1)}, bf16[64,2048]{1,0:T(8,128)(2,1)S(1)}, u32[]{:S(2)}, u32[]{:S(2)}) collective-permute-start(bf16[64,2048]{1,0:T(8,128)(2,1)S(1)} %fusion.26.refs_0_), channel_id=1, source_target_pairs={{0,16},{16,0},{1,17},{17,1},{2,18},{18,2},{3,19},{19,3},{4,20},{20... | collective-permute-start | bytes 786440 | tf_op jit(solution)/shard_map/ppermute | solution.py:313
  561.5 6.1 %collective-permute-start.29 = (bf16[3,1,1,1,1,64,256]{6,5,0,4,3,2,1:T(8,128)(2,1)S(1)}, bf16[3,1,1,1,1,64,256]{6,5,0,4,3,2,1:T(8,128)(2,1)S(1)}, u32[]{:S(2)}, u32[]{:S(2)}) collective-permute-start(bf16[3,1,1,1,1,64,256]{6,5,0,4,3,2,1:T(8,128)(2,1)S(1)} %add_convert_fusion.37), channel_id=1, source_target_pairs={{0,8},{1,9},{2,10},{3,11},{4,12},{5,13},{6,14},{7,15},{8,0},{9,1},... | collective-permute-start | bytes 294920 | tf_op jit(solution)/shard_map/ppermute | solution.py:313
  565.8 6.0 %collective-permute-start.24 = (bf16[3,1,1,1,1,64,256]{6,5,0,4,3,2,1:T(8,128)(2,1)S(1)}, bf16[3,1,1,1,1,64,256]{6,5,0,4,3,2,1:T(8,128)(2,1)S(1)}, u32[]{:S(2)}, u32[]{:S(2)}) collective-permute-start(bf16[3,1,1,1,1,64,256]{6,5,0,4,3,2,1:T(8,128)(2,1)S(1)} %add_convert_fusion.40), channel_id=1, source_target_pairs={{0,8},{1,9},{2,10},{3,11},{4,12},{5,13},{6,14},{7,15},{8,0},{9,1},... | collective-permute-start | bytes 294920 | tf_op jit(solution)/shard_map/ppermute | solution.py:313
  567.6 5.0 collective-permute-start.30
  571.8 1.4 collective-permute-start.25
  (14 other events, 15.0 us)

commit v8 on v7

--- a/solution.py
+++ b/solution.py
@@ -299,7 +299,7 @@
             pltpu.SMEM((frames,), jnp.int32),
         ],
         cost_estimate=pl.CostEstimate(
-            flops=pairs * 10 * PATCHES * PATCHES * 256,
+            flops=pairs * 10 * PATCHES * PATCHES * 64,
             bytes_accessed=x.size * 2 * 5,
             transcendentals=pairs * PATCHES * PATCHES,
         ),

time: 580 us -> 561 us (0.967)
  waiting for transfers between devices: 201 us -> 181 us
  Pallas kernels: 181 us -> 187 us
    all_to_all x2, waiting for transfers between devices: 81.7 us -> 62.9 us  [to_heads(): return lax.all_to_all(array, 'seq', 0, 0, tiled=True)]
    unnamed x90 -> x88, local copies, waits for them, and re-layouts: 15.9 us -> 14.9 us
  transfers between devices with their start and end apart: 36 -> 36, of which waited for: 12 -> 13; matrix products, arithmetic and copies ran while one was open for 15% -> 15% of each run, Pallas kernels for 15% -> 16%
where the time goes in v8:
time: 561 us; the launch traced here: 560 us
  Pallas kernels  187 us (33%)
  waiting for transfers between devices  181 us (32%)
  starting transfers between devices  72.8 us (13%)
  other arithmetic  44.3 us (8%)
  local copies, waits for them, and re-layouts  42.8 us (8%)
  matrix products  25 us (4%)
  between operations  6.13 us (1%)
    ppermute x31, waiting for transfers between devices, exchange(): lax.ppermute(value, axis, [(source, source ^ bit) for source in range(cou...  89.8 us
    all_to_all x2, waiting for transfers between devices, to_heads(): return lax.all_to_all(array, 'seq', 0, 0, tiled=True)  62.9 us
    pallas_call x1, Pallas kernels, attend_back(): pl.pallas_call(functools.partial(attend_back_kernel, per_device), out_sha...  57.7 us
    pallas_call x2, Pallas kernels, feed(): pl.pallas_call(functools.partial(feed_kernel, before is not None), grid_s...  45.2 us
    pallas_call x1, Pallas kernels, attend(): pl.pallas_call(functools.partial(attend_kernel, per_device), out_shape=ou...  43.7 us
    ppermute x31, starting transfers between devices, exchange(): lax.ppermute(value, axis, [(source, source ^ bit) for source in range(cou...  29.4 us
    convert_element_type x22, other arithmetic, pick(): return (pieces[0].astype(F32) + pieces[1].astype(F32)).astype(BF16)  28 us
    all_to_all x2, starting transfers between devices, to_tokens(): return lax.all_to_all(array, 'seq', 0, 0, tiled=True)[:heads]  23.9 us
  transfers between devices with their start and end apart: 36, of which 13 were waited for; matrix products, arithmetic and copies ran while one was open for 15% of the time, Pallas kernels for 16%

profile of v8, /device:TPU:0, one launch (start us, length us, event | category | flops | bytes accessed | tf_op | source)
XLA Modules:
  0.0 559.9 jit_solution(13333944913546576548)
XLA Ops:
  0.6 1.3 fusion.88
  7.5 2.9 fusion.7
  11.2 2.8 copy-done
  14.0 11.4 %project.1 = (bf16[512,1024]{1,0:T(8,128)(2,1)S(1)}, bf16[16,6,64,256]{3,2,1,0:T(8,128)(2,1)S(1)}) custom-call(bf16[512,1024]{1,0:T(8,128)(2,1)S(1)} %bitcast.145, f32[2,1024]{1,0:T(2,128)S(1)} %get-tuple-element.224.shift_ref, f32[2,1024]{1,0:T(2,128)S(1)} %get-tuple-element.223.scale_ref.refs_3_, bf16[1024,3072]{1,0:T(8,128)(2,1)S(1)} %copy-done, ...), custom_call_target="tpu_custom_call" | custom-call | flops 3221225472 | bytes 11534336 | tf_op jit(solution)/shard_map/project/pallas_call | solution.py:490
  25.4 1.6 copy-done.3
  27.0 8.5 %all-to-all-start = ((bf16[16,6,64,256]{3,2,1,0:T(8,128)(2,1)}), bf16[16,6,64,256]{3,2,1,0:T(8,128)(2,1)}, u32[]{:S(2)}, u32[]{:S(2)}) async-start(bf16[16,6,64,256]{3,2,1,0:T(8,128)(2,1)} %copy-done.3), calls=%async_computation | async-start | bytes 6291456 | tf_op jit(solution)/shard_map/all_to_all | solution.py:968
  35.6 4.7 fusion.2
  44.2 52.2 %all-to-all-done.x_ref = bf16[16,6,64,256]{3,2,1,0:T(8,128)(2,1)} async-done(((bf16[16,6,64,256]{3,2,1,0:T(8,128)(2,1)}), bf16[16,6,64,256]{3,2,1,0:T(8,128)(2,1)}, u32[]{:S(2)}, u32[]{:S(2)}) %all-to-all-start) | async-done | bytes 3145760 | tf_op jit(solution)/shard_map/all_to_all | solution.py:968
  96.5 43.7 %attend.1 = (bf16[16,2,64,256]{3,2,1,0:T(8,128)(2,1)S(1)}, f32[16,2,64,256]{3,2,1,0:T(8,128)S(1)}, f32[32,256]{1,0:T(8,128)S(1)}, bf16[32,256,128]{2,1,0:T(8,128)(2,1)S(1)}) custom-call(s32[32]{0:T(128)S(1)} %bitcast.154, s32[32]{0:T(128)S(1)} %bitcast.156, bf16[16,6,64,256]{3,2,1,0:T(8,128)(2,1)} %all-to-all-done.x_ref), custom_call_target="tpu_custom_call" | custom-call | flops 12884901888 | bytes 9437184 | tf_op jit(solution)/shard_map/attend/pallas_call | solution.py:184
  141.1 1.3 copy-done.13
  142.4 1.3 copy-done.14
  144.4 15.3 %all-to-all-start.1 = ((bf16[16,2,64,256]{3,2,1,0:T(8,128)(2,1)}), bf16[16,2,64,256]{3,2,1,0:T(8,128)(2,1)}, u32[]{:S(2)}, u32[]{:S(2)}) async-start(bf16[16,2,64,256]{3,2,1,0:T(8,128)(2,1)} %copy-done.6), calls=%async_computation.1 | async-start | bytes 2097152 | tf_op jit(solution)/shard_map/all_to_all | solution.py:971
  159.7 23.3 %all-to-all-done.1 = bf16[16,2,64,256]{3,2,1,0:T(8,128)(2,1)} async-done(((bf16[16,2,64,256]{3,2,1,0:T(8,128)(2,1)}), bf16[16,2,64,256]{3,2,1,0:T(8,128)(2,1)}, u32[]{:S(2)}, u32[]{:S(2)}) %all-to-all-start.1) | async-done | bytes 1048608 | tf_op jit(solution)/shard_map/all_to_all | solution.py:971
  183.0 1.4 fusion.78
  188.4 3.2 fusion.10
  191.6 21.9 %feed0.1 = (f32[512,1024]{1,0:T(8,128)}, f32[512,1024]{1,0:T(8,128)}, bf16[1024,2048]{1,0:T(8,128)(2,1)}, bf16[2048,1024]{1,0:T(8,128)(2,1)}, f32[1,2048]{1,0:T(1,128)}) custom-call(s32[1]{0:T(128)} %bitcast.20.which_ref, bf16[512,1024]{1,0:T(8,128)(2,1)} %get-tuple-element.139.in_ref, bf16[512,1024]{1,0:T(8,128)(2,1)} %fusion.13.d_out_ref, ...), custom_call_target="tpu_custom_call" | custom-call | flops 12884901888 | bytes 25165824 | tf_op jit(solution)/shard_map/feed0/pallas_call | solution.py:596
  218.0 23.3 %feed1.1 = (f32[512,1024]{1,0:T(8,128)}, f32[512,1024]{1,0:T(8,128)}, bf16[1024,2048]{1,0:T(8,128)(2,1)}, bf16[2048,1024]{1,0:T(8,128)(2,1)}, f32[1,2048]{1,0:T(1,128)}) custom-call(s32[1]{0:T(128)} %bitcast.which_ref.pack_ref, bf16[512,1024]{1,0:T(8,128)(2,1)} %get-tuple-element.139.in_ref, bf16[512,1024]{1,0:T(8,128)(2,1)} %fusion.13.d_out_ref, ...), custom_call_target="tpu_custom_call" | custom-call | flops 12884901888 | bytes 25165824 | tf_op jit(solution)/shard_map/feed1/pallas_call | solution.py:596
  242.2 8.1 %middle_back.1 = (f32[512,1024]{1,0:T(8,128)S(1)}, bf16[512,1024]{1,0:T(8,128)(2,1)S(1)}, bf16[512,1024]{1,0:T(8,128)(2,1)}, bf16[16,3,64,256]{3,2,1,0:T(8,128)(2,1)S(1)}) custom-call(f32[512,1024]{1,0:T(8,128)} %get-tuple-element.85.d_in_ref, f32[512,1024]{1,0:T(8,128)} %get-tuple-element.140.middle_ref, bf16[512,1024]{1,0:T(8,128)(2,1)S(1)} %bitcast.147, ...), custom_call_target="tpu_custom_call" | custom-call | flops 1073741824 | bytes 12582912 | tf_op jit(solution)/shard_map/middle_back/pallas_call | solution.py:720
  250.3 1.3 copy-done.4
  253.7 6.2 %all-to-all-start.2 = ((bf16[16,3,64,256]{3,2,1,0:T(8,128)(2,1)}), bf16[16,3,64,256]{3,2,1,0:T(8,128)(2,1)}, u32[]{:S(2)}, u32[]{:S(2)}) async-start(bf16[16,3,64,256]{3,2,1,0:T(8,128)(2,1)} %copy-done.5), calls=%async_computation.2 | async-start | bytes 3145728 | tf_op jit(solution)/shard_map/all_to_all | solution.py:968
  259.9 7.8 %add_convert_fusion.1 = (bf16[2,2,2,1,128,1024]{5,4,3,2,1,0:T(8,128)(2,1)}, bf16[2,2,2,1,128,1024]{5,4,3,2,1,0:T(8,128)(2,1)}) fusion(bf16[2,2,2,2,128,1024]{5,4,3,2,1,0:T(8,128)(2,1)} %bitcast.33, s32[]{:T(128)S(6)} %select_n.94, bf16[2,2,2,2,128,1024]{5,4,3,2,1,0:T(8,128)(2,1)} %bitcast.168, s32[]{:T(128)S(6)} %select_n.92), kind=kLoop, calls=%fused_computation.5 | loop fusion | flops 8388608 | bytes 12582920 | tf_op jit(solution)/shard_map/convert_element_type | solution.py:346
  267.7 2.0 collective-permute-start.2
  269.8 6.6 %add_convert_fusion = (bf16[2,2,1,2,64,2048]{5,4,3,2,1,0:T(8,128)(2,1)}, bf16[2,2,1,2,64,2048]{5,4,3,2,1,0:T(8,128)(2,1)}) fusion(bf16[2,2,2,2,64,2048]{5,4,3,2,1,0:T(8,128)(2,1)} %bitcast.36, s32[]{:T(128)S(6)} %select_n.95, bf16[2,2,2,2,64,2048]{5,4,3,2,1,0:T(8,128)(2,1)S(1)} %bitcast.167, s32[]{:T(128)S(6)} %select_n.93), kind=kLoop, calls=%fused_computation.4 | loop fusion | flops 8388608 | bytes 12582920 | tf_op jit(solution)/shard_map/convert_element_type | solution.py:346
  276.3 1.5 collective-permute-start.3
  277.8 2.9 convolution_convert_fusion
  280.7 2.9 convolution_convert_fusion.1
  283.6 10.6 %all-to-all-done.2.d_mix_ref = bf16[16,3,64,256]{3,2,1,0:T(8,128)(2,1)} async-done(((bf16[16,3,64,256]{3,2,1,0:T(8,128)(2,1)}), bf16[16,3,64,256]{3,2,1,0:T(8,128)(2,1)}, u32[]{:S(2)}, u32[]{:S(2)}) %all-to-all-start.2) | async-done | bytes 1572896 | tf_op jit(solution)/shard_map/all_to_all | solution.py:968
  299.6 57.7 %attend_back.1 = bf16[16,6,64,256]{3,2,1,0:T(8,128)(2,1)} custom-call(s32[32]{0:T(128)} %bitcast.152, s32[32]{0:T(128)} %bitcast.155, bf16[16,6,64,256]{3,2,1,0:T(8,128)(2,1)} %all-to-all-done.x_ref, bf16[32,256,128]{2,1,0:T(8,128)(2,1)} %copy-done.14, f32[16,2,64,256]{3,2,1,0:T(8,128)} %copy-done.13, f32[32,256]{1,0:T(8,128)} %copy-done.15, ...), custom_call_target="tpu_custom_call" | custom-call | flops 8053063680 | bytes 15728640 | tf_op jit(solution)/shard_map/attend_back/pallas_call | solution.py:292
  357.3 8.6 %all-to-all-start.3 = ((bf16[16,6,64,256]{3,2,1,0:T(8,128)(2,1)}), bf16[16,6,64,256]{3,2,1,0:T(8,128)(2,1)}, u32[]{:S(2)}, u32[]{:S(2)}) async-start(bf16[16,6,64,256]{3,2,1,0:T(8,128)(2,1)} %attend_back.1), calls=%async_computation.3 | async-start | bytes 6291456 | tf_op jit(solution)/shard_map/all_to_all | solution.py:971
  366.1 2.6 fusion.81
  369.5 1.3 fusion.24
  372.6 1.4 fusion.20
  374.1 1.4 fusion.18
  375.6 1.5 fusion.22
  377.8 2.4 add_convert_fusion.5
  380.2 2.1 collective-permute-start.6
  382.3 2.2 add_convert_fusion.7
  384.5 1.5 collective-permute-start.5
  386.0 1.5 add_convert_fusion.15
  389.5 55.1 %collective-permute-done.7 = bf16[2,2,2,1,64,512]{5,4,3,2,1,0:T(8,128)(2,1)S(1)} collective-permute-done((bf16[2,2,2,1,64,512]{5,4,3,2,1,0:T(8,128)(2,1)S(1)}, bf16[2,2,2,1,64,512]{5,4,3,2,1,0:T(8,128)(2,1)S(1)}, u32[]{:S(2)}, u32[]{:S(2)}) %collective-permute-start.7) | collective-permute-done | bytes 524320 | tf_op jit(solution)/shard_map/ppermute | solution.py:313
  448.0 8.3 %unproject0.1 = (f32[512,1024]{1,0:T(8,128)S(1)}, bf16[3,1024,512]{2,1,0:T(8,128)(2,1)}, f32[3,1,512]{2,1,0:T(1,128)S(1)}) custom-call(s32[1]{0:T(128)} %bitcast.20.which_ref, bf16[512,1024]{1,0:T(8,128)(2,1)S(1)} %get-tuple-element.76.in_ref, bf16[16,6,64,256]{3,2,1,0:T(8,128)(2,1)} %all-to-all-done.3.back_ref, bf16[1024,3072]{1,0:T(8,128)(2,1)} %wv_ref.5, ...), custom_call_target="tpu_custom_call" | custom-call | flops 3221225472 | bytes 12582912 | tf_op jit(solution)/shard_map/unproject0/pallas_call | solution.py:883
  456.2 11.3 %unproject1.1 = (bf16[3,1024,512]{2,1,0:T(8,128)(2,1)}, bf16[512,1024]{1,0:T(8,128)(2,1)}, bf16[16,16,1024]{2,1,0:T(8,128)(2,1)}) custom-call(s32[1]{0:T(128)} %bitcast.which_ref.pack_ref, bf16[512,1024]{1,0:T(8,128)(2,1)S(1)} %get-tuple-element.76.in_ref, bf16[16,6,64,256]{3,2,1,0:T(8,128)(2,1)} %all-to-all-done.3.back_ref, bf16[1024,3072]{1,0:T(8,128)(2,1)} %wv_ref.5, ...), custom_call_target="tpu_custom_call" | custom-call | flops 3221225472 | bytes 12582912 | tf_op jit(solution)/shard_map/unproject1/pallas_call | solution.py:883
  467.6 4.7 all-to-all-start.4
  473.0 2.0 collective-permute-start.17
  475.0 1.5 collective-permute-start.11
  477.0 2.1 fusion.76
  479.1 1.4 constant_dynamic-slice_fusion
  481.7 5.4 all-to-all-done.4
  494.6 2.1 fusion.77
  498.1 5.3 collective-permute-done.14
  503.9 1.5 collective-permute-start.26
  505.5 1.5 collective-permute-start.21
  509.7 2.3 collective-permute-start.15
  514.4 2.6 collective-permute-start.19
  517.0 4.5 collective-permute-done.26
  521.7 1.5 collective-permute-start.27
  523.5 1.3 collective-permute-start.22
  524.8 10.7 %collective-permute-done.19 = bf16[1,1,1,1,64,512]{5,4,3,2,1,0:T(8,128)(2,1)S(1)} collective-permute-done((bf16[1,1,1,1,64,512]{5,4,3,2,1,0:T(8,128)(2,1)S(1)}, bf16[1,1,1,1,64,512]{5,4,3,2,1,0:T(8,128)(2,1)S(1)}, u32[]{:S(2)}, u32[]{:S(2)}) %collective-permute-start.19) | collective-permute-done | bytes 65568 | tf_op jit(solution)/shard_map/ppermute | solution.py:313
  537.6 2.1 collective-permute-start.23
  540.8 4.4 collective-permute-done.28
  546.3 3.3 collective-permute-done.23
  550.5 3.1 collective-permute-done.29
  553.7 2.8 collective-permute-done.24
  557.9 1.8 settle.1
  (280 shorter events, 57.0 us)
Async XLA Ops:
  7.4 3.0 copy-start.11
  7.4 3.7 copy-start.1
  7.5 3.7 copy-start.7
  11.2 2.8 copy-start
  25.4 1.6 copy-start.3
  27.0 8.5 %slice-start = ((f32[6144]{0:T(1024)}), f32[4096]{0:T(1024)S(1)}, s32[]{:S(2)}) async-start(f32[6144]{0:T(1024)} %param.23), calls=%async_computation.5 | async-start | bytes 32768 | tf_op jit(solution)/shard_map/slice | solution.py:978
  27.0 69.5 %all-to-all-start = ((bf16[16,6,64,256]{3,2,1,0:T(8,128)(2,1)}), bf16[16,6,64,256]{3,2,1,0:T(8,128)(2,1)}, u32[]{:S(2)}, u32[]{:S(2)}) async-start(bf16[16,6,64,256]{3,2,1,0:T(8,128)(2,1)} %copy-done.3), calls=%async_computation | async-start | bytes 6291456 | tf_op jit(solution)/shard_map/all_to_all | solution.py:968
  35.6 4.7 copy-start.2
  42.9 53.6 %copy-start.12 = (s32[1,32]{1,0:T(1,128)S(1)}, s32[1,32]{1,0:T(1,128)}, u32[]{:S(2)}) copy-start(s32[1,32]{1,0:T(1,128)} %param.20) | copy-start | bytes 388
  144.4 38.6 %all-to-all-start.1 = ((bf16[16,2,64,256]{3,2,1,0:T(8,128)(2,1)}), bf16[16,2,64,256]{3,2,1,0:T(8,128)(2,1)}, u32[]{:S(2)}, u32[]{:S(2)}) async-start(bf16[16,2,64,256]{3,2,1,0:T(8,128)(2,1)} %copy-done.6), calls=%async_computation.1 | async-start | bytes 2097152 | tf_op jit(solution)/shard_map/all_to_all | solution.py:971
  183.0 1.9 copy-start.16
  191.6 22.5 %copy-start.39 = (s32[1,2]{1,0:T(1,128)S(1)}, s32[1,2]{1,0:T(1,128)}, u32[]{:S(2)}) copy-start(s32[1,2]{1,0:T(1,128)} %param.18) | copy-start | bytes 28
  213.5 46.4 %collective-permute-start = (bf16[2048,1024]{1,0:T(8,128)(2,1)}, bf16[2048,1024]{1,0:T(8,128)(2,1)}, u32[]{:S(2)}, u32[]{:S(2)}) collective-permute-start(bf16[2048,1024]{1,0:T(8,128)(2,1)} %get-tuple-element.97), channel_id=1, source_target_pairs={{0,16},{16,0},{1,17},{17,1},{2,18},{18,2},{3,19},{19,3},{4,20},{20... | collective-permute-start | bytes 12582920 | tf_op jit(solution)/shard_map/ppermute | solution.py:313
  213.6 56.2 %collective-permute-start.1 = (bf16[1024,2048]{1,0:T(8,128)(2,1)}, bf16[1024,2048]{1,0:T(8,128)(2,1)}, u32[]{:S(2)}, u32[]{:S(2)}) collective-permute-start(bf16[1024,2048]{1,0:T(8,128)(2,1)} %get-tuple-element.99), channel_id=1, source_target_pairs={{0,16},{16,0},{1,17},{17,1},{2,18},{18,2},{3,19},{19,3},{4,20},{20... | collective-permute-start | bytes 12582920 | tf_op jit(solution)/shard_map/ppermute | solution.py:313
  218.0 23.3 %copy-start.36 = (f32[1,2048]{1,0:T(1,128)S(1)}, f32[1,2048]{1,0:T(1,128)}, u32[]{:S(2)}) copy-start(f32[1,2048]{1,0:T(1,128)} %get-tuple-element.88) | copy-start | bytes 24580
  218.0 24.1 %copy-start.8 = (f32[1024]{0:T(1024)S(1)}, f32[1024]{0:T(1024)}, u32[]{:S(2)}) copy-start(f32[1024]{0:T(1024)} %param.31) | copy-start | bytes 12292
  253.7 40.5 %all-to-all-start.2 = ((bf16[16,3,64,256]{3,2,1,0:T(8,128)(2,1)}), bf16[16,3,64,256]{3,2,1,0:T(8,128)(2,1)}, u32[]{:S(2)}, u32[]{:S(2)}) async-start(bf16[16,3,64,256]{3,2,1,0:T(8,128)(2,1)} %copy-done.5), calls=%async_computation.2 | async-start | bytes 3145728 | tf_op jit(solution)/shard_map/all_to_all | solution.py:968
  259.9 9.8 %copy-start.19 = (bf16[1024,2048]{1,0:T(8,128)(2,1)S(1)}, bf16[1024,2048]{1,0:T(8,128)(2,1)}, u32[]{:S(2)}) copy-start(bf16[1024,2048]{1,0:T(8,128)(2,1)} %get-tuple-element.98) | copy-start | bytes 12582916
  267.7 89.6 %collective-permute-start.2 = (bf16[2,2,2,1,128,1024]{5,4,3,2,1,0:T(8,128)(2,1)}, bf16[2,2,2,1,128,1024]{5,4,3,2,1,0:T(8,128)(2,1)}, u32[]{:S(2)}, u32[]{:S(2)}) collective-permute-start(bf16[2,2,2,1,128,1024]{5,4,3,2,1,0:T(8,128)(2,1)} %get-tuple-element.145), channel_id=1, source_target_pairs={{0,1},{1,0},{2,3},{3,2},{4,5},{5,4},{6,7},{7,6},{8,9},{9,8},{10,11... | collective-permute-start | bytes 6291464 | tf_op jit(solution)/shard_map/ppermute | solution.py:313
  269.7 8.1 %copy-start.10 = (bf16[512,1024]{1,0:T(8,128)(2,1)S(1)}, bf16[512,1024]{1,0:T(8,128)(2,1)}, u32[]{:S(2)}) copy-start(bf16[512,1024]{1,0:T(8,128)(2,1)} %copy-done.9) | copy-start | bytes 3145732
  276.3 81.0 %collective-permute-start.3 = (bf16[2,2,1,2,64,2048]{5,4,3,2,1,0:T(8,128)(2,1)}, bf16[2,2,1,2,64,2048]{5,4,3,2,1,0:T(8,128)(2,1)}, u32[]{:S(2)}, u32[]{:S(2)}) collective-permute-start(bf16[2,2,1,2,64,2048]{5,4,3,2,1,0:T(8,128)(2,1)} %get-tuple-element.143), channel_id=1, source_target_pairs={{0,2},{1,3},{2,0},{3,1},{4,6},{5,7},{6,4},{7,5},{8,10},{9,11},{10,... | collective-permute-start | bytes 6291464 | tf_op jit(solution)/shard_map/ppermute | solution.py:313
  280.7 76.7 %collective-permute-start.4 = (bf16[1024,512]{1,0:T(8,128)(2,1)}, bf16[1024,512]{1,0:T(8,128)(2,1)}, u32[]{:S(2)}, u32[]{:S(2)}) collective-permute-start(bf16[1024,512]{1,0:T(8,128)(2,1)} %convolution_convert_fusion), channel_id=1, source_target_pairs={{0,16},{16,0},{1,17},{17,1},{2,18},{18,2},{3,19},{19,3},{4,20},{20... | collective-permute-start | bytes 3145736 | tf_op jit(solution)/shard_map/ppermute | solution.py:313
  296.1 74.7 %collective-permute-start.8 = (bf16[16,16,1024]{2,1,0:T(8,128)(2,1)}, bf16[16,16,1024]{2,1,0:T(8,128)(2,1)S(1)}, u32[]{:S(2)}, u32[]{:S(2)}) collective-permute-start(bf16[16,16,1024]{2,1,0:T(8,128)(2,1)} %bitcast.66), channel_id=1, source_target_pairs={{0,16},{16,0},{1,17},{17,1},{2,18},{18,2},{3,19},{19,3},{4,20},{20... | collective-permute-start | bytes 1572872 | tf_op jit(solution)/shard_map/ppermute | solution.py:313
  357.3 90.6 %all-to-all-start.3 = ((bf16[16,6,64,256]{3,2,1,0:T(8,128)(2,1)}), bf16[16,6,64,256]{3,2,1,0:T(8,128)(2,1)}, u32[]{:S(2)}, u32[]{:S(2)}) async-start(bf16[16,6,64,256]{3,2,1,0:T(8,128)(2,1)} %attend_back.1), calls=%async_computation.3 | async-start | bytes 6291456 | tf_op jit(solution)/shard_map/all_to_all | solution.py:971
  370.8 1.3 copy-start.32
  372.6 1.5 copy-start.37
  375.6 2.2 copy-start.17
  377.7 4.5 copy-start.18
  380.2 5.8 %copy-start.28 = (bf16[1024,512]{1,0:T(8,128)(2,1)S(1)}, bf16[1024,512]{1,0:T(8,128)(2,1)}, u32[]{:S(2)}) copy-start(bf16[1024,512]{1,0:T(8,128)(2,1)} %convolution_convert_fusion.1) | copy-start | bytes 3145732
  380.2 64.6 %collective-permute-start.6 = (bf16[2,2,1,1,128,1024]{5,4,3,2,1,0:T(8,128)(2,1)S(1)}, bf16[2,2,1,1,128,1024]{5,4,3,2,1,0:T(8,128)(2,1)S(1)}, u32[]{:S(2)}, u32[]{:S(2)}) collective-permute-start(bf16[2,2,1,1,128,1024]{5,4,3,2,1,0:T(8,128)(2,1)S(1)} %get-tuple-element.147), channel_id=1, source_target_pairs={{0,2},{1,3},{2,0},{3,1},{4,6},{5,7},{6,4},{7,5},{8,10},{9,11},{10,... | collective-permute-start | bytes 3145736 | tf_op jit(solution)/shard_map/ppermute | solution.py:313
  384.5 61.5 %collective-permute-start.5 = (bf16[2,2,1,1,64,2048]{5,4,3,2,1,0:T(8,128)(2,1)S(1)}, bf16[2,2,1,1,64,2048]{5,4,3,2,1,0:T(8,128)(2,1)S(1)}, u32[]{:S(2)}, u32[]{:S(2)}) collective-permute-start(bf16[2,2,1,1,64,2048]{5,4,3,2,1,0:T(8,128)(2,1)S(1)} %get-tuple-element.149), channel_id=1, source_target_pairs={{0,1},{1,0},{2,3},{3,2},{4,5},{5,4},{6,7},{7,6},{8,9},{9,8},{10,11... | collective-permute-start | bytes 3145736 | tf_op jit(solution)/shard_map/ppermute | solution.py:313
  387.6 57.0 %collective-permute-start.7 = (bf16[2,2,2,1,64,512]{5,4,3,2,1,0:T(8,128)(2,1)S(1)}, bf16[2,2,2,1,64,512]{5,4,3,2,1,0:T(8,128)(2,1)S(1)}, u32[]{:S(2)}, u32[]{:S(2)}) collective-permute-start(bf16[2,2,2,1,64,512]{5,4,3,2,1,0:T(8,128)(2,1)S(1)} %get-tuple-element.161), channel_id=1, source_target_pairs={{0,1},{1,0},{2,3},{3,2},{4,5},{5,4},{6,7},{7,6},{8,9},{9,8},{10,11... | collective-permute-start | bytes 1572872 | tf_op jit(solution)/shard_map/ppermute | solution.py:313
  444.7 2.4 copy-start.31
  456.2 16.7 %copy-start.38 = (s32[32]{0:T(128)S(1)}, s32[32]{0:T(128)}, u32[]{:S(2)}) copy-start(s32[32]{0:T(128)} %copy-done.37) | copy-start | bytes 388
  467.6 19.5 %all-to-all-start.4 = ((bf16[16,16,1024]{2,1,0:T(8,128)(2,1)}), bf16[16,16,1024]{2,1,0:T(8,128)(2,1)S(1)}, u32[]{:S(2)}, u32[]{:S(2)}) async-start(bf16[16,16,1024]{2,1,0:T(8,128)(2,1)} %get-tuple-element.114), calls=%async_computation.4 | async-start | bytes 1048576 | tf_op jit(solution)/shard_map/all_to_all | solution.py:1130
  473.0 30.6 %collective-permute-start.17 = (bf16[2,2,1,1,64,512]{5,4,3,2,1,0:T(8,128)(2,1)}, bf16[2,2,1,1,64,512]{5,4,3,2,1,0:T(8,128)(2,1)}, u32[]{:S(2)}, u32[]{:S(2)}) collective-permute-start(bf16[2,2,1,1,64,512]{5,4,3,2,1,0:T(8,128)(2,1)} %copy-done.31), channel_id=1, source_target_pairs={{0,2},{1,3},{2,0},{3,1},{4,6},{5,7},{6,4},{7,5},{8,10},{9,11},{10,... | collective-permute-start | bytes 786440 | tf_op jit(solution)/shard_map/ppermute | solution.py:313
  475.0 23.1 %collective-permute-start.11 = (bf16[2,1,1,1,64,2048]{5,4,3,2,1,0:T(8,128)(2,1)}, bf16[2,1,1,1,64,2048]{5,4,3,2,1,0:T(8,128)(2,1)}, u32[]{:S(2)}, u32[]{:S(2)}) collective-permute-start(bf16[2,1,1,1,64,2048]{5,4,3,2,1,0:T(8,128)(2,1)} %copy-done.30), channel_id=1, source_target_pairs={{0,4},{1,5},{2,6},{3,7},{4,0},{5,1},{6,2},{7,3},{8,12},{9,13},{10,... | collective-permute-start | bytes 1572872 | tf_op jit(solution)/shard_map/ppermute | solution.py:313
  476.4 27.0 %collective-permute-start.14 = (bf16[2,1,1,1,128,1024]{5,4,3,2,1,0:T(8,128)(2,1)}, bf16[2,1,1,1,128,1024]{5,4,3,2,1,0:T(8,128)(2,1)}, u32[]{:S(2)}, u32[]{:S(2)}) collective-permute-start(bf16[2,1,1,1,128,1024]{5,4,3,2,1,0:T(8,128)(2,1)} %copy-done.29), channel_id=1, source_target_pairs={{0,4},{1,5},{2,6},{3,7},{4,0},{5,1},{6,2},{7,3},{8,12},{9,13},{10,... | collective-permute-start | bytes 1572872 | tf_op jit(solution)/shard_map/ppermute | solution.py:313
  477.0 17.6 %collective-permute-start.10 = (bf16[3,1024,512]{2,1,0:T(8,128)(2,1)}, bf16[3,1024,512]{2,1,0:T(8,128)(2,1)}, u32[]{:S(2)}, u32[]{:S(2)}) collective-permute-start(bf16[3,1024,512]{2,1,0:T(8,128)(2,1)} %get-tuple-element.116), channel_id=1, source_target_pairs={{0,16},{16,0},{1,17},{17,1},{2,18},{18,2},{3,19},{19,3},{4,20},{20... | collective-permute-start | bytes 9437192 | tf_op jit(solution)/shard_map/ppermute | solution.py:313
  480.5 7.3 %copy-start.33 = (f32[32,64]{1,0:T(8,128)S(1)}, f32[32,64]{1,0:T(8,128)}, u32[]{:S(2)}) copy-start(f32[32,64]{1,0:T(8,128)} %copy-done.32) | copy-start | bytes 24580
  487.1 2.3 collective-permute-start.9
  498.1 5.5 copy-start.22
  503.6 5.1 copy-start.27
  503.6 8.5 %copy-start.26 = (bf16[2,1,1,1,64,2048]{5,4,3,2,1,0:T(8,128)(2,1)S(1)}, bf16[2,1,1,1,64,2048]{5,4,3,2,1,0:T(8,128)(2,1)}, u32[]{:S(2)}) copy-start(bf16[2,1,1,1,64,2048]{5,4,3,2,1,0:T(8,128)(2,1)} %get-tuple-element.119) | copy-start | bytes 1572868
  503.6 10.2 %copy-start.20 = (bf16[3,2,2,1,2,64,256]{6,5,4,3,2,1,0:T(8,128)(2,1)S(1)}, bf16[3,2,2,1,2,64,256]{6,5,4,3,2,1,0:T(8,128)(2,1)}, u32[]{:S(2)}) copy-start(bf16[3,2,2,1,2,64,256]{6,5,4,3,2,1,0:T(8,128)(2,1)} %get-tuple-element.164) | copy-start | bytes 2359300
  503.9 17.5 %collective-permute-start.26 = (bf16[3,2,2,1,2,64,256]{6,5,0,4,3,2,1:T(8,128)(2,1)S(1)}, bf16[3,2,2,1,2,64,256]{6,5,0,4,3,2,1:T(8,128)(2,1)S(1)}, u32[]{:S(2)}, u32[]{:S(2)}) collective-permute-start(bf16[3,2,2,1,2,64,256]{6,5,0,4,3,2,1:T(8,128)(2,1)S(1)} %add_convert_fusion.11), channel_id=1, source_target_pairs={{0,2},{1,3},{2,0},{3,1},{4,6},{5,7},{6,4},{7,5},{8,10},{9,11},{10,... | collective-permute-start | bytes 2359304 | tf_op jit(solution)/shard_map/ppermute | solution.py:313
  505.5 17.8 %collective-permute-start.21 = (bf16[3,2,2,2,1,64,256]{6,5,0,4,3,2,1:T(8,128)(2,1)S(1)}, bf16[3,2,2,2,1,64,256]{6,5,0,4,3,2,1:T(8,128)(2,1)S(1)}, u32[]{:S(2)}, u32[]{:S(2)}) collective-permute-start(bf16[3,2,2,2,1,64,256]{6,5,0,4,3,2,1:T(8,128)(2,1)S(1)} %add_convert_fusion.10), channel_id=1, source_target_pairs={{0,1},{1,0},{2,3},{3,2},{4,5},{5,4},{6,7},{7,6},{8,9},{9,8},{10,11... | collective-permute-start | bytes 2359304 | tf_op jit(solution)/shard_map/ppermute | solution.py:313
  508.0 6.1 %copy-start.21 = (bf16[3,2,2,2,1,64,256]{6,5,4,3,2,1,0:T(8,128)(2,1)S(1)}, bf16[3,2,2,2,1,64,256]{6,5,4,3,2,1,0:T(8,128)(2,1)}, u32[]{:S(2)}) copy-start(bf16[3,2,2,2,1,64,256]{6,5,4,3,2,1,0:T(8,128)(2,1)} %get-tuple-element.170) | copy-start | bytes 2359300
  508.0 6.4 %collective-permute-start.18 = (bf16[2,1,1,1,64,512]{5,4,3,2,1,0:T(8,128)(2,1)S(1)}, bf16[2,1,1,1,64,512]{5,4,3,2,1,0:T(8,128)(2,1)S(1)}, u32[]{:S(2)}, u32[]{:S(2)}) collective-permute-start(bf16[2,1,1,1,64,512]{5,4,3,2,1,0:T(8,128)(2,1)S(1)} %get-tuple-element.183), channel_id=1, source_target_pairs={{0,4},{1,5},{2,6},{3,7},{4,0},{5,1},{6,2},{7,3},{8,12},{9,13},{10,... | collective-permute-start | bytes 393224 | tf_op jit(solution)/shard_map/ppermute | solution.py:313
  509.7 25.9 %collective-permute-start.15 = (bf16[1,1,1,1,128,1024]{5,4,3,2,1,0:T(8,128)(2,1)S(1)}, bf16[1,1,1,1,128,1024]{5,4,3,2,1,0:T(8,128)(2,1)S(1)}, u32[]{:S(2)}, u32[]{:S(2)}) collective-permute-start(bf16[1,1,1,1,128,1024]{5,4,3,2,1,0:T(8,128)(2,1)S(1)} %add_convert_fusion.24), channel_id=1, source_target_pairs={{0,8},{1,9},{2,10},{3,11},{4,12},{5,13},{6,14},{7,15},{8,0},{9,1},... | collective-permute-start | bytes 786440 | tf_op jit(solution)/shard_map/ppermute | solution.py:313
  513.1 26.5 %collective-permute-start.12 = (bf16[1,1,1,1,64,2048]{5,4,3,2,1,0:T(8,128)(2,1)S(1)}, bf16[1,1,1,1,64,2048]{5,4,3,2,1,0:T(8,128)(2,1)S(1)}, u32[]{:S(2)}, u32[]{:S(2)}) collective-permute-start(bf16[1,1,1,1,64,2048]{5,4,3,2,1,0:T(8,128)(2,1)S(1)} %add_convert_fusion.27), channel_id=1, source_target_pairs={{0,8},{1,9},{2,10},{3,11},{4,12},{5,13},{6,14},{7,15},{8,0},{9,1},... | collective-permute-start | bytes 786440 | tf_op jit(solution)/shard_map/ppermute | solution.py:313
  514.4 21.1 %collective-permute-start.19 = (bf16[1,1,1,1,64,512]{5,4,3,2,1,0:T(8,128)(2,1)S(1)}, bf16[1,1,1,1,64,512]{5,4,3,2,1,0:T(8,128)(2,1)S(1)}, u32[]{:S(2)}, u32[]{:S(2)}) collective-permute-start(bf16[1,1,1,1,64,512]{5,4,3,2,1,0:T(8,128)(2,1)S(1)} %add_convert_fusion.43), channel_id=1, source_target_pairs={{0,8},{1,9},{2,10},{3,11},{4,12},{5,13},{6,14},{7,15},{8,0},{9,1},... | collective-permute-start | bytes 196616 | tf_op jit(solution)/shard_map/ppermute | solution.py:313
  521.7 15.5 %collective-permute-start.27 = (bf16[3,2,2,1,1,64,256]{6,5,0,4,3,2,1:T(8,128)(2,1)S(1)}, bf16[3,2,2,1,1,64,256]{6,5,0,4,3,2,1:T(8,128)(2,1)S(1)}, u32[]{:S(2)}, u32[]{:S(2)}) collective-permute-start(bf16[3,2,2,1,1,64,256]{6,5,0,4,3,2,1:T(8,128)(2,1)S(1)} %get-tuple-element.163), channel_id=1, source_target_pairs={{0,1},{1,0},{2,3},{3,2},{4,5},{5,4},{6,7},{7,6},{8,9},{9,8},{10,11... | collective-permute-start | bytes 1179656 | tf_op jit(solution)/shard_map/ppermute | solution.py:313
  523.5 14.0 %collective-permute-start.22 = (bf16[3,2,2,1,1,64,256]{6,5,0,4,3,2,1:T(8,128)(2,1)S(1)}, bf16[3,2,2,1,1,64,256]{6,5,0,4,3,2,1:T(8,128)(2,1)S(1)}, u32[]{:S(2)}, u32[]{:S(2)}) collective-permute-start(bf16[3,2,2,1,1,64,256]{6,5,0,4,3,2,1:T(8,128)(2,1)S(1)} %get-tuple-element.169), channel_id=1, source_target_pairs={{0,2},{1,3},{2,0},{3,1},{4,6},{5,7},{6,4},{7,5},{8,10},{9,11},{10,... | collective-permute-start | bytes 1179656 | tf_op jit(solution)/shard_map/ppermute | solution.py:313
  535.5 21.8 %collective-permute-start.20 = (bf16[64,512]{1,0:T(8,128)(2,1)S(1)}, bf16[64,512]{1,0:T(8,128)(2,1)S(1)}, u32[]{:S(2)}, u32[]{:S(2)}) collective-permute-start(bf16[64,512]{1,0:T(8,128)(2,1)S(1)} %fusion.36.refs_4_), channel_id=1, source_target_pairs={{0,16},{16,0},{1,17},{17,1},{2,18},{18,2},{3,19},{19,3},{4,20},{20... | collective-permute-start | bytes 196616 | tf_op jit(solution)/shard_map/ppermute | solution.py:313
  536.7 20.6 %collective-permute-start.16 = (bf16[128,1024]{1,0:T(8,128)(2,1)S(1)}, bf16[128,1024]{1,0:T(8,128)(2,1)S(1)}, u32[]{:S(2)}, u32[]{:S(2)}) collective-permute-start(bf16[128,1024]{1,0:T(8,128)(2,1)S(1)} %fusion.27.refs_2_), channel_id=1, source_target_pairs={{0,16},{16,0},{1,17},{17,1},{2,18},{18,2},{3,19},{19,3},{4,20},{20... | collective-permute-start | bytes 786440 | tf_op jit(solution)/shard_map/ppermute | solution.py:313
  537.4 19.3 %copy-start.34 = (f32[4096]{0:T(1024)S(1)}, f32[4096]{0:T(1024)}, u32[]{:S(2)}) copy-start(f32[4096]{0:T(1024)} %get-tuple-element.252) | copy-start | bytes 49156
  537.4 7.8 %collective-permute-start.28 = (bf16[3,2,1,1,1,64,256]{6,5,0,4,3,2,1:T(8,128)(2,1)S(1)}, bf16[3,2,1,1,1,64,256]{6,5,0,4,3,2,1:T(8,128)(2,1)S(1)}, u32[]{:S(2)}, u32[]{:S(2)}) collective-permute-start(bf16[3,2,1,1,1,64,256]{6,5,0,4,3,2,1:T(8,128)(2,1)S(1)} %get-tuple-element.179), channel_id=1, source_target_pairs={{0,4},{1,5},{2,6},{3,7},{4,0},{5,1},{6,2},{7,3},{8,12},{9,13},{10,... | collective-permute-start | bytes 589832 | tf_op jit(solution)/shard_map/ppermute | solution.py:313
  537.6 12.0 %collective-permute-start.23 = (bf16[3,2,1,1,1,64,256]{6,5,0,4,3,2,1:T(8,128)(2,1)S(1)}, bf16[3,2,1,1,1,64,256]{6,5,0,4,3,2,1:T(8,128)(2,1)S(1)}, u32[]{:S(2)}, u32[]{:S(2)}) collective-permute-start(bf16[3,2,1,1,1,64,256]{6,5,0,4,3,2,1:T(8,128)(2,1)S(1)} %get-tuple-element.181), channel_id=1, source_target_pairs={{0,4},{1,5},{2,6},{3,7},{4,0},{5,1},{6,2},{7,3},{8,12},{9,13},{10,... | collective-permute-start | bytes 589832 | tf_op jit(solution)/shard_map/ppermute | solution.py:313
  540.7 16.6 %collective-permute-start.13 = (bf16[64,2048]{1,0:T(8,128)(2,1)S(1)}, bf16[64,2048]{1,0:T(8,128)(2,1)S(1)}, u32[]{:S(2)}, u32[]{:S(2)}) collective-permute-start(bf16[64,2048]{1,0:T(8,128)(2,1)S(1)} %fusion.26.refs_0_), channel_id=1, source_target_pairs={{0,16},{16,0},{1,17},{17,1},{2,18},{18,2},{3,19},{19,3},{4,20},{20... | collective-permute-start | bytes 786440 | tf_op jit(solution)/shard_map/ppermute | solution.py:313
  545.2 8.3 %collective-permute-start.29 = (bf16[3,1,1,1,1,64,256]{6,5,0,4,3,2,1:T(8,128)(2,1)S(1)}, bf16[3,1,1,1,1,64,256]{6,5,0,4,3,2,1:T(8,128)(2,1)S(1)}, u32[]{:S(2)}, u32[]{:S(2)}) collective-permute-start(bf16[3,1,1,1,1,64,256]{6,5,0,4,3,2,1:T(8,128)(2,1)S(1)} %add_convert_fusion.37), channel_id=1, source_target_pairs={{0,8},{1,9},{2,10},{3,11},{4,12},{5,13},{6,14},{7,15},{8,0},{9,1},... | collective-permute-start | bytes 294920 | tf_op jit(solution)/shard_map/ppermute | solution.py:313
  549.6 6.9 %collective-permute-start.24 = (bf16[3,1,1,1,1,64,256]{6,5,0,4,3,2,1:T(8,128)(2,1)S(1)}, bf16[3,1,1,1,1,64,256]{6,5,0,4,3,2,1:T(8,128)(2,1)S(1)}, u32[]{:S(2)}, u32[]{:S(2)}) collective-permute-start(bf16[3,1,1,1,1,64,256]{6,5,0,4,3,2,1:T(8,128)(2,1)S(1)} %add_convert_fusion.40), channel_id=1, source_target_pairs={{0,8},{1,9},{2,10},{3,11},{4,12},{5,13},{6,14},{7,15},{8,0},{9,1},... | collective-permute-start | bytes 294920 | tf_op jit(solution)/shard_map/ppermute | solution.py:313
  553.6 3.7 collective-permute-start.30
  556.6 1.4 collective-permute-start.25
  (13 other events, 13.9 us)

commit v9 on v6

--- a/solution.py
+++ b/solution.py
@@ -92,7 +92,7 @@
             both = jnp.concatenate(
                 [x_ref[source, place], x_ref[source, per_device + place]], axis=0
             )
-            kv_ref[source * per_device + place] = both.astype(F32).T.astype(BF16)
+            kv_ref[source * per_device + place] = both.T
         return carry
 
     lax.fori_loop(0, frames // per_device, turn, 0)
@@ -132,6 +132,12 @@
         carry = join([frame], None)
         carry = lax.fori_loop(
             0,
+            lax.div(others, 4),
+            lambda index, state: join([list_ref[4 * index + nth] for nth in range(4)], state),
+            carry,
+        )
+        carry = lax.fori_loop(
+            lax.div(others, 4) * 2,
             lax.div(others, 2),
             lambda index, state: join([list_ref[2 * index], list_ref[2 * index + 1]], state),
             carry,
@@ -212,11 +218,13 @@
     out_ref, dkv_ref, list_ref = refs[-3:]
     frames = kv_ref.shape[0]
 
-    def clear(frame, carry):
-        dkv_ref[frame] = jnp.zeros((PATCHES, 2 * HEAD), F32)
+    def clear(source, carry):
+        for place in range(per_device):
+            if place != part:
+                dkv_ref[source * per_device + place] = jnp.zeros((PATCHES, 2 * HEAD), F32)
         return carry
 
-    lax.fori_loop(0, frames, clear, 0)
+    lax.fori_loop(0, frames // per_device, clear, 0)
 
     def unturn(frame, values):
         lower = values[:HALF]
@@ -231,40 +239,49 @@
         blank = jnp.zeros_like(query)
         query_side = jnp.concatenate([query, blank], axis=0)
         d_mix_side = jnp.concatenate([blank, d_mix], axis=0)
+        turned = jnp.concatenate([query, d_mix], axis=0).T
+        first = lax.broadcasted_iota(jnp.int32, turned.shape, 1) < HEAD
+        nothing = jnp.zeros_like(turned)
         both = jnp.concatenate(
-            [query_side.astype(F32).T.astype(BF16), d_mix_side.astype(F32).T.astype(BF16)], axis=0
+            [jnp.where(first, turned, nothing), jnp.where(first, nothing, turned)], axis=0
         )
         lse = lse_ref[pl.ds(frame, 1), :]
         delta = jnp.sum(d_mix.astype(F32) * wide_ref[source, place], axis=0, keepdims=True)
 
-        def block(other):
+        def block(other, own=False):
             key_value = kv_ref[other]
             scores = jnp.dot(key_value, query_side, preferred_element_type=F32)
             d_weights = jnp.dot(key_value, d_mix_side, preferred_element_type=F32)
             weights = jnp.exp(scores - lse)
             d_scores = (weights * (d_weights - delta)).astype(BF16)
             sides = jnp.concatenate([d_scores, weights.astype(BF16)], axis=1)
-            dkv_ref[other] += jnp.dot(sides, both, preferred_element_type=F32)
+            d_both = jnp.dot(sides, both, preferred_element_type=F32)
+            if own:
+                dkv_ref[other] = d_both
+            else:
+                dkv_ref[other] += d_both
             key = x_ref[lax.div(other, per_device), lax.rem(other, per_device)]
             return jnp.dot(key, d_scores, preferred_element_type=F32)
 
+        others = count - 1
+        d_query = block(frame, True)
         d_query = lax.fori_loop(
             0,
-            lax.div(count, 2),
+            lax.div(others, 2),
             lambda index, state: state
             + block(list_ref[2 * index])
             + block(list_ref[2 * index + 1]),
-            jnp.zeros((HEAD, PATCHES), F32),
+            d_query,
         )
         d_query = lax.fori_loop(
             0,
-            lax.rem(count, 2),
-            lambda unused, state: state + block(list_ref[count - 1]),
+            lax.rem(others, 2),
+            lambda unused, state: state + block(list_ref[others - 1]),
             d_query,
         )
         d_query = unturn(frame, d_query * (HEAD**-0.5)).astype(BF16)
         if last:
-            out_ref[source, 2 * per_device + part] = d_query
+            out_ref[source, 2 * per_device + place] = d_query
         else:
             out_ref[source] = d_query
 
@@ -315,7 +332,7 @@
         out_specs=out_specs,
         scratch_shapes=scratch,
         cost_estimate=pl.CostEstimate(
-            flops=pairs * 10 * PATCHES * PATCHES * 256,
+            flops=pairs * 10 * PATCHES * PATCHES * 64,
             bytes_accessed=x.size * 2 * 5,
             transcendentals=pairs * PATCHES * PATCHES,
         ),
@@ -361,12 +378,16 @@
         pieces = [lax.dynamic_slice_in_dim(part, which, 1, axis) for part in self.parts]
         return (pieces[0].astype(F32) + pieces[1].astype(F32)).astype(BF16)
 
+    def tie_kept(self, value):
+        value, self.parts[0] = lax.optimization_barrier((value, self.parts[0]))
+        return value
+
     def stage(self, later=()):
         bit = self.order.pop(0)
         own_bit = lax.rem(lax.div(self.index, bit), 2)
         send = self.pick(bit, 1 - own_bit)
         for each in later:
-            send = each.tie(send)
+            send = each.tie_kept(send)
         came = exchange(send, "seq", bit)
         self.parts = [self.pick(bit, own_bit), came]
         return send
@@ -1114,9 +1135,11 @@
     mod_sum_early = (early_sum[:4] + early_sum[4:8]).reshape(4 * width)
     before = None
     for part in range(per_device):
+        if halves and part:
+            for each in (up_sum, down_sum, out_sum):
+                before = (each.tie(before[0]), before[1])
         orders = [each.stage() for each in sums]
         if halves and part:
-            before = (out_sum.tie(before[0]), before[1])
             orders.append(out_sum.stage())
         before = attend_back(
             part,
@@ -1133,11 +1156,15 @@
             before,
             orders,
         )
+    for each in sums:
+        before = each.tie(before)
     back = to_tokens(before)
-    orders = [each.stage() for each in sums]
+    orders = []
     if halves:
-        orders.append(out_sum.stage())
-        orders.append(out_sum.stage())
+        out_sum.stage()
+        for each in (up_sum, down_sum, out_sum):
+            each.stage()
+            orders.append(each.parts[1])
     orders += [mod_grad_early] + [part[3] for part in parts]
     which = (1 - pack, pack) if halves else (pack * 0, pack * 0 + 1)
     d_in_theirs, qkv_theirs, bias_theirs = unproject(
@@ -1171,6 +1198,8 @@
         ]
         for each in qkv_sums:
             each.stage((up_sum, down_sum, out_sum))
+        for each in (up_sum, down_sum, out_sum):
+            each.stage(qkv_sums)
         up_weight_grad, down_weight_grad, out_weight_grad, qkv_weight_grad = settle(
             pack, *[each.finish() for each in (up_sum, down_sum, out_sum, *qkv_sums)]
         )

time: 583 us -> 598 us (1.026)
  waiting for transfers between devices: 164 us -> 202 us
  Pallas kernels: 211 us -> 187 us
    ppermute x31, waiting for transfers between devices: 84.3 us -> 107 us  [exchange(): lax.ppermute(value, axis, [(source, source ^ bit) for source in range(cou...]
    pallas_call x2, Pallas kernels: 73.9 us -> 60.7 us  [attend_back(): pl.pallas_call(functools.partial(attend_back_kernel, per_device, part, la...]
    pallas_call x1, Pallas kernels: 51.1 us -> 40.1 us  [attend(): pl.pallas_call(functools.partial(attend_kernel, per_device), out_shape=ou...]
    all_to_all x2, waiting for transfers between devices: 11.7 us -> 22.7 us  [to_tokens(): return lax.all_to_all(array, 'seq', 0, 0, tiled=True)[:heads]]
    unnamed x112 -> x100, local copies, waits for them, and re-layouts: 16.9 us -> 18.1 us
  transfers between devices with their start and end apart: 36 -> 36, of which waited for: 19 -> 17; matrix products, arithmetic and copies ran while one was open for 14% -> 14% of each run, Pallas kernels for 11% -> 16%
where the time goes in v9:
time: 598 us; the launch traced here: 594 us
  waiting for transfers between devices  202 us (34%)
  Pallas kernels  187 us (31%)
  starting transfers between devices  78.5 us (13%)
  local copies, waits for them, and re-layouts  49.8 us (8%)
  other arithmetic  46.9 us (8%)
  matrix products  24 us (4%)
  between operations  6.21 us (1%)
    ppermute x31, waiting for transfers between devices, exchange(): lax.ppermute(value, axis, [(source, source ^ bit) for source in range(cou...  107 us
    all_to_all x2, waiting for transfers between devices, to_heads(): return lax.all_to_all(array, 'seq', 0, 0, tiled=True)  63.4 us
    pallas_call x2, Pallas kernels, attend_back(): pl.pallas_call(functools.partial(attend_back_kernel, per_device, part, la...  60.7 us
    pallas_call x2, Pallas kernels, feed(): pl.pallas_call(functools.partial(feed_kernel, before is not None), grid_s...  45.1 us
    pallas_call x1, Pallas kernels, attend(): pl.pallas_call(functools.partial(attend_kernel, per_device), out_shape=ou...  40.1 us
    convert_element_type x22, other arithmetic, pick(): return (pieces[0].astype(F32) + pieces[1].astype(F32)).astype(BF16)  31.8 us
    ppermute x31, starting transfers between devices, exchange(): lax.ppermute(value, axis, [(source, source ^ bit) for source in range(cou...  28.5 us
    all_to_all x2, starting transfers between devices, to_tokens(): return lax.all_to_all(array, 'seq', 0, 0, tiled=True)[:heads]  24 us
  transfers between devices with their start and end apart: 36, of which 17 were waited for; matrix products, arithmetic and copies ran while one was open for 14% of the time, Pallas kernels for 16%

profile of v9, /device:TPU:0, one launch (start us, length us, event | category | flops | bytes accessed | tf_op | source)
XLA Modules:
  0.0 593.6 jit_solution(10357538775079829277)
XLA Ops:
  7.5 2.9 fusion.7
  11.2 2.8 copy-done
  14.0 11.4 %project.1 = (bf16[512,1024]{1,0:T(8,128)(2,1)S(1)}, bf16[16,6,64,256]{3,2,1,0:T(8,128)(2,1)S(1)}) custom-call(bf16[512,1024]{1,0:T(8,128)(2,1)S(1)} %bitcast.148, f32[2,1024]{1,0:T(2,128)S(1)} %get-tuple-element.252.shift_ref, f32[2,1024]{1,0:T(2,128)S(1)} %get-tuple-element.251.scale_ref.refs_3_, bf16[1024,3072]{1,0:T(8,128)(2,1)S(1)} %copy-done, ...), custom_call_target="tpu_custom_call" | custom-call | flops 3221225472 | bytes 11534336 | tf_op jit(solution)/shard_map/project/pallas_call | solution.py:527
  25.4 1.6 copy-done.3
  27.0 8.5 %all-to-all-start = ((bf16[16,6,64,256]{3,2,1,0:T(8,128)(2,1)}), bf16[16,6,64,256]{3,2,1,0:T(8,128)(2,1)}, u32[]{:S(2)}, u32[]{:S(2)}) async-start(bf16[16,6,64,256]{3,2,1,0:T(8,128)(2,1)} %copy-done.3), calls=%async_computation | async-start | bytes 6291456 | tf_op jit(solution)/shard_map/all_to_all | solution.py:1005
  35.6 4.7 fusion.2
  44.2 52.2 %all-to-all-done.x_ref = bf16[16,6,64,256]{3,2,1,0:T(8,128)(2,1)} async-done(((bf16[16,6,64,256]{3,2,1,0:T(8,128)(2,1)}), bf16[16,6,64,256]{3,2,1,0:T(8,128)(2,1)}, u32[]{:S(2)}, u32[]{:S(2)}) %all-to-all-start) | async-done | bytes 3145760 | tf_op jit(solution)/shard_map/all_to_all | solution.py:1005
  96.5 40.1 %attend.1 = (bf16[16,2,64,256]{3,2,1,0:T(8,128)(2,1)S(1)}, f32[16,2,64,256]{3,2,1,0:T(8,128)S(1)}, f32[32,256]{1,0:T(8,128)S(1)}, bf16[32,256,128]{2,1,0:T(8,128)(2,1)S(1)}) custom-call(s32[32]{0:T(128)S(1)} %bitcast.158, s32[32]{0:T(128)S(1)} %bitcast.161, bf16[16,6,64,256]{3,2,1,0:T(8,128)(2,1)} %all-to-all-done.x_ref), custom_call_target="tpu_custom_call" | custom-call | flops 12884901888 | bytes 9437184 | tf_op jit(solution)/shard_map/attend/pallas_call | solution.py:185
  136.6 1.3 copy-done.5
  140.8 15.5 %all-to-all-start.1 = ((bf16[16,2,64,256]{3,2,1,0:T(8,128)(2,1)}), bf16[16,2,64,256]{3,2,1,0:T(8,128)(2,1)}, u32[]{:S(2)}, u32[]{:S(2)}) async-start(bf16[16,2,64,256]{3,2,1,0:T(8,128)(2,1)} %copy-done.8), calls=%async_computation.1 | async-start | bytes 2097152 | tf_op jit(solution)/shard_map/all_to_all | solution.py:1008
  156.3 22.7 %all-to-all-done.1 = bf16[16,2,64,256]{3,2,1,0:T(8,128)(2,1)} async-done(((bf16[16,2,64,256]{3,2,1,0:T(8,128)(2,1)}), bf16[16,2,64,256]{3,2,1,0:T(8,128)(2,1)}, u32[]{:S(2)}, u32[]{:S(2)}) %all-to-all-start.1) | async-done | bytes 1048608 | tf_op jit(solution)/shard_map/all_to_all | solution.py:1008
  179.0 1.4 fusion.78
  184.4 3.2 fusion.10
  187.5 21.9 %feed0.1 = (f32[512,1024]{1,0:T(8,128)}, f32[512,1024]{1,0:T(8,128)}, bf16[1024,2048]{1,0:T(8,128)(2,1)}, bf16[2048,1024]{1,0:T(8,128)(2,1)}, f32[1,2048]{1,0:T(1,128)}) custom-call(s32[1]{0:T(128)} %bitcast.20.which_ref, bf16[512,1024]{1,0:T(8,128)(2,1)} %get-tuple-element.167.in_ref, bf16[512,1024]{1,0:T(8,128)(2,1)} %fusion.13.d_out_ref, ...), custom_call_target="tpu_custom_call" | custom-call | flops 12884901888 | bytes 25165824 | tf_op jit(solution)/shard_map/feed0/pallas_call | solution.py:633
  209.5 3.8 collective-permute-start.1
  217.3 23.2 %feed1.1 = (f32[512,1024]{1,0:T(8,128)}, f32[512,1024]{1,0:T(8,128)}, bf16[1024,2048]{1,0:T(8,128)(2,1)}, bf16[2048,1024]{1,0:T(8,128)(2,1)}, f32[1,2048]{1,0:T(1,128)}) custom-call(s32[1]{0:T(128)} %bitcast.which_ref.pack_ref, bf16[512,1024]{1,0:T(8,128)(2,1)} %get-tuple-element.167.in_ref, bf16[512,1024]{1,0:T(8,128)(2,1)} %fusion.13.d_out_ref, ...), custom_call_target="tpu_custom_call" | custom-call | flops 12884901888 | bytes 25165824 | tf_op jit(solution)/shard_map/feed1/pallas_call | solution.py:633
  241.4 8.1 %middle_back.1 = (f32[512,1024]{1,0:T(8,128)S(1)}, bf16[512,1024]{1,0:T(8,128)(2,1)S(1)}, bf16[512,1024]{1,0:T(8,128)(2,1)}, bf16[16,3,64,256]{3,2,1,0:T(8,128)(2,1)S(1)}) custom-call(f32[512,1024]{1,0:T(8,128)} %get-tuple-element.99.d_in_ref, f32[512,1024]{1,0:T(8,128)} %get-tuple-element.168.middle_ref, bf16[512,1024]{1,0:T(8,128)(2,1)S(1)} %bitcast.150, ...), custom_call_target="tpu_custom_call" | custom-call | flops 1073741824 | bytes 12582912 | tf_op jit(solution)/shard_map/middle_back/pallas_call | solution.py:757
  249.5 1.3 copy-done.4
  253.0 5.8 all-to-all-start.2
  258.8 8.0 %add_convert_fusion.1 = (bf16[2,2,1,2,64,2048]{5,4,3,2,1,0:T(8,128)(2,1)}, bf16[2,2,1,2,64,2048]{5,4,3,2,1,0:T(8,128)(2,1)}) fusion(bf16[2,2,2,2,64,2048]{5,4,3,2,1,0:T(8,128)(2,1)} %bitcast.36, s32[]{:T(128)S(6)} %select_n.94, bf16[2,2,2,2,64,2048]{5,4,3,2,1,0:T(8,128)(2,1)} %bitcast.173, s32[]{:T(128)S(6)} %select_n.93), kind=kLoop, calls=%fused_computation.5 | loop fusion | flops 8388608 | bytes 12582920 | tf_op jit(solution)/shard_map/convert_element_type | solution.py:379
  266.8 2.0 collective-permute-start.2
  268.8 6.5 %add_convert_fusion = (bf16[2,2,2,1,128,1024]{5,4,3,2,1,0:T(8,128)(2,1)}, bf16[2,2,2,1,128,1024]{5,4,3,2,1,0:T(8,128)(2,1)}) fusion(bf16[2,2,2,2,128,1024]{5,4,3,2,1,0:T(8,128)(2,1)} %bitcast.33, s32[]{:T(128)S(6)} %select_n.95, bf16[2,2,2,2,128,1024]{5,4,3,2,1,0:T(8,128)(2,1)S(1)} %bitcast.172, s32[]{:T(128)S(6)} %select_n.92), kind=kLoop, calls=%fused_computation.4 | loop fusion | flops 8388608 | bytes 12582920 | tf_op jit(solution)/shard_map/convert_element_type | solution.py:379
  275.3 1.5 collective-permute-start.3
  276.8 2.9 convolution_convert_fusion
  282.0 11.2 %all-to-all-done.2.d_mix_ref = bf16[16,3,64,256]{3,2,1,0:T(8,128)(2,1)} async-done(((bf16[16,3,64,256]{3,2,1,0:T(8,128)(2,1)}), bf16[16,3,64,256]{3,2,1,0:T(8,128)(2,1)}, u32[]{:S(2)}, u32[]{:S(2)}) %all-to-all-start.2) | async-done | bytes 1572896 | tf_op jit(solution)/shard_map/all_to_all | solution.py:1005
  293.2 27.3 %attend_back0.1 = (bf16[16,64,256]{2,1,0:T(8,128)(2,1)}, f32[32,256,128]{2,1,0:T(8,128)}) custom-call(s32[32]{0:T(128)} %bitcast.155, s32[32]{0:T(128)} %bitcast.159, bf16[16,6,64,256]{3,2,1,0:T(8,128)(2,1)} %all-to-all-done.x_ref, bf16[32,256,128]{2,1,0:T(8,128)(2,1)} %copy-done.6, f32[16,2,64,256]{3,2,1,0:T(8,128)} %copy-done.5, f32[32,256]{1,0:T(8,128)} %copy-done.10, ...), custom_call_target="tpu_custom_call" | custom-call | flops 4026531840 | bytes 15728640 | tf_op jit(solution)/shard_map/attend_back0/pallas_call | solution.py:328
  320.5 3.8 collective-permute-done.2
  324.3 8.5 %collective-permute-done.3 = bf16[2,2,2,1,128,1024]{5,4,3,2,1,0:T(8,128)(2,1)} collective-permute-done((bf16[2,2,2,1,128,1024]{5,4,3,2,1,0:T(8,128)(2,1)}, bf16[2,2,2,1,128,1024]{5,4,3,2,1,0:T(8,128)(2,1)}, u32[]{:S(2)}, u32[]{:S(2)}) %collective-permute-start.3) | collective-permute-done | bytes 2097184 | tf_op jit(solution)/shard_map/ppermute | solution.py:346
  332.9 4.7 add_convert_fusion.5
  337.5 3.6 add_convert_fusion.4
  342.0 1.9 convolution_convert_fusion.1
  343.9 2.4 add_convert_fusion.14
  350.0 33.4 %attend_back1.1 = bf16[16,6,64,256]{3,2,1,0:T(8,128)(2,1)} custom-call(s32[32]{0:T(128)} %bitcast.156, s32[32]{0:T(128)} %bitcast.160, bf16[16,6,64,256]{3,2,1,0:T(8,128)(2,1)} %all-to-all-done.x_ref, bf16[32,256,128]{2,1,0:T(8,128)(2,1)} %copy-done.6, f32[16,2,64,256]{3,2,1,0:T(8,128)} %copy-done.5, f32[32,256]{1,0:T(8,128)} %copy-done.10, ...), custom_call_target="tpu_custom_call" | custom-call | flops 4026531840 | bytes 15728640 | tf_op jit(solution)/shard_map/attend_back1/pallas_call | solution.py:328
  383.4 8.5 %all-to-all-start.3 = ((bf16[16,6,64,256]{3,2,1,0:T(8,128)(2,1)}), bf16[16,6,64,256]{3,2,1,0:T(8,128)(2,1)}, u32[]{:S(2)}, u32[]{:S(2)}) async-start(bf16[16,6,64,256]{3,2,1,0:T(8,128)(2,1)} %attend_back1.1), calls=%async_computation.3 | async-start | bytes 6291456 | tf_op jit(solution)/shard_map/all_to_all | solution.py:1008
  393.9 4.6 collective-permute-start.12
  399.8 2.6 fusion.81
  403.2 1.3 fusion.24
  407.7 1.4 fusion.20
  409.2 1.4 fusion.18
  411.4 1.4 fusion.22
  413.4 1.7 collective-permute-start.9
  416.5 27.3 %collective-permute-done.9 = bf16[2,2,2,1,64,512]{5,4,3,2,1,0:T(8,128)(2,1)S(1)} collective-permute-done((bf16[2,2,2,1,64,512]{5,4,3,2,1,0:T(8,128)(2,1)S(1)}, bf16[2,2,2,1,64,512]{5,4,3,2,1,0:T(8,128)(2,1)S(1)}, u32[]{:S(2)}, u32[]{:S(2)}) %collective-permute-start.9) | collective-permute-done | bytes 524320 | tf_op jit(solution)/shard_map/ppermute | solution.py:346
  445.1 2.3 add_convert_fusion.12
  448.4 2.3 add_convert_fusion.13
  451.6 7.0 %collective-permute-done.10 = bf16[2,2,1,1,64,512]{5,4,3,2,1,0:T(8,128)(2,1)S(1)} collective-permute-done((bf16[2,2,1,1,64,512]{5,4,3,2,1,0:T(8,128)(2,1)S(1)}, bf16[2,2,1,1,64,512]{5,4,3,2,1,0:T(8,128)(2,1)S(1)}, u32[]{:S(2)}, u32[]{:S(2)}) %collective-permute-start.10) | collective-permute-done | bytes 262176 | tf_op jit(solution)/shard_map/ppermute | solution.py:346
  458.9 22.2 %collective-permute-done.11 = bf16[2,1,1,1,64,512]{5,4,3,2,1,0:T(8,128)(2,1)S(1)} collective-permute-done((bf16[2,1,1,1,64,512]{5,4,3,2,1,0:T(8,128)(2,1)S(1)}, bf16[2,1,1,1,64,512]{5,4,3,2,1,0:T(8,128)(2,1)S(1)}, u32[]{:S(2)}, u32[]{:S(2)}) %collective-permute-start.11) | collective-permute-done | bytes 131104 | tf_op jit(solution)/shard_map/ppermute | solution.py:346
  482.7 8.2 %unproject0.1 = (f32[512,1024]{1,0:T(8,128)S(1)}, bf16[3,1024,512]{2,1,0:T(8,128)(2,1)}, f32[3,1,512]{2,1,0:T(1,128)S(1)}) custom-call(s32[1]{0:T(128)} %bitcast.20.which_ref, bf16[512,1024]{1,0:T(8,128)(2,1)S(1)} %get-tuple-element.90.in_ref, bf16[16,6,64,256]{3,2,1,0:T(8,128)(2,1)} %all-to-all-done.3.back_ref, bf16[1024,3072]{1,0:T(8,128)(2,1)} %wv_ref.5, ...), custom_call_target="tpu_custom_call" | custom-call | flops 3221225472 | bytes 12582912 | tf_op jit(solution)/shard_map/unproject0/pallas_call | solution.py:920
  491.0 11.1 %unproject1.1 = (bf16[3,1024,512]{2,1,0:T(8,128)(2,1)}, bf16[512,1024]{1,0:T(8,128)(2,1)}, bf16[16,16,1024]{2,1,0:T(8,128)(2,1)}) custom-call(s32[1]{0:T(128)} %bitcast.which_ref.pack_ref, bf16[512,1024]{1,0:T(8,128)(2,1)S(1)} %get-tuple-element.90.in_ref, bf16[16,6,64,256]{3,2,1,0:T(8,128)(2,1)} %all-to-all-done.3.back_ref, bf16[1024,3072]{1,0:T(8,128)(2,1)} %wv_ref.5, ...), custom_call_target="tpu_custom_call" | custom-call | flops 3221225472 | bytes 12582912 | tf_op jit(solution)/shard_map/unproject1/pallas_call | solution.py:920
  502.1 11.6 %all-to-all-start.4 = ((bf16[16,16,1024]{2,1,0:T(8,128)(2,1)}), bf16[16,16,1024]{2,1,0:T(8,128)(2,1)S(1)}, u32[]{:S(2)}, u32[]{:S(2)}) async-start(bf16[16,16,1024]{2,1,0:T(8,128)(2,1)} %get-tuple-element.136), calls=%async_computation.4 | async-start | bytes 1048576 | tf_op jit(solution)/shard_map/all_to_all | solution.py:1185
  514.5 2.1 fusion.76
  516.6 1.3 constant_dynamic-slice_fusion.4
  517.9 1.4 constant_dynamic-slice_fusion.2
  519.2 8.9 %all-to-all-done.4 = bf16[16,16,1024]{2,1,0:T(8,128)(2,1)S(1)} async-done(((bf16[16,16,1024]{2,1,0:T(8,128)(2,1)}), bf16[16,16,1024]{2,1,0:T(8,128)(2,1)S(1)}, u32[]{:S(2)}, u32[]{:S(2)}) %all-to-all-start.4) | async-done | bytes 524320 | tf_op jit(solution)/shard_map/all_to_all | solution.py:1185
  535.6 2.1 fusion.77
  543.8 2.2 collective-permute-start.17
  546.7 13.8 %collective-permute-done.26 = bf16[3,2,2,1,2,64,256]{6,5,0,4,3,2,1:T(8,128)(2,1)S(1)} collective-permute-done((bf16[3,2,2,1,2,64,256]{6,5,0,4,3,2,1:T(8,128)(2,1)S(1)}, bf16[3,2,2,1,2,64,256]{6,5,0,4,3,2,1:T(8,128)(2,1)S(1)}, u32[]{:S(2)}, u32[]{:S(2)}) %collective-permute-start.26) | collective-permute-done | bytes 786464 | tf_op jit(solution)/shard_map/ppermute | solution.py:346
  562.9 4.0 collective-permute-done.17
  567.1 4.5 collective-permute-done.27
  571.7 1.4 collective-permute-start.28
  574.2 6.3 %collective-permute-done.28 = bf16[3,2,1,1,1,64,256]{6,5,0,4,3,2,1:T(8,128)(2,1)S(1)} collective-permute-done((bf16[3,2,1,1,1,64,256]{6,5,0,4,3,2,1:T(8,128)(2,1)S(1)}, bf16[3,2,1,1,1,64,256]{6,5,0,4,3,2,1:T(8,128)(2,1)S(1)}, u32[]{:S(2)}, u32[]{:S(2)}) %collective-permute-start.28) | collective-permute-done | bytes 196640 | tf_op jit(solution)/shard_map/ppermute | solution.py:346
  580.6 2.0 collective-permute-done.23
  583.6 4.4 collective-permute-done.29
  588.2 2.0 collective-permute-done.24
  591.6 1.8 settle.1
  (296 shorter events, 63.9 us)
Async XLA Ops:
  7.4 3.0 copy-start.12
  7.4 3.7 copy-start.1
  7.5 3.7 copy-start.9
  11.2 2.8 copy-start
  27.0 8.5 %slice-start = ((f32[6144]{0:T(1024)}), f32[4096]{0:T(1024)S(1)}, s32[]{:S(2)}) async-start(f32[6144]{0:T(1024)} %param.23), calls=%async_computation.5 | async-start | bytes 32768 | tf_op jit(solution)/shard_map/slice | solution.py:1015
  27.0 69.4 %all-to-all-start = ((bf16[16,6,64,256]{3,2,1,0:T(8,128)(2,1)}), bf16[16,6,64,256]{3,2,1,0:T(8,128)(2,1)}, u32[]{:S(2)}, u32[]{:S(2)}) async-start(bf16[16,6,64,256]{3,2,1,0:T(8,128)(2,1)} %copy-done.3), calls=%async_computation | async-start | bytes 6291456 | tf_op jit(solution)/shard_map/all_to_all | solution.py:1005
  35.6 4.7 copy-start.2
  42.9 53.6 %copy-start.13 = (s32[1,32]{1,0:T(1,128)S(1)}, s32[1,32]{1,0:T(1,128)}, u32[]{:S(2)}) copy-start(s32[1,32]{1,0:T(1,128)} %param.20) | copy-start | bytes 388
  140.8 38.1 %all-to-all-start.1 = ((bf16[16,2,64,256]{3,2,1,0:T(8,128)(2,1)}), bf16[16,2,64,256]{3,2,1,0:T(8,128)(2,1)}, u32[]{:S(2)}, u32[]{:S(2)}) async-start(bf16[16,2,64,256]{3,2,1,0:T(8,128)(2,1)} %copy-done.8), calls=%async_computation.1 | async-start | bytes 2097152 | tf_op jit(solution)/shard_map/all_to_all | solution.py:1008
  187.5 25.8 %copy-start.45 = (s32[1,2]{1,0:T(1,128)S(1)}, s32[1,2]{1,0:T(1,128)}, u32[]{:S(2)}) copy-start(s32[1,2]{1,0:T(1,128)} %param.18) | copy-start | bytes 28
  209.5 49.4 %collective-permute-start.1 = (bf16[1024,2048]{1,0:T(8,128)(2,1)}, bf16[1024,2048]{1,0:T(8,128)(2,1)}, u32[]{:S(2)}, u32[]{:S(2)}) collective-permute-start(bf16[1024,2048]{1,0:T(8,128)(2,1)} %get-tuple-element.113), channel_id=1, source_target_pairs={{0,16},{16,0},{1,17},{17,1},{2,18},{18,2},{3,19},{19,3},{4,20},{20... | collective-permute-start | bytes 12582920 | tf_op jit(solution)/shard_map/ppermute | solution.py:346
  213.2 55.6 %collective-permute-start = (bf16[2048,1024]{1,0:T(8,128)(2,1)}, bf16[2048,1024]{1,0:T(8,128)(2,1)}, u32[]{:S(2)}, u32[]{:S(2)}) collective-permute-start(bf16[2048,1024]{1,0:T(8,128)(2,1)} %get-tuple-element.111), channel_id=1, source_target_pairs={{0,16},{16,0},{1,17},{17,1},{2,18},{18,2},{3,19},{19,3},{4,20},{20... | collective-permute-start | bytes 12582920 | tf_op jit(solution)/shard_map/ppermute | solution.py:346
  217.3 23.3 %copy-start.42 = (f32[1,2048]{1,0:T(1,128)S(1)}, f32[1,2048]{1,0:T(1,128)}, u32[]{:S(2)}) copy-start(f32[1,2048]{1,0:T(1,128)} %get-tuple-element.102) | copy-start | bytes 24580
  217.3 24.1 %copy-start.11 = (f32[1024]{0:T(1024)S(1)}, f32[1024]{0:T(1024)}, u32[]{:S(2)}) copy-start(f32[1024]{0:T(1024)} %param.31) | copy-start | bytes 12292
  253.0 40.3 %all-to-all-start.2 = ((bf16[16,3,64,256]{3,2,1,0:T(8,128)(2,1)}), bf16[16,3,64,256]{3,2,1,0:T(8,128)(2,1)}, u32[]{:S(2)}, u32[]{:S(2)}) async-start(bf16[16,3,64,256]{3,2,1,0:T(8,128)(2,1)} %copy-done.7), calls=%async_computation.2 | async-start | bytes 3145728 | tf_op jit(solution)/shard_map/all_to_all | solution.py:1005
  258.8 10.0 %copy-start.18 = (bf16[2048,1024]{1,0:T(8,128)(2,1)S(1)}, bf16[2048,1024]{1,0:T(8,128)(2,1)}, u32[]{:S(2)}) copy-start(bf16[2048,1024]{1,0:T(8,128)(2,1)} %get-tuple-element.110) | copy-start | bytes 12582916
  266.8 57.5 %collective-permute-start.2 = (bf16[2,2,1,2,64,2048]{5,4,3,2,1,0:T(8,128)(2,1)}, bf16[2,2,1,2,64,2048]{5,4,3,2,1,0:T(8,128)(2,1)}, u32[]{:S(2)}, u32[]{:S(2)}) collective-permute-start(bf16[2,2,1,2,64,2048]{5,4,3,2,1,0:T(8,128)(2,1)} %get-tuple-element.173), channel_id=1, source_target_pairs={{0,2},{1,3},{2,0},{3,1},{4,6},{5,7},{6,4},{7,5},{8,10},{9,11},{10,... | collective-permute-start | bytes 6291464 | tf_op jit(solution)/shard_map/ppermute | solution.py:346
  268.8 7.9 %copy-start.15 = (bf16[512,1024]{1,0:T(8,128)(2,1)S(1)}, bf16[512,1024]{1,0:T(8,128)(2,1)}, u32[]{:S(2)}) copy-start(bf16[512,1024]{1,0:T(8,128)(2,1)} %copy-done.14) | copy-start | bytes 3145732
  275.3 57.5 %collective-permute-start.3 = (bf16[2,2,2,1,128,1024]{5,4,3,2,1,0:T(8,128)(2,1)}, bf16[2,2,2,1,128,1024]{5,4,3,2,1,0:T(8,128)(2,1)}, u32[]{:S(2)}, u32[]{:S(2)}) collective-permute-start(bf16[2,2,2,1,128,1024]{5,4,3,2,1,0:T(8,128)(2,1)} %get-tuple-element.171), channel_id=1, source_target_pairs={{0,1},{1,0},{2,3},{3,2},{4,5},{5,4},{6,7},{7,6},{8,9},{9,8},{10,11... | collective-permute-start | bytes 6291464 | tf_op jit(solution)/shard_map/ppermute | solution.py:346
  279.7 64.2 %collective-permute-start.4 = (bf16[1024,512]{1,0:T(8,128)(2,1)}, bf16[1024,512]{1,0:T(8,128)(2,1)}, u32[]{:S(2)}, u32[]{:S(2)}) collective-permute-start(bf16[1024,512]{1,0:T(8,128)(2,1)} %convolution_convert_fusion), channel_id=1, source_target_pairs={{0,16},{16,0},{1,17},{17,1},{2,18},{18,2},{3,19},{19,3},{4,20},{20... | collective-permute-start | bytes 3145736 | tf_op jit(solution)/shard_map/ppermute | solution.py:346
  332.9 4.7 copy-start.17
  337.5 45.9 %collective-permute-start.5 = (bf16[2,2,1,1,128,1024]{5,4,3,2,1,0:T(8,128)(2,1)}, bf16[2,2,1,1,128,1024]{5,4,3,2,1,0:T(8,128)(2,1)}, u32[]{:S(2)}, u32[]{:S(2)}) collective-permute-start(bf16[2,2,1,1,128,1024]{5,4,3,2,1,0:T(8,128)(2,1)} %get-tuple-element.177), channel_id=1, source_target_pairs={{0,2},{1,3},{2,0},{3,1},{4,6},{5,7},{6,4},{7,5},{8,10},{9,11},{10,... | collective-permute-start | bytes 3145736 | tf_op jit(solution)/shard_map/ppermute | solution.py:346
  341.1 42.3 %collective-permute-start.6 = (bf16[2,2,1,1,64,2048]{5,4,3,2,1,0:T(8,128)(2,1)}, bf16[2,2,1,1,64,2048]{5,4,3,2,1,0:T(8,128)(2,1)}, u32[]{:S(2)}, u32[]{:S(2)}) collective-permute-start(bf16[2,2,1,1,64,2048]{5,4,3,2,1,0:T(8,128)(2,1)} %get-tuple-element.175), channel_id=1, source_target_pairs={{0,1},{1,0},{2,3},{3,2},{4,5},{5,4},{6,7},{7,6},{8,9},{9,8},{10,11... | collective-permute-start | bytes 3145736 | tf_op jit(solution)/shard_map/ppermute | solution.py:346
  383.4 99.3 %all-to-all-start.3 = ((bf16[16,6,64,256]{3,2,1,0:T(8,128)(2,1)}), bf16[16,6,64,256]{3,2,1,0:T(8,128)(2,1)}, u32[]{:S(2)}, u32[]{:S(2)}) async-start(bf16[16,6,64,256]{3,2,1,0:T(8,128)(2,1)} %attend_back1.1), calls=%async_computation.3 | async-start | bytes 6291456 | tf_op jit(solution)/shard_map/all_to_all | solution.py:1008
  393.9 10.6 %collective-permute-start.12 = (bf16[16,16,1024]{2,1,0:T(8,128)(2,1)}, bf16[16,16,1024]{2,1,0:T(8,128)(2,1)S(1)}, u32[]{:S(2)}, u32[]{:S(2)}) collective-permute-start(bf16[16,16,1024]{2,1,0:T(8,128)(2,1)} %bitcast.69), channel_id=1, source_target_pairs={{0,16},{16,0},{1,17},{17,1},{2,18},{18,2},{3,19},{19,3},{4,20},{20... | collective-permute-start | bytes 1572872 | tf_op jit(solution)/shard_map/ppermute | solution.py:346
  404.6 6.0 %copy-start.25 = (bf16[16,16,1024]{2,1,0:T(8,128)(2,1)}, bf16[16,16,1024]{2,1,0:T(8,128)(2,1)S(1)}, u32[]{:S(2)}) copy-start(bf16[16,16,1024]{2,1,0:T(8,128)(2,1)S(1)} %collective-permute-done.12) | copy-start | bytes 1572868
  407.7 3.6 copy-start.43
  410.6 2.8 copy-start.37
  411.0 4.1 copy-start.26
  411.0 32.8 %copy-start.31 = (bf16[2,2,2,1,64,512]{5,4,3,2,1,0:T(8,128)(2,1)S(1)}, bf16[2,2,2,1,64,512]{5,4,3,2,1,0:T(8,128)(2,1)}, u32[]{:S(2)}) copy-start(bf16[2,2,2,1,64,512]{5,4,3,2,1,0:T(8,128)(2,1)} %get-tuple-element.188) | copy-start | bytes 1572868
  411.3 33.7 %copy-start.19 = (bf16[2,2,1,1,128,1024]{5,4,3,2,1,0:T(8,128)(2,1)S(1)}, bf16[2,2,1,1,128,1024]{5,4,3,2,1,0:T(8,128)(2,1)}, u32[]{:S(2)}) copy-start(bf16[2,2,1,1,128,1024]{5,4,3,2,1,0:T(8,128)(2,1)} %get-tuple-element.130) | copy-start | bytes 3145732
  413.4 30.4 %collective-permute-start.9 = (bf16[2,2,2,1,64,512]{5,4,3,2,1,0:T(8,128)(2,1)S(1)}, bf16[2,2,2,1,64,512]{5,4,3,2,1,0:T(8,128)(2,1)S(1)}, u32[]{:S(2)}, u32[]{:S(2)}) collective-permute-start(bf16[2,2,2,1,64,512]{5,4,3,2,1,0:T(8,128)(2,1)S(1)} %copy-done.37), channel_id=1, source_target_pairs={{0,1},{1,0},{2,3},{3,2},{4,5},{5,4},{6,7},{7,6},{8,9},{9,8},{10,11... | collective-permute-start | bytes 1572872 | tf_op jit(solution)/shard_map/ppermute | solution.py:346
  443.8 4.6 copy-start.20
  443.9 14.7 %collective-permute-start.10 = (bf16[2,2,1,1,64,512]{5,4,3,2,1,0:T(8,128)(2,1)S(1)}, bf16[2,2,1,1,64,512]{5,4,3,2,1,0:T(8,128)(2,1)S(1)}, u32[]{:S(2)}, u32[]{:S(2)}) collective-permute-start(bf16[2,2,1,1,64,512]{5,4,3,2,1,0:T(8,128)(2,1)S(1)} %get-tuple-element.203), channel_id=1, source_target_pairs={{0,2},{1,3},{2,0},{3,1},{4,6},{5,7},{6,4},{7,5},{8,10},{9,11},{10,... | collective-permute-start | bytes 786440 | tf_op jit(solution)/shard_map/ppermute | solution.py:346
  447.3 33.8 %collective-permute-start.8 = (bf16[2,1,1,1,128,1024]{5,4,3,2,1,0:T(8,128)(2,1)S(1)}, bf16[2,1,1,1,128,1024]{5,4,3,2,1,0:T(8,128)(2,1)S(1)}, u32[]{:S(2)}, u32[]{:S(2)}) collective-permute-start(bf16[2,1,1,1,128,1024]{5,4,3,2,1,0:T(8,128)(2,1)S(1)} %get-tuple-element.185), channel_id=1, source_target_pairs={{0,4},{1,5},{2,6},{3,7},{4,0},{5,1},{6,2},{7,3},{8,12},{9,13},{10,... | collective-permute-start | bytes 1572872 | tf_op jit(solution)/shard_map/ppermute | solution.py:346
  450.7 30.5 %collective-permute-start.7 = (bf16[2,1,1,1,64,2048]{5,4,3,2,1,0:T(8,128)(2,1)S(1)}, bf16[2,1,1,1,64,2048]{5,4,3,2,1,0:T(8,128)(2,1)S(1)}, u32[]{:S(2)}, u32[]{:S(2)}) collective-permute-start(bf16[2,1,1,1,64,2048]{5,4,3,2,1,0:T(8,128)(2,1)S(1)} %get-tuple-element.187), channel_id=1, source_target_pairs={{0,4},{1,5},{2,6},{3,7},{4,0},{5,1},{6,2},{7,3},{8,12},{9,13},{10,... | collective-permute-start | bytes 1572872 | tf_op jit(solution)/shard_map/ppermute | solution.py:346
  458.7 22.4 %collective-permute-start.11 = (bf16[2,1,1,1,64,512]{5,4,3,2,1,0:T(8,128)(2,1)S(1)}, bf16[2,1,1,1,64,512]{5,4,3,2,1,0:T(8,128)(2,1)S(1)}, u32[]{:S(2)}, u32[]{:S(2)}) collective-permute-start(bf16[2,1,1,1,64,512]{5,4,3,2,1,0:T(8,128)(2,1)S(1)} %get-tuple-element.211), channel_id=1, source_target_pairs={{0,4},{1,5},{2,6},{3,7},{4,0},{5,1},{6,2},{7,3},{8,12},{9,13},{10,... | collective-permute-start | bytes 393224 | tf_op jit(solution)/shard_map/ppermute | solution.py:346
  491.0 23.3 %copy-start.44 = (s32[32]{0:T(128)S(1)}, s32[32]{0:T(128)}, u32[]{:S(2)}) copy-start(s32[32]{0:T(128)} %copy-done.43) | copy-start | bytes 388
  502.1 26.0 %all-to-all-start.4 = ((bf16[16,16,1024]{2,1,0:T(8,128)(2,1)}), bf16[16,16,1024]{2,1,0:T(8,128)(2,1)S(1)}, u32[]{:S(2)}, u32[]{:S(2)}) async-start(bf16[16,16,1024]{2,1,0:T(8,128)(2,1)} %get-tuple-element.136), calls=%async_computation.4 | async-start | bytes 1048576 | tf_op jit(solution)/shard_map/all_to_all | solution.py:1185
  514.4 21.2 %collective-permute-start.14 = (bf16[3,1024,512]{2,1,0:T(8,128)(2,1)}, bf16[3,1024,512]{2,1,0:T(8,128)(2,1)}, u32[]{:S(2)}, u32[]{:S(2)}) collective-permute-start(bf16[3,1024,512]{2,1,0:T(8,128)(2,1)} %get-tuple-element.138), channel_id=1, source_target_pairs={{0,16},{16,0},{1,17},{17,1},{2,18},{18,2},{3,19},{19,3},{4,20},{20... | collective-permute-start | bytes 9437192 | tf_op jit(solution)/shard_map/ppermute | solution.py:346
  528.2 2.3 collective-permute-start.13
  528.4 3.5 copy-start.39
  539.1 3.0 copy-start.22
  540.3 2.2 copy-start.29
  540.3 2.2 copy-start.33
  540.5 2.0 copy-start.30
  540.6 2.1 copy-start.21
  540.6 20.0 %collective-permute-start.26 = (bf16[3,2,2,1,2,64,256]{6,5,0,4,3,2,1:T(8,128)(2,1)S(1)}, bf16[3,2,2,1,2,64,256]{6,5,0,4,3,2,1:T(8,128)(2,1)S(1)}, u32[]{:S(2)}, u32[]{:S(2)}) collective-permute-start(bf16[3,2,2,1,2,64,256]{6,5,0,4,3,2,1:T(8,128)(2,1)S(1)} %add_convert_fusion.11), channel_id=1, source_target_pairs={{0,2},{1,3},{2,0},{3,1},{4,6},{5,7},{6,4},{7,5},{8,10},{9,11},{10,... | collective-permute-start | bytes 2359304 | tf_op jit(solution)/shard_map/ppermute | solution.py:346
  541.6 19.9 %collective-permute-start.21 = (bf16[3,2,2,2,1,64,256]{6,5,0,4,3,2,1:T(8,128)(2,1)S(1)}, bf16[3,2,2,2,1,64,256]{6,5,0,4,3,2,1:T(8,128)(2,1)S(1)}, u32[]{:S(2)}, u32[]{:S(2)}) collective-permute-start(bf16[3,2,2,2,1,64,256]{6,5,0,4,3,2,1:T(8,128)(2,1)S(1)} %add_convert_fusion.10), channel_id=1, source_target_pairs={{0,1},{1,0},{2,3},{3,2},{4,5},{5,4},{6,7},{7,6},{8,9},{9,8},{10,11... | collective-permute-start | bytes 2359304 | tf_op jit(solution)/shard_map/ppermute | solution.py:346
  543.0 19.8 %collective-permute-start.19 = (bf16[1,1,1,1,64,512]{5,4,3,2,1,0:T(8,128)(2,1)S(1)}, bf16[1,1,1,1,64,512]{5,4,3,2,1,0:T(8,128)(2,1)S(1)}, u32[]{:S(2)}, u32[]{:S(2)}) collective-permute-start(bf16[1,1,1,1,64,512]{5,4,3,2,1,0:T(8,128)(2,1)S(1)} %add_convert_fusion.43), channel_id=1, source_target_pairs={{0,8},{1,9},{2,10},{3,11},{4,12},{5,13},{6,14},{7,15},{8,0},{9,1},... | collective-permute-start | bytes 196616 | tf_op jit(solution)/shard_map/ppermute | solution.py:346
  543.8 23.1 %collective-permute-start.17 = (bf16[1,1,1,1,128,1024]{5,4,3,2,1,0:T(8,128)(2,1)S(1)}, bf16[1,1,1,1,128,1024]{5,4,3,2,1,0:T(8,128)(2,1)S(1)}, u32[]{:S(2)}, u32[]{:S(2)}) collective-permute-start(bf16[1,1,1,1,128,1024]{5,4,3,2,1,0:T(8,128)(2,1)S(1)} %add_convert_fusion.23), channel_id=1, source_target_pairs={{0,8},{1,9},{2,10},{3,11},{4,12},{5,13},{6,14},{7,15},{8,0},{9,1},... | collective-permute-start | bytes 786440 | tf_op jit(solution)/shard_map/ppermute | solution.py:346
  546.0 28.0 %collective-permute-start.15 = (bf16[1,1,1,1,64,2048]{5,4,3,2,1,0:T(8,128)(2,1)S(1)}, bf16[1,1,1,1,64,2048]{5,4,3,2,1,0:T(8,128)(2,1)S(1)}, u32[]{:S(2)}, u32[]{:S(2)}) collective-permute-start(bf16[1,1,1,1,64,2048]{5,4,3,2,1,0:T(8,128)(2,1)S(1)} %add_convert_fusion.26), channel_id=1, source_target_pairs={{0,8},{1,9},{2,10},{3,11},{4,12},{5,13},{6,14},{7,15},{8,0},{9,1},... | collective-permute-start | bytes 786440 | tf_op jit(solution)/shard_map/ppermute | solution.py:346
  560.9 10.7 %collective-permute-start.27 = (bf16[3,2,2,1,1,64,256]{6,5,0,4,3,2,1:T(8,128)(2,1)S(1)}, bf16[3,2,2,1,1,64,256]{6,5,0,4,3,2,1:T(8,128)(2,1)S(1)}, u32[]{:S(2)}, u32[]{:S(2)}) collective-permute-start(bf16[3,2,2,1,1,64,256]{6,5,0,4,3,2,1:T(8,128)(2,1)S(1)} %get-tuple-element.191), channel_id=1, source_target_pairs={{0,1},{1,0},{2,3},{3,2},{4,5},{5,4},{6,7},{7,6},{8,9},{9,8},{10,11... | collective-permute-start | bytes 1179656 | tf_op jit(solution)/shard_map/ppermute | solution.py:346
  561.7 11.4 %collective-permute-start.22 = (bf16[3,2,2,1,1,64,256]{6,5,0,4,3,2,1:T(8,128)(2,1)S(1)}, bf16[3,2,2,1,1,64,256]{6,5,0,4,3,2,1:T(8,128)(2,1)S(1)}, u32[]{:S(2)}, u32[]{:S(2)}) collective-permute-start(bf16[3,2,2,1,1,64,256]{6,5,0,4,3,2,1:T(8,128)(2,1)S(1)} %get-tuple-element.193), channel_id=1, source_target_pairs={{0,2},{1,3},{2,0},{3,1},{4,6},{5,7},{6,4},{7,5},{8,10},{9,11},{10,... | collective-permute-start | bytes 1179656 | tf_op jit(solution)/shard_map/ppermute | solution.py:346
  562.8 28.2 %collective-permute-start.20 = (bf16[64,512]{1,0:T(8,128)(2,1)S(1)}, bf16[64,512]{1,0:T(8,128)(2,1)S(1)}, u32[]{:S(2)}, u32[]{:S(2)}) collective-permute-start(bf16[64,512]{1,0:T(8,128)(2,1)S(1)} %fusion.36.refs_4_), channel_id=1, source_target_pairs={{0,16},{16,0},{1,17},{17,1},{2,18},{18,2},{3,19},{19,3},{4,20},{20... | collective-permute-start | bytes 196616 | tf_op jit(solution)/shard_map/ppermute | solution.py:346
  567.0 24.0 %collective-permute-start.18 = (bf16[128,1024]{1,0:T(8,128)(2,1)S(1)}, bf16[128,1024]{1,0:T(8,128)(2,1)S(1)}, u32[]{:S(2)}, u32[]{:S(2)}) collective-permute-start(bf16[128,1024]{1,0:T(8,128)(2,1)S(1)} %fusion.27.refs_2_), channel_id=1, source_target_pairs={{0,16},{16,0},{1,17},{17,1},{2,18},{18,2},{3,19},{19,3},{4,20},{20... | collective-permute-start | bytes 786440 | tf_op jit(solution)/shard_map/ppermute | solution.py:346
  571.7 18.6 %copy-start.40 = (f32[4096]{0:T(1024)S(1)}, f32[4096]{0:T(1024)}, u32[]{:S(2)}) copy-start(f32[4096]{0:T(1024)} %get-tuple-element.280) | copy-start | bytes 49156
  571.7 8.8 %collective-permute-start.28 = (bf16[3,2,1,1,1,64,256]{6,5,0,4,3,2,1:T(8,128)(2,1)S(1)}, bf16[3,2,1,1,1,64,256]{6,5,0,4,3,2,1:T(8,128)(2,1)S(1)}, u32[]{:S(2)}, u32[]{:S(2)}) collective-permute-start(bf16[3,2,1,1,1,64,256]{6,5,0,4,3,2,1:T(8,128)(2,1)S(1)} %get-tuple-element.207), channel_id=1, source_target_pairs={{0,4},{1,5},{2,6},{3,7},{4,0},{5,1},{6,2},{7,3},{8,12},{9,13},{10,... | collective-permute-start | bytes 589832 | tf_op jit(solution)/shard_map/ppermute | solution.py:346
  573.2 9.4 %collective-permute-start.23 = (bf16[3,2,1,1,1,64,256]{6,5,0,4,3,2,1:T(8,128)(2,1)S(1)}, bf16[3,2,1,1,1,64,256]{6,5,0,4,3,2,1:T(8,128)(2,1)S(1)}, u32[]{:S(2)}, u32[]{:S(2)}) collective-permute-start(bf16[3,2,1,1,1,64,256]{6,5,0,4,3,2,1:T(8,128)(2,1)S(1)} %get-tuple-element.209), channel_id=1, source_target_pairs={{0,4},{1,5},{2,6},{3,7},{4,0},{5,1},{6,2},{7,3},{8,12},{9,13},{10,... | collective-permute-start | bytes 589832 | tf_op jit(solution)/shard_map/ppermute | solution.py:346
  574.1 16.9 %collective-permute-start.16 = (bf16[64,2048]{1,0:T(8,128)(2,1)S(1)}, bf16[64,2048]{1,0:T(8,128)(2,1)S(1)}, u32[]{:S(2)}, u32[]{:S(2)}) collective-permute-start(bf16[64,2048]{1,0:T(8,128)(2,1)S(1)} %fusion.26.refs_0_), channel_id=1, source_target_pairs={{0,16},{16,0},{1,17},{17,1},{2,18},{18,2},{3,19},{19,3},{4,20},{20... | collective-permute-start | bytes 786440 | tf_op jit(solution)/shard_map/ppermute | solution.py:346
  580.6 7.5 %collective-permute-start.29 = (bf16[3,1,1,1,1,64,256]{6,5,0,4,3,2,1:T(8,128)(2,1)S(1)}, bf16[3,1,1,1,1,64,256]{6,5,0,4,3,2,1:T(8,128)(2,1)S(1)}, u32[]{:S(2)}, u32[]{:S(2)}) collective-permute-start(bf16[3,1,1,1,1,64,256]{6,5,0,4,3,2,1:T(8,128)(2,1)S(1)} %add_convert_fusion.37), channel_id=1, source_target_pairs={{0,8},{1,9},{2,10},{3,11},{4,12},{5,13},{6,14},{7,15},{8,0},{9,1},... | collective-permute-start | bytes 294920 | tf_op jit(solution)/shard_map/ppermute | solution.py:346
  582.7 7.5 %collective-permute-start.24 = (bf16[3,1,1,1,1,64,256]{6,5,0,4,3,2,1:T(8,128)(2,1)S(1)}, bf16[3,1,1,1,1,64,256]{6,5,0,4,3,2,1:T(8,128)(2,1)S(1)}, u32[]{:S(2)}, u32[]{:S(2)}) collective-permute-start(bf16[3,1,1,1,1,64,256]{6,5,0,4,3,2,1:T(8,128)(2,1)S(1)} %add_convert_fusion.40), channel_id=1, source_target_pairs={{0,8},{1,9},{2,10},{3,11},{4,12},{5,13},{6,14},{7,15},{8,0},{9,1},... | collective-permute-start | bytes 294920 | tf_op jit(solution)/shard_map/ppermute | solution.py:346
  588.1 2.9 collective-permute-start.30
  590.2 1.4 collective-permute-start.25
  (19 other events, 21.6 us)

commit v10 on v8

--- a/solution.py
+++ b/solution.py
@@ -345,15 +345,21 @@
         pieces = [lax.dynamic_slice_in_dim(part, which, 1, axis) for part in self.parts]
         return (pieces[0].astype(F32) + pieces[1].astype(F32)).astype(BF16)
 
-    def stage(self, later=()):
+    def tie_kept(self, value):
+        value, self.parts[0] = lax.optimization_barrier((value, self.parts[0]))
+        return value
+
+    def stage(self, later=(), value=None):
         bit = self.order.pop(0)
         own_bit = lax.rem(lax.div(self.index, bit), 2)
         send = self.pick(bit, 1 - own_bit)
         for each in later:
-            send = each.tie(send)
+            send = each.tie_kept(send)
+        if value is not None:
+            send, value = lax.optimization_barrier((send, value))
         came = exchange(send, "seq", bit)
         self.parts = [self.pick(bit, own_bit), came]
-        return send
+        return send if value is None else value
 
     def tie(self, value):
         value, *self.parts = lax.optimization_barrier((value, *self.parts))
@@ -1127,13 +1133,6 @@
         (hidden[0], d_middle, attn_scale, bias_theirs),
     )
     hidden_grad = hidden_grad.reshape(1, tokens, width)
-    late_rows = lax.all_to_all(late, "seq", 0, 0, tiled=True)
-
-    def halves_in_order(own, other):
-        if halves:
-            return jnp.where(pack == 0, own, other), jnp.where(pack == 0, other, own)
-        return other, own
-
     if halves:
         came = exchange(qkv_theirs, "pack", 1)
         split = width // 4
@@ -1142,7 +1141,15 @@
             RowSum(qkv_mine[..., split:], came[..., split:], (2, 1, 4, 8)),
         ]
         for each in qkv_sums:
-            each.stage((up_sum, down_sum, out_sum))
+            late = each.stage((up_sum, down_sum, out_sum), late)
+    late_rows = lax.all_to_all(late, "seq", 0, 0, tiled=True)
+
+    def halves_in_order(own, other):
+        if halves:
+            return jnp.where(pack == 0, own, other), jnp.where(pack == 0, other, own)
+        return other, own
+
+    if halves:
         up_weight_grad, down_weight_grad, out_weight_grad, qkv_weight_grad = settle(
             pack, *[each.finish() for each in (up_sum, down_sum, out_sum, *qkv_sums)]
         )

time: 561 us -> 595 us (1.061)
  other arithmetic: 44.3 us -> 65 us
  waiting for transfers between devices: 181 us -> 162 us
  local copies, waits for them, and re-layouts: 42.8 us -> 58.7 us
  starting transfers between devices: 72.8 us -> 86.6 us
    convert_element_type x22, other arithmetic: 28 us -> 43 us  [pick(): return (pieces[0].astype(F32) + pieces[1].astype(F32)).astype(BF16)]
    ppermute x31, waiting for transfers between devices: 89.8 us -> 78 us  [exchange(): lax.ppermute(value, axis, [(source, source ^ bit) for source in range(cou...]
    reshape x12, local copies, waits for them, and re-layouts: 0.36 us -> 8.32 us  [frames_of(): return jnp.concatenate([jnp.stack([rows[:, frame * per_frame + kind] for...]
    all_to_all x1, starting transfers between devices: 4.74 us -> 11.5 us  [local(): late_rows = lax.all_to_all(late, 'seq', 0, 0, tiled=True)]
    ppermute x31, starting transfers between devices: 29.4 us -> 35.8 us  [exchange(): lax.ppermute(value, axis, [(source, source ^ bit) for source in range(cou...]
    unnamed x88 -> x108, local copies, waits for them, and re-layouts: 14.9 us -> 20.5 us
  transfers between devices with their start and end apart: 36 -> 36, of which waited for: 13 -> 11; matrix products, arithmetic and copies ran while one was open for 15% -> 20% of each run, Pallas kernels for 16% -> 17%
where the time goes in v10:
time: 595 us; the launch traced here: 589 us
  Pallas kernels  182 us (31%)
  waiting for transfers between devices  162 us (27%)
  starting transfers between devices  86.6 us (15%)
  other arithmetic  65 us (11%)
  local copies, waits for them, and re-layouts  58.7 us (10%)
  matrix products  28.3 us (5%)
    ppermute x31, waiting for transfers between devices, exchange(): lax.ppermute(value, axis, [(source, source ^ bit) for source in range(cou...  78 us
    all_to_all x2, waiting for transfers between devices, to_heads(): return lax.all_to_all(array, 'seq', 0, 0, tiled=True)  60.5 us
    pallas_call x1, Pallas kernels, attend_back(): pl.pallas_call(functools.partial(attend_back_kernel, per_device), out_sha...  55.4 us
    pallas_call x2, Pallas kernels, feed(): pl.pallas_call(functools.partial(feed_kernel, before is not None), grid_s...  45.2 us
    convert_element_type x22, other arithmetic, pick(): return (pieces[0].astype(F32) + pieces[1].astype(F32)).astype(BF16)  43 us
    pallas_call x1, Pallas kernels, attend(): pl.pallas_call(functools.partial(attend_kernel, per_device), out_shape=ou...  41 us
    ppermute x31, starting transfers between devices, exchange(): lax.ppermute(value, axis, [(source, source ^ bit) for source in range(cou...  35.8 us
    all_to_all x2, starting transfers between devices, to_tokens(): return lax.all_to_all(array, 'seq', 0, 0, tiled=True)[:heads]  24.2 us
  transfers between devices with their start and end apart: 36, of which 11 were waited for; matrix products, arithmetic and copies ran while one was open for 20% of the time, Pallas kernels for 17%

profile of v10, /device:TPU:0, one launch (start us, length us, event | category | flops | bytes accessed | tf_op | source)
XLA Modules:
  0.0 588.9 jit_solution(55616633695799956)
XLA Ops:
  7.5 2.9 fusion.7
  11.2 2.8 copy-done
  14.0 11.4 %project.1 = (bf16[512,1024]{1,0:T(8,128)(2,1)S(1)}, bf16[16,6,64,256]{3,2,1,0:T(8,128)(2,1)S(1)}) custom-call(bf16[512,1024]{1,0:T(8,128)(2,1)S(1)} %bitcast.145, f32[2,1024]{1,0:T(2,128)S(1)} %get-tuple-element.220.shift_ref, f32[2,1024]{1,0:T(2,128)S(1)} %get-tuple-element.219.scale_ref.refs_3_, bf16[1024,3072]{1,0:T(8,128)(2,1)S(1)} %copy-done, ...), custom_call_target="tpu_custom_call" | custom-call | flops 3221225472 | bytes 11534336 | tf_op jit(solution)/shard_map/project/pallas_call | solution.py:496
  25.4 1.6 copy-done.3
  27.0 8.5 %all-to-all-start = ((bf16[16,6,64,256]{3,2,1,0:T(8,128)(2,1)}), bf16[16,6,64,256]{3,2,1,0:T(8,128)(2,1)}, u32[]{:S(2)}, u32[]{:S(2)}) async-start(bf16[16,6,64,256]{3,2,1,0:T(8,128)(2,1)} %copy-done.3), calls=%async_computation | async-start | bytes 6291456 | tf_op jit(solution)/shard_map/all_to_all | solution.py:974
  35.6 4.7 fusion.2
  44.2 52.2 %all-to-all-done.x_ref = bf16[16,6,64,256]{3,2,1,0:T(8,128)(2,1)} async-done(((bf16[16,6,64,256]{3,2,1,0:T(8,128)(2,1)}), bf16[16,6,64,256]{3,2,1,0:T(8,128)(2,1)}, u32[]{:S(2)}, u32[]{:S(2)}) %all-to-all-start) | async-done | bytes 3145760 | tf_op jit(solution)/shard_map/all_to_all | solution.py:974
  96.5 41.0 %attend.1 = (bf16[16,2,64,256]{3,2,1,0:T(8,128)(2,1)S(1)}, f32[16,2,64,256]{3,2,1,0:T(8,128)S(1)}, f32[32,256]{1,0:T(8,128)S(1)}, bf16[32,256,128]{2,1,0:T(8,128)(2,1)S(1)}) custom-call(s32[32]{0:T(128)S(1)} %bitcast.154, s32[32]{0:T(128)S(1)} %bitcast.156, bf16[16,6,64,256]{3,2,1,0:T(8,128)(2,1)} %all-to-all-done.x_ref), custom_call_target="tpu_custom_call" | custom-call | flops 12884901888 | bytes 9437184 | tf_op jit(solution)/shard_map/attend/pallas_call | solution.py:184
  141.7 15.3 %all-to-all-start.1 = ((bf16[16,2,64,256]{3,2,1,0:T(8,128)(2,1)}), bf16[16,2,64,256]{3,2,1,0:T(8,128)(2,1)}, u32[]{:S(2)}, u32[]{:S(2)}) async-start(bf16[16,2,64,256]{3,2,1,0:T(8,128)(2,1)} %copy-done.8), calls=%async_computation.1 | async-start | bytes 2097152 | tf_op jit(solution)/shard_map/all_to_all | solution.py:977
  157.1 23.4 %all-to-all-done.1 = bf16[16,2,64,256]{3,2,1,0:T(8,128)(2,1)} async-done(((bf16[16,2,64,256]{3,2,1,0:T(8,128)(2,1)}), bf16[16,2,64,256]{3,2,1,0:T(8,128)(2,1)}, u32[]{:S(2)}, u32[]{:S(2)}) %all-to-all-start.1) | async-done | bytes 1048608 | tf_op jit(solution)/shard_map/all_to_all | solution.py:977
  180.5 1.4 fusion.78
  185.9 3.2 fusion.10
  189.1 21.9 %feed0.1 = (f32[512,1024]{1,0:T(8,128)}, f32[512,1024]{1,0:T(8,128)}, bf16[1024,2048]{1,0:T(8,128)(2,1)}, bf16[2048,1024]{1,0:T(8,128)(2,1)}, f32[1,2048]{1,0:T(1,128)}) custom-call(s32[1]{0:T(128)} %bitcast.20.which_ref, bf16[512,1024]{1,0:T(8,128)(2,1)} %get-tuple-element.135.in_ref, bf16[512,1024]{1,0:T(8,128)(2,1)} %fusion.13.d_out_ref, ...), custom_call_target="tpu_custom_call" | custom-call | flops 12884901888 | bytes 25165824 | tf_op jit(solution)/shard_map/feed0/pallas_call | solution.py:602
  211.0 2.3 collective-permute-start
  217.3 23.3 %feed1.1 = (f32[512,1024]{1,0:T(8,128)}, f32[512,1024]{1,0:T(8,128)}, bf16[1024,2048]{1,0:T(8,128)(2,1)}, bf16[2048,1024]{1,0:T(8,128)(2,1)}, f32[1,2048]{1,0:T(1,128)}) custom-call(s32[1]{0:T(128)} %bitcast.which_ref.pack_ref, bf16[512,1024]{1,0:T(8,128)(2,1)} %get-tuple-element.135.in_ref, bf16[512,1024]{1,0:T(8,128)(2,1)} %fusion.13.d_out_ref, ...), custom_call_target="tpu_custom_call" | custom-call | flops 12884901888 | bytes 25165824 | tf_op jit(solution)/shard_map/feed1/pallas_call | solution.py:602
  241.5 8.1 %middle_back.1 = (f32[512,1024]{1,0:T(8,128)S(1)}, bf16[512,1024]{1,0:T(8,128)(2,1)S(1)}, bf16[512,1024]{1,0:T(8,128)(2,1)}, bf16[16,3,64,256]{3,2,1,0:T(8,128)(2,1)S(1)}) custom-call(f32[512,1024]{1,0:T(8,128)} %get-tuple-element.83.d_in_ref, f32[512,1024]{1,0:T(8,128)} %get-tuple-element.136.middle_ref, bf16[512,1024]{1,0:T(8,128)(2,1)S(1)} %bitcast.147, ...), custom_call_target="tpu_custom_call" | custom-call | flops 1073741824 | bytes 12582912 | tf_op jit(solution)/shard_map/middle_back/pallas_call | solution.py:726
  253.1 6.5 %all-to-all-start.2 = ((bf16[16,3,64,256]{3,2,1,0:T(8,128)(2,1)}), bf16[16,3,64,256]{3,2,1,0:T(8,128)(2,1)}, u32[]{:S(2)}, u32[]{:S(2)}) async-start(bf16[16,3,64,256]{3,2,1,0:T(8,128)(2,1)} %copy-done.7), calls=%async_computation.2 | async-start | bytes 3145728 | tf_op jit(solution)/shard_map/all_to_all | solution.py:974
  259.6 7.9 %add_convert_fusion.1 = (bf16[2,2,2,1,128,1024]{5,4,3,2,1,0:T(8,128)(2,1)}, bf16[2,2,2,1,128,1024]{5,4,3,2,1,0:T(8,128)(2,1)}) fusion(bf16[2,2,2,2,128,1024]{5,4,3,2,1,0:T(8,128)(2,1)} %bitcast.33, s32[]{:T(128)S(6)} %select_n.94, bf16[2,2,2,2,128,1024]{5,4,3,2,1,0:T(8,128)(2,1)} %bitcast.168, s32[]{:T(128)S(6)} %select_n.92), kind=kLoop, calls=%fused_computation.5 | loop fusion | flops 8388608 | bytes 12582920 | tf_op jit(solution)/shard_map/convert_element_type | solution.py:346
  267.4 2.0 collective-permute-start.2
  269.5 6.6 %add_convert_fusion = (bf16[2,2,1,2,64,2048]{5,4,3,2,1,0:T(8,128)(2,1)}, bf16[2,2,1,2,64,2048]{5,4,3,2,1,0:T(8,128)(2,1)}) fusion(bf16[2,2,2,2,64,2048]{5,4,3,2,1,0:T(8,128)(2,1)} %bitcast.36, s32[]{:T(128)S(6)} %select_n.95, bf16[2,2,2,2,64,2048]{5,4,3,2,1,0:T(8,128)(2,1)S(1)} %bitcast.167, s32[]{:T(128)S(6)} %select_n.93), kind=kLoop, calls=%fused_computation.4 | loop fusion | flops 8388608 | bytes 12582920 | tf_op jit(solution)/shard_map/convert_element_type | solution.py:346
  276.1 1.5 collective-permute-start.3
  277.6 2.9 convolution_convert_fusion
  280.4 2.9 convolution_convert_fusion.1
  285.7 8.3 %all-to-all-done.2.d_mix_ref = bf16[16,3,64,256]{3,2,1,0:T(8,128)(2,1)} async-done(((bf16[16,3,64,256]{3,2,1,0:T(8,128)(2,1)}), bf16[16,3,64,256]{3,2,1,0:T(8,128)(2,1)}, u32[]{:S(2)}, u32[]{:S(2)}) %all-to-all-start.2) | async-done | bytes 1572896 | tf_op jit(solution)/shard_map/all_to_all | solution.py:974
  293.9 55.4 %attend_back.1 = bf16[16,6,64,256]{3,2,1,0:T(8,128)(2,1)} custom-call(s32[32]{0:T(128)} %bitcast.152, s32[32]{0:T(128)} %bitcast.155, bf16[16,6,64,256]{3,2,1,0:T(8,128)(2,1)} %all-to-all-done.x_ref, bf16[32,256,128]{2,1,0:T(8,128)(2,1)} %copy-done.16, f32[16,2,64,256]{3,2,1,0:T(8,128)} %copy-done.15, f32[32,256]{1,0:T(8,128)} %copy-done.17, ...), custom_call_target="tpu_custom_call" | custom-call | flops 8053063680 | bytes 15728640 | tf_op jit(solution)/shard_map/attend_back/pallas_call | solution.py:292
  349.3 8.9 %all-to-all-start.3 = ((bf16[16,6,64,256]{3,2,1,0:T(8,128)(2,1)}), bf16[16,6,64,256]{3,2,1,0:T(8,128)(2,1)}, u32[]{:S(2)}, u32[]{:S(2)}) async-start(bf16[16,6,64,256]{3,2,1,0:T(8,128)(2,1)} %attend_back.1), calls=%async_computation.3 | async-start | bytes 6291456 | tf_op jit(solution)/shard_map/all_to_all | solution.py:977
  360.2 3.1 collective-permute-start.8
  364.5 2.6 fusion.81
  377.2 1.5 reshape.509
  378.7 1.5 reshape.510
  382.5 1.4 fusion.20
  384.0 1.4 fusion.18
  385.4 2.3 fusion.74
  387.7 3.7 add_convert_fusion.5
  391.4 1.7 collective-permute-start.6
  393.2 3.5 add_convert_fusion.7
  396.7 1.5 collective-permute-start.5
  399.0 1.9 add_convert_fusion.15
  404.3 42.8 %collective-permute-done.7 = bf16[2,2,2,1,64,512]{5,4,3,2,1,0:T(8,128)(2,1)S(1)} collective-permute-done((bf16[2,2,2,1,64,512]{5,4,3,2,1,0:T(8,128)(2,1)S(1)}, bf16[2,2,2,1,64,512]{5,4,3,2,1,0:T(8,128)(2,1)S(1)}, u32[]{:S(2)}, u32[]{:S(2)}) %collective-permute-start.7) | collective-permute-done | bytes 524320 | tf_op jit(solution)/shard_map/ppermute | solution.py:313
  448.7 2.3 add_convert_fusion.12
  451.0 2.5 add_convert_fusion.13
  454.3 8.2 %unproject0.1 = (f32[512,1024]{1,0:T(8,128)S(1)}, bf16[3,1024,512]{2,1,0:T(8,128)(2,1)}, f32[3,1,512]{2,1,0:T(1,128)S(1)}) custom-call(s32[1]{0:T(128)} %bitcast.20.which_ref, bf16[512,1024]{1,0:T(8,128)(2,1)S(1)} %get-tuple-element.74.in_ref, bf16[16,6,64,256]{3,2,1,0:T(8,128)(2,1)} %all-to-all-done.3.back_ref, bf16[1024,3072]{1,0:T(8,128)(2,1)} %wv_ref.5, ...), custom_call_target="tpu_custom_call" | custom-call | flops 3221225472 | bytes 12582912 | tf_op jit(solution)/shard_map/unproject0/pallas_call | solution.py:889
  467.4 2.3 collective-permute-start.14
  469.7 1.6 copy-done.6
  471.3 11.3 %unproject1.1 = (bf16[3,1024,512]{2,1,0:T(8,128)(2,1)}, bf16[512,1024]{1,0:T(8,128)(2,1)}, bf16[16,16,1024]{2,1,0:T(8,128)(2,1)}) custom-call(s32[1]{0:T(128)} %bitcast.which_ref.pack_ref, bf16[512,1024]{1,0:T(8,128)(2,1)S(1)} %get-tuple-element.74.in_ref, bf16[16,6,64,256]{3,2,1,0:T(8,128)(2,1)} %all-to-all-done.3.back_ref, bf16[1024,3072]{1,0:T(8,128)(2,1)} %wv_ref.5, ...), custom_call_target="tpu_custom_call" | custom-call | flops 3221225472 | bytes 12582912 | tf_op jit(solution)/shard_map/unproject1/pallas_call | solution.py:889
  482.6 2.1 fusion.76
  485.8 2.1 fusion.77
  492.3 11.5 %all-to-all-start.4 = ((bf16[16,16,1024]{2,1,0:T(8,128)(2,1)}), bf16[16,16,1024]{2,1,0:T(8,128)(2,1)S(1)}, u32[]{:S(2)}, u32[]{:S(2)}) async-start(bf16[16,16,1024]{2,1,0:T(8,128)(2,1)} %get-tuple-element.125), calls=%async_computation.4 | async-start | bytes 1048576 | tf_op jit(solution)/shard_map/all_to_all | solution.py:1145
  503.8 2.0 collective-permute-start.26
  505.8 1.5 collective-permute-start.21
  508.3 1.5 collective-permute-start.18
  511.0 2.4 collective-permute-start.15
  516.6 4.5 collective-permute-start.19
  521.5 21.9 %collective-permute-done.19 = bf16[1,1,1,1,64,512]{5,4,3,2,1,0:T(8,128)(2,1)S(1)} collective-permute-done((bf16[1,1,1,1,64,512]{5,4,3,2,1,0:T(8,128)(2,1)S(1)}, bf16[1,1,1,1,64,512]{5,4,3,2,1,0:T(8,128)(2,1)S(1)}, u32[]{:S(2)}, u32[]{:S(2)}) %collective-permute-start.19) | collective-permute-done | bytes 65568 | tf_op jit(solution)/shard_map/ppermute | solution.py:313
  547.2 1.5 collective-permute-start.27
  549.7 1.5 collective-permute-start.22
  552.0 1.8 fusion.47
  554.0 4.5 collective-permute-done.27
  558.6 1.8 add_convert_fusion.31
  561.4 1.9 add_convert_fusion.33
  564.7 1.6 fusion.82
  574.6 2.3 collective-permute-start.24
  576.9 6.2 %collective-permute-done.29 = bf16[3,1,1,1,1,64,256]{6,5,0,4,3,2,1:T(8,128)(2,1)S(1)} collective-permute-done((bf16[3,1,1,1,1,64,256]{6,5,0,4,3,2,1:T(8,128)(2,1)S(1)}, bf16[3,1,1,1,1,64,256]{6,5,0,4,3,2,1:T(8,128)(2,1)S(1)}, u32[]{:S(2)}, u32[]{:S(2)}) %collective-permute-start.29) | collective-permute-done | bytes 98336 | tf_op jit(solution)/shard_map/ppermute | solution.py:313
  586.9 1.8 settle.1
  (300 shorter events, 84.5 us)
Async XLA Ops:
  7.4 3.7 copy-start.1
  7.5 3.7 copy-start.9
  27.0 8.5 %slice-start = ((f32[6144]{0:T(1024)}), f32[4096]{0:T(1024)S(1)}, s32[]{:S(2)}) async-start(f32[6144]{0:T(1024)} %param.23), calls=%async_computation.5 | async-start | bytes 32768 | tf_op jit(solution)/shard_map/slice | solution.py:984
  27.0 69.5 %all-to-all-start = ((bf16[16,6,64,256]{3,2,1,0:T(8,128)(2,1)}), bf16[16,6,64,256]{3,2,1,0:T(8,128)(2,1)}, u32[]{:S(2)}, u32[]{:S(2)}) async-start(bf16[16,6,64,256]{3,2,1,0:T(8,128)(2,1)} %copy-done.3), calls=%async_computation | async-start | bytes 6291456 | tf_op jit(solution)/shard_map/all_to_all | solution.py:974
  35.6 4.7 copy-start.2
  42.9 53.6 %copy-start.14 = (s32[1,32]{1,0:T(1,128)S(1)}, s32[1,32]{1,0:T(1,128)}, u32[]{:S(2)}) copy-start(s32[1,32]{1,0:T(1,128)} %param.20) | copy-start | bytes 388
  141.7 38.8 %all-to-all-start.1 = ((bf16[16,2,64,256]{3,2,1,0:T(8,128)(2,1)}), bf16[16,2,64,256]{3,2,1,0:T(8,128)(2,1)}, u32[]{:S(2)}, u32[]{:S(2)}) async-start(bf16[16,2,64,256]{3,2,1,0:T(8,128)(2,1)} %copy-done.8), calls=%async_computation.1 | async-start | bytes 2097152 | tf_op jit(solution)/shard_map/all_to_all | solution.py:977
  189.1 24.3 %copy-start.49 = (s32[1,2]{1,0:T(1,128)S(1)}, s32[1,2]{1,0:T(1,128)}, u32[]{:S(2)}) copy-start(s32[1,2]{1,0:T(1,128)} %param.18) | copy-start | bytes 28
  211.0 48.5 %collective-permute-start = (bf16[2048,1024]{1,0:T(8,128)(2,1)}, bf16[2048,1024]{1,0:T(8,128)(2,1)}, u32[]{:S(2)}, u32[]{:S(2)}) collective-permute-start(bf16[2048,1024]{1,0:T(8,128)(2,1)} %get-tuple-element.95), channel_id=1, source_target_pairs={{0,16},{16,0},{1,17},{17,1},{2,18},{18,2},{3,19},{19,3},{4,20},{20... | collective-permute-start | bytes 12582920 | tf_op jit(solution)/shard_map/ppermute | solution.py:313
  213.3 56.2 %collective-permute-start.1 = (bf16[1024,2048]{1,0:T(8,128)(2,1)}, bf16[1024,2048]{1,0:T(8,128)(2,1)}, u32[]{:S(2)}, u32[]{:S(2)}) collective-permute-start(bf16[1024,2048]{1,0:T(8,128)(2,1)} %get-tuple-element.97), channel_id=1, source_target_pairs={{0,16},{16,0},{1,17},{17,1},{2,18},{18,2},{3,19},{19,3},{4,20},{20... | collective-permute-start | bytes 12582920 | tf_op jit(solution)/shard_map/ppermute | solution.py:313
  217.3 23.3 %copy-start.48 = (f32[1,2048]{1,0:T(1,128)S(1)}, f32[1,2048]{1,0:T(1,128)}, u32[]{:S(2)}) copy-start(f32[1,2048]{1,0:T(1,128)} %get-tuple-element.86) | copy-start | bytes 24580
  217.3 24.2 %copy-start.10 = (f32[1024]{0:T(1024)S(1)}, f32[1024]{0:T(1024)}, u32[]{:S(2)}) copy-start(f32[1024]{0:T(1024)} %param.31) | copy-start | bytes 12292
  253.1 40.9 %all-to-all-start.2 = ((bf16[16,3,64,256]{3,2,1,0:T(8,128)(2,1)}), bf16[16,3,64,256]{3,2,1,0:T(8,128)(2,1)}, u32[]{:S(2)}, u32[]{:S(2)}) async-start(bf16[16,3,64,256]{3,2,1,0:T(8,128)(2,1)} %copy-done.7), calls=%async_computation.2 | async-start | bytes 3145728 | tf_op jit(solution)/shard_map/all_to_all | solution.py:974
  259.5 9.9 %copy-start.21 = (bf16[1024,2048]{1,0:T(8,128)(2,1)S(1)}, bf16[1024,2048]{1,0:T(8,128)(2,1)}, u32[]{:S(2)}) copy-start(bf16[1024,2048]{1,0:T(8,128)(2,1)} %get-tuple-element.96) | copy-start | bytes 12582916
  267.4 81.9 %collective-permute-start.2 = (bf16[2,2,2,1,128,1024]{5,4,3,2,1,0:T(8,128)(2,1)}, bf16[2,2,2,1,128,1024]{5,4,3,2,1,0:T(8,128)(2,1)}, u32[]{:S(2)}, u32[]{:S(2)}) collective-permute-start(bf16[2,2,2,1,128,1024]{5,4,3,2,1,0:T(8,128)(2,1)} %get-tuple-element.141), channel_id=1, source_target_pairs={{0,1},{1,0},{2,3},{3,2},{4,5},{5,4},{6,7},{7,6},{8,9},{9,8},{10,11... | collective-permute-start | bytes 6291464 | tf_op jit(solution)/shard_map/ppermute | solution.py:313
  269.5 8.1 %copy-start.12 = (bf16[512,1024]{1,0:T(8,128)(2,1)S(1)}, bf16[512,1024]{1,0:T(8,128)(2,1)}, u32[]{:S(2)}) copy-start(bf16[512,1024]{1,0:T(8,128)(2,1)} %copy-done.11) | copy-start | bytes 3145732
  276.1 73.3 %collective-permute-start.3 = (bf16[2,2,1,2,64,2048]{5,4,3,2,1,0:T(8,128)(2,1)}, bf16[2,2,1,2,64,2048]{5,4,3,2,1,0:T(8,128)(2,1)}, u32[]{:S(2)}, u32[]{:S(2)}) collective-permute-start(bf16[2,2,1,2,64,2048]{5,4,3,2,1,0:T(8,128)(2,1)} %get-tuple-element.139), channel_id=1, source_target_pairs={{0,2},{1,3},{2,0},{3,1},{4,6},{5,7},{6,4},{7,5},{8,10},{9,11},{10,... | collective-permute-start | bytes 6291464 | tf_op jit(solution)/shard_map/ppermute | solution.py:313
  280.4 68.9 %collective-permute-start.4 = (bf16[1024,512]{1,0:T(8,128)(2,1)}, bf16[1024,512]{1,0:T(8,128)(2,1)}, u32[]{:S(2)}, u32[]{:S(2)}) collective-permute-start(bf16[1024,512]{1,0:T(8,128)(2,1)} %convolution_convert_fusion), channel_id=1, source_target_pairs={{0,16},{16,0},{1,17},{17,1},{2,18},{18,2},{3,19},{19,3},{4,20},{20... | collective-permute-start | bytes 3145736 | tf_op jit(solution)/shard_map/ppermute | solution.py:313
  349.3 104.9 %all-to-all-start.3 = ((bf16[16,6,64,256]{3,2,1,0:T(8,128)(2,1)}), bf16[16,6,64,256]{3,2,1,0:T(8,128)(2,1)}, u32[]{:S(2)}, u32[]{:S(2)}) async-start(bf16[16,6,64,256]{3,2,1,0:T(8,128)(2,1)} %attend_back.1), calls=%async_computation.3 | async-start | bytes 6291456 | tf_op jit(solution)/shard_map/all_to_all | solution.py:977
  360.2 13.8 %collective-permute-start.8 = (bf16[16,16,1024]{2,1,0:T(8,128)(2,1)}, bf16[16,16,1024]{2,1,0:T(8,128)(2,1)S(1)}, u32[]{:S(2)}, u32[]{:S(2)}) collective-permute-start(bf16[16,16,1024]{2,1,0:T(8,128)(2,1)} %bitcast.66), channel_id=1, source_target_pairs={{0,16},{16,0},{1,17},{17,1},{2,18},{18,2},{3,19},{19,3},{4,20},{20... | collective-permute-start | bytes 1572872 | tf_op jit(solution)/shard_map/ppermute | solution.py:313
  380.5 7.2 %copy-start.19 = (bf16[2,2,2,1,128,1024]{5,4,3,2,1,0:T(8,128)(2,1)S(1)}, bf16[2,2,2,1,128,1024]{5,4,3,2,1,0:T(8,128)(2,1)}, u32[]{:S(2)}) copy-start(bf16[2,2,2,1,128,1024]{5,4,3,2,1,0:T(8,128)(2,1)} %get-tuple-element.104) | copy-start | bytes 6291460
  385.4 16.2 %copy-start.41 = (f32[32,64]{1,0:T(8,128)}, f32[32,64]{1,0:T(8,128)S(1)}, u32[]{:S(2)}) copy-start(f32[32,64]{1,0:T(8,128)S(1)} %fusion.18) | copy-start | bytes 24580
  387.7 5.5 copy-start.20
  391.4 57.2 %collective-permute-start.6 = (bf16[2,2,1,1,128,1024]{5,4,3,2,1,0:T(8,128)(2,1)}, bf16[2,2,1,1,128,1024]{5,4,3,2,1,0:T(8,128)(2,1)}, u32[]{:S(2)}, u32[]{:S(2)}) collective-permute-start(bf16[2,2,1,1,128,1024]{5,4,3,2,1,0:T(8,128)(2,1)} %get-tuple-element.143), channel_id=1, source_target_pairs={{0,2},{1,3},{2,0},{3,1},{4,6},{5,7},{6,4},{7,5},{8,10},{9,11},{10,... | collective-permute-start | bytes 3145736 | tf_op jit(solution)/shard_map/ppermute | solution.py:313
  396.7 54.3 %collective-permute-start.5 = (bf16[2,2,1,1,64,2048]{5,4,3,2,1,0:T(8,128)(2,1)}, bf16[2,2,1,1,64,2048]{5,4,3,2,1,0:T(8,128)(2,1)}, u32[]{:S(2)}, u32[]{:S(2)}) collective-permute-start(bf16[2,2,1,1,64,2048]{5,4,3,2,1,0:T(8,128)(2,1)} %get-tuple-element.145), channel_id=1, source_target_pairs={{0,1},{1,0},{2,3},{3,2},{4,5},{5,4},{6,7},{7,6},{8,9},{9,8},{10,11... | collective-permute-start | bytes 3145736 | tf_op jit(solution)/shard_map/ppermute | solution.py:313
  401.0 46.1 %collective-permute-start.7 = (bf16[2,2,2,1,64,512]{5,4,3,2,1,0:T(8,128)(2,1)S(1)}, bf16[2,2,2,1,64,512]{5,4,3,2,1,0:T(8,128)(2,1)S(1)}, u32[]{:S(2)}, u32[]{:S(2)}) collective-permute-start(bf16[2,2,2,1,64,512]{5,4,3,2,1,0:T(8,128)(2,1)S(1)} %get-tuple-element.157), channel_id=1, source_target_pairs={{0,1},{1,0},{2,3},{3,2},{4,5},{5,4},{6,7},{7,6},{8,9},{9,8},{10,11... | collective-permute-start | bytes 1572872 | tf_op jit(solution)/shard_map/ppermute | solution.py:313
  401.6 47.0 %copy-start.26 = (bf16[2,2,1,1,128,1024]{5,4,3,2,1,0:T(8,128)(2,1)S(1)}, bf16[2,2,1,1,128,1024]{5,4,3,2,1,0:T(8,128)(2,1)}, u32[]{:S(2)}) copy-start(bf16[2,2,1,1,128,1024]{5,4,3,2,1,0:T(8,128)(2,1)} %get-tuple-element.142) | copy-start | bytes 3145732
  404.2 46.7 %copy-start.44 = (f32[32,64]{1,0:T(8,128)}, f32[32,64]{1,0:T(8,128)S(1)}, u32[]{:S(2)}) copy-start(f32[32,64]{1,0:T(8,128)S(1)} %fusion.22) | copy-start | bytes 24580
  447.0 3.9 copy-start.25
  463.9 21.9 %collective-permute-start.9 = (bf16[3,1024,512]{2,1,0:T(8,128)(2,1)}, bf16[3,1024,512]{2,1,0:T(8,128)(2,1)}, u32[]{:S(2)}, u32[]{:S(2)}) collective-permute-start(bf16[3,1024,512]{2,1,0:T(8,128)(2,1)} %get-tuple-element.113), channel_id=1, source_target_pairs={{0,16},{16,0},{1,17},{17,1},{2,18},{18,2},{3,19},{19,3},{4,20},{20... | collective-permute-start | bytes 9437192 | tf_op jit(solution)/shard_map/ppermute | solution.py:313
  467.4 39.9 %collective-permute-start.17 = (bf16[2,2,1,1,64,512]{5,4,3,2,1,0:T(8,128)(2,1)}, bf16[2,2,1,1,64,512]{5,4,3,2,1,0:T(8,128)(2,1)}, u32[]{:S(2)}, u32[]{:S(2)}) collective-permute-start(bf16[2,2,1,1,64,512]{5,4,3,2,1,0:T(8,128)(2,1)} %get-tuple-element.171), channel_id=1, source_target_pairs={{0,2},{1,3},{2,0},{3,1},{4,6},{5,7},{6,4},{7,5},{8,10},{9,11},{10,... | collective-permute-start | bytes 786440 | tf_op jit(solution)/shard_map/ppermute | solution.py:313
  467.4 42.5 %collective-permute-start.14 = (bf16[2,1,1,1,128,1024]{5,4,3,2,1,0:T(8,128)(2,1)}, bf16[2,1,1,1,128,1024]{5,4,3,2,1,0:T(8,128)(2,1)}, u32[]{:S(2)}, u32[]{:S(2)}) collective-permute-start(bf16[2,1,1,1,128,1024]{5,4,3,2,1,0:T(8,128)(2,1)} %copy-done.38), channel_id=1, source_target_pairs={{0,4},{1,5},{2,6},{3,7},{4,0},{5,1},{6,2},{7,3},{8,12},{9,13},{10,... | collective-permute-start | bytes 1572872 | tf_op jit(solution)/shard_map/ppermute | solution.py:313
  469.7 43.7 %collective-permute-start.11 = (bf16[2,1,1,1,64,2048]{5,4,3,2,1,0:T(8,128)(2,1)}, bf16[2,1,1,1,64,2048]{5,4,3,2,1,0:T(8,128)(2,1)}, u32[]{:S(2)}, u32[]{:S(2)}) collective-permute-start(bf16[2,1,1,1,64,2048]{5,4,3,2,1,0:T(8,128)(2,1)} %copy-done.39), channel_id=1, source_target_pairs={{0,4},{1,5},{2,6},{3,7},{4,0},{5,1},{6,2},{7,3},{8,12},{9,13},{10,... | collective-permute-start | bytes 1572872 | tf_op jit(solution)/shard_map/ppermute | solution.py:313
  491.1 16.2 %copy-start.36 = (bf16[2,2,1,1,64,512]{5,4,3,2,1,0:T(8,128)(2,1)S(1)}, bf16[2,2,1,1,64,512]{5,4,3,2,1,0:T(8,128)(2,1)}, u32[]{:S(2)}) copy-start(bf16[2,2,1,1,64,512]{5,4,3,2,1,0:T(8,128)(2,1)} %get-tuple-element.128) | copy-start | bytes 786436
  491.1 22.3 %copy-start.32 = (bf16[2,1,1,1,64,2048]{5,4,3,2,1,0:T(8,128)(2,1)S(1)}, bf16[2,1,1,1,64,2048]{5,4,3,2,1,0:T(8,128)(2,1)}, u32[]{:S(2)}) copy-start(bf16[2,1,1,1,64,2048]{5,4,3,2,1,0:T(8,128)(2,1)} %get-tuple-element.126) | copy-start | bytes 1572868
  492.3 22.8 %copy-start.28 = (bf16[3,2,2,1,2,64,256]{6,5,4,3,2,1,0:T(8,128)(2,1)S(1)}, bf16[3,2,2,1,2,64,256]{6,5,4,3,2,1,0:T(8,128)(2,1)}, u32[]{:S(2)}) copy-start(bf16[3,2,2,1,2,64,256]{6,5,4,3,2,1,0:T(8,128)(2,1)} %get-tuple-element.160) | copy-start | bytes 2359300
  492.3 58.9 %all-to-all-start.4 = ((bf16[16,16,1024]{2,1,0:T(8,128)(2,1)}), bf16[16,16,1024]{2,1,0:T(8,128)(2,1)S(1)}, u32[]{:S(2)}, u32[]{:S(2)}) async-start(bf16[16,16,1024]{2,1,0:T(8,128)(2,1)} %get-tuple-element.125), calls=%async_computation.4 | async-start | bytes 1048576 | tf_op jit(solution)/shard_map/all_to_all | solution.py:1145
  503.8 11.2 %copy-start.29 = (bf16[3,2,2,1,2,64,256]{6,5,4,3,2,1,0:T(8,128)(2,1)S(1)}, bf16[3,2,2,1,2,64,256]{6,5,4,3,2,1,0:T(8,128)(2,1)}, u32[]{:S(2)}) copy-start(bf16[3,2,2,1,2,64,256]{6,5,4,3,2,1,0:T(8,128)(2,1)} %get-tuple-element.162) | copy-start | bytes 2359300
  503.8 42.3 %collective-permute-start.26 = (bf16[3,2,2,1,2,64,256]{6,5,0,4,3,2,1:T(8,128)(2,1)}, bf16[3,2,2,1,2,64,256]{6,5,0,4,3,2,1:T(8,128)(2,1)S(1)}, u32[]{:S(2)}, u32[]{:S(2)}) collective-permute-start(bf16[3,2,2,1,2,64,256]{6,5,0,4,3,2,1:T(8,128)(2,1)} %add_convert_fusion.11), channel_id=1, source_target_pairs={{0,2},{1,3},{2,0},{3,1},{4,6},{5,7},{6,4},{7,5},{8,10},{9,11},{10,... | collective-permute-start | bytes 2359304 | tf_op jit(solution)/shard_map/ppermute | solution.py:313
  505.8 42.8 %collective-permute-start.21 = (bf16[3,2,2,2,1,64,256]{6,5,0,4,3,2,1:T(8,128)(2,1)}, bf16[3,2,2,2,1,64,256]{6,5,0,4,3,2,1:T(8,128)(2,1)S(1)}, u32[]{:S(2)}, u32[]{:S(2)}) collective-permute-start(bf16[3,2,2,2,1,64,256]{6,5,0,4,3,2,1:T(8,128)(2,1)} %add_convert_fusion.10), channel_id=1, source_target_pairs={{0,1},{1,0},{2,3},{3,2},{4,5},{5,4},{6,7},{7,6},{8,9},{9,8},{10,11... | collective-permute-start | bytes 2359304 | tf_op jit(solution)/shard_map/ppermute | solution.py:313
  508.3 12.8 %copy-start.27 = (bf16[3,2,2,2,1,64,256]{6,5,4,3,2,1,0:T(8,128)(2,1)S(1)}, bf16[3,2,2,2,1,64,256]{6,5,4,3,2,1,0:T(8,128)(2,1)}, u32[]{:S(2)}) copy-start(bf16[3,2,2,2,1,64,256]{6,5,4,3,2,1,0:T(8,128)(2,1)} %get-tuple-element.168) | copy-start | bytes 2359300
  508.3 8.3 %collective-permute-start.18 = (bf16[2,1,1,1,64,512]{5,4,3,2,1,0:T(8,128)(2,1)S(1)}, bf16[2,1,1,1,64,512]{5,4,3,2,1,0:T(8,128)(2,1)S(1)}, u32[]{:S(2)}, u32[]{:S(2)}) collective-permute-start(bf16[2,1,1,1,64,512]{5,4,3,2,1,0:T(8,128)(2,1)S(1)} %get-tuple-element.179), channel_id=1, source_target_pairs={{0,4},{1,5},{2,6},{3,7},{4,0},{5,1},{6,2},{7,3},{8,12},{9,13},{10,... | collective-permute-start | bytes 393224 | tf_op jit(solution)/shard_map/ppermute | solution.py:313
  511.0 32.4 %collective-permute-start.15 = (bf16[1,1,1,1,128,1024]{5,4,3,2,1,0:T(8,128)(2,1)S(1)}, bf16[1,1,1,1,128,1024]{5,4,3,2,1,0:T(8,128)(2,1)S(1)}, u32[]{:S(2)}, u32[]{:S(2)}) collective-permute-start(bf16[1,1,1,1,128,1024]{5,4,3,2,1,0:T(8,128)(2,1)S(1)} %add_convert_fusion.23), channel_id=1, source_target_pairs={{0,8},{1,9},{2,10},{3,11},{4,12},{5,13},{6,14},{7,15},{8,0},{9,1},... | collective-permute-start | bytes 786440 | tf_op jit(solution)/shard_map/ppermute | solution.py:313
  514.4 30.6 %collective-permute-start.12 = (bf16[1,1,1,1,64,2048]{5,4,3,2,1,0:T(8,128)(2,1)S(1)}, bf16[1,1,1,1,64,2048]{5,4,3,2,1,0:T(8,128)(2,1)S(1)}, u32[]{:S(2)}, u32[]{:S(2)}) collective-permute-start(bf16[1,1,1,1,64,2048]{5,4,3,2,1,0:T(8,128)(2,1)S(1)} %add_convert_fusion.26), channel_id=1, source_target_pairs={{0,8},{1,9},{2,10},{3,11},{4,12},{5,13},{6,14},{7,15},{8,0},{9,1},... | collective-permute-start | bytes 786440 | tf_op jit(solution)/shard_map/ppermute | solution.py:313
  515.1 28.4 %copy-start.34 = (bf16[2,1,1,1,128,1024]{5,4,3,2,1,0:T(8,128)(2,1)S(1)}, bf16[2,1,1,1,128,1024]{5,4,3,2,1,0:T(8,128)(2,1)}, u32[]{:S(2)}) copy-start(bf16[2,1,1,1,128,1024]{5,4,3,2,1,0:T(8,128)(2,1)} %get-tuple-element.127) | copy-start | bytes 1572868
  515.3 29.8 %copy-start.33 = (bf16[2,1,1,1,64,2048]{5,4,3,2,1,0:T(8,128)(2,1)S(1)}, bf16[2,1,1,1,64,2048]{5,4,3,2,1,0:T(8,128)(2,1)}, u32[]{:S(2)}) copy-start(bf16[2,1,1,1,64,2048]{5,4,3,2,1,0:T(8,128)(2,1)} %get-tuple-element.126) | copy-start | bytes 1572868
  516.6 26.7 %collective-permute-start.19 = (bf16[1,1,1,1,64,512]{5,4,3,2,1,0:T(8,128)(2,1)S(1)}, bf16[1,1,1,1,64,512]{5,4,3,2,1,0:T(8,128)(2,1)S(1)}, u32[]{:S(2)}, u32[]{:S(2)}) collective-permute-start(bf16[1,1,1,1,64,512]{5,4,3,2,1,0:T(8,128)(2,1)S(1)} %add_convert_fusion.43), channel_id=1, source_target_pairs={{0,8},{1,9},{2,10},{3,11},{4,12},{5,13},{6,14},{7,15},{8,0},{9,1},... | collective-permute-start | bytes 196616 | tf_op jit(solution)/shard_map/ppermute | solution.py:313
  543.3 43.0 %collective-permute-start.20 = (bf16[64,512]{1,0:T(8,128)(2,1)S(1)}, bf16[64,512]{1,0:T(8,128)(2,1)S(1)}, u32[]{:S(2)}, u32[]{:S(2)}) collective-permute-start(bf16[64,512]{1,0:T(8,128)(2,1)S(1)} %fusion.36.refs_4_), channel_id=1, source_target_pairs={{0,16},{16,0},{1,17},{17,1},{2,18},{18,2},{3,19},{19,3},{4,20},{20... | collective-permute-start | bytes 196616 | tf_op jit(solution)/shard_map/ppermute | solution.py:313
  544.5 41.8 %collective-permute-start.16 = (bf16[128,1024]{1,0:T(8,128)(2,1)S(1)}, bf16[128,1024]{1,0:T(8,128)(2,1)S(1)}, u32[]{:S(2)}, u32[]{:S(2)}) collective-permute-start(bf16[128,1024]{1,0:T(8,128)(2,1)S(1)} %fusion.27.refs_2_), channel_id=1, source_target_pairs={{0,16},{16,0},{1,17},{17,1},{2,18},{18,2},{3,19},{19,3},{4,20},{20... | collective-permute-start | bytes 786440 | tf_op jit(solution)/shard_map/ppermute | solution.py:313
  547.2 11.4 %collective-permute-start.27 = (bf16[3,2,2,1,1,64,256]{6,5,0,4,3,2,1:T(8,128)(2,1)}, bf16[3,2,2,1,1,64,256]{6,5,0,4,3,2,1:T(8,128)(2,1)}, u32[]{:S(2)}, u32[]{:S(2)}) collective-permute-start(bf16[3,2,2,1,1,64,256]{6,5,0,4,3,2,1:T(8,128)(2,1)} %get-tuple-element.159), channel_id=1, source_target_pairs={{0,1},{1,0},{2,3},{3,2},{4,5},{5,4},{6,7},{7,6},{8,9},{9,8},{10,11... | collective-permute-start | bytes 1179656 | tf_op jit(solution)/shard_map/ppermute | solution.py:313
  549.7 11.0 %collective-permute-start.22 = (bf16[3,2,2,1,1,64,256]{6,5,0,4,3,2,1:T(8,128)(2,1)}, bf16[3,2,2,1,1,64,256]{6,5,0,4,3,2,1:T(8,128)(2,1)S(1)}, u32[]{:S(2)}, u32[]{:S(2)}) collective-permute-start(bf16[3,2,2,1,1,64,256]{6,5,0,4,3,2,1:T(8,128)(2,1)} %get-tuple-element.165), channel_id=1, source_target_pairs={{0,2},{1,3},{2,0},{3,1},{4,6},{5,7},{6,4},{7,5},{8,10},{9,11},{10,... | collective-permute-start | bytes 1179656 | tf_op jit(solution)/shard_map/ppermute | solution.py:313
  553.8 9.5 %collective-permute-start.10 = (bf16[16,8,1024]{2,1,0:T(8,128)(2,1)S(1)}, bf16[16,8,1024]{2,1,0:T(8,128)(2,1)S(1)}, u32[]{:S(2)}, u32[]{:S(2)}) collective-permute-start(bf16[16,8,1024]{2,1,0:T(8,128)(2,1)S(1)} %slice.320), channel_id=1, source_target_pairs={{0,16},{16,0},{1,17},{17,1},{2,18},{18,2},{3,19},{19,3},{4,20},{20... | collective-permute-start | bytes 786440 | tf_op jit(solution)/shard_map/ppermute | solution.py:313
  558.6 27.7 %collective-permute-start.13 = (bf16[64,2048]{1,0:T(8,128)(2,1)S(1)}, bf16[64,2048]{1,0:T(8,128)(2,1)S(1)}, u32[]{:S(2)}, u32[]{:S(2)}) collective-permute-start(bf16[64,2048]{1,0:T(8,128)(2,1)S(1)} %fusion.26.refs_0_), channel_id=1, source_target_pairs={{0,16},{16,0},{1,17},{17,1},{2,18},{18,2},{3,19},{19,3},{4,20},{20... | collective-permute-start | bytes 786440 | tf_op jit(solution)/shard_map/ppermute | solution.py:313
  560.7 11.3 %collective-permute-start.28 = (bf16[3,2,1,1,1,64,256]{6,5,0,4,3,2,1:T(8,128)(2,1)}, bf16[3,2,1,1,1,64,256]{6,5,0,4,3,2,1:T(8,128)(2,1)}, u32[]{:S(2)}, u32[]{:S(2)}) collective-permute-start(bf16[3,2,1,1,1,64,256]{6,5,0,4,3,2,1:T(8,128)(2,1)} %get-tuple-element.175), channel_id=1, source_target_pairs={{0,4},{1,5},{2,6},{3,7},{4,0},{5,1},{6,2},{7,3},{8,12},{9,13},{10,... | collective-permute-start | bytes 589832 | tf_op jit(solution)/shard_map/ppermute | solution.py:313
  561.4 7.6 %copy-start.23 = (f32[64,4096]{1,0:T(8,128)S(1)}, f32[64,4096]{1,0:T(8,128)}, u32[]{:S(2)}) copy-start(f32[64,4096]{1,0:T(8,128)} %copy-done.22) | copy-start | bytes 3145732
  563.3 10.4 %collective-permute-start.23 = (bf16[3,2,1,1,1,64,256]{6,5,0,4,3,2,1:T(8,128)(2,1)}, bf16[3,2,1,1,1,64,256]{6,5,0,4,3,2,1:T(8,128)(2,1)}, u32[]{:S(2)}, u32[]{:S(2)}) collective-permute-start(bf16[3,2,1,1,1,64,256]{6,5,0,4,3,2,1:T(8,128)(2,1)} %get-tuple-element.177), channel_id=1, source_target_pairs={{0,4},{1,5},{2,6},{3,7},{4,0},{5,1},{6,2},{7,3},{8,12},{9,13},{10,... | collective-permute-start | bytes 589832 | tf_op jit(solution)/shard_map/ppermute | solution.py:313
  567.9 3.0 copy-start.42
  568.0 3.0 copy-start.43
  568.0 3.0 copy-start.45
  569.0 16.6 %copy-start.46 = (f32[4096]{0:T(1024)S(1)}, f32[4096]{0:T(1024)}, u32[]{:S(2)}) copy-start(f32[4096]{0:T(1024)} %get-tuple-element.248) | copy-start | bytes 49156
  572.9 10.1 %collective-permute-start.29 = (bf16[3,1,1,1,1,64,256]{6,5,0,4,3,2,1:T(8,128)(2,1)S(1)}, bf16[3,1,1,1,1,64,256]{6,5,0,4,3,2,1:T(8,128)(2,1)S(1)}, u32[]{:S(2)}, u32[]{:S(2)}) collective-permute-start(bf16[3,1,1,1,1,64,256]{6,5,0,4,3,2,1:T(8,128)(2,1)S(1)} %add_convert_fusion.37), channel_id=1, source_target_pairs={{0,8},{1,9},{2,10},{3,11},{4,12},{5,13},{6,14},{7,15},{8,0},{9,1},... | collective-permute-start | bytes 294920 | tf_op jit(solution)/shard_map/ppermute | solution.py:313
  574.6 10.0 %collective-permute-start.24 = (bf16[3,1,1,1,1,64,256]{6,5,0,4,3,2,1:T(8,128)(2,1)S(1)}, bf16[3,1,1,1,1,64,256]{6,5,0,4,3,2,1:T(8,128)(2,1)S(1)}, u32[]{:S(2)}, u32[]{:S(2)}) collective-permute-start(bf16[3,1,1,1,1,64,256]{6,5,0,4,3,2,1:T(8,128)(2,1)S(1)} %add_convert_fusion.40), channel_id=1, source_target_pairs={{0,8},{1,9},{2,10},{3,11},{4,12},{5,13},{6,14},{7,15},{8,0},{9,1},... | collective-permute-start | bytes 294920 | tf_op jit(solution)/shard_map/ppermute | solution.py:313
  584.0 2.3 collective-permute-start.30
  585.5 1.4 collective-permute-start.25
  (23 other events, 33.4 us)
